TPU v7x, 32 devices: a whole 2x2x4 slice. The times are simulated.
32 devices in a mesh: ctx: 8 (over z, y), shard: 4 (over x, core).
Axes of the slice: x: 2, y: 2, z: 4, core: 2. Of those that a mesh axis runs over, the one named last changes fastest.
Arguments:
- tokens: bfloat16 [4, 1024, 768], P('shard', 'ctx'), may hold values from -6 to 6
- cotangent: bfloat16 [4, 1024, 768], P('shard', 'ctx'), may hold values from -6 to 6
- seq_ids: int32 [4, 1024], P('shard', 'ctx'), may hold values from 0 to 2, never falling along the last dimension, each value on 1 to 512 neighbouring positions
- w_query: bfloat16 [768, 768], P('shard'), may hold values from -0.3125 to 0.3125
- b_query: bfloat16 [768], P('shard'), may hold values from -3 to 3
- w_key: bfloat16 [768, 768], P('shard'), may hold values from -0.3125 to 0.3125
- w_value: bfloat16 [768, 768], P('shard'), may hold values from -0.21875 to 0.21875
- b_value: bfloat16 [768], P('shard'), may hold values from -3 to 3
- w_out: bfloat16 [768, 768], P('shard'), may hold values from -0.875 to 0.875
- b_out: bfloat16 [768], P('shard'), may hold values from -1.75 to 1.75
- attn_gain: bfloat16 [768], P('shard'), may hold values from 0.099609375 to 1.8984375
- attn_shift: bfloat16 [768], P('shard'), may hold values from -3 to 3
- w_up: bfloat16 [768, 3072], P('shard'), may hold values from -0.21875 to 0.21875
- b_up: bfloat16 [3072], P('shard'), may hold values from -3 to 3
- w_down: bfloat16 [3072, 768], P('shard'), may hold values from -0.15625 to 0.15625
- b_down: bfloat16 [768], P('shard'), may hold values from -3 to 3
- ffn_gain: bfloat16 [768], P('shard'), may hold values from 0.099609375 to 1.8984375
- ffn_shift: bfloat16 [768], P('shard'), may hold values from -3 to 3
Outputs:
- hidden_out: bfloat16 [4, 1024, 768], P('shard', 'ctx')
- tokens_grad: bfloat16 [4, 1024, 768], P('shard', 'ctx')
- w_query_grad: float32 [768, 768], P('shard')
- b_query_grad: float32 [768], P('shard')
- w_key_grad: float32 [768, 768], P('shard')
- w_value_grad: float32 [768, 768], P('shard')
- b_value_grad: float32 [768], P('shard')
- w_out_grad: float32 [768, 768], P('shard')
- b_out_grad: float32 [768], P('shard')
- attn_gain_grad: float32 [768], P('shard')
- attn_shift_grad: float32 [768], P('shard')
- w_up_grad: float32 [768, 3072], P('shard')
- b_up_grad: float32 [3072], P('shard')
- w_down_grad: float32 [3072, 768], P('shard')
- b_down_grad: float32 [768], P('shard')
- ffn_gain_grad: float32 [768], P('shard')
- ffn_shift_grad: float32 [768], P('shard')
Inputs may be any that keep to these rules, and one draw needn't show every extreme that they name: `seq_ids`: in each group ids never fall along the tokens; each sequence has 1 to 512 tokens, one exactly 512.
All inputs are finite; a program needn't handle non-finite values.
Results may differ from a plain program's by a relative error of at most 0.035.
Values may be sent and summed in bfloat16 or wider, within the bound.
No kernel may reach another device: no remote copies, remote signals or barrier semaphores. Data moves between devices by JAX's collectives and lax.ppermute only.
A program may use at most 128 MiB of HBM per device.

v0:
```python
import math

import jax
import jax.numpy as jnp
from jax import lax
from jax.sharding import PartitionSpec as P

HEAD_DIM = 64


ln_eps = 1e-12
masked_fill = -1e30


def from_behind(block, axis, distance):
    devices = range(lax.axis_size(axis))
    route = [((i - distance) % len(devices), i) for i in devices]
    return lax.ppermute(block, axis, route)


def matmul(left, right):
    return jnp.dot(left, right, preferred_element_type=jnp.float32)


def matmul_tn(left, right):
    return lax.dot_general(
        left, right, (((0,), (0,)), ((), ())), preferred_element_type=jnp.float32
    )


def matmul_nt(left, right):
    return lax.dot_general(
        left, right, (((1,), (1,)), ((), ())), preferred_element_type=jnp.float32
    )


def apply_layer_norm(value, gain, shift):
    mean = jnp.mean(value, axis=-1, keepdims=True)
    centered = value - mean
    rstd = lax.rsqrt(jnp.mean(centered * centered, axis=-1, keepdims=True) + ln_eps)
    normed = centered * rstd
    return (normed * gain + shift, normed, rstd)


def norm_back(grad, normed, rstd, gain):
    d_gain = jnp.sum(grad * normed, axis=0)
    d_shift = jnp.sum(grad, axis=0)
    scaled = grad * gain
    d_value = rstd * (
        scaled
        - jnp.mean(scaled, axis=-1, keepdims=True)
        - normed * jnp.mean(scaled * normed, axis=-1, keepdims=True)
    )
    return (d_value, d_gain, d_shift)


def gelu_slope(value):
    normal_cdf = 0.5 * (1.0 + lax.erf(value * (1.0 / math.sqrt(2.0))))
    density = jnp.exp(-0.5 * value * value) * (1.0 / math.sqrt(2.0 * math.pi))
    return normal_cdf + value * density


def scores_of(query, keys, q_ids, k_ids, scale):
    raw = jnp.einsum("qhd,khd->hqk", query, keys, preferred_element_type=jnp.float32) * scale
    match = (q_ids[:, None] == k_ids[None, :])[None, :, :]
    return (raw, match)


def attend(query, q_ids, keys, values, k_ids, stats, scale):
    top, total, accum = stats
    raw, match = scores_of(query, keys, q_ids, k_ids, scale)
    masked = jnp.where(match, raw, masked_fill)
    new_top = jnp.maximum(top, jnp.max(masked, axis=-1))
    weights = jnp.where(match, jnp.exp(masked - new_top[:, :, None]), 0.0)
    factor = jnp.exp(top - new_top)
    total = total * factor + jnp.sum(weights, axis=-1)
    accum = accum * factor[:, :, None] + jnp.einsum(
        "hqk,khd->hqd", weights.astype(jnp.bfloat16), values, preferred_element_type=jnp.float32
    )
    return (new_top, total, accum)


def block_grads(query, q_ids, d_out, log_total, delta, keys, values, k_ids, scale):
    raw, match = scores_of(query, keys, q_ids, k_ids, scale)
    probs = jnp.exp(jnp.where(match, raw - log_total[:, :, None], masked_fill))
    d_values = jnp.einsum(
        "hqk,qhd->khd", probs.astype(jnp.bfloat16), d_out, preferred_element_type=jnp.float32
    )
    d_probs = jnp.einsum("qhd,khd->hqk", d_out, values, preferred_element_type=jnp.float32)
    d_scores = (probs * (d_probs - delta[:, :, None])).astype(jnp.bfloat16)
    d_query = jnp.einsum("hqk,khd->qhd", d_scores, keys, preferred_element_type=jnp.float32) * scale
    d_keys = jnp.einsum("hqk,qhd->khd", d_scores, query, preferred_element_type=jnp.float32) * scale
    return (d_query, d_keys, d_values)


def local(
    tokens,
    cotangent,
    seq_ids,
    w_query,
    b_query,
    w_key,
    w_value,
    b_value,
    w_out,
    b_out,
    attn_gain,
    attn_shift,
    w_up,
    b_up,
    w_down,
    b_down,
    ffn_gain,
    ffn_shift,
):
    cycle = lax.axis_size("ctx")
    tok_rows = tokens.shape[1]
    width = tokens.shape[2]
    heads = width // HEAD_DIM
    scale = 1.0 / math.sqrt(HEAD_DIM)
    share = tok_rows // cycle
    got_tokens, got_grads, got_ids = (
        lax.all_to_all(
            tokens[0].reshape(share, cycle, width), "ctx", split_axis=1, concat_axis=1, tiled=True
        ),
        lax.all_to_all(
            cotangent[0].reshape(share, cycle, width),
            "ctx",
            split_axis=1,
            concat_axis=1,
            tiled=True,
        ),
        lax.all_to_all(
            seq_ids[0].reshape(share, cycle), "ctx", split_axis=1, concat_axis=1, tiled=True
        ),
    )
    x_local = got_tokens.reshape(tok_rows, width)
    local_gradient = got_grads.reshape(tok_rows, width).astype(jnp.float32)
    local_ids = got_ids.reshape(tok_rows)
    (
        query_mat,
        query_bias,
        key_mat,
        value_mat,
        value_bias,
        out_mat,
        out_bias,
        attention_norm_gain,
        first_shift,
        up_mat,
        up_bias,
        down_mat,
        down_bias,
        feedforward_norm_gain,
        second_shift,
    ) = (
        lax.all_gather(w_query, "shard", axis=0, tiled=True),
        lax.all_gather(b_query, "shard", axis=0, tiled=True),
        lax.all_gather(w_key, "shard", axis=0, tiled=True),
        lax.all_gather(w_value, "shard", axis=0, tiled=True),
        lax.all_gather(b_value, "shard", axis=0, tiled=True),
        lax.all_gather(w_out, "shard", axis=0, tiled=True),
        lax.all_gather(b_out, "shard", axis=0, tiled=True),
        lax.all_gather(attn_gain, "shard", axis=0, tiled=True),
        lax.all_gather(attn_shift, "shard", axis=0, tiled=True),
        lax.all_gather(w_up, "shard", axis=0, tiled=True),
        lax.all_gather(b_up, "shard", axis=0, tiled=True),
        lax.all_gather(w_down, "shard", axis=0, tiled=True),
        lax.all_gather(b_down, "shard", axis=0, tiled=True),
        lax.all_gather(ffn_gain, "shard", axis=0, tiled=True),
        lax.all_gather(ffn_shift, "shard", axis=0, tiled=True),
    )
    query = (matmul(x_local, query_mat) + query_bias.astype(jnp.float32)).astype(jnp.bfloat16)
    keys = matmul(x_local, key_mat).astype(jnp.bfloat16)
    values = (matmul(x_local, value_mat) + value_bias.astype(jnp.float32)).astype(jnp.bfloat16)
    q_heads = query.reshape(tok_rows, heads, HEAD_DIM)
    start_stats = (
        jnp.full((heads, tok_rows), masked_fill, jnp.float32),
        jnp.zeros((heads, tok_rows), jnp.float32),
        jnp.zeros((heads, tok_rows, HEAD_DIM), jnp.float32),
    )

    def forward_step(step, carry):
        block, stats = carry
        stats = attend(
            q_heads,
            local_ids,
            block[0].reshape(tok_rows, heads, HEAD_DIM),
            block[1].reshape(tok_rows, heads, HEAD_DIM),
            block[2],
            stats,
            scale,
        )
        block = from_behind((block[0], block[1], block[2]), "ctx", 1)
        return (block, stats)

    block, stats = lax.fori_loop(
        0, cycle - 1, forward_step, ((keys, values, local_ids), start_stats)
    )
    top, total, accum = attend(
        q_heads,
        local_ids,
        block[0].reshape(tok_rows, heads, HEAD_DIM),
        block[1].reshape(tok_rows, heads, HEAD_DIM),
        block[2],
        stats,
        scale,
    )
    attn_out = (
        (accum / total[:, :, None]).transpose(1, 0, 2).reshape(tok_rows, width).astype(jnp.bfloat16)
    )
    log_total = top + jnp.log(total)
    attn_proj = matmul(attn_out, out_mat) + out_bias.astype(jnp.float32)
    first_sum = x_local.astype(jnp.float32) + attn_proj
    first_normalized_rows, first_centered_scaled, first_inverse_deviation = apply_layer_norm(
        first_sum, attention_norm_gain.astype(jnp.float32), first_shift.astype(jnp.float32)
    )
    normed_low = first_normalized_rows.astype(jnp.bfloat16)
    up_pre = matmul(normed_low, up_mat) + up_bias.astype(jnp.float32)
    up_act = jax.nn.gelu(up_pre, approximate=False).astype(jnp.bfloat16)
    down_pre = matmul(up_act, down_mat) + down_bias.astype(jnp.float32)
    layer_output, second_centered_scaled, second_inverse_deviation = apply_layer_norm(
        first_normalized_rows + down_pre,
        feedforward_norm_gain.astype(jnp.float32),
        second_shift.astype(jnp.float32),
    )
    (
        query_mat,
        key_mat,
        value_mat,
        out_mat,
        attention_norm_gain,
        up_mat,
        down_mat,
        feedforward_norm_gain,
    ) = (
        lax.all_gather(w_query, "shard", axis=0, tiled=True),
        lax.all_gather(w_key, "shard", axis=0, tiled=True),
        lax.all_gather(w_value, "shard", axis=0, tiled=True),
        lax.all_gather(w_out, "shard", axis=0, tiled=True),
        lax.all_gather(attn_gain, "shard", axis=0, tiled=True),
        lax.all_gather(w_up, "shard", axis=0, tiled=True),
        lax.all_gather(w_down, "shard", axis=0, tiled=True),
        lax.all_gather(ffn_gain, "shard", axis=0, tiled=True),
    )
    grad_two, d_second_gain, d_second_shift = norm_back(
        local_gradient,
        second_centered_scaled,
        second_inverse_deviation,
        feedforward_norm_gain.astype(jnp.float32),
    )
    grad_down = grad_two.astype(jnp.bfloat16)
    d_down_bias = jnp.sum(grad_down, axis=0, dtype=jnp.float32)
    d_down_mat = matmul_tn(up_act, grad_down)
    grad_up = (matmul_nt(grad_down, down_mat) * gelu_slope(up_pre)).astype(jnp.bfloat16)
    d_up_bias = jnp.sum(grad_up, axis=0, dtype=jnp.float32)
    d_up_mat = matmul_tn(normed_low, grad_up)
    first_norm_gradient = grad_two + matmul_nt(grad_up, up_mat)
    grad_first, d_first_gain, d_first_shift = norm_back(
        first_norm_gradient,
        first_centered_scaled,
        first_inverse_deviation,
        attention_norm_gain.astype(jnp.float32),
    )
    grad_proj = grad_first.astype(jnp.bfloat16)
    d_out_bias = jnp.sum(grad_proj, axis=0, dtype=jnp.float32)
    d_out_mat = matmul_tn(attn_out, grad_proj)
    grad_attn = matmul_nt(grad_proj, out_mat).astype(jnp.bfloat16)
    grad_heads = grad_attn.reshape(tok_rows, heads, HEAD_DIM)
    delta = jnp.einsum(
        "qhd,qhd->hq",
        grad_heads,
        attn_out.reshape(tok_rows, heads, HEAD_DIM),
        preferred_element_type=jnp.float32,
    )
    zero_rows = jnp.zeros((tok_rows, width), jnp.float32)

    def key_step(step, carry):
        block, sums, acc_query = carry
        d_query, d_keys, d_values = block_grads(
            q_heads,
            local_ids,
            grad_heads,
            log_total,
            delta,
            block[0].reshape(tok_rows, heads, HEAD_DIM),
            block[1].reshape(tok_rows, heads, HEAD_DIM),
            block[2],
            scale,
        )
        sums = (
            sums[0] + d_keys.reshape(tok_rows, width),
            sums[1] + d_values.reshape(tok_rows, width),
        )
        block = from_behind((block[0], block[1], block[2]), "ctx", 1)
        sums = (
            from_behind(sums[0].astype(jnp.bfloat16), "ctx", 1).astype(jnp.float32),
            from_behind(sums[1].astype(jnp.bfloat16), "ctx", 1).astype(jnp.float32),
        )
        return (block, sums, acc_query + d_query.reshape(tok_rows, width))

    block, sums, d_query_sum = lax.fori_loop(
        0, cycle, key_step, ((keys, values, local_ids), (zero_rows, zero_rows), zero_rows)
    )
    d_keys_sum, d_values_sum = sums
    grad_query = d_query_sum.astype(jnp.bfloat16)
    grad_keys = d_keys_sum.astype(jnp.bfloat16)
    grad_values = d_values_sum.astype(jnp.bfloat16)
    d_query_bias = jnp.sum(grad_query, axis=0, dtype=jnp.float32)
    d_value_bias = jnp.sum(grad_values, axis=0, dtype=jnp.float32)
    d_query_mat = matmul_tn(x_local, grad_query)
    d_key_mat = matmul_tn(x_local, grad_keys)
    d_value_mat = matmul_tn(x_local, grad_values)
    grad_input = (
        grad_first
        + matmul_nt(grad_query, query_mat)
        + matmul_nt(grad_keys, key_mat)
        + matmul_nt(grad_values, value_mat)
    )
    home_hidden, home_grad = (
        lax.all_to_all(
            layer_output.astype(jnp.bfloat16).reshape(share, cycle, width),
            "ctx",
            split_axis=1,
            concat_axis=1,
            tiled=True,
        ),
        lax.all_to_all(
            grad_input.astype(jnp.bfloat16).reshape(share, cycle, width),
            "ctx",
            split_axis=1,
            concat_axis=1,
            tiled=True,
        ),
    )
    hidden_out = home_hidden.reshape(tok_rows, width)[None]
    tokens_grad = home_grad.reshape(tok_rows, width)[None]
    shares = (
        lax.psum_scatter(
            d_query_mat.astype(jnp.bfloat16), "shard", scatter_dimension=0, tiled=True
        ).astype(jnp.float32),
        lax.psum_scatter(
            d_query_bias.astype(jnp.bfloat16), "shard", scatter_dimension=0, tiled=True
        ).astype(jnp.float32),
        lax.psum_scatter(
            d_key_mat.astype(jnp.bfloat16), "shard", scatter_dimension=0, tiled=True
        ).astype(jnp.float32),
        lax.psum_scatter(
            d_value_mat.astype(jnp.bfloat16), "shard", scatter_dimension=0, tiled=True
        ).astype(jnp.float32),
        lax.psum_scatter(
            d_value_bias.astype(jnp.bfloat16), "shard", scatter_dimension=0, tiled=True
        ).astype(jnp.float32),
        lax.psum_scatter(
            d_out_mat.astype(jnp.bfloat16), "shard", scatter_dimension=0, tiled=True
        ).astype(jnp.float32),
        lax.psum_scatter(
            d_out_bias.astype(jnp.bfloat16), "shard", scatter_dimension=0, tiled=True
        ).astype(jnp.float32),
        lax.psum_scatter(
            d_first_gain.astype(jnp.bfloat16), "shard", scatter_dimension=0, tiled=True
        ).astype(jnp.float32),
        lax.psum_scatter(
            d_first_shift.astype(jnp.bfloat16), "shard", scatter_dimension=0, tiled=True
        ).astype(jnp.float32),
        lax.psum_scatter(
            d_up_mat.astype(jnp.bfloat16), "shard", scatter_dimension=0, tiled=True
        ).astype(jnp.float32),
        lax.psum_scatter(
            d_up_bias.astype(jnp.bfloat16), "shard", scatter_dimension=0, tiled=True
        ).astype(jnp.float32),
        lax.psum_scatter(
            d_down_mat.astype(jnp.bfloat16), "shard", scatter_dimension=0, tiled=True
        ).astype(jnp.float32),
        lax.psum_scatter(
            d_down_bias.astype(jnp.bfloat16), "shard", scatter_dimension=0, tiled=True
        ).astype(jnp.float32),
        lax.psum_scatter(
            d_second_gain.astype(jnp.bfloat16), "shard", scatter_dimension=0, tiled=True
        ).astype(jnp.float32),
        lax.psum_scatter(
            d_second_shift.astype(jnp.bfloat16), "shard", scatter_dimension=0, tiled=True
        ).astype(jnp.float32),
    )
    totals = lax.psum(
        (
            shares[0],
            shares[1],
            shares[2],
            shares[3],
            shares[4],
            shares[5],
            shares[6],
            shares[7],
            shares[8],
            shares[9],
            shares[10],
            shares[11],
            shares[12],
            shares[13],
            shares[14],
        ),
        "ctx",
    )
    return (hidden_out, tokens_grad) + tuple(totals)


def solution(mesh):
    return jax.shard_map(
        local,
        mesh=mesh,
        in_specs=(
            P("shard", "ctx", None),
            P("shard", "ctx", None),
            P("shard", "ctx"),
            P("shard", None),
            P("shard"),
            P("shard", None),
            P("shard", None),
            P("shard"),
            P("shard", None),
            P("shard"),
            P("shard"),
            P("shard"),
            P("shard", None),
            P("shard"),
            P("shard", None),
            P("shard"),
            P("shard"),
            P("shard"),
        ),
        out_specs=(
            P("shard", "ctx", None),
            P("shard", "ctx", None),
            P("shard", None),
            P("shard"),
            P("shard", None),
            P("shard", None),
            P("shard"),
            P("shard", None),
            P("shard"),
            P("shard"),
            P("shard"),
            P("shard", None),
            P("shard"),
            P("shard", None),
            P("shard"),
            P("shard"),
            P("shard"),
        ),
        check_vma=False,
    )
```

profile of v0, /device:TPU:0, one launch (start us, length us, event | category | flops | bytes accessed | tf_op | source)
XLA Modules:
  0.0 870.6 jit_solution(6538694910349278965)
XLA Ops:
  12.6 7.3 all-to-all-start.1
  20.6 5.7 all-to-all-done.1
  26.3 3.4 all-to-all-start.3
  33.3 10.9 %all-reduce.19 = (bf16[768]{0:T(1024)(128)(2,1)S(1)}, bf16[768]{0:T(1024)(128)(2,1)S(1)}, bf16[768]{0:T(1024)(128)(2,1)S(1)}, bf16[768]{0:T(1024)(128)(2,1)S(1)}...) all-reduce(bf16[768]{0:T(1024)(128)(2,1)S(1)} %dynamic-update-slice, ...), channel_id=1, replica_groups=mesh['ctx'=8,'shard'=4] {'shard'}, use_global_device_ids=true, to_apply=%add | all-reduce | flops 5376 | bytes 21504
  44.2 5.2 all-gather
  52.2 5.6 all-to-all-start
  58.8 7.4 all-to-all-done
  66.3 1.7 convolution_convert_fusion.7
  69.7 1.6 fusion.41
  73.1 1.6 fusion.42
  74.8 81.0 %while.44 = (s32[]{:T(128)}, bf16[128,768]{0,1:T(8,128)(2,1)S(1)}, bf16[128,768]{0,1:T(8,128)(2,1)S(1)}, s32[128]{0:T(128)S(1)}, f32[12,128]{1,0:T(8,128)S(1)}, ...) while((s32[]{:T(128)}, bf16[128,768]{0,1:T(8,128)(2,1)S(1)}, ...), condition=%wide.wide.region_3.4_spmd.clone, body=%wide.wide.region_0.3_spmd.clone.sunk | while | flops 52420096 | bytes 6263033 | solution.py:197
  78.9 8.6 collective-permute-done.2
  89.0 10.0 %collective-permute-done.2 = s32[128]{0:T(128)S(1)} collective-permute-done((s32[128]{0:T(128)S(1)}, s32[128]{0:T(128)S(1)}, u32[]{:S(2)}, u32[]{:S(2)}) %collective-permute-start.2) | collective-permute-done | bytes 544 | tf_op jit(solution)/shard_map/while/body/eval_jaxpr/ppermute | solution.py:18
  100.2 9.5 %collective-permute-done.2 = s32[128]{0:T(128)S(1)} collective-permute-done((s32[128]{0:T(128)S(1)}, s32[128]{0:T(128)S(1)}, u32[]{:S(2)}, u32[]{:S(2)}) %collective-permute-start.2) | collective-permute-done | bytes 544 | tf_op jit(solution)/shard_map/while/body/eval_jaxpr/ppermute | solution.py:18
  110.8 9.6 %collective-permute-done.2 = s32[128]{0:T(128)S(1)} collective-permute-done((s32[128]{0:T(128)S(1)}, s32[128]{0:T(128)S(1)}, u32[]{:S(2)}, u32[]{:S(2)}) %collective-permute-start.2) | collective-permute-done | bytes 544 | tf_op jit(solution)/shard_map/while/body/eval_jaxpr/ppermute | solution.py:18
  121.6 10.7 %collective-permute-done.2 = s32[128]{0:T(128)S(1)} collective-permute-done((s32[128]{0:T(128)S(1)}, s32[128]{0:T(128)S(1)}, u32[]{:S(2)}, u32[]{:S(2)}) %collective-permute-start.2) | collective-permute-done | bytes 544 | tf_op jit(solution)/shard_map/while/body/eval_jaxpr/ppermute | solution.py:18
  133.4 11.8 %collective-permute-done.2 = s32[128]{0:T(128)S(1)} collective-permute-done((s32[128]{0:T(128)S(1)}, s32[128]{0:T(128)S(1)}, u32[]{:S(2)}, u32[]{:S(2)}) %collective-permute-start.2) | collective-permute-done | bytes 544 | tf_op jit(solution)/shard_map/while/body/eval_jaxpr/ppermute | solution.py:18
  146.3 9.4 %collective-permute-done.2 = s32[128]{0:T(128)S(1)} collective-permute-done((s32[128]{0:T(128)S(1)}, s32[128]{0:T(128)S(1)}, u32[]{:S(2)}, u32[]{:S(2)}) %collective-permute-start.2) | collective-permute-done | bytes 544 | tf_op jit(solution)/shard_map/while/body/eval_jaxpr/ppermute | solution.py:18
  157.9 1.8 fusion.84
  160.0 7.7 fusion.21
  167.6 3.5 fusion.85
  173.2 2.3 fusion.86
  175.6 2.3 multiply_reduce_fusion
  180.3 166.6 %while.45 = (s32[]{:T(128)}, bf16[128,768]{0,1:T(8,128)(2,1)}, bf16[128,768]{0,1:T(8,128)(2,1)}, s32[128]{0:T(128)}, f32[128,768]{0,1:T(8,128)S(1)}, /*index=5*/...) while((s32[]{:T(128)}, bf16[128,768]{0,1:T(8,128)(2,1)}, ...), condition=%wide.wide.region_15.16_spmd.clone, body=%wide.wide.region_14.15_spmd.clone.sunk | while | flops 128401408 | bytes 14401889 | solution.py:302
  191.9 7.0 collective-permute-done.6
  199.0 2.6 collective-permute-done.7
  209.6 2.4 collective-permute-start.6
  212.8 8.1 collective-permute-done.6
  220.9 2.3 collective-permute-done.7
  229.5 2.6 collective-permute-start.6
  232.4 1.8 collective-permute-start.7
  234.7 7.7 collective-permute-done.6
  242.4 2.1 collective-permute-done.7
  250.9 2.7 collective-permute-start.6
  253.9 1.7 collective-permute-start.7
  256.1 6.8 collective-permute-done.6
  262.9 2.1 collective-permute-done.7
  271.6 3.4 collective-permute-start.6
  275.2 1.6 collective-permute-start.7
  277.3 6.0 collective-permute-done.6
  283.3 2.1 collective-permute-done.7
  287.3 1.9 collective-permute-start.4
  293.7 1.7 collective-permute-start.6
  297.3 6.5 collective-permute-done.6
  303.8 2.1 collective-permute-done.7
  312.5 3.4 collective-permute-start.6
  317.7 6.5 collective-permute-done.6
  324.3 2.1 collective-permute-done.7
  333.2 3.2 collective-permute-start.6
  338.3 6.4 collective-permute-done.6
  344.7 2.1 collective-permute-done.7
  355.5 3.6 convolution_convert_fusion.1
  360.4 3.6 convolution_convert_fusion
  366.1 10.8 %all-reduce.18 = (bf16[768]{0:T(1024)(128)(2,1)S(1)}, bf16[768]{0:T(1024)(128)(2,1)S(1)}, bf16[768]{0:T(1024)(128)(2,1)S(1)}, bf16[768]{0:T(1024)(128)(2,1)S(1)}...) all-reduce(bf16[768]{0:T(1024)(128)(2,1)S(1)} %dynamic-update-slice, ...), channel_id=1, replica_groups=mesh['ctx'=8,'shard'=4] {'shard'}, use_global_device_ids=true, to_apply=%add.7 | all-reduce | flops 9984 | bytes 39936
  377.8 3.4 all-to-all-start.2
  381.3 1.8 convolution_add_fusion.4
  387.1 1.8 all-to-all-done.2
  388.9 4.1 all-to-all-start.4
  395.7 5.1 all-to-all-done.4
  403.9 26.2 %reduce-scatter.23.cloned.1.call-done = bf16[192,768]{1,0:T(8,128)(2,1)} async-done(((bf16[768,768]{1,0:T(8,128)(2,1)}), bf16[192,768]{1,0:T(8,128)(2,1)}) %reduce-scatter.23.cloned.1.call-update) | async-done | bytes 294928
  431.2 27.2 %reduce-scatter.13.cloned.1.call-done = bf16[192,768]{1,0:T(8,128)(2,1)} async-done(((bf16[768,768]{1,0:T(8,128)(2,1)}), bf16[192,768]{1,0:T(8,128)(2,1)}) %reduce-scatter.13.cloned.1.call-update) | async-done | bytes 294928 | tf_op jit(solution)/shard_map/reduce_scatter | solution.py:354
  458.4 50.4 %reduce-scatter.15.cloned.1.call-done = bf16[192,3072]{1,0:T(8,128)(2,1)} async-done(((bf16[768,3072]{1,0:T(8,128)(2,1)}), bf16[192,3072]{1,0:T(8,128)(2,1)}) %reduce-scatter.15.cloned.1.call-update) | async-done | bytes 1179664 | tf_op jit(solution)/shard_map/reduce_scatter | solution.py:366
  508.8 50.4 %reduce-scatter.17.cloned.1.call-done = bf16[768,768]{1,0:T(8,128)(2,1)} async-done(((bf16[3072,768]{1,0:T(8,128)(2,1)}), bf16[768,768]{1,0:T(8,128)(2,1)}) %reduce-scatter.17.cloned.1.call-update) | async-done | bytes 1179664 | tf_op jit(solution)/shard_map/reduce_scatter | solution.py:372
  559.2 301.3 %all-reduce.21 = (f32[192,768]{0,1:T(8,128)S(1)}, f32[192]{0:T(256)}, f32[192,768]{0,1:T(8,128)S(1)}, f32[192,768]{0,1:T(8,128)S(1)}, f32[192]{0:T(256)}, /*inde...) all-reduce(bf16[192,768]{0,1:T(8,128)(2,1)S(1)} %copy.142, ...), channel_id=1, replica_groups=mesh['ctx'=8,'shard'=4] {'ctx'}, use_global_device_ids=true, to_apply=%region_17.18 | all-reduce | flops 1771776 | bytes 10635264 | tf_op jit(solution)/shard_map/psum | solution.py:385
  (521 shorter events, 125.5 us)
Async XLA Ops:
  7.2 59.1 %all-gather.8.cloned.1.call-start = ((), (), s32[]{:S(2)}) async-start(), calls=%async_computation.11 | async-start | bytes 1474560 | tf_op jit(solution)/shard_map/all_gather | solution.py:159
  7.9 61.8 %all-gather.10.cloned.1.call-start = ((), (), s32[]{:S(2)}) async-start(), calls=%async_computation.12 | async-start | bytes 1474560 | tf_op jit(solution)/shard_map/all_gather | solution.py:160
  8.7 64.4 %all-gather.12.cloned.1.call-start = ((), (), s32[]{:S(2)}) async-start(), calls=%async_computation.13 | async-start | bytes 1474560 | tf_op jit(solution)/shard_map/all_gather | solution.py:157
  9.4 148.5 %all-gather.14.cloned.1.call-start = ((), (), s32[]{:S(2)}) async-start(), calls=%async_computation.14 | async-start | bytes 1474560 | tf_op jit(solution)/shard_map/all_gather | solution.py:162
  10.1 149.9 %all-gather.16.cloned.1.call-start = ((), (), s32[]{:S(2)}) async-start(), calls=%async_computation.15 | async-start | bytes 5898240 | tf_op jit(solution)/shard_map/all_gather | solution.py:166
  12.6 13.7 %all-to-all-start.1 = ((s32[16,8,1]{0,2,1:T(1,128)}), s32[16,8,1]{0,2,1:T(1,128)S(1)}, u32[]{:S(2)}, u32[]{:S(2)}) async-start(s32[16,8,1]{0,2,1:T(1,128)} %copy.110), calls=%async_computation.1 | async-start | bytes 8192 | tf_op jit(solution)/shard_map/all_to_all | solution.py:133
  26.3 25.9 %all-to-all-start.3 = ((bf16[16,8,768]{2,0,1:T(8,128)(2,1)}), bf16[16,8,768]{2,0,1:T(8,128)(2,1)S(1)}, u32[]{:S(2)}, u32[]{:S(2)}) async-start(bf16[16,8,768]{2,0,1:T(8,128)(2,1)} %copy.119), calls=%async_computation.3 | async-start | bytes 393216 | tf_op jit(solution)/shard_map/all_to_all | solution.py:126
  29.7 137.9 %all-gather.18.cloned.1.call-start = ((), (), s32[]{:S(2)}) async-start(), calls=%async_computation.16 | async-start | bytes 5898240 | tf_op jit(solution)/shard_map/all_gather | solution.py:168
  52.2 14.0 %all-to-all-start = ((bf16[16,8,768]{2,0,1:T(8,128)(2,1)}), bf16[16,8,768]{2,0,1:T(8,128)(2,1)S(1)}, u32[]{:S(2)}, u32[]{:S(2)}) async-start(bf16[16,8,768]{2,0,1:T(8,128)(2,1)} %copy.108), calls=%async_computation | async-start | bytes 393216 | tf_op jit(solution)/shard_map/all_to_all | solution.py:123
  57.9 343.7 %reduce-scatter.19.cloned.1.call-start = ((), (), s32[]{:S(2)}) async-start(), calls=%async_computation.20 | async-start | bytes 1474560
  75.0 12.5 %collective-permute-start = (bf16[128,768]{0,1:T(8,128)(2,1)S(1)}, bf16[128,768]{0,1:T(8,128)(2,1)S(1)}, u32[]{:S(2)}, u32[]{:S(2)}) collective-permute-start(bf16[128,768]{0,1:T(8,128)(2,1)S(1)} %copy.196), channel_id=1, source_target_pairs={{28,0},{0,4},{4,8},{8,12},{12,16},{16,20},{20,24},{24,28},{29,1},{... | collective-permute-start | bytes 589832 | tf_op jit(solution)/shard_map/while/body/eval_jaxpr/ppermute | solution.py:18
  76.1 11.4 %collective-permute-start.1 = (bf16[128,768]{0,1:T(8,128)(2,1)S(1)}, bf16[128,768]{0,1:T(8,128)(2,1)S(1)}, u32[]{:S(2)}, u32[]{:S(2)}) collective-permute-start(bf16[128,768]{0,1:T(8,128)(2,1)S(1)} %copy.197), channel_id=1, source_target_pairs={{28,0},{0,4},{4,8},{8,12},{12,16},{16,20},{20,24},{24,28},{29,1},{... | collective-permute-start | bytes 589832 | tf_op jit(solution)/shard_map/while/body/eval_jaxpr/ppermute | solution.py:18
  87.5 11.5 %collective-permute-start = (bf16[128,768]{0,1:T(8,128)(2,1)S(1)}, bf16[128,768]{0,1:T(8,128)(2,1)S(1)}, u32[]{:S(2)}, u32[]{:S(2)}) collective-permute-start(bf16[128,768]{0,1:T(8,128)(2,1)S(1)} %copy.196), channel_id=1, source_target_pairs={{28,0},{0,4},{4,8},{8,12},{12,16},{16,20},{20,24},{24,28},{29,1},{... | collective-permute-start | bytes 589832 | tf_op jit(solution)/shard_map/while/body/eval_jaxpr/ppermute | solution.py:18
  87.6 11.4 %collective-permute-start.1 = (bf16[128,768]{0,1:T(8,128)(2,1)S(1)}, bf16[128,768]{0,1:T(8,128)(2,1)S(1)}, u32[]{:S(2)}, u32[]{:S(2)}) collective-permute-start(bf16[128,768]{0,1:T(8,128)(2,1)S(1)} %copy.197), channel_id=1, source_target_pairs={{28,0},{0,4},{4,8},{8,12},{12,16},{16,20},{20,24},{24,28},{29,1},{... | collective-permute-start | bytes 589832 | tf_op jit(solution)/shard_map/while/body/eval_jaxpr/ppermute | solution.py:18
  87.8 11.2 %collective-permute-start.2 = (s32[128]{0:T(128)S(1)}, s32[128]{0:T(128)S(1)}, u32[]{:S(2)}, u32[]{:S(2)}) collective-permute-start(s32[128]{0:T(128)S(1)} %copy.198), channel_id=1, source_target_pairs={{28,0},{0,4},{4,8},{8,12},{12,16},{16,20},{20,24},{24,28},{29,1},{... | collective-permute-start | bytes 1544 | tf_op jit(solution)/shard_map/while/body/eval_jaxpr/ppermute | solution.py:18
  109.6 10.7 %collective-permute-start = (bf16[128,768]{0,1:T(8,128)(2,1)S(1)}, bf16[128,768]{0,1:T(8,128)(2,1)S(1)}, u32[]{:S(2)}, u32[]{:S(2)}) collective-permute-start(bf16[128,768]{0,1:T(8,128)(2,1)S(1)} %copy.196), channel_id=1, source_target_pairs={{28,0},{0,4},{4,8},{8,12},{12,16},{16,20},{20,24},{24,28},{29,1},{... | collective-permute-start | bytes 589832 | tf_op jit(solution)/shard_map/while/body/eval_jaxpr/ppermute | solution.py:18
  120.4 11.8 %collective-permute-start = (bf16[128,768]{0,1:T(8,128)(2,1)S(1)}, bf16[128,768]{0,1:T(8,128)(2,1)S(1)}, u32[]{:S(2)}, u32[]{:S(2)}) collective-permute-start(bf16[128,768]{0,1:T(8,128)(2,1)S(1)} %copy.196), channel_id=1, source_target_pairs={{28,0},{0,4},{4,8},{8,12},{12,16},{16,20},{20,24},{24,28},{29,1},{... | collective-permute-start | bytes 589832 | tf_op jit(solution)/shard_map/while/body/eval_jaxpr/ppermute | solution.py:18
  120.5 11.7 %collective-permute-start.1 = (bf16[128,768]{0,1:T(8,128)(2,1)S(1)}, bf16[128,768]{0,1:T(8,128)(2,1)S(1)}, u32[]{:S(2)}, u32[]{:S(2)}) collective-permute-start(bf16[128,768]{0,1:T(8,128)(2,1)S(1)} %copy.197), channel_id=1, source_target_pairs={{28,0},{0,4},{4,8},{8,12},{12,16},{16,20},{20,24},{24,28},{29,1},{... | collective-permute-start | bytes 589832 | tf_op jit(solution)/shard_map/while/body/eval_jaxpr/ppermute | solution.py:18
  120.6 11.7 %collective-permute-start.2 = (s32[128]{0:T(128)S(1)}, s32[128]{0:T(128)S(1)}, u32[]{:S(2)}, u32[]{:S(2)}) collective-permute-start(s32[128]{0:T(128)S(1)} %copy.198), channel_id=1, source_target_pairs={{28,0},{0,4},{4,8},{8,12},{12,16},{16,20},{20,24},{24,28},{29,1},{... | collective-permute-start | bytes 1544 | tf_op jit(solution)/shard_map/while/body/eval_jaxpr/ppermute | solution.py:18
  132.3 12.9 %collective-permute-start = (bf16[128,768]{0,1:T(8,128)(2,1)S(1)}, bf16[128,768]{0,1:T(8,128)(2,1)S(1)}, u32[]{:S(2)}, u32[]{:S(2)}) collective-permute-start(bf16[128,768]{0,1:T(8,128)(2,1)S(1)} %copy.196), channel_id=1, source_target_pairs={{28,0},{0,4},{4,8},{8,12},{12,16},{16,20},{20,24},{24,28},{29,1},{... | collective-permute-start | bytes 589832 | tf_op jit(solution)/shard_map/while/body/eval_jaxpr/ppermute | solution.py:18
  132.4 12.8 %collective-permute-start.1 = (bf16[128,768]{0,1:T(8,128)(2,1)S(1)}, bf16[128,768]{0,1:T(8,128)(2,1)S(1)}, u32[]{:S(2)}, u32[]{:S(2)}) collective-permute-start(bf16[128,768]{0,1:T(8,128)(2,1)S(1)} %copy.197), channel_id=1, source_target_pairs={{28,0},{0,4},{4,8},{8,12},{12,16},{16,20},{20,24},{24,28},{29,1},{... | collective-permute-start | bytes 589832 | tf_op jit(solution)/shard_map/while/body/eval_jaxpr/ppermute | solution.py:18
  132.4 12.7 %collective-permute-start.2 = (s32[128]{0:T(128)S(1)}, s32[128]{0:T(128)S(1)}, u32[]{:S(2)}, u32[]{:S(2)}) collective-permute-start(s32[128]{0:T(128)S(1)} %copy.198), channel_id=1, source_target_pairs={{28,0},{0,4},{4,8},{8,12},{12,16},{16,20},{20,24},{24,28},{29,1},{... | collective-permute-start | bytes 1544 | tf_op jit(solution)/shard_map/while/body/eval_jaxpr/ppermute | solution.py:18
  181.5 20.1 %collective-permute-start.3 = (bf16[128,768]{0,1:T(8,128)(2,1)S(1)}, bf16[128,768]{0,1:T(8,128)(2,1)}, u32[]{:S(2)}, u32[]{:S(2)}) collective-permute-start(bf16[128,768]{0,1:T(8,128)(2,1)S(1)} %copy.218), channel_id=1, source_target_pairs={{28,0},{0,4},{4,8},{8,12},{12,16},{16,20},{20,24},{24,28},{29,1},{... | collective-permute-start | bytes 589832 | tf_op jit(solution)/shard_map/while/body/eval_jaxpr/ppermute | solution.py:18
  182.4 19.2 %collective-permute-start.4 = (bf16[128,768]{0,1:T(8,128)(2,1)S(1)}, bf16[128,768]{0,1:T(8,128)(2,1)}, u32[]{:S(2)}, u32[]{:S(2)}) collective-permute-start(bf16[128,768]{0,1:T(8,128)(2,1)S(1)} %copy.219), channel_id=1, source_target_pairs={{28,0},{0,4},{4,8},{8,12},{12,16},{16,20},{20,24},{24,28},{29,1},{... | collective-permute-start | bytes 589832 | tf_op jit(solution)/shard_map/while/body/eval_jaxpr/ppermute | solution.py:18
  183.5 18.0 %collective-permute-start.5 = (s32[128]{0:T(128)}, s32[128]{0:T(128)}, u32[]{:S(2)}, u32[]{:S(2)}) collective-permute-start(s32[128]{0:T(128)} %copy.220), channel_id=1, source_target_pairs={{28,0},{0,4},{4,8},{8,12},{12,16},{16,20},{20,24},{24,28},{29,1},{... | collective-permute-start | bytes 1544 | tf_op jit(solution)/shard_map/while/body/eval_jaxpr/ppermute | solution.py:18
  188.2 10.8 %collective-permute-start.6 = (bf16[128,768]{0,1:T(8,128)(2,1)}, bf16[128,768]{0,1:T(8,128)(2,1)S(1)}, u32[]{:S(2)}, u32[]{:S(2)}) collective-permute-start(bf16[128,768]{0,1:T(8,128)(2,1)} %fusion.183), channel_id=1, source_target_pairs={{28,0},{0,4},{4,8},{8,12},{12,16},{16,20},{20,24},{24,28},{29,1},{... | collective-permute-start | bytes 589832 | tf_op jit(solution)/shard_map/while/body/eval_jaxpr/ppermute | solution.py:18
  189.9 11.6 %collective-permute-start.7 = (bf16[128,768]{0,1:T(8,128)(2,1)S(1)}, bf16[128,768]{0,1:T(8,128)(2,1)S(1)}, u32[]{:S(2)}, u32[]{:S(2)}) collective-permute-start(bf16[128,768]{0,1:T(8,128)(2,1)S(1)} %fusion.185), channel_id=1, source_target_pairs={{28,0},{0,4},{4,8},{8,12},{12,16},{16,20},{20,24},{24,28},{29,1},{... | collective-permute-start | bytes 589832 | tf_op jit(solution)/shard_map/while/body/eval_jaxpr/ppermute | solution.py:18
  202.5 20.7 %collective-permute-start.3 = (bf16[128,768]{0,1:T(8,128)(2,1)S(1)}, bf16[128,768]{0,1:T(8,128)(2,1)}, u32[]{:S(2)}, u32[]{:S(2)}) collective-permute-start(bf16[128,768]{0,1:T(8,128)(2,1)S(1)} %copy.218), channel_id=1, source_target_pairs={{28,0},{0,4},{4,8},{8,12},{12,16},{16,20},{20,24},{24,28},{29,1},{... | collective-permute-start | bytes 589832 | tf_op jit(solution)/shard_map/while/body/eval_jaxpr/ppermute | solution.py:18
  203.5 19.8 %collective-permute-start.4 = (bf16[128,768]{0,1:T(8,128)(2,1)S(1)}, bf16[128,768]{0,1:T(8,128)(2,1)}, u32[]{:S(2)}, u32[]{:S(2)}) collective-permute-start(bf16[128,768]{0,1:T(8,128)(2,1)S(1)} %copy.219), channel_id=1, source_target_pairs={{28,0},{0,4},{4,8},{8,12},{12,16},{16,20},{20,24},{24,28},{29,1},{... | collective-permute-start | bytes 589832 | tf_op jit(solution)/shard_map/while/body/eval_jaxpr/ppermute | solution.py:18
  205.7 17.5 %collective-permute-start.5 = (s32[128]{0:T(128)}, s32[128]{0:T(128)}, u32[]{:S(2)}, u32[]{:S(2)}) collective-permute-start(s32[128]{0:T(128)} %copy.220), channel_id=1, source_target_pairs={{28,0},{0,4},{4,8},{8,12},{12,16},{16,20},{20,24},{24,28},{29,1},{... | collective-permute-start | bytes 1544 | tf_op jit(solution)/shard_map/while/body/eval_jaxpr/ppermute | solution.py:18
  209.6 11.3 %collective-permute-start.6 = (bf16[128,768]{0,1:T(8,128)(2,1)}, bf16[128,768]{0,1:T(8,128)(2,1)S(1)}, u32[]{:S(2)}, u32[]{:S(2)}) collective-permute-start(bf16[128,768]{0,1:T(8,128)(2,1)} %fusion.183), channel_id=1, source_target_pairs={{28,0},{0,4},{4,8},{8,12},{12,16},{16,20},{20,24},{24,28},{29,1},{... | collective-permute-start | bytes 589832 | tf_op jit(solution)/shard_map/while/body/eval_jaxpr/ppermute | solution.py:18
  212.3 10.9 %collective-permute-start.7 = (bf16[128,768]{0,1:T(8,128)(2,1)S(1)}, bf16[128,768]{0,1:T(8,128)(2,1)S(1)}, u32[]{:S(2)}, u32[]{:S(2)}) collective-permute-start(bf16[128,768]{0,1:T(8,128)(2,1)S(1)} %fusion.185), channel_id=1, source_target_pairs={{28,0},{0,4},{4,8},{8,12},{12,16},{16,20},{20,24},{24,28},{29,1},{... | collective-permute-start | bytes 589832 | tf_op jit(solution)/shard_map/while/body/eval_jaxpr/ppermute | solution.py:18
  224.2 20.4 %collective-permute-start.3 = (bf16[128,768]{0,1:T(8,128)(2,1)S(1)}, bf16[128,768]{0,1:T(8,128)(2,1)}, u32[]{:S(2)}, u32[]{:S(2)}) collective-permute-start(bf16[128,768]{0,1:T(8,128)(2,1)S(1)} %copy.218), channel_id=1, source_target_pairs={{28,0},{0,4},{4,8},{8,12},{12,16},{16,20},{20,24},{24,28},{29,1},{... | collective-permute-start | bytes 589832 | tf_op jit(solution)/shard_map/while/body/eval_jaxpr/ppermute | solution.py:18
  225.1 19.5 %collective-permute-start.4 = (bf16[128,768]{0,1:T(8,128)(2,1)S(1)}, bf16[128,768]{0,1:T(8,128)(2,1)}, u32[]{:S(2)}, u32[]{:S(2)}) collective-permute-start(bf16[128,768]{0,1:T(8,128)(2,1)S(1)} %copy.219), channel_id=1, source_target_pairs={{28,0},{0,4},{4,8},{8,12},{12,16},{16,20},{20,24},{24,28},{29,1},{... | collective-permute-start | bytes 589832 | tf_op jit(solution)/shard_map/while/body/eval_jaxpr/ppermute | solution.py:18
  226.3 18.3 %collective-permute-start.5 = (s32[128]{0:T(128)}, s32[128]{0:T(128)}, u32[]{:S(2)}, u32[]{:S(2)}) collective-permute-start(s32[128]{0:T(128)} %copy.220), channel_id=1, source_target_pairs={{28,0},{0,4},{4,8},{8,12},{12,16},{16,20},{20,24},{24,28},{29,1},{... | collective-permute-start | bytes 1544 | tf_op jit(solution)/shard_map/while/body/eval_jaxpr/ppermute | solution.py:18
  229.5 12.9 %collective-permute-start.6 = (bf16[128,768]{0,1:T(8,128)(2,1)}, bf16[128,768]{0,1:T(8,128)(2,1)S(1)}, u32[]{:S(2)}, u32[]{:S(2)}) collective-permute-start(bf16[128,768]{0,1:T(8,128)(2,1)} %fusion.183), channel_id=1, source_target_pairs={{28,0},{0,4},{4,8},{8,12},{12,16},{16,20},{20,24},{24,28},{29,1},{... | collective-permute-start | bytes 589832 | tf_op jit(solution)/shard_map/while/body/eval_jaxpr/ppermute | solution.py:18
  232.4 12.1 %collective-permute-start.7 = (bf16[128,768]{0,1:T(8,128)(2,1)S(1)}, bf16[128,768]{0,1:T(8,128)(2,1)S(1)}, u32[]{:S(2)}, u32[]{:S(2)}) collective-permute-start(bf16[128,768]{0,1:T(8,128)(2,1)S(1)} %fusion.185), channel_id=1, source_target_pairs={{28,0},{0,4},{4,8},{8,12},{12,16},{16,20},{20,24},{24,28},{29,1},{... | collective-permute-start | bytes 589832 | tf_op jit(solution)/shard_map/while/body/eval_jaxpr/ppermute | solution.py:18
  245.5 19.5 %collective-permute-start.3 = (bf16[128,768]{0,1:T(8,128)(2,1)S(1)}, bf16[128,768]{0,1:T(8,128)(2,1)}, u32[]{:S(2)}, u32[]{:S(2)}) collective-permute-start(bf16[128,768]{0,1:T(8,128)(2,1)S(1)} %copy.218), channel_id=1, source_target_pairs={{28,0},{0,4},{4,8},{8,12},{12,16},{16,20},{20,24},{24,28},{29,1},{... | collective-permute-start | bytes 589832 | tf_op jit(solution)/shard_map/while/body/eval_jaxpr/ppermute | solution.py:18
  246.5 18.5 %collective-permute-start.4 = (bf16[128,768]{0,1:T(8,128)(2,1)S(1)}, bf16[128,768]{0,1:T(8,128)(2,1)}, u32[]{:S(2)}, u32[]{:S(2)}) collective-permute-start(bf16[128,768]{0,1:T(8,128)(2,1)S(1)} %copy.219), channel_id=1, source_target_pairs={{28,0},{0,4},{4,8},{8,12},{12,16},{16,20},{20,24},{24,28},{29,1},{... | collective-permute-start | bytes 589832 | tf_op jit(solution)/shard_map/while/body/eval_jaxpr/ppermute | solution.py:18
  247.6 17.4 %collective-permute-start.5 = (s32[128]{0:T(128)}, s32[128]{0:T(128)}, u32[]{:S(2)}, u32[]{:S(2)}) collective-permute-start(s32[128]{0:T(128)} %copy.220), channel_id=1, source_target_pairs={{28,0},{0,4},{4,8},{8,12},{12,16},{16,20},{20,24},{24,28},{29,1},{... | collective-permute-start | bytes 1544 | tf_op jit(solution)/shard_map/while/body/eval_jaxpr/ppermute | solution.py:18
  250.9 11.9 %collective-permute-start.6 = (bf16[128,768]{0,1:T(8,128)(2,1)}, bf16[128,768]{0,1:T(8,128)(2,1)S(1)}, u32[]{:S(2)}, u32[]{:S(2)}) collective-permute-start(bf16[128,768]{0,1:T(8,128)(2,1)} %fusion.183), channel_id=1, source_target_pairs={{28,0},{0,4},{4,8},{8,12},{12,16},{16,20},{20,24},{24,28},{29,1},{... | collective-permute-start | bytes 589832 | tf_op jit(solution)/shard_map/while/body/eval_jaxpr/ppermute | solution.py:18
  253.9 11.0 %collective-permute-start.7 = (bf16[128,768]{0,1:T(8,128)(2,1)S(1)}, bf16[128,768]{0,1:T(8,128)(2,1)S(1)}, u32[]{:S(2)}, u32[]{:S(2)}) collective-permute-start(bf16[128,768]{0,1:T(8,128)(2,1)S(1)} %fusion.185), channel_id=1, source_target_pairs={{28,0},{0,4},{4,8},{8,12},{12,16},{16,20},{20,24},{24,28},{29,1},{... | collective-permute-start | bytes 589832 | tf_op jit(solution)/shard_map/while/body/eval_jaxpr/ppermute | solution.py:18
  265.9 19.5 %collective-permute-start.3 = (bf16[128,768]{0,1:T(8,128)(2,1)S(1)}, bf16[128,768]{0,1:T(8,128)(2,1)}, u32[]{:S(2)}, u32[]{:S(2)}) collective-permute-start(bf16[128,768]{0,1:T(8,128)(2,1)S(1)} %copy.218), channel_id=1, source_target_pairs={{28,0},{0,4},{4,8},{8,12},{12,16},{16,20},{20,24},{24,28},{29,1},{... | collective-permute-start | bytes 589832 | tf_op jit(solution)/shard_map/while/body/eval_jaxpr/ppermute | solution.py:18
  266.9 18.6 %collective-permute-start.4 = (bf16[128,768]{0,1:T(8,128)(2,1)S(1)}, bf16[128,768]{0,1:T(8,128)(2,1)}, u32[]{:S(2)}, u32[]{:S(2)}) collective-permute-start(bf16[128,768]{0,1:T(8,128)(2,1)S(1)} %copy.219), channel_id=1, source_target_pairs={{28,0},{0,4},{4,8},{8,12},{12,16},{16,20},{20,24},{24,28},{29,1},{... | collective-permute-start | bytes 589832 | tf_op jit(solution)/shard_map/while/body/eval_jaxpr/ppermute | solution.py:18
  268.0 17.4 %collective-permute-start.5 = (s32[128]{0:T(128)}, s32[128]{0:T(128)}, u32[]{:S(2)}, u32[]{:S(2)}) collective-permute-start(s32[128]{0:T(128)} %copy.220), channel_id=1, source_target_pairs={{28,0},{0,4},{4,8},{8,12},{12,16},{16,20},{20,24},{24,28},{29,1},{... | collective-permute-start | bytes 1544 | tf_op jit(solution)/shard_map/while/body/eval_jaxpr/ppermute | solution.py:18
  271.6 11.7 %collective-permute-start.6 = (bf16[128,768]{0,1:T(8,128)(2,1)}, bf16[128,768]{0,1:T(8,128)(2,1)S(1)}, u32[]{:S(2)}, u32[]{:S(2)}) collective-permute-start(bf16[128,768]{0,1:T(8,128)(2,1)} %fusion.183), channel_id=1, source_target_pairs={{28,0},{0,4},{4,8},{8,12},{12,16},{16,20},{20,24},{24,28},{29,1},{... | collective-permute-start | bytes 589832 | tf_op jit(solution)/shard_map/while/body/eval_jaxpr/ppermute | solution.py:18
  286.4 19.5 %collective-permute-start.3 = (bf16[128,768]{0,1:T(8,128)(2,1)S(1)}, bf16[128,768]{0,1:T(8,128)(2,1)}, u32[]{:S(2)}, u32[]{:S(2)}) collective-permute-start(bf16[128,768]{0,1:T(8,128)(2,1)S(1)} %copy.218), channel_id=1, source_target_pairs={{28,0},{0,4},{4,8},{8,12},{12,16},{16,20},{20,24},{24,28},{29,1},{... | collective-permute-start | bytes 589832 | tf_op jit(solution)/shard_map/while/body/eval_jaxpr/ppermute | solution.py:18
  287.3 18.6 %collective-permute-start.4 = (bf16[128,768]{0,1:T(8,128)(2,1)S(1)}, bf16[128,768]{0,1:T(8,128)(2,1)}, u32[]{:S(2)}, u32[]{:S(2)}) collective-permute-start(bf16[128,768]{0,1:T(8,128)(2,1)S(1)} %copy.219), channel_id=1, source_target_pairs={{28,0},{0,4},{4,8},{8,12},{12,16},{16,20},{20,24},{24,28},{29,1},{... | collective-permute-start | bytes 589832 | tf_op jit(solution)/shard_map/while/body/eval_jaxpr/ppermute | solution.py:18
  290.4 15.5 %collective-permute-start.5 = (s32[128]{0:T(128)}, s32[128]{0:T(128)}, u32[]{:S(2)}, u32[]{:S(2)}) collective-permute-start(s32[128]{0:T(128)} %copy.220), channel_id=1, source_target_pairs={{28,0},{0,4},{4,8},{8,12},{12,16},{16,20},{20,24},{24,28},{29,1},{... | collective-permute-start | bytes 1544 | tf_op jit(solution)/shard_map/while/body/eval_jaxpr/ppermute | solution.py:18
  306.9 19.5 %collective-permute-start.3 = (bf16[128,768]{0,1:T(8,128)(2,1)S(1)}, bf16[128,768]{0,1:T(8,128)(2,1)}, u32[]{:S(2)}, u32[]{:S(2)}) collective-permute-start(bf16[128,768]{0,1:T(8,128)(2,1)S(1)} %copy.218), channel_id=1, source_target_pairs={{28,0},{0,4},{4,8},{8,12},{12,16},{16,20},{20,24},{24,28},{29,1},{... | collective-permute-start | bytes 589832 | tf_op jit(solution)/shard_map/while/body/eval_jaxpr/ppermute | solution.py:18
  307.8 18.6 %collective-permute-start.4 = (bf16[128,768]{0,1:T(8,128)(2,1)S(1)}, bf16[128,768]{0,1:T(8,128)(2,1)}, u32[]{:S(2)}, u32[]{:S(2)}) collective-permute-start(bf16[128,768]{0,1:T(8,128)(2,1)S(1)} %copy.219), channel_id=1, source_target_pairs={{28,0},{0,4},{4,8},{8,12},{12,16},{16,20},{20,24},{24,28},{29,1},{... | collective-permute-start | bytes 589832 | tf_op jit(solution)/shard_map/while/body/eval_jaxpr/ppermute | solution.py:18
  309.0 17.4 %collective-permute-start.5 = (s32[128]{0:T(128)}, s32[128]{0:T(128)}, u32[]{:S(2)}, u32[]{:S(2)}) collective-permute-start(s32[128]{0:T(128)} %copy.220), channel_id=1, source_target_pairs={{28,0},{0,4},{4,8},{8,12},{12,16},{16,20},{20,24},{24,28},{29,1},{... | collective-permute-start | bytes 1544 | tf_op jit(solution)/shard_map/while/body/eval_jaxpr/ppermute | solution.py:18
  312.5 11.8 %collective-permute-start.6 = (bf16[128,768]{0,1:T(8,128)(2,1)}, bf16[128,768]{0,1:T(8,128)(2,1)S(1)}, u32[]{:S(2)}, u32[]{:S(2)}) collective-permute-start(bf16[128,768]{0,1:T(8,128)(2,1)} %fusion.183), channel_id=1, source_target_pairs={{28,0},{0,4},{4,8},{8,12},{12,16},{16,20},{20,24},{24,28},{29,1},{... | collective-permute-start | bytes 589832 | tf_op jit(solution)/shard_map/while/body/eval_jaxpr/ppermute | solution.py:18
  327.4 19.5 %collective-permute-start.3 = (bf16[128,768]{0,1:T(8,128)(2,1)S(1)}, bf16[128,768]{0,1:T(8,128)(2,1)}, u32[]{:S(2)}, u32[]{:S(2)}) collective-permute-start(bf16[128,768]{0,1:T(8,128)(2,1)S(1)} %copy.218), channel_id=1, source_target_pairs={{28,0},{0,4},{4,8},{8,12},{12,16},{16,20},{20,24},{24,28},{29,1},{... | collective-permute-start | bytes 589832 | tf_op jit(solution)/shard_map/while/body/eval_jaxpr/ppermute | solution.py:18
  328.3 18.6 %collective-permute-start.4 = (bf16[128,768]{0,1:T(8,128)(2,1)S(1)}, bf16[128,768]{0,1:T(8,128)(2,1)}, u32[]{:S(2)}, u32[]{:S(2)}) collective-permute-start(bf16[128,768]{0,1:T(8,128)(2,1)S(1)} %copy.219), channel_id=1, source_target_pairs={{28,0},{0,4},{4,8},{8,12},{12,16},{16,20},{20,24},{24,28},{29,1},{... | collective-permute-start | bytes 589832 | tf_op jit(solution)/shard_map/while/body/eval_jaxpr/ppermute | solution.py:18
  329.9 17.0 %collective-permute-start.5 = (s32[128]{0:T(128)}, s32[128]{0:T(128)}, u32[]{:S(2)}, u32[]{:S(2)}) collective-permute-start(s32[128]{0:T(128)} %copy.220), channel_id=1, source_target_pairs={{28,0},{0,4},{4,8},{8,12},{12,16},{16,20},{20,24},{24,28},{29,1},{... | collective-permute-start | bytes 1544 | tf_op jit(solution)/shard_map/while/body/eval_jaxpr/ppermute | solution.py:18
  333.2 11.5 %collective-permute-start.6 = (bf16[128,768]{0,1:T(8,128)(2,1)}, bf16[128,768]{0,1:T(8,128)(2,1)S(1)}, u32[]{:S(2)}, u32[]{:S(2)}) collective-permute-start(bf16[128,768]{0,1:T(8,128)(2,1)} %fusion.183), channel_id=1, source_target_pairs={{28,0},{0,4},{4,8},{8,12},{12,16},{16,20},{20,24},{24,28},{29,1},{... | collective-permute-start | bytes 589832 | tf_op jit(solution)/shard_map/while/body/eval_jaxpr/ppermute | solution.py:18
  349.8 52.9 %reduce-scatter.21.cloned.1.call-start = ((), (), s32[]{:S(2)}) async-start(), calls=%async_computation.21 | async-start | bytes 1474560
  351.8 78.3 %reduce-scatter.23.cloned.1.call-start = ((), (), s32[]{:S(2)}) async-start(), calls=%async_computation.22 | async-start | bytes 1474560
  353.9 104.5 %reduce-scatter.13.cloned.1.call-start = ((), (), s32[]{:S(2)}) async-start(), calls=%async_computation.17 | async-start | bytes 1474560 | tf_op jit(solution)/shard_map/reduce_scatter | solution.py:354
  355.4 153.4 %reduce-scatter.15.cloned.1.call-start = ((), (), s32[]{:S(2)}) async-start(), calls=%async_computation.18 | async-start | bytes 5898240 | tf_op jit(solution)/shard_map/reduce_scatter | solution.py:366
  359.2 200.0 %reduce-scatter.17.cloned.1.call-start = ((), (), s32[]{:S(2)}) async-start(), calls=%async_computation.19 | async-start | bytes 5898240 | tf_op jit(solution)/shard_map/reduce_scatter | solution.py:372
  377.8 11.1 %all-to-all-start.2 = ((bf16[16,8,768]{2,0,1:T(8,128)(2,1)}), bf16[16,8,768]{2,0,1:T(8,128)(2,1)S(1)}, u32[]{:S(2)}, u32[]{:S(2)}) async-start(bf16[16,8,768]{2,0,1:T(8,128)(2,1)} %copy.117), calls=%async_computation.2 | async-start | bytes 393216 | tf_op jit(solution)/shard_map/all_to_all | solution.py:321
  388.9 11.9 %all-to-all-start.4 = ((bf16[16,8,768]{2,0,1:T(8,128)(2,1)}), bf16[16,8,768]{2,0,1:T(8,128)(2,1)S(1)}, u32[]{:S(2)}, u32[]{:S(2)}) async-start(bf16[16,8,768]{2,0,1:T(8,128)(2,1)} %copy.126), calls=%async_computation.4 | async-start | bytes 393216 | tf_op jit(solution)/shard_map/all_to_all | solution.py:328
  (69 other events, 848.8 us)
Sparse Core Ops, SparseCore 0:
  9.6 20.1 all-gather.7
  31.4 17.5 all-gather.9
  50.5 17.4 all-gather.11
  69.5 17.4 all-gather.13
  88.4 37.4 all-gather.15
  127.3 37.4 all-gather.17
  349.9 22.3 reduce-scatter.18
  375.6 26.0 reduce-scatter.20
  404.2 25.7 reduce-scatter.22
  432.6 25.7 reduce-scatter.12
  460.9 47.8 reduce-scatter.14
  511.3 47.8 reduce-scatter.16
where the time goes:
time: 873 us; the launch traced here: 871 us
  blocking collectives  328 us (38%)
  waiting for transfers between devices  320 us (37%)
  starting transfers between devices  65.6 us (8%)
  matrix products  60.7 us (7%)
  local copies, waits for them, and re-layouts  52.2 us (6%)
  other arithmetic  24.8 us (3%)
  between operations  17.2 us (2%)
    psum x1, blocking collectives, local(): lax.psum((shares[0], shares[1], shares[2], shares[3], shares[4], shares[5...  301 us
    ppermute x61, waiting for transfers between devices, from_behind(): return lax.ppermute(block, axis, route)  142 us
    reduce_scatter x1, waiting for transfers between devices, local(): lax.psum_scatter(d_up_mat.astype(jnp.bfloat16), 'shard', scatter_dimensio...  50.4 us
    reduce_scatter x1, waiting for transfers between devices, local(): lax.psum_scatter(d_down_mat.astype(jnp.bfloat16), 'shard', scatter_dimens...  50.4 us
    ppermute x61, starting transfers between devices, from_behind(): return lax.ppermute(block, axis, route)  41.4 us
    unnamed x15, waiting for transfers between devices  29.9 us
    reduce_scatter x1, waiting for transfers between devices, local(): lax.psum_scatter(d_out_mat.astype(jnp.bfloat16), 'shard', scatter_dimensi...  27.2 us
    while x52, local copies, waits for them, and re-layouts  24.2 us
  transfers between devices with their start and end apart: 78, of which 31 were waited for; matrix products, arithmetic and copies ran while one was open for 13% of the time, Pallas kernels for 0%

commit v1 on v0

--- a/solution.py
+++ b/solution.py
@@ -3,6 +3,9 @@
 import jax
 import jax.numpy as jnp
 from jax import lax
+from jax.experimental import pallas as pl
+from jax.experimental.pallas import tpu as pltpu
+from jax.sharding import Mesh
 from jax.sharding import PartitionSpec as P
 
 HEAD_DIM = 64
@@ -93,7 +96,7 @@
     return (d_query, d_keys, d_values)
 
 
-def local(
+def ring_local(
     tokens,
     cotangent,
     seq_ids,
@@ -405,9 +408,9 @@
     return (hidden_out, tokens_grad) + tuple(totals)
 
 
-def solution(mesh):
+def ring_solution(mesh):
     return jax.shard_map(
-        local,
+        ring_local,
         mesh=mesh,
         in_specs=(
             P("shard", "ctx", None),
@@ -450,3 +453,674 @@
         ),
         check_vma=False,
     )
+
+
+AXES = ("q", "r", "x", "c")
+ANY = pl.BlockSpec(memory_space=pl.ANY)
+WHOLE = pl.BlockSpec(memory_space=pltpu.VMEM)
+
+
+def moved(block, move):
+    sizes = [lax.axis_size(a) for a in AXES]
+
+    def number(spot):
+        place = 0
+        for size, at in zip(sizes, spot):
+            place = place * size + at
+        return place
+
+    spots = [
+        (q, r, x, c)
+        for q in range(sizes[0])
+        for r in range(sizes[1])
+        for x in range(sizes[2])
+        for c in range(sizes[3])
+    ]
+    return lax.ppermute(block, AXES, [(number(s), number(move(*s))) for s in spots])
+
+
+def swap_x(block):
+    return moved(block, lambda q, r, x, c: (q, r, 1 - x, c))
+
+
+def swap_c(block):
+    return moved(block, lambda q, r, x, c: (q, r, x, 1 - c))
+
+
+def swap_r(block):
+    return moved(block, lambda q, r, x, c: (q, r ^ 1, x, c))
+
+
+def swap_rc(block):
+    return moved(block, lambda q, r, x, c: (q, r ^ 1, x, 1 - c))
+
+
+def swap_near(block):
+    return moved(block, lambda q, r, x, c: (q ^ 1, r, x, c))
+
+
+def swap_far(block):
+    return moved(block, lambda q, r, x, c: (q ^ 2, r, x, c))
+
+
+def regroup(block):
+    return moved(block, lambda q, r, x, c: (2 * c + x, r, q & 1, q >> 1))
+
+
+def in_order(mine, theirs, bit):
+    first, second = jnp.stack([mine, theirs]), jnp.stack([theirs, mine])
+    return jnp.where(bit == 0, first, second)
+
+
+def take(stacked, at):
+    return lax.dynamic_index_in_dim(stacked, at, 0, keepdims=False)
+
+
+def dot(left, right):
+    return jnp.dot(left, right, preferred_element_type=jnp.float32)
+
+
+def dot_nt(left, right):
+    return lax.dot_general(
+        left, right, (((1,), (1,)), ((), ())), preferred_element_type=jnp.float32
+    )
+
+
+class Copies:
+    def __init__(self, sems):
+        self.sems = sems
+        self.count = 0
+        self.held = []
+
+    def start(self, source, target):
+        copy = pltpu.make_async_copy(source, target, self.sems.at[self.count])
+        copy.start()
+        self.count += 1
+        self.held.append(copy)
+
+    def wait(self):
+        for copy in self.held:
+            copy.wait()
+        self.held = []
+
+
+def spot():
+    return tuple(lax.axis_index(a) for a in AXES)
+
+
+def fill_mask(ids, mask, own):
+    blocks, rows = ids.shape
+    mine = jnp.concatenate([ids[pl.ds(own, 1), :], ids[pl.ds(own + 1, 1), :]], axis=1)
+    across = jnp.transpose(ids[...])
+    for b in range(blocks):
+        mask[rows * b : rows * (b + 1), :] = jnp.where(across[:, b : b + 1] == mine, 0.0, masked_fill)
+
+
+def attend_kernel(
+    b0, b1, b2, b3, b4, b5, b6, b7, w_q, w_k, w_v, w_x, w_m, w_mx, w_o, w_om, bias,
+    x_out, w_out, wo_out, k_out, v_out, q_out, o_out, lse_out, ids_out, a_out, a_low,
+    xs, raw, w, wo, k3, v3, vt, q3, ot, mask, sems, outs,
+):
+    q, r, x, c = spot()
+    rows = xs.shape[0] // 8
+    part = w.shape[0] // 4
+    half = wo.shape[0]
+    width = w.shape[0]
+    me, shard = 4 * r + 2 * c + x, 2 * x + c
+    ins = Copies(sems)
+    for j, block in enumerate((b0, b1, b2, b3, b4, b5, b6, b7)):
+        at = me ^ j
+        ins.start(block.at[pl.ds(0, rows)], xs.at[pl.ds(pl.multiple_of(rows * at, rows), rows)])
+        ins.start(block.at[pl.ds(rows, 16)], raw.at[at])
+    columns = pl.ds(pl.multiple_of(half * x, 128), half)
+    for t, own in enumerate((w_q, w_k, w_v)):
+        place = pl.ds(half * t, half)
+        ins.start(own.at[:, columns], w.at[pl.ds(pl.multiple_of(part * shard, 64), part), place])
+        for flip, piece in ((2, w_x), (1, w_m), (3, w_mx)):
+            at = pl.ds(pl.multiple_of(part * (shard ^ flip), 64), part)
+            ins.start(piece.at[t], w.at[at, place])
+    ins.start(w_o, wo.at[pl.ds(pl.multiple_of(part * c, 64), part)])
+    ins.start(w_om, wo.at[pl.ds(pl.multiple_of(part * (1 - c), 64), part)])
+    ins.wait()
+    backs = Copies(outs)
+    backs.start(xs, x_out)
+    backs.start(w, w_out)
+    backs.start(wo, wo_out)
+    for b in range(8):
+        ids_out[b : b + 1, :] = raw[b, 0:1, 0:rows].astype(jnp.float32)
+    fill_mask(ids_out, mask, 4 * r + 2 * c)
+    keyed = dot(xs[...], w[:, half : 2 * half]).astype(jnp.bfloat16)
+    valued = dot(xs[...], w[:, 2 * half : 3 * half]) + bias[1:2, :]
+    own = pl.ds(pl.multiple_of(rows * (4 * r + 2 * c), rows), 2 * rows)
+    asked = (dot(xs[own, :], w[:, 0:half]) + bias[0:1, :]).astype(jnp.bfloat16)
+    turned = jnp.transpose(valued).astype(jnp.bfloat16)
+    valued = valued.astype(jnp.bfloat16)
+    pairs = half // 128
+    for p in range(pairs):
+        k3[p] = keyed[:, 128 * p : 128 * (p + 1)]
+        v3[p] = valued[:, 128 * p : 128 * (p + 1)]
+        q3[p] = asked[:, 128 * p : 128 * (p + 1)]
+    for h in range(2 * pairs):
+        vt[h] = turned[64 * h : 64 * (h + 1), :]
+    backs.start(k3, k_out)
+    backs.start(v3, v_out)
+    q_out[...] = q3[...]
+    lane = lax.broadcasted_iota(jnp.int32, (2 * rows, 128), 1) // 64
+
+    def head(h, carry):
+        query = jnp.where(lane == h % 2, q3[h // 2], 0) * 0.125
+        scores = dot_nt(k3[h // 2], query.astype(jnp.bfloat16)) + mask[...]
+        top = jnp.max(scores, axis=0, keepdims=True)
+        weights = jnp.exp(scores - top)
+        total = jnp.sum(weights, axis=0, keepdims=True)
+        ot[h] = dot(vt[h], weights.astype(jnp.bfloat16)) / total
+        lse_out[pl.ds(h, 1), :] = top + jnp.log(total)
+        return carry
+
+    lax.fori_loop(0, 2 * pairs, head, 0)
+    mixed = jnp.transpose(ot[...].reshape(half, 2 * rows)).astype(jnp.bfloat16)
+    o_out[...] = mixed
+    partial = dot(mixed, wo[...])
+    a_out[...] = partial
+    a_low[...] = partial.astype(jnp.bfloat16)
+    backs.wait()
+
+
+def load_feedforward(copies, up, down, u_own, u_x, u_m, u_mx, d_own, d_m):
+    q, r, x, c = spot()
+    part = up.shape[0] // 4
+    wide = up.shape[1] // 4
+    shard = 2 * x + c
+    for j in range(4):
+        at = pl.ds(wide * j, wide)
+        slot = (2 * c + r) ^ j
+        pieces = ((0, u_own, 4 * wide * x), (2, u_x, 0), (1, u_m, 0), (3, u_mx, 0))
+        for flip, piece, base in pieces:
+            rows = pl.ds(pl.multiple_of(part * (shard ^ flip), 64), part)
+            columns = pl.ds(pl.multiple_of(base + wide * slot, 128), wide)
+            copies.start(piece.at[:, columns], up.at[rows, at])
+        source = d_own if j < 2 else d_m
+        copies.start(source.at[pl.ds(pl.multiple_of(wide * (r ^ (j & 1)), 128), wide)], down.at[at])
+
+
+def norm_of(value):
+    mean = jnp.mean(value, axis=-1, keepdims=True)
+    centered = value - mean
+    rstd = lax.rsqrt(jnp.mean(centered * centered, axis=-1, keepdims=True) + ln_eps)
+    return centered * rstd, rstd
+
+
+def norm_pull(scaled, normed, rstd):
+    return rstd * (
+        scaled
+        - jnp.mean(scaled, axis=-1, keepdims=True)
+        - normed * jnp.mean(scaled * normed, axis=-1, keepdims=True)
+    )
+
+
+def forward_kernel(
+    a_own, a_got, xs, vecs, b_up, u_own, u_x, u_m, u_mx, d_own, d_m,
+    h_out, n_out, r_out, z_out, slope_out, y_out, y_low,
+    up, down, x_own, sems, more,
+):
+    q, r, x, c = spot()
+    rows = x_own.shape[0]
+    first = Copies(more)
+    first.start(xs.at[pl.ds(pl.multiple_of(rows * (2 * r + c), rows), rows)], x_own)
+    copies = Copies(sems)
+    load_feedforward(copies, up, down, u_own, u_x, u_m, u_mx, d_own, d_m)
+    first.wait()
+    total = x_own[...].astype(jnp.float32) + (a_own[...] + a_got[...].astype(jnp.float32) + vecs[0:1, :])
+    normed, rstd = norm_of(total)
+    n_out[...] = normed
+    r_out[...] = jnp.broadcast_to(rstd, r_out.shape)
+    low = (normed * vecs[1:2, :] + vecs[2:3, :]).astype(jnp.bfloat16)
+    h_out[...] = low
+    copies.wait()
+    wide = up.shape[1] // 4
+    for j in range(4):
+        pre = dot(low, up[:, wide * j : wide * (j + 1)]) + b_up[(2 * c + r) ^ j, 0:1, :]
+        cdf = 0.5 * (1.0 + lax.erf(pre * (1.0 / math.sqrt(2.0))))
+        density = jnp.exp(-0.5 * pre * pre) * (1.0 / math.sqrt(2.0 * math.pi))
+        z_out[j] = (pre * cdf).astype(jnp.bfloat16)
+        slope_out[j] = cdf + pre * density
+    result = dot(z_out[0], down[0:wide, :])
+    for j in range(1, 4):
+        result += dot(z_out[j], down[wide * j : wide * (j + 1), :])
+    y_out[...] = result
+    y_low[...] = result.astype(jnp.bfloat16)
+
+
+def backward_kernel(
+    y_own, y_got, normed1, g_own, g_x, slope, vecs, u_own, u_x, u_m, u_mx, d_own, d_m,
+    hid_out, dy_out, du_out, s_out, p_low, sums, up_sums,
+    up, down, grad, hid, sems, more,
+):
+    q, r, x, c = spot()
+    rows = grad.shape[0] // 2
+    first = Copies(more)
+    first.start(g_own, grad.at[pl.ds(pl.multiple_of(rows * x, rows), rows)])
+    first.start(g_x, grad.at[pl.ds(pl.multiple_of(rows * (1 - x), rows), rows)])
+    copies = Copies(sems)
+    load_feedforward(copies, up, down, u_own, u_x, u_m, u_mx, d_own, d_m)
+    first.wait()
+    h1 = normed1[...] * vecs[1:2, :] + vecs[2:3, :]
+    normed, rstd = norm_of(h1 + (y_own[...] + y_got[...].astype(jnp.float32) + vecs[3:4, :]))
+    hid[...] = (normed * vecs[4:5, :] + vecs[5:6, :]).astype(jnp.bfloat16)
+    hid_out[...] = hid[pl.ds(pl.multiple_of(rows * x, rows), rows), :]
+    cot = grad[...].astype(jnp.float32)
+    dy = norm_pull(cot * vecs[4:5, :], normed, rstd)
+    low = dy.astype(jnp.bfloat16)
+    dy_out[...] = low
+    sums[...] = jnp.zeros_like(sums)
+    sums[0:1, :] = jnp.sum(low.astype(jnp.float32), axis=0, keepdims=True)
+    sums[1:2, :] = jnp.sum(cot * normed, axis=0, keepdims=True)
+    sums[2:3, :] = jnp.sum(cot, axis=0, keepdims=True)
+    copies.wait()
+    wide = up.shape[1] // 4
+    result = jnp.zeros(dy.shape, jnp.float32)
+    for j in range(4):
+        du = (dot_nt(low, down[wide * j : wide * (j + 1), :]) * slope[j]).astype(jnp.bfloat16)
+        du_out[j] = du
+        total = jnp.sum(du.astype(jnp.float32), axis=0, keepdims=True)
+        up_sums[j] = jnp.broadcast_to(total, up_sums.shape[1:])
+        result += dot_nt(du, up[:, wide * j : wide * (j + 1)])
+    s_out[...] = dy + result
+    p_low[...] = result.astype(jnp.bfloat16)
+
+
+def attend_back_kernel(
+    s_own, p_got, normed1, rstd1, vecs, wo, mixed, q3, k3, v3, kt, lse, ids,
+    dr_out, da_out, dq_out, dkv_out, sums, qv_sums,
+    mask, do3, delta, dk, dv, dqt, whole,
+):
+    q, r, x, c = spot()
+    rows = dr_out.shape[0]
+    pairs = q3.shape[0]
+    half = 128 * pairs
+    fill_mask(ids, mask, 4 * r + 2 * c)
+    dh = s_own[...] + p_got[...].astype(jnp.float32)
+    normed = normed1[...]
+    dr = norm_pull(dh * vecs[1:2, :], normed, rstd1[:, 0:1])
+    whole[...] = dr
+    dr_out[...] = whole[pl.ds(pl.multiple_of(rows * x, rows), rows), :]
+    low = dr.astype(jnp.bfloat16)
+    da_out[...] = low
+    sums[...] = jnp.zeros_like(sums)
+    sums[0:1, :] = jnp.sum(low.astype(jnp.float32), axis=0, keepdims=True)
+    sums[1:2, :] = jnp.sum(dh * normed, axis=0, keepdims=True)
+    sums[2:3, :] = jnp.sum(dh, axis=0, keepdims=True)
+    d_o = dot_nt(low, wo[...]).astype(jnp.bfloat16)
+    products = jnp.transpose(d_o.astype(jnp.float32) * mixed[...].astype(jnp.float32))
+    for h in range(2 * pairs):
+        delta[h : h + 1, :] = jnp.sum(products[64 * h : 64 * (h + 1), :], axis=0, keepdims=True)
+    for p in range(pairs):
+        do3[p] = d_o[:, 128 * p : 128 * (p + 1)]
+    dk[...] = jnp.zeros_like(dk)
+    dv[...] = jnp.zeros_like(dv)
+    lane = lax.broadcasted_iota(jnp.int32, (2 * rows, 128), 1) // 64
+
+    def head(h, carry):
+        p = h // 2
+        here = lane == h % 2
+        query = (jnp.where(here, q3[p], 0) * 0.125).astype(jnp.bfloat16)
+        d_here = jnp.where(here, do3[p], 0).astype(jnp.bfloat16)
+        probs = jnp.exp(dot_nt(k3[p], query) + mask[...] - lse[pl.ds(h, 1), :])
+        d_probs = dot_nt(v3[p], d_here)
+        d_scores = (probs * (d_probs - delta[pl.ds(h, 1), :])).astype(jnp.bfloat16)
+        dv[p] += dot(probs.astype(jnp.bfloat16), d_here)
+        dk[p] += dot(d_scores, query)
+        dqt[h] = dot(kt[h], d_scores)
+        return carry
+
+    lax.fori_loop(0, 2 * pairs, head, 0)
+    dq = (jnp.transpose(dqt[...].reshape(half, 2 * rows)) * 0.125).astype(jnp.bfloat16)
+    dq_out[...] = dq
+    qv_sums[...] = jnp.zeros_like(qv_sums)
+    qv_sums[0:1, :] = jnp.sum(dq.astype(jnp.float32), axis=0, keepdims=True)
+    for p in range(pairs):
+        at = slice(128 * p, 128 * (p + 1))
+        dkv_out[:, at] = dk[p].astype(jnp.bfloat16)
+        value = dv[p].astype(jnp.bfloat16)
+        dkv_out[:, half + 128 * p : half + 128 * (p + 1)] = value
+        qv_sums[1:2, at] = jnp.sum(value.astype(jnp.float32), axis=0, keepdims=True)
+
+
+def input_grad_kernel(dq, dkv, w, send, keep, whole):
+    q, r, x, c = spot()
+    half = dq.shape[1]
+    rows = dq.shape[0] // 2
+    whole[...] = dot_nt(dkv[...], w[:, half:])
+    own = pl.ds(pl.multiple_of(rows * (4 * r + 2 * c), rows), 2 * rows)
+    whole[own, :] += dot_nt(dq[...], w[:, 0:half])
+    for b in range(2):
+        mine = pl.ds(pl.multiple_of(rows * (4 * b + 2 * c), rows), 2 * rows)
+        keep[b] = whole[mine, :]
+        theirs = pl.ds(pl.multiple_of(rows * (4 * b + 2 * (1 - c)), rows), 2 * rows)
+        send[b] = whole[theirs, :].astype(jnp.bfloat16)
+
+
+def kernel_call(body, name, ins, outs, scratch, cost, args):
+    return pl.pallas_call(
+        body,
+        name=name,
+        out_shape=[jax.ShapeDtypeStruct(shape, dtype) for shape, dtype, _ in outs],
+        in_specs=ins,
+        out_specs=[spec for _, _, spec in outs],
+        scratch_shapes=scratch,
+        cost_estimate=pl.CostEstimate(flops=cost, bytes_accessed=8 << 20, transcendentals=0),
+    )(*args)
+
+
+def plane_local(
+    tokens, cotangent, seq_ids, w_query, b_query, w_key, w_value, b_value, w_out, b_out,
+    attn_gain, attn_shift, w_up, b_up, w_down, b_down, ffn_gain, ffn_shift,
+):
+    q, r, x, c = spot()
+    q1, q0 = q // 2, q % 2
+    low, wide_type = jnp.bfloat16, jnp.float32
+    rows, width = tokens.shape[1:]
+    part = w_query.shape[0]
+    half = width // 2
+    inner = w_up.shape[1]
+    wide = inner // 8
+    keys = 8 * rows
+    pairs = half // 128
+
+    ids_rows = jnp.pad(seq_ids.astype(low), ((0, 15), (0, width - rows)))
+    blocks = [regroup(jnp.concatenate([tokens[0], ids_rows]))]
+    blocks.append(swap_x(blocks[0]))
+    blocks.append(swap_c(blocks[0]))
+    blocks.append(swap_c(blocks[1]))
+    blocks.append(swap_r(blocks[0]))
+    blocks.append(swap_r(blocks[1]))
+    blocks.append(swap_c(blocks[4]))
+    blocks.append(swap_c(blocks[5]))
+
+    def cut(w, side, size):
+        return lax.dynamic_slice_in_dim(w, side * size, size, 1)
+
+    qkv = (w_query, w_key, w_value)
+    qkv_x = swap_x(jnp.stack([cut(w, 1 - x, half) for w in qkv]))
+    qkv_m = swap_c(jnp.stack([cut(w, x, half) for w in qkv]))
+    qkv_mx = swap_c(qkv_x)
+    out_m = swap_c(w_out)
+    small = jnp.concatenate(
+        [b_query, b_value, b_out, attn_gain, attn_shift, b_down, ffn_gain, ffn_shift, b_up]
+    ).reshape(-1, half)
+    small = jnp.pad(small, ((0, 8 - small.shape[0]), (0, 0)))
+    small_x = swap_x(small)
+    small_m = swap_c(small)
+    small_mx = swap_c(small_x)
+    up_x = swap_x(cut(w_up, 1 - x, 4 * wide))
+    up_m = swap_c(cut(w_up, x, 4 * wide))
+    up_mx = swap_c(up_x)
+    down_m = swap_c(w_down)
+
+    chip = in_order(small, small_m, c).astype(wide_type)
+    other = in_order(small_x, small_mx, c).astype(wide_type)
+    every = in_order(chip, other, x).reshape(4, -1)
+    mine = chip.reshape(2, -1)
+    names = ("b_q", "b_v", "b_out", "gain1", "shift1", "b_down", "gain2", "shift2")
+    vec = {n: every[:, part * i : part * (i + 1)].reshape(1, width) for i, n in enumerate(names)}
+    vecs = jnp.concatenate(
+        [vec[n] for n in names[2:]] + [jnp.zeros((2, width), wide_type)]
+    )
+    bias = jnp.concatenate(
+        [mine[:, part * i : part * (i + 1)].reshape(1, half) for i in range(2)]
+        + [jnp.zeros((6, half), wide_type)]
+    )
+    up_bias = mine[:, 8 * part : 8 * part + 2 * wide].reshape(4, 1, wide)
+    up_bias = jnp.broadcast_to(up_bias, (4, 8, wide))
+
+    own = 2 * rows
+    x_all, w_all, wo_all, k3, v3, q3, mixed, lse, ids, a_own, a_low = kernel_call(
+        attend_kernel,
+        "attend",
+        [ANY] * 16 + [WHOLE],
+        [
+            ((keys, width), low, ANY),
+            ((width, 3 * half), low, ANY),
+            ((half, width), low, ANY),
+            ((pairs, keys, 128), low, ANY),
+            ((pairs, keys, 128), low, ANY),
+            ((pairs, own, 128), low, WHOLE),
+            ((own, half), low, WHOLE),
+            ((8, own), wide_type, WHOLE),
+            ((8, rows), wide_type, WHOLE),
+            ((own, width), wide_type, WHOLE),
+            ((own, width), low, WHOLE),
+        ],
+        [
+            pltpu.VMEM((keys, width), low),
+            pltpu.VMEM((8, 16, width), low),
+            pltpu.VMEM((width, 3 * half), low),
+            pltpu.VMEM((half, width), low),
+            pltpu.VMEM((pairs, keys, 128), low),
+            pltpu.VMEM((pairs, keys, 128), low),
+            pltpu.VMEM((2 * pairs, 64, keys), low),
+            pltpu.VMEM((pairs, own, 128), low),
+            pltpu.VMEM((2 * pairs, 64, own), wide_type),
+            pltpu.VMEM((keys, own), wide_type),
+            pltpu.SemaphoreType.DMA((30,)),
+            pltpu.SemaphoreType.DMA((5,)),
+        ],
+        6 * 10**9,
+        (*blocks, *qkv, qkv_x, qkv_m, qkv_mx, w_out, out_m, bias),
+    )
+    a_got = swap_x(a_low)
+    kt = jnp.swapaxes(k3, 1, 2).reshape(2 * pairs, 64, keys)
+
+    inner_weights = (w_up, up_x, up_m, up_mx, w_down, down_m)
+    inner_scratch = [
+        pltpu.VMEM((width, 4 * wide), low),
+        pltpu.VMEM((4 * wide, width), low),
+    ]
+    h_low, normed1, rstd1, z, slope, y_own, y_low = kernel_call(
+        forward_kernel,
+        "feedforward",
+        [WHOLE, WHOLE, ANY, WHOLE, WHOLE] + [ANY] * 6,
+        [
+            ((own, width), low, WHOLE),
+            ((own, width), wide_type, WHOLE),
+            ((own, 128), wide_type, WHOLE),
+            ((4, own, wide), low, WHOLE),
+            ((4, own, wide), wide_type, WHOLE),
+            ((own, width), wide_type, WHOLE),
+            ((own, width), low, WHOLE),
+        ],
+        inner_scratch
+        + [pltpu.VMEM((own, width), low), pltpu.SemaphoreType.DMA((20,)), pltpu.SemaphoreType.DMA((1,))],
+        2 * 10**9,
+        (a_own, a_got, x_all, vecs, up_bias, *inner_weights),
+    )
+    y_got = swap_x(y_low)
+
+    def over_plane(pieces):
+        return jnp.concatenate([pieces[0], swap_r(pieces[1]), swap_c(pieces[2]), swap_rc(pieces[3])])
+
+    def whole_plane(block):
+        beside = swap_r(block)
+        return jnp.concatenate([block, beside, swap_c(block), swap_c(beside)])
+
+    z_plane = over_plane([z[j] for j in range(4)])
+    h_plane = whole_plane(h_low)
+
+    cot = regroup(cotangent[0])
+    cot_x = swap_x(cot)
+    hidden, dy, du, s_own, p_low, sums2, up_sums = kernel_call(
+        backward_kernel,
+        "feedforward_back",
+        [WHOLE, WHOLE, WHOLE, ANY, ANY, WHOLE, WHOLE] + [ANY] * 6,
+        [
+            ((rows, width), low, WHOLE),
+            ((own, width), low, WHOLE),
+            ((4, own, wide), low, WHOLE),
+            ((own, width), wide_type, WHOLE),
+            ((own, width), low, WHOLE),
+            ((8, width), wide_type, WHOLE),
+            ((4, 8, wide), wide_type, WHOLE),
+        ],
+        inner_scratch
+        + [
+            pltpu.VMEM((own, width), low),
+            pltpu.VMEM((own, width), low),
+            pltpu.SemaphoreType.DMA((20,)),
+            pltpu.SemaphoreType.DMA((2,)),
+        ],
+        2 * 10**9,
+        (y_own, y_got, normed1, cot, cot_x, slope, vecs, *inner_weights),
+    )
+    p_got = swap_x(p_low)
+    hidden_out = regroup(hidden)[None]
+
+    dr, da, dq, dkv, sums1, qv_sums = kernel_call(
+        attend_back_kernel,
+        "attend_back",
+        [WHOLE] * 13,
+        [
+            ((rows, width), wide_type, WHOLE),
+            ((own, width), low, WHOLE),
+            ((own, half), low, WHOLE),
+            ((keys, 2 * half), low, WHOLE),
+            ((8, width), wide_type, WHOLE),
+            ((8, half), wide_type, WHOLE),
+        ],
+        [
+            pltpu.VMEM((keys, own), wide_type),
+            pltpu.VMEM((pairs, own, 128), low),
+            pltpu.VMEM((8, own), wide_type),
+            pltpu.VMEM((pairs, keys, 128), wide_type),
+            pltpu.VMEM((pairs, keys, 128), wide_type),
+            pltpu.VMEM((2 * pairs, 64, own), wide_type),
+            pltpu.VMEM((own, width), wide_type),
+        ],
+        6 * 10**9,
+        (s_own, p_got, normed1, rstd1, vecs, wo_all, mixed, q3, k3, v3, kt, lse, ids),
+    )
+
+    send, keep = kernel_call(
+        input_grad_kernel,
+        "input_grad",
+        [WHOLE] * 3,
+        [((2, own, width), low, WHOLE), ((2, own, width), wide_type, WHOLE)],
+        [pltpu.VMEM((keys, width), wide_type)],
+        10**9,
+        (dq, dkv, w_all),
+    )
+
+    def folded(kept, got):
+        return kept + got.astype(wide_type)
+
+    total = folded(keep, swap_c(send))
+    total = folded(take(total, r), swap_r(take(total, 1 - r).astype(low))).reshape(2, rows, width)
+    total = folded(take(total, x), swap_x(take(total, 1 - x).astype(low)))
+    tokens_grad = regroup((total + dr).astype(low))[None]
+
+    def swept(grad):
+        total = folded(take(grad, q0), swap_near(take(grad, 1 - q0).astype(low)))
+        return folded(take(total, q1), swap_far(take(total, 1 - q1).astype(low)))
+
+    def spread(block):
+        block = in_order(block, swap_far(block), q1)
+        block = in_order(block, swap_near(block), q0)
+        return in_order(block, swap_r(block), r)
+
+    dy_plane = whole_plane(dy)
+    du_plane = over_plane([du[j] for j in range(4)])
+    d_down = matmul_tn(z_plane, dy_plane).reshape(2, 2, wide // 4, width)
+    d_down = spread(swept(jnp.swapaxes(d_down, 0, 1)).astype(low))
+    w_down_grad = jnp.swapaxes(d_down, 1, 2).reshape(2 * wide, width).astype(wide_type)
+
+    d_up = matmul_tn(h_plane, du_plane).reshape(4, 2, 2, part // 4, wide)
+    d_up = swept(d_up.transpose(2, 1, 0, 3, 4)).astype(low).reshape(2, 2, part // 4, wide)
+    d_up = in_order(take(d_up, x), swap_x(take(d_up, 1 - x)), x)
+    d_up = jnp.swapaxes(d_up, 0, 1)
+    d_up = in_order(take(d_up, c), swap_c(take(d_up, 1 - c)), c)
+    d_up = spread(d_up)
+    w_up_grad = d_up.transpose(2, 1, 5, 4, 3, 0, 6).reshape(part, inner).astype(wide_type)
+
+    thin = part // 8
+    own_x = lax.dynamic_slice_in_dim(x_all, own * (2 * r + c), own, 0)
+    d_kv = matmul_tn(x_all, dkv).reshape(2, 2, 2, 2, 2, thin, 2, half)
+    d_q = matmul_tn(own_x, dq).reshape(2, 2, 2, 2, 2, thin, 1, half)
+    packed = jnp.concatenate([d_q, d_kv], axis=6).transpose(1, 2, 4, 3, 0, 6, 5, 7)
+    d_o = matmul_tn(mixed, da).reshape(2, 2, 2, 2, thin, 2, half).transpose(0, 1, 3, 2, 5, 4, 6)
+    packed = jnp.concatenate([packed.reshape(2, 2, 2, 2, 6, thin, half), d_o], axis=4)
+    packed = packed.reshape(2, 8, 8 * thin, half)
+
+    bits = up_sums[:, 0, :].reshape(2, 2, wide)
+    bits = jnp.where(c == 0, bits, bits[::-1])
+    bits = jnp.where(r == 0, bits, bits[:, ::-1]).reshape(4, wide)
+    wides = jnp.concatenate([sums1[:3], sums2[:3]]).reshape(6, 2, half)
+    wides = jnp.where(x == 0, wides[:, 0], wides[:, 1])
+    lines = jnp.concatenate([qv_sums[:2], bits, wides, jnp.zeros((4, half), wide_type)])
+
+    def step(block, lines, swap, bit):
+        block = block.reshape((2, -1, half))
+        out = jnp.concatenate([take(block, 1 - bit), lines]).astype(low)
+        got = swap(out).astype(wide_type)
+        count = block.shape[1]
+        return take(block, bit) + got[:count], lines + got[count:]
+
+    block, lines = step(packed, lines, swap_c, c)
+    block, lines = step(block, lines, swap_r, r)
+    block, lines = step(block, lines, swap_near, q0)
+    block, lines = step(block, lines, swap_far, q1)
+    block = block.astype(low)
+    sides = block[: 6 * thin].reshape(2, 3 * thin, half)
+    sides = in_order(take(sides, x), swap_x(take(sides, 1 - x)), x).reshape(6 * thin, half)
+    block = spread(jnp.concatenate([sides, block[6 * thin :]]).reshape(8, thin, half))
+    block = block.transpose(0, 2, 1, 4, 3, 5).reshape(part, 8, half).astype(wide_type)
+    w_query_grad, w_key_grad, w_value_grad = (
+        jnp.concatenate([block[:, t], block[:, 3 + t]], axis=1) for t in range(3)
+    )
+    w_out_grad = block[:, 6:8].reshape(part, width)
+
+    pieces = take(jnp.swapaxes(lines.reshape(-1, 2, part), 0, 1), c)
+    b_up_grad = take(lines[2:6].reshape(2, 2 * wide), c)
+    return (
+        hidden_out,
+        tokens_grad,
+        w_query_grad,
+        pieces[0],
+        w_key_grad,
+        w_value_grad,
+        pieces[1],
+        w_out_grad,
+        pieces[6],
+        pieces[7],
+        pieces[8],
+        w_up_grad,
+        b_up_grad,
+        w_down_grad,
+        pieces[9],
+        pieces[10],
+        pieces[11],
+    )
+
+
+def plane_solution(mesh):
+    planes, cycle = mesh.shape["shard"], mesh.shape["ctx"]
+    grid = Mesh(mesh.devices.reshape(planes, cycle // planes, 2, 2), AXES)
+    shard, ctx = ("x", "c"), ("q", "r")
+    tokens, matrix, vector = P(shard, ctx, None), P(shard, None), P(shard)
+    return jax.shard_map(
+        plane_local,
+        mesh=grid,
+        in_specs=(
+            tokens, tokens, P(shard, ctx), matrix, vector, matrix, matrix, vector, matrix, vector,
+            vector, vector, matrix, vector, matrix, vector, vector, vector,
+        ),
+        out_specs=(
+            tokens, tokens, matrix, vector, matrix, matrix, vector, matrix, vector,
+            vector, vector, matrix, vector, matrix, vector, vector, vector,
+        ),
+        check_vma=False,
+    )
+
+
+def solution(mesh):
+    if mesh.shape["shard"] == 4 and mesh.shape["ctx"] == 8:
+        return plane_solution(mesh)
+    return ring_solution(mesh)

time: 873 us -> 317 us (0.36)
  blocking collectives: 328 us -> 0 us
  waiting for transfers between devices: 320 us -> 114 us
  matrix products: 60.7 us -> 11.8 us
  Pallas kernels: 0 us -> 43.7 us
  between operations: 17.2 us -> 1.68 us
    psum x1 -> x0, blocking collectives: 301 us -> none  [local(): lax.psum((shares[0], shares[1], shares[2], shares[3], shares[4], shares[5...]
    reduce_scatter x3 -> x0, waiting for transfers between devices: 128 us -> none  [the longest x1 50.4 us: local(): lax.psum_scatter(d_up_mat.astype(jnp.bfloat16), 'shard', scatter_dimensio...]
    dot_general x68 -> x0, matrix products: 49.7 us -> none  [the longest x6 17.8 us: matmul(): return jnp.dot(left, right, preferred_element_type=jnp.float32)]
    pallas_call x0 -> x5, Pallas kernels: none -> 43.7 us  [kernel_call(): pl.pallas_call(body, name=name, out_shape=[jax.ShapeDtypeStruct(shape, dt...]
    unnamed x15 -> x0, waiting for transfers between devices: 29.9 us -> none
    ppermute x61, starting transfers between devices: 41.4 us -> 70.3 us  [moved(): lax.ppermute(block, AXES, [(number(s), number(move(*s))) for s in spots])]
    ppermute x61, waiting for transfers between devices: 142 us -> 114 us  [moved(): lax.ppermute(block, AXES, [(number(s), number(move(*s))) for s in spots])]
    while x52 -> x0, local copies, waits for them, and re-layouts: 24.2 us -> none
  transfers between devices with their start and end apart: 78 -> 61, of which waited for: 31 -> 18; matrix products, arithmetic and copies ran while one was open for 13% -> 22% of each run, Pallas kernels for 0% -> 14%
where the time goes in v1:
time: 317 us; the launch traced here: 315 us
  waiting for transfers between devices  114 us (36%)
  starting transfers between devices  70.3 us (22%)
  local copies, waits for them, and re-layouts  52.1 us (16%)
  Pallas kernels  43.7 us (14%)
  other arithmetic  21.3 us (7%)
  matrix products  11.8 us (4%)
    ppermute x61, waiting for transfers between devices, moved(): lax.ppermute(block, AXES, [(number(s), number(move(*s))) for s in spots])  114 us
    ppermute x61, starting transfers between devices, moved(): lax.ppermute(block, AXES, [(number(s), number(move(*s))) for s in spots])  70.3 us
    pallas_call x5, Pallas kernels, kernel_call(): pl.pallas_call(body, name=name, out_shape=[jax.ShapeDtypeStruct(shape, dt...  43.7 us
    dot_general x5, matrix products, matmul_tn(): lax.dot_general(left, right, (((0,), (0,)), ((), ())), preferred_element_...  11.8 us
    reshape x6, local copies, waits for them, and re-layouts, plane_local(): every[:, part * i:part * (i + 1)].reshape(1, width)  6.71 us
  transfers between devices with their start and end apart: 61, of which 18 were waited for; matrix products, arithmetic and copies ran while one was open for 22% of the time, Pallas kernels for 14%

profile of v1, /device:TPU:0, one launch (start us, length us, event | category | flops | bytes accessed | tf_op | source)
XLA Modules:
  0.0 315.1 jit_solution(17756446983212795477)
XLA Ops:
  0.7 6.1 %concatenate.266 = bf16[2304]{0:T(1024)(128)(2,1)S(1)} concatenate(bf16[192]{0:T(256)(128)(2,1)} %param.22, bf16[192]{0:T(256)(128)(2,1)} %param.25, bf16[192]{0:T(256)(128)(2,1)} %param.27, bf16[192]{0:T(256)(128)(2,1)} %param.28, bf16[192]{0:T(256)(128)(2,1)} %param.29, bf16[192]{0:T(256)(128)(2,1)} %param.33, bf16[192]{0:T(256)(128)(2,1)} %param.34, bf16[192]{0:T(256)(128)(2,1)} %param.35, ...), dimensions={0} | concatenate | bytes 9216 | tf_op jit(solution)/shard_map/concatenate | solution.py:848
  7.3 2.6 collective-permute-start.14
  10.5 1.6 fusion.46
  12.2 3.5 %collective-permute-start = (bf16[144,768]{1,0:T(8,128)(2,1)}, bf16[144,768]{1,0:T(8,128)(2,1)}, u32[]{:S(2)}, u32[]{:S(2)}) collective-permute-start(bf16[144,768]{1,0:T(8,128)(2,1)} %fusion.46), channel_id=1, source_target_pairs={{0,0},{1,16},{2,8},{3,24},{4,4},{5,20},{6,12},{7,28},{8,2},{9,18},... | collective-permute-start | bytes 663560 | tf_op jit(solution)/shard_map/ppermute | solution.py:479
  18.7 1.5 collective-permute-start.8
  20.2 1.9 collective-permute-start.11
  24.8 1.8 collective-permute-start.1
  26.8 23.5 %collective-permute-done.1.b1 = bf16[144,768]{1,0:T(8,128)(2,1)} collective-permute-done((bf16[144,768]{1,0:T(8,128)(2,1)}, bf16[144,768]{1,0:T(8,128)(2,1)}, u32[]{:S(2)}, u32[]{:S(2)}) %collective-permute-start.1) | collective-permute-done | bytes 221216 | tf_op jit(solution)/shard_map/ppermute | solution.py:479
  50.3 1.9 collective-permute-start.4
  53.7 5.1 %collective-permute-done.4.b4 = bf16[144,768]{1,0:T(8,128)(2,1)} collective-permute-done((bf16[144,768]{1,0:T(8,128)(2,1)}, bf16[144,768]{1,0:T(8,128)(2,1)}, u32[]{:S(2)}, u32[]{:S(2)}) %collective-permute-start.4) | collective-permute-done | bytes 221216 | tf_op jit(solution)/shard_map/ppermute | solution.py:479
  59.4 3.7 %collective-permute-done.5.b5 = bf16[144,768]{1,0:T(8,128)(2,1)} collective-permute-done((bf16[144,768]{1,0:T(8,128)(2,1)}, bf16[144,768]{1,0:T(8,128)(2,1)}, u32[]{:S(2)}, u32[]{:S(2)}) %collective-permute-start.5) | collective-permute-done | bytes 221216 | tf_op jit(solution)/shard_map/ppermute | solution.py:479
  63.1 1.4 maximum_maximum_fusion.bias
  66.9 3.1 collective-permute-start.21
  70.5 11.4 %attend.1 = (bf16[1024,768]{1,0:T(8,128)(2,1)}, bf16[768,1152]{1,0:T(8,128)(2,1)}, bf16[384,768]{1,0:T(8,128)(2,1)}, bf16[3,1024,128]{2,1,0:T(8,128)(2,1)}, bf16...) custom-call(bf16[144,768]{1,0:T(8,128)(2,1)} %collective-permute-don, ...), custom_call_target="tpu_custom_call" | custom-call | flops 6000000000 | bytes 8388608 | tf_op jit(solution)/shard_map/attend/pallas_call | solution.py:804
  81.9 4.6 %collective-permute-start.13 = (bf16[256,768]{1,0:T(8,128)(2,1)}, bf16[256,768]{1,0:T(8,128)(2,1)}, u32[]{:S(2)}, u32[]{:S(2)}) collective-permute-start(bf16[256,768]{1,0:T(8,128)(2,1)} %get-tuple-element.51), channel_id=1, source_target_pairs={{0,2},{1,3},{2,0},{3,1},{4,6},{5,7},{6,4},{7,5},{8,10},{9,11},{10,... | collective-permute-start | bytes 1179656 | tf_op jit(solution)/shard_map/ppermute | solution.py:479
  92.9 1.4 reshape.955
  95.6 1.4 concatenate.268.vecs
  98.2 7.8 %feedforward.1 = (bf16[256,768]{1,0:T(8,128)(2,1)}, f32[256,768]{1,0:T(8,128)}, f32[256,128]{1,0:T(8,128)}, bf16[4,256,384]{2,1,0:T(8,128)(2,1)}, f32[4,256,384]...) custom-call(f32[256,768]{1,0:T(8,128)} %get-tuple-element.50.a_own, ...), custom_call_target="tpu_custom_call" | custom-call | flops 2000000000 | bytes 8388608 | tf_op jit(solution)/shard_map/feedforward/pallas_call | solution.py:804
  109.4 1.5 collective-permute-start.37
  111.9 9.7 %collective-permute-done.22.g_x = bf16[128,768]{1,0:T(8,128)(2,1)S(1)} collective-permute-done((bf16[128,768]{1,0:T(8,128)(2,1)}, bf16[128,768]{1,0:T(8,128)(2,1)S(1)}, u32[]{:S(2)}, u32[]{:S(2)}) %collective-permute-start.22) | collective-permute-done | bytes 196640 | tf_op jit(solution)/shard_map/ppermute | solution.py:479
  122.5 8.8 %feedforward_back.1 = (bf16[128,768]{1,0:T(8,128)(2,1)}, bf16[256,768]{1,0:T(8,128)(2,1)}, bf16[4,256,384]{2,1,0:T(8,128)(2,1)}, f32[256,768]{1,0:T(8,128)}, bf1...) custom-call(f32[256,768]{1,0:T(8,128)} %get-tuple-element.53.y_own, bf16[256,768]{1,0:T(8,128)(2,1)} %copy-done.13, ...), custom_call_target="tpu_custom_call" | custom-call | flops 2000000000 | bytes 8388608 | tf_op jit(solution)/shard_map/feedforward_back/pallas_call | solution.py:804
  131.2 1.6 collective-permute-start.23
  136.1 2.1 slice_bitcast_fusion.14
  138.2 1.9 collective-permute-start.42
  140.9 1.5 collective-permute-start.40
  142.4 5.3 %collective-permute-done.24.p_got = bf16[256,768]{1,0:T(8,128)(2,1)S(1)} collective-permute-done((bf16[256,768]{1,0:T(8,128)(2,1)}, bf16[256,768]{1,0:T(8,128)(2,1)S(1)}, u32[]{:S(2)}, u32[]{:S(2)}) %collective-permute-start.24) | collective-permute-done | bytes 393248 | tf_op jit(solution)/shard_map/ppermute | solution.py:479
  148.4 10.3 %attend_back.1 = (f32[128,768]{1,0:T(8,128)}, bf16[256,768]{1,0:T(8,128)(2,1)}, bf16[256,384]{1,0:T(8,128)(2,1)}, bf16[1024,768]{1,0:T(8,128)(2,1)}, f32[8,768]{1,0:T(8,128)}, /*index=5*/f32[8,384]{1,0:T(8,128)}) custom-call(f32[256,768]{1,0:T(8,128)} %get-tuple-element.58.s_own, bf16[256,768]{1,0:T(8,128)(2,1)} %copy-done.29, ...), custom_call_target="tpu_custom_call" | custom-call | flops 6000000000 | bytes 8388608 | tf_op jit(solution)/shard_map/attend_back/pallas_call | solution.py:804
  162.1 4.3 %fusion.65 = f32[768,768]{1,0:T(8,128)} fusion(bf16[1024,768]{1,0:T(8,128)(2,1)S(1)} %copy-done.4, bf16[1024,768]{1,0:T(8,128)(2,1)} %get-tuple-element.69.dkv), kind=kOutput, calls=%fused_computation.175 | convolution fusion | flops 1207959552 | bytes 5505024 | tf_op jit(solution)/shard_map/dot_general | solution.py:29
  166.4 2.9 reshape.961
  170.0 1.4 collective-permute-start.52
  172.2 2.6 fusion
  175.6 1.4 fusion.38
  177.3 2.8 pad_maximum_fusion
  180.7 1.8 fusion.16
  182.5 1.8 collective-permute-done.43
  187.0 5.6 %input_grad.1 = (bf16[2,256,768]{2,1,0:T(8,128)(2,1)}, f32[2,256,768]{2,1,0:T(8,128)}) custom-call(bf16[256,384]{1,0:T(8,128)(2,1)} %get-tuple-element.68.dq, bf16[1024,768]{1,0:T(8,128)(2,1)} %get-tuple-element.69.dkv, bf16[768,1152]{1,0:T(8,128)(2,1)} %get-tuple-element.70.w), custom_call_target="tpu_custom_call" | custom-call | flops 1000000000 | bytes 8388608 | tf_op jit(solution)/shard_map/input_grad/pallas_call | solution.py:804
  192.6 1.5 collective-permute-done.44
  194.1 1.5 collective-permute-start.50
  196.2 4.5 %collective-permute-done.50 = bf16[256,384]{1,0:T(8,128)(2,1)S(1)} collective-permute-done((bf16[256,384]{1,0:T(8,128)(2,1)S(1)}, bf16[256,384]{1,0:T(8,128)(2,1)S(1)}, u32[]{:S(2)}, u32[]{:S(2)}) %collective-permute-start.50) | collective-permute-done | bytes 196640 | tf_op jit(solution)/shard_map/ppermute | solution.py:479
  200.7 2.4 collective-permute-start.45
  203.1 2.2 fusion.8
  206.9 2.2 collective-permute-start.47
  209.1 9.1 %collective-permute-done.56 = bf16[2,96,768]{2,1,0:T(8,128)(2,1)S(1)} collective-permute-done((bf16[2,96,768]{2,1,0:T(8,128)(2,1)S(1)}, bf16[2,96,768]{2,1,0:T(8,128)(2,1)S(1)}, u32[]{:S(2)}, u32[]{:S(2)}) %collective-permute-start.56) | collective-permute-done | bytes 294944 | tf_op jit(solution)/shard_map/ppermute | solution.py:479
  218.5 2.5 collective-permute-start.48
  221.2 6.2 %collective-permute-done.57 = bf16[96,768]{1,0:T(8,128)(2,1)S(1)} collective-permute-done((bf16[96,768]{1,0:T(8,128)(2,1)S(1)}, bf16[96,768]{1,0:T(8,128)(2,1)S(1)}, u32[]{:S(2)}, u32[]{:S(2)}) %collective-permute-start.57) | collective-permute-done | bytes 147488 | tf_op jit(solution)/shard_map/ppermute | solution.py:479
  227.8 1.5 collective-permute-start.26
  229.3 7.5 %collective-permute-done.58 = bf16[96,768]{1,0:T(8,128)(2,1)S(1)} collective-permute-done((bf16[96,768]{1,0:T(8,128)(2,1)S(1)}, bf16[96,768]{1,0:T(8,128)(2,1)S(1)}, u32[]{:S(2)}, u32[]{:S(2)}) %collective-permute-start.58) | collective-permute-done | bytes 147488 | tf_op jit(solution)/shard_map/ppermute | solution.py:479
  237.6 1.5 collective-permute-start.30
  240.1 2.0 collective-permute-start.27
  242.1 12.0 %collective-permute-done.30 = bf16[784,384]{1,0:T(8,128)(2,1)S(1)} collective-permute-done((bf16[784,384]{1,0:T(8,128)(2,1)S(1)}, bf16[784,384]{1,0:T(8,128)(2,1)S(1)}, u32[]{:S(2)}, u32[]{:S(2)}) %collective-permute-start.30) | collective-permute-done | bytes 602144 | tf_op jit(solution)/shard_map/ppermute | solution.py:479
  254.5 2.1 collective-permute-start.31
  258.3 1.4 collective-permute-start.60
  260.6 3.5 %collective-permute-done.31 = bf16[400,384]{1,0:T(8,128)(2,1)S(1)} collective-permute-done((bf16[400,384]{1,0:T(8,128)(2,1)S(1)}, bf16[400,384]{1,0:T(8,128)(2,1)S(1)}, u32[]{:S(2)}, u32[]{:S(2)}) %collective-permute-start.31) | collective-permute-done | bytes 307232 | tf_op jit(solution)/shard_map/ppermute | solution.py:479
  264.3 2.6 collective-permute-start.32
  267.1 1.8 copy.76
  268.9 3.2 %reshape.978 = f32[192,3072]{1,0:T(8,128)} reshape(f32[2,2,48,2,2,2,384]{6,5,4,3,2,1,0:T(2,128)S(1)} %copy.76) | data formatting | bytes 4718592 | tf_op jit(solution)/shard_map/convert_element_type | solution.py:1041
  273.3 7.5 %collective-permute-start.33 = (bf16[72,384]{1,0:T(8,128)(2,1)S(1)}, bf16[72,384]{1,0:T(8,128)(2,1)S(1)}, u32[]{:S(2)}, u32[]{:S(2)}) collective-permute-start(bf16[72,384]{1,0:T(8,128)(2,1)S(1)} %get-tuple-element.117), channel_id=1, source_target_pairs={{0,2},{1,3},{2,0},{3,1},{4,6},{5,7},{6,4},{7,5},{8,10},{9,11},{10,... | collective-permute-start | bytes 165896 | tf_op jit(solution)/shard_map/ppermute | solution.py:479
  280.8 1.5 convert_bitcast_fusion
  282.3 1.6 copy.77
  283.9 2.2 collective-permute-start.34
  287.6 4.0 %collective-permute-done.34 = bf16[8,24,384]{2,1,0:T(8,128)(2,1)S(1)} collective-permute-done((bf16[8,24,384]{2,1,0:T(8,128)(2,1)S(1)}, bf16[8,24,384]{2,1,0:T(8,128)(2,1)S(1)}, u32[]{:S(2)}, u32[]{:S(2)}) %collective-permute-start.34) | collective-permute-done | bytes 147488 | tf_op jit(solution)/shard_map/ppermute | solution.py:479
  291.9 6.6 %collective-permute-done.35 = bf16[2,8,24,384]{3,2,0,1:T(8,128)(2,1)S(1)} collective-permute-done((bf16[2,8,24,384]{3,2,0,1:T(8,128)(2,1)S(1)}, bf16[2,8,24,384]{3,2,0,1:T(8,128)(2,1)S(1)}, u32[]{:S(2)}, u32[]{:S(2)}) %collective-permute-start.35) | collective-permute-done | bytes 294944 | tf_op jit(solution)/shard_map/ppermute | solution.py:479
  298.6 1.5 collective-permute-start.36
  301.0 8.9 %collective-permute-done.36 = bf16[2,2,8,24,384]{4,3,0,1,2:T(8,128)(2,1)S(1)} collective-permute-done((bf16[2,2,8,24,384]{4,3,0,1,2:T(8,128)(2,1)S(1)}, bf16[2,2,8,24,384]{4,3,0,1,2:T(8,128)(2,1)S(1)}, u32[]{:S(2)}, u32[]{:S(2)}) %collective-permute-start.36) | collective-permute-done | bytes 589856 | tf_op jit(solution)/shard_map/ppermute | solution.py:479
  (278 shorter events, 57.1 us)
Async XLA Ops:
  6.8 16.1 %collective-permute-start.12 = (bf16[8,384]{1,0:T(8,128)(2,1)S(1)}, bf16[8,384]{1,0:T(8,128)(2,1)S(1)}, u32[]{:S(2)}, u32[]{:S(2)}) collective-permute-start(bf16[8,384]{1,0:T(8,128)(2,1)S(1)} %get-tuple-element.135), channel_id=1, source_target_pairs={{0,1},{1,0},{2,3},{3,2},{4,5},{5,4},{6,7},{7,6},{8,9},{9,8},{10,11... | collective-permute-start | bytes 18440 | tf_op jit(solution)/shard_map/ppermute | solution.py:479
  7.3 17.3 %collective-permute-start.14 = (bf16[8,384]{1,0:T(8,128)(2,1)S(1)}, bf16[8,384]{1,0:T(8,128)(2,1)S(1)}, u32[]{:S(2)}, u32[]{:S(2)}) collective-permute-start(bf16[8,384]{1,0:T(8,128)(2,1)S(1)} %get-tuple-element.135), channel_id=1, source_target_pairs={{0,2},{1,3},{2,0},{3,1},{4,6},{5,7},{6,4},{7,5},{8,10},{9,11},{10,... | collective-permute-start | bytes 18440 | tf_op jit(solution)/shard_map/ppermute | solution.py:479
  12.2 12.6 %collective-permute-start = (bf16[144,768]{1,0:T(8,128)(2,1)}, bf16[144,768]{1,0:T(8,128)(2,1)}, u32[]{:S(2)}, u32[]{:S(2)}) collective-permute-start(bf16[144,768]{1,0:T(8,128)(2,1)} %fusion.46), channel_id=1, source_target_pairs={{0,0},{1,16},{2,8},{3,24},{4,4},{5,20},{6,12},{7,28},{8,2},{9,18},... | collective-permute-start | bytes 663560 | tf_op jit(solution)/shard_map/ppermute | solution.py:479
  18.7 33.6 %collective-permute-start.8 = (bf16[3,192,384]{2,1,0:T(8,128)(2,1)}, bf16[3,192,384]{2,1,0:T(8,128)(2,1)}, u32[]{:S(2)}, u32[]{:S(2)}) collective-permute-start(bf16[3,192,384]{2,1,0:T(8,128)(2,1)} %pad_maximum_fusion.8), channel_id=1, source_target_pairs={{0,2},{1,3},{2,0},{3,1},{4,6},{5,7},{6,4},{7,5},{8,10},{9,11},{10,... | collective-permute-start | bytes 1327112 | tf_op jit(solution)/shard_map/ppermute | solution.py:479
  20.2 6.4 %collective-permute-start.11 = (bf16[192,768]{1,0:T(8,128)(2,1)}, bf16[192,768]{1,0:T(8,128)(2,1)}, u32[]{:S(2)}, u32[]{:S(2)}) collective-permute-start(bf16[192,768]{1,0:T(8,128)(2,1)} %w_o.1), channel_id=1, source_target_pairs={{0,1},{1,0},{2,3},{3,2},{4,5},{5,4},{6,7},{7,6},{8,9},{9,8},{10,11... | collective-permute-start | bytes 884744 | tf_op jit(solution)/shard_map/ppermute | solution.py:479
  22.0 36.8 %copy-start.2 = (bf16[768,768]{1,0:T(8,128)(2,1)S(1)}, bf16[768,768]{1,0:T(8,128)(2,1)}, u32[]{:S(2)}) copy-start(bf16[768,768]{1,0:T(8,128)(2,1)} %d_own.3) | copy-start | bytes 3538948
  22.9 36.4 %collective-permute-start.16 = (bf16[192,1536]{1,0:T(8,128)(2,1)S(1)}, bf16[192,1536]{1,0:T(8,128)(2,1)S(1)}, u32[]{:S(2)}, u32[]{:S(2)}) collective-permute-start(bf16[192,1536]{1,0:T(8,128)(2,1)S(1)} %get-tuple-element.92), channel_id=1, source_target_pairs={{0,2},{1,3},{2,0},{3,1},{4,6},{5,7},{6,4},{7,5},{8,10},{9,11},{10,... | collective-permute-start | bytes 1769480 | tf_op jit(solution)/shard_map/ppermute | solution.py:479
  24.7 29.0 %copy-start.26 = (bf16[8,384]{1,0:T(8,128)(2,1)}, bf16[8,384]{1,0:T(8,128)(2,1)S(1)}, u32[]{:S(2)}) copy-start(bf16[8,384]{1,0:T(8,128)(2,1)S(1)} %collective-permute-done.14) | copy-start | bytes 18436
  24.7 34.2 %collective-permute-start.9 = (bf16[3,192,384]{2,1,0:T(8,128)(2,1)}, bf16[3,192,384]{2,1,0:T(8,128)(2,1)}, u32[]{:S(2)}, u32[]{:S(2)}) collective-permute-start(bf16[3,192,384]{2,1,0:T(8,128)(2,1)} %pad_maximum_fusion.9), channel_id=1, source_target_pairs={{0,1},{1,0},{2,3},{3,2},{4,5},{5,4},{6,7},{7,6},{8,9},{9,8},{10,11... | collective-permute-start | bytes 1327112 | tf_op jit(solution)/shard_map/ppermute | solution.py:479
  24.8 25.5 %collective-permute-start.1 = (bf16[144,768]{1,0:T(8,128)(2,1)}, bf16[144,768]{1,0:T(8,128)(2,1)}, u32[]{:S(2)}, u32[]{:S(2)}) collective-permute-start(bf16[144,768]{1,0:T(8,128)(2,1)} %collective-permute-done.b0), channel_id=1, source_target_pairs={{0,2},{1,3},{2,0},{3,1},{4,6},{5,7},{6,4},{7,5},{8,10},{9,11},{10,... | collective-permute-start | bytes 663560 | tf_op jit(solution)/shard_map/ppermute | solution.py:479
  26.6 25.6 %collective-permute-start.2 = (bf16[144,768]{1,0:T(8,128)(2,1)}, bf16[144,768]{1,0:T(8,128)(2,1)S(1)}, u32[]{:S(2)}, u32[]{:S(2)}) collective-permute-start(bf16[144,768]{1,0:T(8,128)(2,1)} %collective-permute-done.b0), channel_id=1, source_target_pairs={{0,1},{1,0},{2,3},{3,2},{4,5},{5,4},{6,7},{7,6},{8,9},{9,8},{10,11... | collective-permute-start | bytes 663560 | tf_op jit(solution)/shard_map/ppermute | solution.py:479
  50.3 8.5 %collective-permute-start.4 = (bf16[144,768]{1,0:T(8,128)(2,1)}, bf16[144,768]{1,0:T(8,128)(2,1)}, u32[]{:S(2)}, u32[]{:S(2)}) collective-permute-start(bf16[144,768]{1,0:T(8,128)(2,1)} %collective-permute-done.b0), channel_id=1, source_target_pairs={{0,4},{1,5},{2,6},{3,7},{4,0},{5,1},{6,2},{7,3},{8,12},{9,13},{10,... | collective-permute-start | bytes 663560 | tf_op jit(solution)/shard_map/ppermute | solution.py:479
  52.2 10.9 %collective-permute-start.5 = (bf16[144,768]{1,0:T(8,128)(2,1)}, bf16[144,768]{1,0:T(8,128)(2,1)}, u32[]{:S(2)}, u32[]{:S(2)}) collective-permute-start(bf16[144,768]{1,0:T(8,128)(2,1)} %collective-permute-done.1.b1), channel_id=1, source_target_pairs={{0,4},{1,5},{2,6},{3,7},{4,0},{5,1},{6,2},{7,3},{8,12},{9,13},{10,... | collective-permute-start | bytes 663560 | tf_op jit(solution)/shard_map/ppermute | solution.py:479
  52.3 17.7 %collective-permute-start.10 = (bf16[3,192,384]{2,1,0:T(8,128)(2,1)}, bf16[3,192,384]{2,1,0:T(8,128)(2,1)}, u32[]{:S(2)}, u32[]{:S(2)}) collective-permute-start(bf16[3,192,384]{2,1,0:T(8,128)(2,1)} %collective-permute-done.8.w_x), channel_id=1, source_target_pairs={{0,1},{1,0},{2,3},{3,2},{4,5},{5,4},{6,7},{7,6},{8,9},{9,8},{10,11... | collective-permute-start | bytes 1327112 | tf_op jit(solution)/shard_map/ppermute | solution.py:479
  58.8 38.1 %collective-permute-start.19 = (bf16[768,768]{1,0:T(8,128)(2,1)S(1)}, bf16[768,768]{1,0:T(8,128)(2,1)S(1)}, u32[]{:S(2)}, u32[]{:S(2)}) collective-permute-start(bf16[768,768]{1,0:T(8,128)(2,1)S(1)} %copy-done.2), channel_id=1, source_target_pairs={{0,1},{1,0},{2,3},{3,2},{4,5},{5,4},{6,7},{7,6},{8,9},{9,8},{10,11... | collective-permute-start | bytes 3538952 | tf_op jit(solution)/shard_map/ppermute | solution.py:479
  58.8 7.5 %collective-permute-start.3 = (bf16[144,768]{1,0:T(8,128)(2,1)}, bf16[144,768]{1,0:T(8,128)(2,1)}, u32[]{:S(2)}, u32[]{:S(2)}) collective-permute-start(bf16[144,768]{1,0:T(8,128)(2,1)} %collective-permute-done.1.b1), channel_id=1, source_target_pairs={{0,1},{1,0},{2,3},{3,2},{4,5},{5,4},{6,7},{7,6},{8,9},{9,8},{10,11... | collective-permute-start | bytes 663560 | tf_op jit(solution)/shard_map/ppermute | solution.py:479
  59.4 7.5 %collective-permute-start.6 = (bf16[144,768]{1,0:T(8,128)(2,1)}, bf16[144,768]{1,0:T(8,128)(2,1)}, u32[]{:S(2)}, u32[]{:S(2)}) collective-permute-start(bf16[144,768]{1,0:T(8,128)(2,1)} %collective-permute-done.4.b4), channel_id=1, source_target_pairs={{0,1},{1,0},{2,3},{3,2},{4,5},{5,4},{6,7},{7,6},{8,9},{9,8},{10,11... | collective-permute-start | bytes 663560 | tf_op jit(solution)/shard_map/ppermute | solution.py:479
  63.1 6.9 %collective-permute-start.7 = (bf16[144,768]{1,0:T(8,128)(2,1)}, bf16[144,768]{1,0:T(8,128)(2,1)}, u32[]{:S(2)}, u32[]{:S(2)}) collective-permute-start(bf16[144,768]{1,0:T(8,128)(2,1)} %collective-permute-done.5.b5), channel_id=1, source_target_pairs={{0,1},{1,0},{2,3},{3,2},{4,5},{5,4},{6,7},{7,6},{8,9},{9,8},{10,11... | collective-permute-start | bytes 663560 | tf_op jit(solution)/shard_map/ppermute | solution.py:479
  66.4 30.6 %collective-permute-start.17 = (bf16[192,1536]{1,0:T(8,128)(2,1)}, bf16[192,1536]{1,0:T(8,128)(2,1)S(1)}, u32[]{:S(2)}, u32[]{:S(2)}) collective-permute-start(bf16[192,1536]{1,0:T(8,128)(2,1)} %get-tuple-element.91), channel_id=1, source_target_pairs={{0,1},{1,0},{2,3},{3,2},{4,5},{5,4},{6,7},{7,6},{8,9},{9,8},{10,11... | collective-permute-start | bytes 1769480 | tf_op jit(solution)/shard_map/ppermute | solution.py:479
  66.9 30.1 %copy-start.25 = (f32[4,384]{1,0:T(4,128)S(1)}, f32[4,384]{1,0:T(4,128)}, u32[]{:S(2)}) copy-start(f32[4,384]{1,0:T(4,128)} %broadcast_in_dim.26) | copy-start | bytes 18436
  66.9 40.0 %collective-permute-start.21 = (bf16[128,768]{1,0:T(8,128)(2,1)}, bf16[128,768]{1,0:T(8,128)(2,1)}, u32[]{:S(2)}, u32[]{:S(2)}) collective-permute-start(bf16[128,768]{1,0:T(8,128)(2,1)} %bitcast.280), channel_id=1, source_target_pairs={{0,0},{1,16},{2,8},{3,24},{4,4},{5,20},{6,12},{7,28},{8,2},{9,18},... | collective-permute-start | bytes 589832 | tf_op jit(solution)/shard_map/ppermute | solution.py:479
  70.0 11.9 %collective-permute-start.15 = (bf16[8,384]{1,0:T(8,128)(2,1)}, bf16[8,384]{1,0:T(8,128)(2,1)}, u32[]{:S(2)}, u32[]{:S(2)}) collective-permute-start(bf16[8,384]{1,0:T(8,128)(2,1)} %copy-done.26), channel_id=1, source_target_pairs={{0,1},{1,0},{2,3},{3,2},{4,5},{5,4},{6,7},{7,6},{8,9},{9,8},{10,11... | collective-permute-start | bytes 18440 | tf_op jit(solution)/shard_map/ppermute | solution.py:479
  70.0 26.9 %collective-permute-start.18 = (bf16[192,1536]{1,0:T(8,128)(2,1)S(1)}, bf16[192,1536]{1,0:T(8,128)(2,1)}, u32[]{:S(2)}, u32[]{:S(2)}) collective-permute-start(bf16[192,1536]{1,0:T(8,128)(2,1)S(1)} %collective-permute-done.16.u_x), channel_id=1, source_target_pairs={{0,1},{1,0},{2,3},{3,2},{4,5},{5,4},{6,7},{7,6},{8,9},{9,8},{10,11... | collective-permute-start | bytes 1769480 | tf_op jit(solution)/shard_map/ppermute | solution.py:479
  81.9 15.0 %collective-permute-start.13 = (bf16[256,768]{1,0:T(8,128)(2,1)}, bf16[256,768]{1,0:T(8,128)(2,1)}, u32[]{:S(2)}, u32[]{:S(2)}) collective-permute-start(bf16[256,768]{1,0:T(8,128)(2,1)} %get-tuple-element.51), channel_id=1, source_target_pairs={{0,2},{1,3},{2,0},{3,1},{4,6},{5,7},{6,4},{7,5},{8,10},{9,11},{10,... | collective-permute-start | bytes 1179656 | tf_op jit(solution)/shard_map/ppermute | solution.py:479
  106.0 15.7 %collective-permute-start.20 = (bf16[256,768]{1,0:T(8,128)(2,1)}, bf16[256,768]{1,0:T(8,128)(2,1)S(1)}, u32[]{:S(2)}, u32[]{:S(2)}) collective-permute-start(bf16[256,768]{1,0:T(8,128)(2,1)} %get-tuple-element.54), channel_id=1, source_target_pairs={{0,2},{1,3},{2,0},{3,1},{4,6},{5,7},{6,4},{7,5},{8,10},{9,11},{10,... | collective-permute-start | bytes 1179656 | tf_op jit(solution)/shard_map/ppermute | solution.py:479
  106.9 14.7 %collective-permute-start.22 = (bf16[128,768]{1,0:T(8,128)(2,1)}, bf16[128,768]{1,0:T(8,128)(2,1)S(1)}, u32[]{:S(2)}, u32[]{:S(2)}) collective-permute-start(bf16[128,768]{1,0:T(8,128)(2,1)} %collective-permute-done.21.g_own), channel_id=1, source_target_pairs={{0,2},{1,3},{2,0},{3,1},{4,6},{5,7},{6,4},{7,5},{8,10},{9,11},{10,... | collective-permute-start | bytes 589832 | tf_op jit(solution)/shard_map/ppermute | solution.py:479
  109.4 31.5 %collective-permute-start.37 = (bf16[256,768]{1,0:T(8,128)(2,1)}, bf16[256,768]{1,0:T(8,128)(2,1)}, u32[]{:S(2)}, u32[]{:S(2)}) collective-permute-start(bf16[256,768]{1,0:T(8,128)(2,1)} %get-tuple-element.79), channel_id=1, source_target_pairs={{0,4},{1,5},{2,6},{3,7},{4,0},{5,1},{6,2},{7,3},{8,12},{9,13},{10,... | collective-permute-start | bytes 1179656 | tf_op jit(solution)/shard_map/ppermute | solution.py:479
  110.9 59.1 %collective-permute-start.38 = (bf16[256,768]{1,0:T(8,128)(2,1)}, bf16[256,768]{1,0:T(8,128)(2,1)}, u32[]{:S(2)}, u32[]{:S(2)}) collective-permute-start(bf16[256,768]{1,0:T(8,128)(2,1)} %get-tuple-element.79), channel_id=1, source_target_pairs={{0,1},{1,0},{2,3},{3,2},{4,5},{5,4},{6,7},{7,6},{8,9},{9,8},{10,11... | collective-permute-start | bytes 1179656 | tf_op jit(solution)/shard_map/ppermute | solution.py:479
  131.2 8.9 %collective-permute-start.23 = (bf16[128,768]{1,0:T(8,128)(2,1)}, bf16[128,768]{1,0:T(8,128)(2,1)S(1)}, u32[]{:S(2)}, u32[]{:S(2)}) collective-permute-start(bf16[128,768]{1,0:T(8,128)(2,1)} %get-tuple-element.57), channel_id=1, source_target_pairs={{0,0},{1,16},{2,8},{3,24},{4,4},{5,20},{6,12},{7,28},{8,2},{9,18},... | collective-permute-start | bytes 589832 | tf_op jit(solution)/shard_map/ppermute | solution.py:479
  132.8 14.8 %collective-permute-start.24 = (bf16[256,768]{1,0:T(8,128)(2,1)}, bf16[256,768]{1,0:T(8,128)(2,1)S(1)}, u32[]{:S(2)}, u32[]{:S(2)}) collective-permute-start(bf16[256,768]{1,0:T(8,128)(2,1)} %get-tuple-element.59), channel_id=1, source_target_pairs={{0,2},{1,3},{2,0},{3,1},{4,6},{5,7},{6,4},{7,5},{8,10},{9,11},{10,... | collective-permute-start | bytes 1179656 | tf_op jit(solution)/shard_map/ppermute | solution.py:479
  138.2 33.2 %collective-permute-start.42 = (bf16[256,384]{1,0:T(8,128)(2,1)}, bf16[256,384]{1,0:T(8,128)(2,1)}, u32[]{:S(2)}, u32[]{:S(2)}) collective-permute-start(bf16[256,384]{1,0:T(8,128)(2,1)} %get-tuple-element.98), channel_id=1, source_target_pairs={{0,5},{1,4},{2,7},{3,6},{4,1},{5,0},{6,3},{7,2},{8,13},{9,12},{10,... | collective-permute-start | bytes 589832 | tf_op jit(solution)/shard_map/ppermute | solution.py:479
  140.1 31.5 %collective-permute-start.41 = (bf16[256,384]{1,0:T(8,128)(2,1)}, bf16[256,384]{1,0:T(8,128)(2,1)}, u32[]{:S(2)}, u32[]{:S(2)}) collective-permute-start(bf16[256,384]{1,0:T(8,128)(2,1)} %get-tuple-element.99), channel_id=1, source_target_pairs={{0,1},{1,0},{2,3},{3,2},{4,5},{5,4},{6,7},{7,6},{8,9},{9,8},{10,11... | collective-permute-start | bytes 589832 | tf_op jit(solution)/shard_map/ppermute | solution.py:479
  140.9 31.3 %collective-permute-start.40 = (bf16[256,384]{1,0:T(8,128)(2,1)}, bf16[256,384]{1,0:T(8,128)(2,1)}, u32[]{:S(2)}, u32[]{:S(2)}) collective-permute-start(bf16[256,384]{1,0:T(8,128)(2,1)} %get-tuple-element.100), channel_id=1, source_target_pairs={{0,4},{1,5},{2,6},{3,7},{4,0},{5,1},{6,2},{7,3},{8,12},{9,13},{10,... | collective-permute-start | bytes 589832 | tf_op jit(solution)/shard_map/ppermute | solution.py:479
  147.7 24.5 %collective-permute-start.39 = (bf16[256,768]{1,0:T(8,128)(2,1)}, bf16[256,768]{1,0:T(8,128)(2,1)}, u32[]{:S(2)}, u32[]{:S(2)}) collective-permute-start(bf16[256,768]{1,0:T(8,128)(2,1)} %collective-permute-done.37), channel_id=1, source_target_pairs={{0,1},{1,0},{2,3},{3,2},{4,5},{5,4},{6,7},{7,6},{8,9},{9,8},{10,11... | collective-permute-start | bytes 1179656 | tf_op jit(solution)/shard_map/ppermute | solution.py:479
  170.0 25.6 %collective-permute-start.52 = (bf16[256,384]{1,0:T(8,128)(2,1)}, bf16[256,384]{1,0:T(8,128)(2,1)}, u32[]{:S(2)}, u32[]{:S(2)}) collective-permute-start(bf16[256,384]{1,0:T(8,128)(2,1)} %get-tuple-element.94), channel_id=1, source_target_pairs={{0,5},{1,4},{2,7},{3,6},{4,1},{5,0},{6,3},{7,2},{8,13},{9,12},{10,... | collective-permute-start | bytes 589832 | tf_op jit(solution)/shard_map/ppermute | solution.py:479
  171.4 24.3 %collective-permute-start.51 = (bf16[256,384]{1,0:T(8,128)(2,1)}, bf16[256,384]{1,0:T(8,128)(2,1)}, u32[]{:S(2)}, u32[]{:S(2)}) collective-permute-start(bf16[256,384]{1,0:T(8,128)(2,1)} %get-tuple-element.95), channel_id=1, source_target_pairs={{0,1},{1,0},{2,3},{3,2},{4,5},{5,4},{6,7},{7,6},{8,9},{9,8},{10,11... | collective-permute-start | bytes 589832 | tf_op jit(solution)/shard_map/ppermute | solution.py:479
  171.6 15.3 %collective-permute-start.53 = (bf16[256,768]{1,0:T(8,128)(2,1)}, bf16[256,768]{1,0:T(8,128)(2,1)}, u32[]{:S(2)}, u32[]{:S(2)}) collective-permute-start(bf16[256,768]{1,0:T(8,128)(2,1)} %get-tuple-element.82), channel_id=1, source_target_pairs={{0,4},{1,5},{2,6},{3,7},{4,0},{5,1},{6,2},{7,3},{8,12},{9,13},{10,... | collective-permute-start | bytes 1179656 | tf_op jit(solution)/shard_map/ppermute | solution.py:479
  172.2 31.0 %collective-permute-start.54 = (bf16[256,768]{1,0:T(8,128)(2,1)}, bf16[256,768]{1,0:T(8,128)(2,1)}, u32[]{:S(2)}, u32[]{:S(2)}) collective-permute-start(bf16[256,768]{1,0:T(8,128)(2,1)} %get-tuple-element.82), channel_id=1, source_target_pairs={{0,1},{1,0},{2,3},{3,2},{4,5},{5,4},{6,7},{7,6},{8,9},{9,8},{10,11... | collective-permute-start | bytes 1179656 | tf_op jit(solution)/shard_map/ppermute | solution.py:479
  174.8 9.5 %collective-permute-start.43 = (bf16[2,4,48,384]{3,2,1,0:T(8,128)(2,1)S(1)}, bf16[2,4,48,384]{3,2,1,0:T(8,128)(2,1)S(1)}, u32[]{:S(2)}, u32[]{:S(2)}) collective-permute-start(bf16[2,4,48,384]{3,2,1,0:T(8,128)(2,1)S(1)} %fusion.42), channel_id=1, source_target_pairs={{0,8},{1,9},{2,10},{3,11},{4,12},{5,13},{6,14},{7,15},{8,0},{9,1},... | collective-permute-start | bytes 884744 | tf_op jit(solution)/shard_map/ppermute | solution.py:479
  184.4 9.7 %collective-permute-start.44 = (bf16[4,48,384]{2,1,0:T(8,128)(2,1)S(1)}, bf16[4,48,384]{2,1,0:T(8,128)(2,1)S(1)}, u32[]{:S(2)}, u32[]{:S(2)}) collective-permute-start(bf16[4,48,384]{2,1,0:T(8,128)(2,1)S(1)} %fusion.49), channel_id=1, source_target_pairs={{0,16},{1,17},{2,18},{3,19},{4,20},{5,21},{6,22},{7,23},{8,24},{9,... | collective-permute-start | bytes 442376 | tf_op jit(solution)/shard_map/ppermute | solution.py:479
  187.0 16.2 %collective-permute-start.55 = (bf16[256,768]{1,0:T(8,128)(2,1)}, bf16[256,768]{1,0:T(8,128)(2,1)S(1)}, u32[]{:S(2)}, u32[]{:S(2)}) collective-permute-start(bf16[256,768]{1,0:T(8,128)(2,1)} %collective-permute-done.53), channel_id=1, source_target_pairs={{0,1},{1,0},{2,3},{3,2},{4,5},{5,4},{6,7},{7,6},{8,9},{9,8},{10,11... | collective-permute-start | bytes 1179656 | tf_op jit(solution)/shard_map/ppermute | solution.py:479
  194.1 6.7 %collective-permute-start.50 = (bf16[256,384]{1,0:T(8,128)(2,1)S(1)}, bf16[256,384]{1,0:T(8,128)(2,1)S(1)}, u32[]{:S(2)}, u32[]{:S(2)}) collective-permute-start(bf16[256,384]{1,0:T(8,128)(2,1)S(1)} %copy-done.16), channel_id=1, source_target_pairs={{0,4},{1,5},{2,6},{3,7},{4,0},{5,1},{6,2},{7,3},{8,12},{9,13},{10,... | collective-permute-start | bytes 589832 | tf_op jit(solution)/shard_map/ppermute | solution.py:479
  195.6 31.8 %collective-permute-start.25 = (bf16[2,256,768]{2,1,0:T(8,128)(2,1)}, bf16[2,256,768]{2,1,0:T(8,128)(2,1)S(1)}, u32[]{:S(2)}, u32[]{:S(2)}) collective-permute-start(bf16[2,256,768]{2,1,0:T(8,128)(2,1)} %get-tuple-element.72), channel_id=1, source_target_pairs={{0,1},{1,0},{2,3},{3,2},{4,5},{5,4},{6,7},{7,6},{8,9},{9,8},{10,11... | collective-permute-start | bytes 2359304 | tf_op jit(solution)/shard_map/ppermute | solution.py:479
  195.7 41.2 %collective-permute-start.29 = (bf16[1552,384]{1,0:T(8,128)(2,1)S(1)}, bf16[1552,384]{1,0:T(8,128)(2,1)S(1)}, u32[]{:S(2)}, u32[]{:S(2)}) collective-permute-start(bf16[1552,384]{1,0:T(8,128)(2,1)S(1)} %concatenate.272), channel_id=1, source_target_pairs={{0,1},{1,0},{2,3},{3,2},{4,5},{5,4},{6,7},{7,6},{8,9},{9,8},{10,11... | collective-permute-start | bytes 3575816 | tf_op jit(solution)/shard_map/ppermute | solution.py:479
  200.7 4.7 %collective-permute-start.45 = (bf16[2,48,384]{2,1,0:T(8,128)(2,1)S(1)}, bf16[2,48,384]{2,1,0:T(8,128)(2,1)S(1)}, u32[]{:S(2)}, u32[]{:S(2)}) collective-permute-start(bf16[2,48,384]{2,1,0:T(8,128)(2,1)S(1)} %get-tuple-element.115), channel_id=1, source_target_pairs={{0,2},{1,3},{2,0},{3,1},{4,6},{5,7},{6,4},{7,5},{8,10},{9,11},{10,... | collective-permute-start | bytes 221192 | tf_op jit(solution)/shard_map/ppermute | solution.py:479
  205.5 1.3 collective-permute-start.46
  205.7 12.6 %collective-permute-start.56 = (bf16[2,96,768]{2,1,0:T(8,128)(2,1)S(1)}, bf16[2,96,768]{2,1,0:T(8,128)(2,1)S(1)}, u32[]{:S(2)}, u32[]{:S(2)}) collective-permute-start(bf16[2,96,768]{2,1,0:T(8,128)(2,1)S(1)} %fusion.41), channel_id=1, source_target_pairs={{0,8},{1,9},{2,10},{3,11},{4,12},{5,13},{6,14},{7,15},{8,0},{9,1},... | collective-permute-start | bytes 884744 | tf_op jit(solution)/shard_map/ppermute | solution.py:479
  206.9 11.6 %collective-permute-start.47 = (bf16[2,2,48,384]{3,2,1,0:T(8,128)(2,1)S(1)}, bf16[2,2,48,384]{3,2,1,0:T(8,128)(2,1)S(1)}, u32[]{:S(2)}, u32[]{:S(2)}) collective-permute-start(bf16[2,2,48,384]{3,2,1,0:T(8,128)(2,1)S(1)} %maximum_select_fusion.15), channel_id=1, source_target_pairs={{0,16},{1,17},{2,18},{3,19},{4,20},{5,21},{6,22},{7,23},{8,24},{9,... | collective-permute-start | bytes 442376 | tf_op jit(solution)/shard_map/ppermute | solution.py:479
  218.4 9.0 %collective-permute-start.57 = (bf16[96,768]{1,0:T(8,128)(2,1)S(1)}, bf16[96,768]{1,0:T(8,128)(2,1)S(1)}, u32[]{:S(2)}, u32[]{:S(2)}) collective-permute-start(bf16[96,768]{1,0:T(8,128)(2,1)S(1)} %fusion.50), channel_id=1, source_target_pairs={{0,16},{1,17},{2,18},{3,19},{4,20},{5,21},{6,22},{7,23},{8,24},{9,... | collective-permute-start | bytes 442376 | tf_op jit(solution)/shard_map/ppermute | solution.py:479
  218.5 20.6 %collective-permute-start.48 = (bf16[2,2,2,48,384]{4,3,2,1,0:T(8,128)(2,1)S(1)}, bf16[2,2,2,48,384]{4,3,2,1,0:T(8,128)(2,1)S(1)}, u32[]{:S(2)}, u32[]{:S(2)}) collective-permute-start(bf16[2,2,2,48,384]{4,3,2,1,0:T(8,128)(2,1)S(1)} %maximum_select_fusion.10), channel_id=1, source_target_pairs={{0,8},{1,9},{2,10},{3,11},{4,12},{5,13},{6,14},{7,15},{8,0},{9,1},... | collective-permute-start | bytes 884744 | tf_op jit(solution)/shard_map/ppermute | solution.py:479
  227.4 9.3 %collective-permute-start.58 = (bf16[96,768]{1,0:T(8,128)(2,1)S(1)}, bf16[96,768]{1,0:T(8,128)(2,1)S(1)}, u32[]{:S(2)}, u32[]{:S(2)}) collective-permute-start(bf16[96,768]{1,0:T(8,128)(2,1)S(1)} %fusion.44), channel_id=1, source_target_pairs={{0,16},{1,17},{2,18},{3,19},{4,20},{5,21},{6,22},{7,23},{8,24},{9,... | collective-permute-start | bytes 442376 | tf_op jit(solution)/shard_map/ppermute | solution.py:479
  227.8 12.2 %collective-permute-start.26 = (bf16[256,768]{1,0:T(8,128)(2,1)S(1)}, bf16[256,768]{1,0:T(8,128)(2,1)S(1)}, u32[]{:S(2)}, u32[]{:S(2)}) collective-permute-start(bf16[256,768]{1,0:T(8,128)(2,1)S(1)} %fusion.35), channel_id=1, source_target_pairs={{0,4},{1,5},{2,6},{3,7},{4,0},{5,1},{6,2},{7,3},{8,12},{9,13},{10,... | collective-permute-start | bytes 1179656 | tf_op jit(solution)/shard_map/ppermute | solution.py:479
  236.8 20.6 %collective-permute-start.59 = (bf16[2,96,768]{2,1,0:T(8,128)(2,1)S(1)}, bf16[2,96,768]{2,1,0:T(8,128)(2,1)S(1)}, u32[]{:S(2)}, u32[]{:S(2)}) collective-permute-start(bf16[2,96,768]{2,1,0:T(8,128)(2,1)S(1)} %maximum_select_fusion.12), channel_id=1, source_target_pairs={{0,8},{1,9},{2,10},{3,11},{4,12},{5,13},{6,14},{7,15},{8,0},{9,1},... | collective-permute-start | bytes 884744 | tf_op jit(solution)/shard_map/ppermute | solution.py:479
  237.6 16.5 %collective-permute-start.30 = (bf16[784,384]{1,0:T(8,128)(2,1)S(1)}, bf16[784,384]{1,0:T(8,128)(2,1)S(1)}, u32[]{:S(2)}, u32[]{:S(2)}) collective-permute-start(bf16[784,384]{1,0:T(8,128)(2,1)S(1)} %pad_maximum_fusion.2), channel_id=1, source_target_pairs={{0,4},{1,5},{2,6},{3,7},{4,0},{5,1},{6,2},{7,3},{8,12},{9,13},{10,... | collective-permute-start | bytes 1806344 | tf_op jit(solution)/shard_map/ppermute | solution.py:479
  239.2 27.6 %collective-permute-start.49 = (bf16[2,2,2,2,48,384]{5,4,3,2,1,0:T(8,128)(2,1)S(1)}, bf16[2,2,2,2,48,384]{5,4,3,2,1,0:T(8,128)(2,1)S(1)}, u32[]{:S(2)}, u32[]{:S(2)}) collective-permute-start(bf16[2,2,2,2,48,384]{5,4,3,2,1,0:T(8,128)(2,1)S(1)} %maximum_select_fusion.5), channel_id=1, source_target_pairs={{0,4},{1,5},{2,6},{3,7},{4,0},{5,1},{6,2},{7,3},{8,12},{9,13},{10,... | collective-permute-start | bytes 1769480 | tf_op jit(solution)/shard_map/ppermute | solution.py:479
  240.1 16.5 %collective-permute-start.27 = (bf16[128,768]{1,0:T(8,128)(2,1)S(1)}, bf16[128,768]{1,0:T(8,128)(2,1)S(1)}, u32[]{:S(2)}, u32[]{:S(2)}) collective-permute-start(bf16[128,768]{1,0:T(8,128)(2,1)S(1)} %fusion.47), channel_id=1, source_target_pairs={{0,2},{1,3},{2,0},{3,1},{4,6},{5,7},{6,4},{7,5},{8,10},{9,11},{10,... | collective-permute-start | bytes 589832 | tf_op jit(solution)/shard_map/ppermute | solution.py:479
  254.5 9.6 %collective-permute-start.31 = (bf16[400,384]{1,0:T(8,128)(2,1)S(1)}, bf16[400,384]{1,0:T(8,128)(2,1)S(1)}, u32[]{:S(2)}, u32[]{:S(2)}) collective-permute-start(bf16[400,384]{1,0:T(8,128)(2,1)S(1)} %pad_maximum_fusion.10), channel_id=1, source_target_pairs={{0,8},{1,9},{2,10},{3,11},{4,12},{5,13},{6,14},{7,15},{8,0},{9,1},... | collective-permute-start | bytes 921608 | tf_op jit(solution)/shard_map/ppermute | solution.py:479
  256.7 3.9 %collective-permute-start.28 = (bf16[128,768]{1,0:T(8,128)(2,1)S(1)}, bf16[128,768]{1,0:T(8,128)(2,1)S(1)}, u32[]{:S(2)}, u32[]{:S(2)}) collective-permute-start(bf16[128,768]{1,0:T(8,128)(2,1)S(1)} %fusion.37), channel_id=1, source_target_pairs={{0,0},{1,16},{2,8},{3,24},{4,4},{5,20},{6,12},{7,28},{8,2},{9,18},... | collective-permute-start | bytes 589832 | tf_op jit(solution)/shard_map/ppermute | solution.py:479
  258.3 22.5 %collective-permute-start.60 = (bf16[2,2,96,768]{3,2,1,0:T(8,128)(2,1)}, bf16[2,2,96,768]{3,2,1,0:T(8,128)(2,1)}, u32[]{:S(2)}, u32[]{:S(2)}) collective-permute-start(bf16[2,2,96,768]{3,2,1,0:T(8,128)(2,1)} %maximum_select_fusion.7), channel_id=1, source_target_pairs={{0,4},{1,5},{2,6},{3,7},{4,0},{5,1},{6,2},{7,3},{8,12},{9,13},{10,... | collective-permute-start | bytes 1769480 | tf_op jit(solution)/shard_map/ppermute | solution.py:479
  264.3 7.9 %collective-permute-start.32 = (bf16[208,384]{1,0:T(8,128)(2,1)S(1)}, bf16[208,384]{1,0:T(8,128)(2,1)S(1)}, u32[]{:S(2)}, u32[]{:S(2)}) collective-permute-start(bf16[208,384]{1,0:T(8,128)(2,1)S(1)} %pad_maximum_fusion.13), channel_id=1, source_target_pairs={{0,16},{1,17},{2,18},{3,19},{4,20},{5,21},{6,22},{7,23},{8,24},{9,... | collective-permute-start | bytes 479240 | tf_op jit(solution)/shard_map/ppermute | solution.py:479
  273.3 10.6 %collective-permute-start.33 = (bf16[72,384]{1,0:T(8,128)(2,1)S(1)}, bf16[72,384]{1,0:T(8,128)(2,1)S(1)}, u32[]{:S(2)}, u32[]{:S(2)}) collective-permute-start(bf16[72,384]{1,0:T(8,128)(2,1)S(1)} %get-tuple-element.117), channel_id=1, source_target_pairs={{0,2},{1,3},{2,0},{3,1},{4,6},{5,7},{6,4},{7,5},{8,10},{9,11},{10,... | collective-permute-start | bytes 165896 | tf_op jit(solution)/shard_map/ppermute | solution.py:479
  283.9 7.7 %collective-permute-start.34 = (bf16[8,24,384]{2,1,0:T(8,128)(2,1)S(1)}, bf16[8,24,384]{2,1,0:T(8,128)(2,1)S(1)}, u32[]{:S(2)}, u32[]{:S(2)}) collective-permute-start(bf16[8,24,384]{2,1,0:T(8,128)(2,1)S(1)} %bitcast.226), channel_id=1, source_target_pairs={{0,16},{1,17},{2,18},{3,19},{4,20},{5,21},{6,22},{7,23},{8,24},{9,... | collective-permute-start | bytes 442376 | tf_op jit(solution)/shard_map/ppermute | solution.py:479
  291.7 6.8 %collective-permute-start.35 = (bf16[2,8,24,384]{3,2,0,1:T(8,128)(2,1)S(1)}, bf16[2,8,24,384]{3,2,0,1:T(8,128)(2,1)S(1)}, u32[]{:S(2)}, u32[]{:S(2)}) collective-permute-start(bf16[2,8,24,384]{3,2,0,1:T(8,128)(2,1)S(1)} %maximum_select_fusion.8), channel_id=1, source_target_pairs={{0,8},{1,9},{2,10},{3,11},{4,12},{5,13},{6,14},{7,15},{8,0},{9,1},... | collective-permute-start | bytes 884744 | tf_op jit(solution)/shard_map/ppermute | solution.py:479
  298.6 11.3 %collective-permute-start.36 = (bf16[2,2,8,24,384]{4,3,0,1,2:T(8,128)(2,1)S(1)}, bf16[2,2,8,24,384]{4,3,0,1,2:T(8,128)(2,1)S(1)}, u32[]{:S(2)}, u32[]{:S(2)}) collective-permute-start(bf16[2,2,8,24,384]{4,3,0,1,2:T(8,128)(2,1)S(1)} %maximum_select_fusion.3), channel_id=1, source_target_pairs={{0,4},{1,5},{2,6},{3,7},{4,0},{5,1},{6,2},{7,3},{8,12},{9,13},{10,... | collective-permute-start | bytes 1769480 | tf_op jit(solution)/shard_map/ppermute | solution.py:479
  (30 other events, 235.8 us)

commit v2 on v1

--- a/solution.py
+++ b/solution.py
@@ -507,13 +507,12 @@
     return moved(block, lambda q, r, x, c: (2 * c + x, r, q & 1, q >> 1))
 
 
-def in_order(mine, theirs, bit):
-    first, second = jnp.stack([mine, theirs]), jnp.stack([theirs, mine])
-    return jnp.where(bit == 0, first, second)
-
-
-def take(stacked, at):
-    return lax.dynamic_index_in_dim(stacked, at, 0, keepdims=False)
+def swap_xc(block):
+    return moved(block, lambda q, r, x, c: (q, r, 1 - x, 1 - c))
+
+
+def beside(mine, got):
+    return jnp.concatenate([mine, got])
 
 
 def dot(left, right):
@@ -523,6 +522,12 @@
 def dot_nt(left, right):
     return lax.dot_general(
         left, right, (((1,), (1,)), ((), ())), preferred_element_type=jnp.float32
+    )
+
+
+def dot_tn(left, right):
+    return lax.dot_general(
+        left, right, (((0,), (0,)), ((), ())), preferred_element_type=jnp.float32
     )
 
 
@@ -556,16 +561,47 @@
         mask[rows * b : rows * (b + 1), :] = jnp.where(across[:, b : b + 1] == mine, 0.0, masked_fill)
 
 
+def block_kernel(tokens, ids, block):
+    rows = tokens.shape[0]
+    block[0:rows, :] = tokens[...]
+    block[rows:, :] = jnp.zeros((16, block.shape[1]), block.dtype)
+    line = ids[...].astype(jnp.float32)
+    block[rows:, 0:rows] = jnp.broadcast_to(line, (16, rows)).astype(block.dtype)
+
+
+def pack_kernel(w_q, w_k, w_v, *refs):
+    vectors, b_up, theirs, mine, lines = refs[:8], refs[8], refs[9], refs[10], refs[11]
+    q, r, x, c = spot()
+    part, width = w_q.shape
+    half = width // 2
+    for t, w in enumerate((w_q, w_k, w_v)):
+        rows = slice(part * t, part * (t + 1))
+        mine[rows, :] = w[:, pl.ds(pl.multiple_of(half * x, 128), half)]
+        theirs[rows, :] = w[:, pl.ds(pl.multiple_of(half * (1 - x), 128), half)]
+    lines[...] = jnp.zeros_like(lines)
+    for i, vector in enumerate(vectors):
+        line = vector[...].astype(jnp.float32).reshape(1, part)
+        none = jnp.zeros_like(line)
+        first = jnp.concatenate([line, none], axis=1)
+        second = jnp.concatenate([none, line], axis=1)
+        lines[i : i + 1, :] = jnp.where(c == 0, first, second)
+    wide = b_up[...].astype(jnp.float32).reshape(1, width)
+    lines[pl.ds(8 + 2 * c, 1), :] = wide[:, 0:half]
+    lines[pl.ds(9 + 2 * c, 1), :] = wide[:, half:]
+    low = lines[...].astype(jnp.bfloat16)
+    mine[3 * part :, :] = low
+    theirs[3 * part :, :] = low
+
+
 def attend_kernel(
-    b0, b1, b2, b3, b4, b5, b6, b7, w_q, w_k, w_v, w_x, w_m, w_mx, w_o, w_om, bias,
-    x_out, w_out, wo_out, k_out, v_out, q_out, o_out, lse_out, ids_out, a_out, a_low,
-    xs, raw, w, wo, k3, v3, vt, q3, ot, mask, sems, outs,
+    b0, b1, b2, b3, b4, b5, b6, b7, w_q, w_k, w_v, w_x, w_m, w_mx, own_lines, w_o, w_om,
+    x_out, w_out, wo_out, k_out, v_out, q_out, o_out, lse_out, ids_out, a_out, a_low, vecs, up_bias,
+    xs, raw, w, wo, lines, k3, v3, vt, q3, ot, mask, sems, outs,
 ):
     q, r, x, c = spot()
     rows = xs.shape[0] // 8
     part = w.shape[0] // 4
     half = wo.shape[0]
-    width = w.shape[0]
     me, shard = 4 * r + 2 * c + x, 2 * x + c
     ins = Copies(sems)
     for j, block in enumerate((b0, b1, b2, b3, b4, b5, b6, b7)):
@@ -578,7 +614,9 @@
         ins.start(own.at[:, columns], w.at[pl.ds(pl.multiple_of(part * shard, 64), part), place])
         for flip, piece in ((2, w_x), (1, w_m), (3, w_mx)):
             at = pl.ds(pl.multiple_of(part * (shard ^ flip), 64), part)
-            ins.start(piece.at[t], w.at[at, place])
+            ins.start(piece.at[pl.ds(part * t, part)], w.at[at, place])
+    for i, piece in enumerate((own_lines, w_m, w_x, w_mx)):
+        ins.start(piece.at[pl.ds(3 * part, 16)], lines.at[i])
     ins.start(w_o, wo.at[pl.ds(pl.multiple_of(part * c, 64), part)])
     ins.start(w_om, wo.at[pl.ds(pl.multiple_of(part * (1 - c), 64), part)])
     ins.wait()
@@ -586,15 +624,21 @@
     backs.start(xs, x_out)
     backs.start(w, w_out)
     backs.start(wo, wo_out)
+    mine = lines[0].astype(jnp.float32) + lines[1].astype(jnp.float32)
+    other = lines[2].astype(jnp.float32) + lines[3].astype(jnp.float32)
+    vecs[:, columns] = mine[0:8, :]
+    vecs[:, pl.ds(pl.multiple_of(half * (1 - x), 128), half)] = other[0:8, :]
+    for i in range(4):
+        up_bias[i] = jnp.broadcast_to(mine[8 + i : 9 + i, :], (8, half))
     for b in range(8):
         ids_out[b : b + 1, :] = raw[b, 0:1, 0:rows].astype(jnp.float32)
     fill_mask(ids_out, mask, 4 * r + 2 * c)
     keyed = dot(xs[...], w[:, half : 2 * half]).astype(jnp.bfloat16)
-    valued = dot(xs[...], w[:, 2 * half : 3 * half]) + bias[1:2, :]
+    valued = dot(xs[...], w[:, 2 * half : 3 * half]) + mine[1:2, :]
     own = pl.ds(pl.multiple_of(rows * (4 * r + 2 * c), rows), 2 * rows)
-    asked = (dot(xs[own, :], w[:, 0:half]) + bias[0:1, :]).astype(jnp.bfloat16)
-    turned = jnp.transpose(valued).astype(jnp.bfloat16)
+    asked = (dot(xs[own, :], w[:, 0:half]) + mine[0:1, :]).astype(jnp.bfloat16)
     valued = valued.astype(jnp.bfloat16)
+    turned = jnp.transpose(valued)
     pairs = half // 128
     for p in range(pairs):
         k3[p] = keyed[:, 128 * p : 128 * (p + 1)]
@@ -660,8 +704,8 @@
 
 def forward_kernel(
     a_own, a_got, xs, vecs, b_up, u_own, u_x, u_m, u_mx, d_own, d_m,
-    h_out, n_out, r_out, z_out, slope_out, y_out, y_low,
-    up, down, x_own, sems, more,
+    to_r, to_c, z_own, n_out, r_out, slope_out, y_out, y_low,
+    up, down, x_own, z, sems, more,
 ):
     q, r, x, c = spot()
     rows = x_own.shape[0]
@@ -670,30 +714,33 @@
     copies = Copies(sems)
     load_feedforward(copies, up, down, u_own, u_x, u_m, u_mx, d_own, d_m)
     first.wait()
-    total = x_own[...].astype(jnp.float32) + (a_own[...] + a_got[...].astype(jnp.float32) + vecs[0:1, :])
+    total = x_own[...].astype(jnp.float32) + (a_own[...] + a_got[...].astype(jnp.float32) + vecs[2:3, :])
     normed, rstd = norm_of(total)
     n_out[...] = normed
     r_out[...] = jnp.broadcast_to(rstd, r_out.shape)
-    low = (normed * vecs[1:2, :] + vecs[2:3, :]).astype(jnp.bfloat16)
-    h_out[...] = low
+    low = (normed * vecs[3:4, :] + vecs[4:5, :]).astype(jnp.bfloat16)
+    wide = up.shape[1] // 4
+    to_r[:, 2 * wide :] = low
+    to_c[:, wide:] = low
     copies.wait()
-    wide = up.shape[1] // 4
     for j in range(4):
         pre = dot(low, up[:, wide * j : wide * (j + 1)]) + b_up[(2 * c + r) ^ j, 0:1, :]
         cdf = 0.5 * (1.0 + lax.erf(pre * (1.0 / math.sqrt(2.0))))
         density = jnp.exp(-0.5 * pre * pre) * (1.0 / math.sqrt(2.0 * math.pi))
-        z_out[j] = (pre * cdf).astype(jnp.bfloat16)
+        z[:, wide * j : wide * (j + 1)] = (pre * cdf).astype(jnp.bfloat16)
         slope_out[j] = cdf + pre * density
-    result = dot(z_out[0], down[0:wide, :])
-    for j in range(1, 4):
-        result += dot(z_out[j], down[wide * j : wide * (j + 1), :])
+    result = dot(z[...], down[...])
     y_out[...] = result
     y_low[...] = result.astype(jnp.bfloat16)
+    z_own[...] = z[:, 0:wide]
+    to_r[:, 0:wide] = z[:, wide : 2 * wide]
+    to_r[:, wide : 2 * wide] = z[:, 3 * wide :]
+    to_c[:, 0:wide] = z[:, 2 * wide : 3 * wide]
 
 
 def backward_kernel(
     y_own, y_got, normed1, g_own, g_x, slope, vecs, u_own, u_x, u_m, u_mx, d_own, d_m,
-    hid_out, dy_out, du_out, s_out, p_low, sums, up_sums,
+    hid_out, to_r, to_c, du_own, s_out, p_low, sums, up_sums,
     up, down, grad, hid, sems, more,
 ):
     q, r, x, c = spot()
@@ -704,24 +751,26 @@
     copies = Copies(sems)
     load_feedforward(copies, up, down, u_own, u_x, u_m, u_mx, d_own, d_m)
     first.wait()
-    h1 = normed1[...] * vecs[1:2, :] + vecs[2:3, :]
-    normed, rstd = norm_of(h1 + (y_own[...] + y_got[...].astype(jnp.float32) + vecs[3:4, :]))
-    hid[...] = (normed * vecs[4:5, :] + vecs[5:6, :]).astype(jnp.bfloat16)
+    h1 = normed1[...] * vecs[3:4, :] + vecs[4:5, :]
+    normed, rstd = norm_of(h1 + (y_own[...] + y_got[...].astype(jnp.float32) + vecs[5:6, :]))
+    hid[...] = (normed * vecs[6:7, :] + vecs[7:8, :]).astype(jnp.bfloat16)
     hid_out[...] = hid[pl.ds(pl.multiple_of(rows * x, rows), rows), :]
     cot = grad[...].astype(jnp.float32)
-    dy = norm_pull(cot * vecs[4:5, :], normed, rstd)
+    dy = norm_pull(cot * vecs[6:7, :], normed, rstd)
     low = dy.astype(jnp.bfloat16)
-    dy_out[...] = low
+    wide = up.shape[1] // 4
+    to_r[:, 2 * wide :] = low
+    to_c[:, wide:] = low
     sums[...] = jnp.zeros_like(sums)
     sums[0:1, :] = jnp.sum(low.astype(jnp.float32), axis=0, keepdims=True)
     sums[1:2, :] = jnp.sum(cot * normed, axis=0, keepdims=True)
     sums[2:3, :] = jnp.sum(cot, axis=0, keepdims=True)
     copies.wait()
-    wide = up.shape[1] // 4
     result = jnp.zeros(dy.shape, jnp.float32)
+    places = (du_own.at[...], to_r.at[:, 0:wide], to_c.at[:, 0:wide], to_r.at[:, wide : 2 * wide])
     for j in range(4):
         du = (dot_nt(low, down[wide * j : wide * (j + 1), :]) * slope[j]).astype(jnp.bfloat16)
-        du_out[j] = du
+        places[j][...] = du
         total = jnp.sum(du.astype(jnp.float32), axis=0, keepdims=True)
         up_sums[j] = jnp.broadcast_to(total, up_sums.shape[1:])
         result += dot_nt(du, up[:, wide * j : wide * (j + 1)])
@@ -741,7 +790,7 @@
     fill_mask(ids, mask, 4 * r + 2 * c)
     dh = s_own[...] + p_got[...].astype(jnp.float32)
     normed = normed1[...]
-    dr = norm_pull(dh * vecs[1:2, :], normed, rstd1[:, 0:1])
+    dr = norm_pull(dh * vecs[3:4, :], normed, rstd1[:, 0:1])
     whole[...] = dr
     dr_out[...] = whole[pl.ds(pl.multiple_of(rows * x, rows), rows), :]
     low = dr.astype(jnp.bfloat16)
@@ -800,35 +849,229 @@
         send[b] = whole[theirs, :].astype(jnp.bfloat16)
 
 
-def kernel_call(body, name, ins, outs, scratch, cost, args):
+def down_grad_kernel(z0, r0, c0, f0, dc, dr_, df, c_own, send, keep, whole):
+    q, r, x, c = spot()
+    wide = z0.shape[1]
+    total = dot_tn(z0[...], c_own[:, wide:])
+    total += dot_tn(r0[:, 0:wide], dr_[:, 2 * wide :])
+    total += dot_tn(c0[:, 0:wide], dc[:, wide:])
+    total += dot_tn(f0[:, wide : 2 * wide], df[:, 2 * wide :])
+    whole[...] = total
+    count = wide // 4
+    for b in range(2):
+        theirs = pl.ds(pl.multiple_of(2 * count * b + count * (1 - q % 2), 32), count)
+        mine = pl.ds(pl.multiple_of(2 * count * b + count * (q % 2), 32), count)
+        send[b] = whole[theirs, :].astype(jnp.bfloat16)
+        keep[b] = whole[mine, :]
+
+
+def up_grad_kernel(h0, hr, hc, hf, d0, dr_, dc, df, send, keep, whole):
+    q, r, x, c = spot()
+    wide = d0.shape[1]
+    total = dot_tn(h0[:, wide:], d0[...])
+    total += dot_tn(hr[:, 2 * wide :], dr_[:, 0:wide])
+    total += dot_tn(hc[:, wide:], dc[:, 0:wide])
+    total += dot_tn(hf[:, 2 * wide :], df[:, wide : 2 * wide])
+    whole[...] = total
+    count = whole.shape[0] // 16
+    for b in range(2):
+        for s in range(4):
+            at = 4 * count * s + 2 * count * b
+            rows = slice(count * s, count * (s + 1))
+            theirs = pl.ds(pl.multiple_of(at + count * (1 - q % 2), 16), count)
+            mine = pl.ds(pl.multiple_of(at + count * (q % 2), 16), count)
+            send[b, rows, :] = whole[theirs, :].astype(jnp.bfloat16)
+            keep[b, rows, :] = whole[mine, :]
+
+
+def fold_kernel(bit, keep, got, send, kept):
+    at = bit(*spot())
+    send[...] = (keep[1 - at] + got[1 - at].astype(jnp.float32)).astype(send.dtype)
+    kept[...] = keep[at] + got[at].astype(jnp.float32)
+
+
+def sum_kernel(keep, got, out):
+    out[...] = (keep[...] + got[...].astype(jnp.float32)).astype(out.dtype)
+
+
+def share_kernel(keep, got, *out):
+    q, r, x, c = spot()
+    count = keep.shape[0] // 4
+    for k in range(4):
+        rows = pl.ds(pl.multiple_of(count * ((2 * x + c) ^ k), 16), count)
+        out[k][...] = (keep[rows, :] + got[rows, :].astype(jnp.float32)).astype(jnp.bfloat16)
+
+
+def weight_grad_kernel(
+    xs, dkv, dq, mixed, da, sums1, sums2, qv_sums, up_sums, send, keep, packed, sems
+):
+    q, r, x, c = spot()
+    width = xs.shape[1]
+    own, half = dq.shape
+    thin = width // 32
+    for_c = 64 * thin
+    own_rows = pl.ds(pl.multiple_of(own * (2 * r + c), own), own)
+    asked = dot_tn(xs[own_rows, :], dq[...])
+    kept = dot_tn(xs[...], dkv[...])
+    outer = dot_tn(mixed[...], da[...])
+    for cc in range(2):
+        for rr in range(2):
+            for q1 in range(2):
+                for q0 in range(2):
+                    at = ((4 * rr + 2 * q0 + q1) * 8) * thin
+                    within = (4 * rr + 2 * q1 + q0) * thin
+                    for xx in range(2):
+                        rows = slice((16 * xx + 8 * cc) * thin + within, (16 * xx + 8 * cc + 1) * thin + within)
+                        for t, piece in enumerate((asked, kept[:, 0:half], kept[:, half:])):
+                            to = at + (3 * xx + t) * thin
+                            packed[cc, to : to + thin, :] = piece[rows, :]
+                    rows = slice(8 * cc * thin + within, (8 * cc + 1) * thin + within)
+                    for t in range(2):
+                        to = at + (6 + t) * thin
+                        packed[cc, to : to + thin, :] = outer[rows, half * t : half * (t + 1)]
+    columns = pl.ds(pl.multiple_of(half * x, 128), half)
+    for cc in range(2):
+        packed[cc, for_c : for_c + 16, :] = jnp.zeros((16, half), jnp.float32)
+        packed[cc, for_c : for_c + 2, :] = qv_sums[0:2, :]
+        for j in range(4):
+            packed[cc, pl.ds(for_c + 2 + ((2 * c + r) ^ j), 1), :] = up_sums[j, 0:1, :]
+        packed[cc, for_c + 6 : for_c + 9, :] = sums1[0:3, columns]
+        packed[cc, for_c + 9 : for_c + 12, :] = sums2[0:3, columns]
+    send[...] = packed[1 - c].astype(jnp.bfloat16)
+    copy = pltpu.make_async_copy(packed.at[c], keep, sems.at[0])
+    copy.start()
+    copy.wait()
+
+
+def step_kernel(bit, keep, got, send, kept, whole):
+    at = bit(*spot())
+    count = send.shape[0] - 16
+    whole[...] = keep[...] + got[...].astype(jnp.float32)
+    theirs = pl.ds(pl.multiple_of(count * (1 - at), 64), count)
+    mine = pl.ds(pl.multiple_of(count * at, 64), count)
+    send[0:count, :] = whole[theirs, :].astype(jnp.bfloat16)
+    send[count:, :] = whole[2 * count :, :].astype(jnp.bfloat16)
+    kept[0:count, :] = whole[mine, :]
+    kept[count:, :] = whole[2 * count :, :]
+
+
+def last_step_kernel(keep, got, side, base, lines, whole):
+    q, r, x, c = spot()
+    count = side.shape[0]
+    whole[...] = keep[...] + got[...].astype(jnp.float32)
+    theirs = pl.ds(pl.multiple_of(count * (1 - x), 8), count)
+    mine = pl.ds(pl.multiple_of(count * x, 8), count)
+    side[...] = whole[theirs, :].astype(jnp.bfloat16)
+    rest = slice(2 * count, whole.shape[0] - 16)
+    base[...] = jnp.concatenate([whole[mine, :], whole[rest, :]]).astype(jnp.bfloat16)
+    lines[...] = whole[whole.shape[0] - 16 :, :]
+
+
+def down_out_kernel(near, far, out):
+    q, r, x, c = spot()
+    count = near.shape[0] // 4
+    for d, piece in enumerate((near, far)):
+        for k in range(4):
+            at = 4 * (r ^ d) + 2 * ((q // 2) ^ (k & 1)) + ((q % 2) ^ (k >> 1))
+            rows = pl.ds(pl.multiple_of(count * at, 32), count)
+            out[rows, :] = piece[count * k : count * (k + 1), :].astype(jnp.float32)
+
+
+def up_out_kernel(near, far, out):
+    q, r, x, c = spot()
+    count, wide = near.shape[0] // 16, near.shape[1]
+    for d, piece in enumerate((near, far)):
+        for k in range(4):
+            at = 2 * ((q // 2) ^ (k & 1)) + ((q % 2) ^ (k >> 1))
+            rows = pl.ds(pl.multiple_of(count * at, 16), count)
+            for s in range(4):
+                place = 2 * ((2 * x + c) ^ s) + (r ^ d)
+                columns = pl.ds(pl.multiple_of(wide * place, 128), wide)
+                first = count * (4 * k + s)
+                out[rows, columns] = piece[first : first + count, :].astype(jnp.float32)
+
+
+def rest_out_kernel(near, far, out_q, out_k, out_v, out_o, whole):
+    q, r, x, c = spot()
+    half = near.shape[1]
+    thin = near.shape[0] // 32
+    ours = pl.ds(pl.multiple_of(half * x, 128), half)
+    other = pl.ds(pl.multiple_of(half * (1 - x), 128), half)
+    for d, piece in enumerate((near, far)):
+        whole[...] = piece[...].astype(jnp.float32)
+        for k in range(4):
+            at = 4 * (r ^ d) + 2 * ((q // 2) ^ (k & 1)) + ((q % 2) ^ (k >> 1))
+            rows = pl.ds(pl.multiple_of(thin * at, 8), thin)
+            first = 8 * thin * k
+            for t, out in enumerate((out_q, out_k, out_v)):
+                out[rows, ours] = whole[first + thin * t : first + thin * (t + 1), :]
+                out[rows, other] = whole[first + thin * (5 + t) : first + thin * (6 + t), :]
+            for t in range(2):
+                columns = slice(half * t, half * (t + 1))
+                out_o[rows, columns] = whole[first + thin * (3 + t) : first + thin * (4 + t), :]
+
+
+def kernel_call(body, name, ins, outs, scratch, args, after=(), flops=10**8):
+    count = len(args)
+
+    def run(*refs):
+        body(*refs[:count], *refs[count + len(after) :])
+
     return pl.pallas_call(
-        body,
+        run,
         name=name,
         out_shape=[jax.ShapeDtypeStruct(shape, dtype) for shape, dtype, _ in outs],
-        in_specs=ins,
+        in_specs=list(ins) + [ANY] * len(after),
         out_specs=[spec for _, _, spec in outs],
         scratch_shapes=scratch,
-        cost_estimate=pl.CostEstimate(flops=cost, bytes_accessed=8 << 20, transcendentals=0),
-    )(*args)
+        cost_estimate=pl.CostEstimate(flops=flops, bytes_accessed=4 << 20, transcendentals=0),
+    )(*args, *after)
+
+
+def once(value, *after):
+    return pl.pallas_call(
+        lambda *refs: None,
+        name="once",
+        out_shape=jax.ShapeDtypeStruct(value.shape, value.dtype),
+        in_specs=[ANY] * (1 + len(after)),
+        out_specs=ANY,
+        input_output_aliases={0: 0},
+    )(value, *after)
 
 
 def plane_local(
     tokens, cotangent, seq_ids, w_query, b_query, w_key, w_value, b_value, w_out, b_out,
     attn_gain, attn_shift, w_up, b_up, w_down, b_down, ffn_gain, ffn_shift,
 ):
-    q, r, x, c = spot()
-    q1, q0 = q // 2, q % 2
-    low, wide_type = jnp.bfloat16, jnp.float32
+    x = lax.axis_index("x")
+    low, exact = jnp.bfloat16, jnp.float32
     rows, width = tokens.shape[1:]
     part = w_query.shape[0]
     half = width // 2
     inner = w_up.shape[1]
     wide = inner // 8
     keys = 8 * rows
+    own = 2 * rows
     pairs = half // 128
 
-    ids_rows = jnp.pad(seq_ids.astype(low), ((0, 15), (0, width - rows)))
-    blocks = [regroup(jnp.concatenate([tokens[0], ids_rows]))]
+    def call(body, name, ins, outs, scratch, args, after=(), flops=10**8):
+        return kernel_call(body, name, ins, outs, scratch, args, after, flops)
+
+    (block,) = call(
+        block_kernel, "block", [WHOLE] * 2, [((rows + 16, width), low, WHOLE)], [],
+        (tokens[0], seq_ids),
+    )
+    blocks = [regroup(block)]
+    theirs, mine = call(
+        pack_kernel,
+        "pack",
+        [WHOLE] * 12,
+        [((3 * part + 16, half), low, WHOLE)] * 2,
+        [pltpu.VMEM((16, half), exact)],
+        (w_query, w_key, w_value, b_query, b_value, b_out, attn_gain, attn_shift, b_down, ffn_gain, ffn_shift, b_up),
+    )
+    qkv_x = swap_x(theirs)
+    qkv_m = swap_c(mine)
     blocks.append(swap_x(blocks[0]))
     blocks.append(swap_c(blocks[0]))
     blocks.append(swap_c(blocks[1]))
@@ -836,48 +1079,25 @@
     blocks.append(swap_r(blocks[1]))
     blocks.append(swap_c(blocks[4]))
     blocks.append(swap_c(blocks[5]))
+    qkv_mx = swap_c(qkv_x)
+    out_m = swap_c(w_out)
 
     def cut(w, side, size):
         return lax.dynamic_slice_in_dim(w, side * size, size, 1)
 
-    qkv = (w_query, w_key, w_value)
-    qkv_x = swap_x(jnp.stack([cut(w, 1 - x, half) for w in qkv]))
-    qkv_m = swap_c(jnp.stack([cut(w, x, half) for w in qkv]))
-    qkv_mx = swap_c(qkv_x)
-    out_m = swap_c(w_out)
-    small = jnp.concatenate(
-        [b_query, b_value, b_out, attn_gain, attn_shift, b_down, ffn_gain, ffn_shift, b_up]
-    ).reshape(-1, half)
-    small = jnp.pad(small, ((0, 8 - small.shape[0]), (0, 0)))
-    small_x = swap_x(small)
-    small_m = swap_c(small)
-    small_mx = swap_c(small_x)
-    up_x = swap_x(cut(w_up, 1 - x, 4 * wide))
+    up_x = swap_x(once(cut(w_up, 1 - x, 4 * wide), blocks[1]))
     up_m = swap_c(cut(w_up, x, 4 * wide))
     up_mx = swap_c(up_x)
     down_m = swap_c(w_down)
-
-    chip = in_order(small, small_m, c).astype(wide_type)
-    other = in_order(small_x, small_mx, c).astype(wide_type)
-    every = in_order(chip, other, x).reshape(4, -1)
-    mine = chip.reshape(2, -1)
-    names = ("b_q", "b_v", "b_out", "gain1", "shift1", "b_down", "gain2", "shift2")
-    vec = {n: every[:, part * i : part * (i + 1)].reshape(1, width) for i, n in enumerate(names)}
-    vecs = jnp.concatenate(
-        [vec[n] for n in names[2:]] + [jnp.zeros((2, width), wide_type)]
-    )
-    bias = jnp.concatenate(
-        [mine[:, part * i : part * (i + 1)].reshape(1, half) for i in range(2)]
-        + [jnp.zeros((6, half), wide_type)]
-    )
-    up_bias = mine[:, 8 * part : 8 * part + 2 * wide].reshape(4, 1, wide)
-    up_bias = jnp.broadcast_to(up_bias, (4, 8, wide))
-
-    own = 2 * rows
-    x_all, w_all, wo_all, k3, v3, q3, mixed, lse, ids, a_own, a_low = kernel_call(
+    cot = regroup(once(cotangent[0], blocks[5]))
+    cot_x = swap_x(cot)
+
+    (
+        x_all, w_all, wo_all, k3, v3, q3, mixed, lse, ids, a_own, a_low, vecs, up_bias
+    ) = call(
         attend_kernel,
         "attend",
-        [ANY] * 16 + [WHOLE],
+        [ANY] * 17,
         [
             ((keys, width), low, ANY),
             ((width, 3 * half), low, ANY),
@@ -886,27 +1106,30 @@
             ((pairs, keys, 128), low, ANY),
             ((pairs, own, 128), low, WHOLE),
             ((own, half), low, WHOLE),
-            ((8, own), wide_type, WHOLE),
-            ((8, rows), wide_type, WHOLE),
-            ((own, width), wide_type, WHOLE),
+            ((8, own), exact, WHOLE),
+            ((8, rows), exact, WHOLE),
+            ((own, width), exact, WHOLE),
             ((own, width), low, WHOLE),
+            ((8, width), exact, WHOLE),
+            ((4, 8, wide), exact, WHOLE),
         ],
         [
             pltpu.VMEM((keys, width), low),
             pltpu.VMEM((8, 16, width), low),
             pltpu.VMEM((width, 3 * half), low),
             pltpu.VMEM((half, width), low),
+            pltpu.VMEM((4, 16, half), low),
             pltpu.VMEM((pairs, keys, 128), low),
             pltpu.VMEM((pairs, keys, 128), low),
             pltpu.VMEM((2 * pairs, 64, keys), low),
             pltpu.VMEM((pairs, own, 128), low),
-            pltpu.VMEM((2 * pairs, 64, own), wide_type),
-            pltpu.VMEM((keys, own), wide_type),
-            pltpu.SemaphoreType.DMA((30,)),
+            pltpu.VMEM((2 * pairs, 64, own), exact),
+            pltpu.VMEM((keys, own), exact),
+            pltpu.SemaphoreType.DMA((34,)),
             pltpu.SemaphoreType.DMA((5,)),
         ],
-        6 * 10**9,
-        (*blocks, *qkv, qkv_x, qkv_m, qkv_mx, w_out, out_m, bias),
+        (*blocks, w_query, w_key, w_value, qkv_x, qkv_m, qkv_mx, mine, w_out, out_m),
+        flops=3 * 10**9,
     )
     a_got = swap_x(a_low)
     kt = jnp.swapaxes(k3, 1, 2).reshape(2 * pairs, 64, keys)
@@ -916,50 +1139,48 @@
         pltpu.VMEM((width, 4 * wide), low),
         pltpu.VMEM((4 * wide, width), low),
     ]
-    h_low, normed1, rstd1, z, slope, y_own, y_low = kernel_call(
+    f_r, f_c, z_own, normed1, rstd1, slope, y_own, y_low = call(
         forward_kernel,
         "feedforward",
         [WHOLE, WHOLE, ANY, WHOLE, WHOLE] + [ANY] * 6,
         [
-            ((own, width), low, WHOLE),
-            ((own, width), wide_type, WHOLE),
-            ((own, 128), wide_type, WHOLE),
-            ((4, own, wide), low, WHOLE),
-            ((4, own, wide), wide_type, WHOLE),
-            ((own, width), wide_type, WHOLE),
+            ((own, 2 * wide + width), low, WHOLE),
+            ((own, wide + width), low, WHOLE),
+            ((own, wide), low, WHOLE),
+            ((own, width), exact, WHOLE),
+            ((own, 128), exact, WHOLE),
+            ((4, own, wide), exact, WHOLE),
+            ((own, width), exact, WHOLE),
             ((own, width), low, WHOLE),
         ],
         inner_scratch
-        + [pltpu.VMEM((own, width), low), pltpu.SemaphoreType.DMA((20,)), pltpu.SemaphoreType.DMA((1,))],
-        2 * 10**9,
+        + [
+            pltpu.VMEM((own, width), low),
+            pltpu.VMEM((own, 4 * wide), low),
+            pltpu.SemaphoreType.DMA((20,)),
+            pltpu.SemaphoreType.DMA((1,)),
+        ],
         (a_own, a_got, x_all, vecs, up_bias, *inner_weights),
+        flops=2 * 10**9,
     )
     y_got = swap_x(y_low)
-
-    def over_plane(pieces):
-        return jnp.concatenate([pieces[0], swap_r(pieces[1]), swap_c(pieces[2]), swap_rc(pieces[3])])
-
-    def whole_plane(block):
-        beside = swap_r(block)
-        return jnp.concatenate([block, beside, swap_c(block), swap_c(beside)])
-
-    z_plane = over_plane([z[j] for j in range(4)])
-    h_plane = whole_plane(h_low)
-
-    cot = regroup(cotangent[0])
-    cot_x = swap_x(cot)
-    hidden, dy, du, s_own, p_low, sums2, up_sums = kernel_call(
+    f_from_r = swap_r(f_r)
+    f_from_c = swap_c(f_c)
+    f_from_rc = swap_c(f_from_r)
+
+    hidden, b_r, b_c, du_own, s_own, p_low, sums2, up_sums = call(
         backward_kernel,
         "feedforward_back",
         [WHOLE, WHOLE, WHOLE, ANY, ANY, WHOLE, WHOLE] + [ANY] * 6,
         [
             ((rows, width), low, WHOLE),
+            ((own, 2 * wide + width), low, WHOLE),
+            ((own, wide + width), low, WHOLE),
+            ((own, wide), low, WHOLE),
+            ((own, width), exact, WHOLE),
             ((own, width), low, WHOLE),
-            ((4, own, wide), low, WHOLE),
-            ((own, width), wide_type, WHOLE),
-            ((own, width), low, WHOLE),
-            ((8, width), wide_type, WHOLE),
-            ((4, 8, wide), wide_type, WHOLE),
+            ((8, width), exact, WHOLE),
+            ((4, 8, wide), exact, WHOLE),
         ],
         inner_scratch
         + [
@@ -968,117 +1189,173 @@
             pltpu.SemaphoreType.DMA((20,)),
             pltpu.SemaphoreType.DMA((2,)),
         ],
-        2 * 10**9,
         (y_own, y_got, normed1, cot, cot_x, slope, vecs, *inner_weights),
+        flops=2 * 10**9,
     )
     p_got = swap_x(p_low)
-    hidden_out = regroup(hidden)[None]
-
-    dr, da, dq, dkv, sums1, qv_sums = kernel_call(
+    b_from_r = swap_r(b_r)
+    b_from_c = swap_c(b_c)
+    b_from_rc = swap_c(b_from_r)
+
+    dr, da, dq, dkv, sums1, qv_sums = call(
         attend_back_kernel,
         "attend_back",
         [WHOLE] * 13,
         [
-            ((rows, width), wide_type, WHOLE),
+            ((rows, width), exact, WHOLE),
             ((own, width), low, WHOLE),
             ((own, half), low, WHOLE),
             ((keys, 2 * half), low, WHOLE),
-            ((8, width), wide_type, WHOLE),
-            ((8, half), wide_type, WHOLE),
+            ((8, width), exact, WHOLE),
+            ((8, half), exact, WHOLE),
         ],
         [
-            pltpu.VMEM((keys, own), wide_type),
+            pltpu.VMEM((keys, own), exact),
             pltpu.VMEM((pairs, own, 128), low),
-            pltpu.VMEM((8, own), wide_type),
-            pltpu.VMEM((pairs, keys, 128), wide_type),
-            pltpu.VMEM((pairs, keys, 128), wide_type),
-            pltpu.VMEM((2 * pairs, 64, own), wide_type),
-            pltpu.VMEM((own, width), wide_type),
+            pltpu.VMEM((8, own), exact),
+            pltpu.VMEM((pairs, keys, 128), exact),
+            pltpu.VMEM((pairs, keys, 128), exact),
+            pltpu.VMEM((2 * pairs, 64, own), exact),
+            pltpu.VMEM((own, width), exact),
         ],
-        6 * 10**9,
         (s_own, p_got, normed1, rstd1, vecs, wo_all, mixed, q3, k3, v3, kt, lse, ids),
-    )
-
-    send, keep = kernel_call(
+        after=(f_from_rc, f_from_c),
+        flops=3 * 10**9,
+    )
+
+    thin = part // 8
+    count = 64 * thin
+    send, keep = call(
+        weight_grad_kernel,
+        "weight_grad",
+        [WHOLE] * 9,
+        [((count + 16, half), low, WHOLE), ((count + 16, half), exact, ANY)],
+        [pltpu.VMEM((2, count + 16, half), exact), pltpu.SemaphoreType.DMA((1,))],
+        (x_all, dkv, dq, mixed, da, sums1, sums2, qv_sums, up_sums),
+        flops=2 * 10**9,
+    )
+    rest_got = swap_c(send)
+    rest_keep = keep
+
+    quarter = wide // 4
+    down_send, down_keep = call(
+        down_grad_kernel,
+        "down_grad",
+        [WHOLE] * 8,
+        [((2, quarter, width), low, WHOLE), ((2, quarter, width), exact, WHOLE)],
+        [pltpu.VMEM((wide, width), exact)],
+        (z_own, f_from_r, f_from_c, f_from_rc, b_from_c, b_from_r, b_from_rc, b_c),
+        after=(send,),
+        flops=10**9,
+    )
+    down_got = swap_near(down_send)
+    up_send, up_keep = call(
+        up_grad_kernel,
+        "up_grad",
+        [WHOLE] * 8,
+        [((2, part, wide), low, WHOLE), ((2, part, wide), exact, WHOLE)],
+        [pltpu.VMEM((width, wide), exact)],
+        (f_c, f_from_r, f_from_c, f_from_rc, du_own, b_from_r, b_from_c, b_from_rc),
+        after=(down_send,),
+        flops=10**9,
+    )
+    up_got = swap_near(up_send)
+
+    x_send, x_keep = call(
         input_grad_kernel,
         "input_grad",
         [WHOLE] * 3,
-        [((2, own, width), low, WHOLE), ((2, own, width), wide_type, WHOLE)],
-        [pltpu.VMEM((keys, width), wide_type)],
-        10**9,
+        [((2, own, width), low, WHOLE), ((2, own, width), exact, WHOLE)],
+        [pltpu.VMEM((keys, width), exact)],
         (dq, dkv, w_all),
-    )
-
-    def folded(kept, got):
-        return kept + got.astype(wide_type)
-
-    total = folded(keep, swap_c(send))
-    total = folded(take(total, r), swap_r(take(total, 1 - r).astype(low))).reshape(2, rows, width)
-    total = folded(take(total, x), swap_x(take(total, 1 - x).astype(low)))
+        after=(up_send,),
+        flops=10**9,
+    )
+    x_got = swap_c(x_send)
+
+    def fold(name, bit, keep, got):
+        shape = keep.shape[1:]
+        return call(
+            lambda *refs: fold_kernel(bit, *refs),
+            name,
+            [WHOLE] * 2,
+            [(shape, low, WHOLE), (shape, exact, WHOLE)],
+            [],
+            (keep, got),
+        )
+
+    def step(name, bit, keep, got, size):
+        return call(
+            lambda *refs: step_kernel(bit, *refs),
+            name,
+            [WHOLE] * 2,
+            [((size + 16, half), low, WHOLE), ((size + 16, half), exact, WHOLE)],
+            [pltpu.VMEM((2 * size + 16, half), exact)],
+            (keep, got),
+        )
+
+    def spread(block):
+        block = beside(block, swap_far(block))
+        block = beside(block, swap_near(block))
+        return block, swap_r(block)
+
+    rest_send, rest_keep = step("rest_r", lambda q, r, x, c: r, rest_keep, rest_got, count // 2)
+    rest_got = swap_r(rest_send)
+    down_send, down_keep = fold("down_far", lambda q, r, x, c: q // 2, down_keep, down_got)
+    down_got = swap_far(down_send)
+    up_send, up_keep = fold("up_far", lambda q, r, x, c: q // 2, up_keep, up_got)
+    up_got = swap_far(up_send)
+    rest_send, rest_keep = step("rest_near", lambda q, r, x, c: q % 2, rest_keep, rest_got, count // 4)
+    rest_got = swap_near(rest_send)
+    (down_sum,) = call(
+        sum_kernel, "down_sum", [WHOLE] * 2, [((quarter, width), low, WHOLE)], [], (down_keep, down_got)
+    )
+    down_near, down_far = spread(down_sum)
+    shares = call(
+        share_kernel, "up_share", [WHOLE] * 2, [((part // 4, wide), low, WHOLE)] * 4, [], (up_keep, up_got)
+    )
+    up_sum = jnp.concatenate([shares[0], swap_c(shares[1]), swap_x(shares[2]), swap_xc(shares[3])])
+    up_near, up_far = spread(up_sum)
+    rest_send, rest_keep = step("rest_far", lambda q, r, x, c: q // 2, rest_keep, rest_got, count // 8)
+    rest_got = swap_far(rest_send)
+    side, base, lines = call(
+        last_step_kernel,
+        "rest_last",
+        [WHOLE] * 2,
+        [((3 * thin, half), low, WHOLE), ((5 * thin, half), low, WHOLE), ((16, half), exact, WHOLE)],
+        [pltpu.VMEM((8 * thin + 16, half), exact)],
+        (rest_keep, rest_got),
+    )
+    rest_near, rest_far = spread(beside(base, swap_x(side)))
+
+    x_send, x_keep = fold("input_r", lambda q, r, x, c: r, x_keep, x_got)
+    x_got = swap_r(x_send)
+    x_send, x_keep = fold(
+        "input_x", lambda q, r, x, c: x, x_keep.reshape(2, rows, width), x_got.reshape(2, rows, width)
+    )
+    total = x_keep + swap_x(x_send).astype(exact)
     tokens_grad = regroup((total + dr).astype(low))[None]
-
-    def swept(grad):
-        total = folded(take(grad, q0), swap_near(take(grad, 1 - q0).astype(low)))
-        return folded(take(total, q1), swap_far(take(total, 1 - q1).astype(low)))
-
-    def spread(block):
-        block = in_order(block, swap_far(block), q1)
-        block = in_order(block, swap_near(block), q0)
-        return in_order(block, swap_r(block), r)
-
-    dy_plane = whole_plane(dy)
-    du_plane = over_plane([du[j] for j in range(4)])
-    d_down = matmul_tn(z_plane, dy_plane).reshape(2, 2, wide // 4, width)
-    d_down = spread(swept(jnp.swapaxes(d_down, 0, 1)).astype(low))
-    w_down_grad = jnp.swapaxes(d_down, 1, 2).reshape(2 * wide, width).astype(wide_type)
-
-    d_up = matmul_tn(h_plane, du_plane).reshape(4, 2, 2, part // 4, wide)
-    d_up = swept(d_up.transpose(2, 1, 0, 3, 4)).astype(low).reshape(2, 2, part // 4, wide)
-    d_up = in_order(take(d_up, x), swap_x(take(d_up, 1 - x)), x)
-    d_up = jnp.swapaxes(d_up, 0, 1)
-    d_up = in_order(take(d_up, c), swap_c(take(d_up, 1 - c)), c)
-    d_up = spread(d_up)
-    w_up_grad = d_up.transpose(2, 1, 5, 4, 3, 0, 6).reshape(part, inner).astype(wide_type)
-
-    thin = part // 8
-    own_x = lax.dynamic_slice_in_dim(x_all, own * (2 * r + c), own, 0)
-    d_kv = matmul_tn(x_all, dkv).reshape(2, 2, 2, 2, 2, thin, 2, half)
-    d_q = matmul_tn(own_x, dq).reshape(2, 2, 2, 2, 2, thin, 1, half)
-    packed = jnp.concatenate([d_q, d_kv], axis=6).transpose(1, 2, 4, 3, 0, 6, 5, 7)
-    d_o = matmul_tn(mixed, da).reshape(2, 2, 2, 2, thin, 2, half).transpose(0, 1, 3, 2, 5, 4, 6)
-    packed = jnp.concatenate([packed.reshape(2, 2, 2, 2, 6, thin, half), d_o], axis=4)
-    packed = packed.reshape(2, 8, 8 * thin, half)
-
-    bits = up_sums[:, 0, :].reshape(2, 2, wide)
-    bits = jnp.where(c == 0, bits, bits[::-1])
-    bits = jnp.where(r == 0, bits, bits[:, ::-1]).reshape(4, wide)
-    wides = jnp.concatenate([sums1[:3], sums2[:3]]).reshape(6, 2, half)
-    wides = jnp.where(x == 0, wides[:, 0], wides[:, 1])
-    lines = jnp.concatenate([qv_sums[:2], bits, wides, jnp.zeros((4, half), wide_type)])
-
-    def step(block, lines, swap, bit):
-        block = block.reshape((2, -1, half))
-        out = jnp.concatenate([take(block, 1 - bit), lines]).astype(low)
-        got = swap(out).astype(wide_type)
-        count = block.shape[1]
-        return take(block, bit) + got[:count], lines + got[count:]
-
-    block, lines = step(packed, lines, swap_c, c)
-    block, lines = step(block, lines, swap_r, r)
-    block, lines = step(block, lines, swap_near, q0)
-    block, lines = step(block, lines, swap_far, q1)
-    block = block.astype(low)
-    sides = block[: 6 * thin].reshape(2, 3 * thin, half)
-    sides = in_order(take(sides, x), swap_x(take(sides, 1 - x)), x).reshape(6 * thin, half)
-    block = spread(jnp.concatenate([sides, block[6 * thin :]]).reshape(8, thin, half))
-    block = block.transpose(0, 2, 1, 4, 3, 5).reshape(part, 8, half).astype(wide_type)
-    w_query_grad, w_key_grad, w_value_grad = (
-        jnp.concatenate([block[:, t], block[:, 3 + t]], axis=1) for t in range(3)
-    )
-    w_out_grad = block[:, 6:8].reshape(part, width)
-
-    pieces = take(jnp.swapaxes(lines.reshape(-1, 2, part), 0, 1), c)
-    b_up_grad = take(lines[2:6].reshape(2, 2 * wide), c)
+    hidden_out = regroup(hidden)[None]
+
+    (w_down_grad,) = call(
+        down_out_kernel, "down_out", [WHOLE] * 2, [((2 * wide, width), exact, WHOLE)], [], (down_near, down_far)
+    )
+    (w_up_grad,) = call(
+        up_out_kernel, "up_out", [WHOLE] * 2, [((part, inner), exact, WHOLE)], [], (up_near, up_far)
+    )
+    w_query_grad, w_key_grad, w_value_grad, w_out_grad = call(
+        rest_out_kernel,
+        "rest_out",
+        [WHOLE] * 2,
+        [((part, width), exact, WHOLE)] * 4,
+        [pltpu.VMEM((32 * thin, half), exact)],
+        (rest_near, rest_far),
+    )
+
+    c = lax.axis_index("c")
+    pieces = jnp.where(c == 0, lines[:, :part], lines[:, part:])
+    ups = jnp.where(c == 0, lines[2:4], lines[4:6])
+    b_up_grad = ups.reshape(2 * wide)
     return (
         hidden_out,
         tokens_grad,

time: 317 us -> 289 us (0.912)
  Pallas kernels: 43.7 us -> 92.9 us
  local copies, waits for them, and re-layouts: 52.1 us -> 25.2 us
  waiting for transfers between devices: 114 us -> 91.5 us
  other arithmetic: 21.3 us -> 2.77 us
  matrix products: 11.8 us -> 0 us
  starting transfers between devices: 70.3 us -> 74.7 us
    pallas_call x5 -> x25, Pallas kernels: 43.7 us -> 92.9 us  [the longest x23 92.9 us: kernel_call(): pl.pallas_call(run, name=name, out_shape=[jax.ShapeDtypeStruct(shape, dty...]
    ppermute x61 -> x53, waiting for transfers between devices: 114 us -> 91.5 us  [moved(): lax.ppermute(block, AXES, [(number(s), number(move(*s))) for s in spots])]
    unnamed x75 -> x96, local copies, waits for them, and re-layouts: 5.3 us -> 20 us
    reshape x18 -> x1, local copies, waits for them, and re-layouts: 13.6 us -> 0.6 us  [plane_local(): b_up_grad = ups.reshape(2 * wide)]
    dot_general x5 -> x0, matrix products: 11.8 us -> none  [matmul_tn(): lax.dot_general(left, right, (((0,), (0,)), ((), ())), preferred_element_...]
    concatenate x12 -> x5, other arithmetic: 8.72 us -> 1.03 us  [the longest x4 1.02 us: beside(): return jnp.concatenate([mine, got])]
    concatenate x5 -> x3, local copies, waits for them, and re-layouts: 9.13 us -> 1.75 us  [beside(): return jnp.concatenate([mine, got])]
    convert_element_type x9 -> x0, local copies, waits for them, and re-layouts: 6.8 us -> none  [the longest x2 5.02 us: plane_local(): d_up.transpose(2, 1, 5, 4, 3, 0, 6).reshape(part, inner).astype(wide_type)]
  transfers between devices with their start and end apart: 61 -> 53, of which waited for: 18 -> 18; matrix products, arithmetic and copies ran while one was open for 22% -> 4% of each run, Pallas kernels for 14% -> 28%
where the time goes in v2:
time: 289 us; the launch traced here: 288 us
  Pallas kernels  92.9 us (32%)
  waiting for transfers between devices  91.5 us (32%)
  starting transfers between devices  74.7 us (26%)
  local copies, waits for them, and re-layouts  25.2 us (9%)
    pallas_call x23, Pallas kernels, kernel_call(): pl.pallas_call(run, name=name, out_shape=[jax.ShapeDtypeStruct(shape, dty...  92.9 us
    ppermute x53, waiting for transfers between devices, moved(): lax.ppermute(block, AXES, [(number(s), number(move(*s))) for s in spots])  91.5 us
    ppermute x53, starting transfers between devices, moved(): lax.ppermute(block, AXES, [(number(s), number(move(*s))) for s in spots])  74.7 us
    unnamed x96, local copies, waits for them, and re-layouts  20 us
  transfers between devices with their start and end apart: 53, of which 18 were waited for; matrix products, arithmetic and copies ran while one was open for 4% of the time, Pallas kernels for 28%

profile of v2, /device:TPU:0, one launch (start us, length us, event | category | flops | bytes accessed | tf_op | source)
XLA Modules:
  0.0 288.1 jit_solution(7364682132278323679)
XLA Ops:
  0.7 1.7 copy.55
  2.4 1.6 block.1
  4.0 1.6 collective-permute-start
  5.6 14.7 %collective-permute-start.1 = (bf16[144,768]{1,0:T(8,128)(2,1)S(1)}, bf16[144,768]{1,0:T(8,128)(2,1)S(1)}, u32[]{:S(2)}, u32[]{:S(2)}) collective-permute-start(bf16[144,768]{1,0:T(8,128)(2,1)S(1)} %collective-permute-done.refs_0_), channel_id=1, source_target_pairs={{0,2},{1,3},{2,0},{3,1},{4,6},{5,7},{6,4},{7,5},{8,10},{9,11},{10,... | collective-permute-start | bytes 663560 | tf_op jit(solution)/shard_map/ppermute | solution.py:479
  20.3 2.2 pack.1
  23.1 1.5 collective-permute-start.4
  24.6 1.4 collective-permute-done.1.refs_1_
  27.2 2.6 collective-permute-start.13
  30.6 5.6 %collective-permute-done.8.refs_11_ = bf16[592,384]{1,0:T(8,128)(2,1)} collective-permute-done((bf16[592,384]{1,0:T(8,128)(2,1)}, bf16[592,384]{1,0:T(8,128)(2,1)}, u32[]{:S(2)}, u32[]{:S(2)}) %collective-permute-start.8) | collective-permute-done | bytes 454688 | tf_op jit(solution)/shard_map/ppermute | solution.py:479
  36.2 1.5 collective-permute-start.5
  38.0 6.3 %collective-permute-done.5.refs_5_.refs_1_ = bf16[144,768]{1,0:T(8,128)(2,1)S(1)} collective-permute-done((bf16[144,768]{1,0:T(8,128)(2,1)}, bf16[144,768]{1,0:T(8,128)(2,1)S(1)}, u32[]{:S(2)}, u32[]{:S(2)}) %collective-permute-start.5) | collective-permute-done | bytes 221216 | tf_op jit(solution)/shard_map/ppermute | solution.py:479
  44.8 1.2 collective-permute-done.6.refs_6_
  47.7 10.8 %attend.1 = (bf16[1024,768]{1,0:T(8,128)(2,1)}, bf16[768,1152]{1,0:T(8,128)(2,1)}, bf16[384,768]{1,0:T(8,128)(2,1)}, bf16[3,1024,128]{2,1,0:T(8,128)(2,1)}, bf16...) custom-call(bf16[144,768]{1,0:T(8,128)(2,1)} %copy-done.39, ...), custom_call_target="tpu_custom_call" | custom-call | flops 3000000000 | bytes 4194304 | tf_op jit(solution)/shard_map/attend/pallas_call | solution.py:1020
  58.6 1.9 collective-permute-start.12
  60.5 9.8 %collective-permute-done.12.refs_1_ = bf16[256,768]{1,0:T(8,128)(2,1)S(1)} collective-permute-done((bf16[256,768]{1,0:T(8,128)(2,1)}, bf16[256,768]{1,0:T(8,128)(2,1)S(1)}, u32[]{:S(2)}, u32[]{:S(2)}) %collective-permute-start.12) | collective-permute-done | bytes 393248 | tf_op jit(solution)/shard_map/ppermute | solution.py:479
  71.1 7.7 %feedforward.1 = (bf16[256,1536]{1,0:T(8,128)(2,1)}, bf16[256,1152]{1,0:T(8,128)(2,1)}, bf16[256,384]{1,0:T(8,128)(2,1)}, f32[256,768]{1,0:T(8,128)}, f32[256,12...) custom-call(f32[256,768]{1,0:T(8,128)} %get-tuple-element.89.refs_0_, ...), custom_call_target="tpu_custom_call" | custom-call | flops 2000000000 | bytes 4194304 | tf_op jit(solution)/shard_map/feedforward/pallas_call | solution.py:1020
  78.8 1.6 collective-permute-start.22
  80.4 1.6 collective-permute-start.18
  82.0 2.7 collective-permute-start.17
  84.7 9.1 %collective-permute-start.19 = (bf16[128,768]{1,0:T(8,128)(2,1)S(1)}, bf16[128,768]{1,0:T(8,128)(2,1)S(1)}, u32[]{:S(2)}, u32[]{:S(2)}) collective-permute-start(bf16[128,768]{1,0:T(8,128)(2,1)S(1)} %collective-permute-done.18.refs_3_), channel_id=1, source_target_pairs={{0,2},{1,3},{2,0},{3,1},{4,6},{5,7},{6,4},{7,5},{8,10},{9,11},{10,... | collective-permute-start | bytes 589832 | tf_op jit(solution)/shard_map/ppermute | solution.py:479
  93.8 7.8 %collective-permute-done.19.refs_4_ = bf16[128,768]{1,0:T(8,128)(2,1)S(1)} collective-permute-done((bf16[128,768]{1,0:T(8,128)(2,1)S(1)}, bf16[128,768]{1,0:T(8,128)(2,1)S(1)}, u32[]{:S(2)}, u32[]{:S(2)}) %collective-permute-start.19) | collective-permute-done | bytes 196640 | tf_op jit(solution)/shard_map/ppermute | solution.py:479
  102.4 9.0 %feedforward_back.1 = (bf16[128,768]{1,0:T(8,128)(2,1)}, bf16[256,1536]{1,0:T(8,128)(2,1)}, bf16[256,1152]{1,0:T(8,128)(2,1)}, bf16[256,384]{1,0:T(8,128)(2,1)},...) custom-call(f32[256,768]{1,0:T(8,128)} %get-tuple-element.94.refs_0_, ...), custom_call_target="tpu_custom_call" | custom-call | flops 2000000000 | bytes 4194304 | tf_op jit(solution)/shard_map/feedforward_back/pallas_call | solution.py:1020
  113.2 2.2 collective-permute-start.21
  115.4 1.2 copy.37
  116.7 15.2 %collective-permute-done.25.refs_5_ = bf16[256,1536]{1,0:T(8,128)(2,1)S(1)} collective-permute-done((bf16[256,1536]{1,0:T(8,128)(2,1)}, bf16[256,1536]{1,0:T(8,128)(2,1)S(1)}, u32[]{:S(2)}, u32[]{:S(2)}) %collective-permute-start.25) | collective-permute-done | bytes 786464 | tf_op jit(solution)/shard_map/ppermute | solution.py:479
  133.0 10.4 %attend_back.1 = (f32[128,768]{1,0:T(8,128)}, bf16[256,768]{1,0:T(8,128)(2,1)}, bf16[256,384]{1,0:T(8,128)(2,1)}, bf16[1024,768]{1,0:T(8,128)(2,1)}, f32[8,768]{1,0:T(8,128)}, /*index=5*/f32[8,384]{1,0:T(8,128)}) custom-call(f32[256,768]{1,0:T(8,128)} %get-tuple-element.99.refs_0_, bf16[256,768]{1,0:T(8,128)(2,1)} %collective-permute-done.21.refs_1_, ...), custom_call_target="tpu_custom_call" | custom-call | flops 3000000000 | bytes 4194304 | tf_op jit(solution)/shard_map/attend_back/pallas_call | solution.py:1020
  143.5 6.4 %weight_grad.1 = (bf16[1552,384]{1,0:T(8,128)(2,1)}, f32[1552,384]{1,0:T(8,128)}) custom-call(bf16[1024,768]{1,0:T(8,128)(2,1)} %get-tuple-element.91.refs_2_.refs_0_, bf16[1024,768]{1,0:T(8,128)(2,1)} %get-tuple-element.112.refs_1_, bf16[256,384]{1,0:T(8,128)(2,1)} %get-tuple-element.111.refs_2_.refs_0_, ...), custom_call_target="tpu_custom_call" | custom-call | flops 2000000000 | bytes 4194304 | tf_op jit(solution)/shard_map/weight_grad/pallas_call | solution.py:1020
  151.1 4.3 %down_grad.1 = (bf16[2,96,768]{2,1,0:T(8,128)(2,1)}, f32[2,96,768]{2,1,0:T(8,128)}) custom-call(bf16[256,384]{1,0:T(8,128)(2,1)} %get-tuple-element.117.refs_0_, bf16[256,1536]{1,0:T(8,128)(2,1)} %copy-done.3, bf16[256,1152]{1,0:T(8,128)(2,1)} %collective-permute-done.24.refs_14_.refs_2_, bf16[256,1536]{1,0:T(8,128)(2,1)} %copy-done.5, ...), custom_call_target="tpu_custom_call" | custom-call | flops 1000000000 | bytes 4194304 | tf_op jit(solution)/shard_map/down_grad/pallas_call | solution.py:1020
  155.4 1.9 collective-permute-start.48
  157.2 4.4 %up_grad.1 = (bf16[2,192,384]{2,1,0:T(8,128)(2,1)}, f32[2,192,384]{2,1,0:T(8,128)}) custom-call(bf16[256,1152]{1,0:T(8,128)(2,1)} %get-tuple-element.110.refs_0_, bf16[256,1536]{1,0:T(8,128)(2,1)} %copy-done.3, bf16[256,1152]{1,0:T(8,128)(2,1)} %collective-permute-done.24.refs_14_.refs_2_, bf16[256,1536]{1,0:T(8,128)(2,1)} %copy-done.5, ...), custom_call_target="tpu_custom_call" | custom-call | flops 1000000000 | bytes 4194304 | tf_op jit(solution)/shard_map/up_grad/pallas_call | solution.py:1020
  161.8 3.2 %collective-permute-done.48.refs_1_ = bf16[2,96,768]{2,1,0:T(8,128)(2,1)S(1)} collective-permute-done((bf16[2,96,768]{2,1,0:T(8,128)(2,1)}, bf16[2,96,768]{2,1,0:T(8,128)(2,1)S(1)}, u32[]{:S(2)}, u32[]{:S(2)}) %collective-permute-start.48) | collective-permute-done | bytes 294944 | tf_op jit(solution)/shard_map/ppermute | solution.py:479
  165.8 1.9 down_far.1
  168.6 3.4 %collective-permute-done.40.refs_1_ = bf16[2,192,384]{2,1,0:T(8,128)(2,1)S(1)} collective-permute-done((bf16[2,192,384]{2,1,0:T(8,128)(2,1)}, bf16[2,192,384]{2,1,0:T(8,128)(2,1)S(1)}, u32[]{:S(2)}, u32[]{:S(2)}) %collective-permute-start.40) | collective-permute-done | bytes 294944 | tf_op jit(solution)/shard_map/ppermute | solution.py:479
  172.8 1.9 up_far.1
  175.6 5.4 %input_grad.1 = (bf16[2,256,768]{2,1,0:T(8,128)(2,1)}, f32[2,256,768]{2,1,0:T(8,128)}) custom-call(bf16[256,384]{1,0:T(8,128)(2,1)} %get-tuple-element.111.refs_2_.refs_0_, bf16[1024,768]{1,0:T(8,128)(2,1)} %get-tuple-element.112.refs_1_, bf16[768,1152]{1,0:T(8,128)(2,1)} %get-tuple-element.113.refs_2_, bf16[2,192,384]{2,1,0:T(8,128)(2,1)} %get-tuple-element.125.refs_3_), custom_call_target="tpu_custom_call" | custom-call | flops 1000000000 | bytes 4194304 | tf_op jit(solution)/shard_map/input_grad/pallas_call | solution.py:1020
  181.0 2.1 collective-permute-done.41.refs_1_
  183.8 1.7 up_share.1
  185.4 2.7 collective-permute-start.43
  189.1 3.6 %rest_r.1 = (bf16[784,384]{1,0:T(8,128)(2,1)}, f32[784,384]{1,0:T(8,128)}) custom-call(f32[1552,384]{1,0:T(8,128)} %get-tuple-element.133.refs_0_, bf16[1552,384]{1,0:T(8,128)(2,1)} %copy-done.11), custom_call_target="tpu_custom_call" | custom-call | flops 100000000 | bytes 4194304 | tf_op jit(solution)/shard_map/rest_r/pallas_call | solution.py:1020
  193.9 1.7 down_sum.1
  195.7 2.9 collective-permute-start.45
  199.8 7.5 %collective-permute-done.50 = bf16[96,768]{1,0:T(8,128)(2,1)S(1)} collective-permute-done((bf16[96,768]{1,0:T(8,128)(2,1)}, bf16[96,768]{1,0:T(8,128)(2,1)S(1)}, u32[]{:S(2)}, u32[]{:S(2)}) %collective-permute-start.50) | collective-permute-done | bytes 147488 | tf_op jit(solution)/shard_map/ppermute | solution.py:479
  209.8 2.7 input_r.1
  212.5 1.5 collective-permute-start.29
  214.9 2.6 rest_near.1
  217.5 2.0 collective-permute-start.34
  220.8 3.9 %collective-permute-done.29 = bf16[256,768]{1,0:T(8,128)(2,1)S(1)} collective-permute-done((bf16[256,768]{1,0:T(8,128)(2,1)}, bf16[256,768]{1,0:T(8,128)(2,1)S(1)}, u32[]{:S(2)}, u32[]{:S(2)}) %collective-permute-start.29) | collective-permute-done | bytes 393248 | tf_op jit(solution)/shard_map/ppermute | solution.py:479
  225.5 2.1 input_x.1
  229.3 2.0 rest_far.1
  231.4 2.6 collective-permute-start.35
  235.0 2.2 collective-permute-start.47
  237.2 3.0 %collective-permute-start.20 = (bf16[128,768]{1,0:T(8,128)(2,1)}, bf16[128,768]{1,0:T(8,128)(2,1)}, u32[]{:S(2)}, u32[]{:S(2)}) collective-permute-start(bf16[128,768]{1,0:T(8,128)(2,1)} %get-tuple-element.98), channel_id=1, source_target_pairs={{0,0},{1,16},{2,8},{3,24},{4,4},{5,20},{6,12},{7,28},{8,2},{9,18},... | collective-permute-start | bytes 589832 | tf_op jit(solution)/shard_map/ppermute | solution.py:479
  240.9 1.7 rest_last.1
  243.2 1.7 add_convert_fusion
  244.9 1.6 collective-permute-start.31
  247.5 2.8 collective-permute-start.37
  251.1 2.8 down_out.1
  254.7 2.8 up_out.1
  257.5 4.2 %collective-permute-done.37 = bf16[192,384]{1,0:T(8,128)(2,1)S(1)} collective-permute-done((bf16[192,384]{1,0:T(8,128)(2,1)S(1)}, bf16[192,384]{1,0:T(8,128)(2,1)S(1)}, u32[]{:S(2)}, u32[]{:S(2)}) %collective-permute-start.37) | collective-permute-done | bytes 147488 | tf_op jit(solution)/shard_map/ppermute | solution.py:479
  261.9 7.1 %collective-permute-done.38 = bf16[384,384]{1,0:T(8,128)(2,1)S(1)} collective-permute-done((bf16[384,384]{1,0:T(8,128)(2,1)S(1)}, bf16[384,384]{1,0:T(8,128)(2,1)S(1)}, u32[]{:S(2)}, u32[]{:S(2)}) %collective-permute-start.38) | collective-permute-done | bytes 294944 | tf_op jit(solution)/shard_map/ppermute | solution.py:479
  269.1 1.8 collective-permute-start.39
  272.1 10.0 %collective-permute-done.39.refs_1_ = bf16[768,384]{1,0:T(8,128)(2,1)S(1)} collective-permute-done((bf16[768,384]{1,0:T(8,128)(2,1)S(1)}, bf16[768,384]{1,0:T(8,128)(2,1)S(1)}, u32[]{:S(2)}, u32[]{:S(2)}) %collective-permute-start.39) | collective-permute-done | bytes 589856 | tf_op jit(solution)/shard_map/ppermute | solution.py:479
  283.0 2.8 rest_out.1
  285.8 1.6 copy.56
  (178 shorter events, 33.6 us)
Async XLA Ops:
  0.7 22.0 %copy-start.38 = (bf16[192,768]{1,0:T(8,128)(2,1)S(1)}, bf16[192,768]{1,0:T(8,128)(2,1)}, u32[]{:S(2)}) copy-start(bf16[192,768]{1,0:T(8,128)(2,1)} %refs_15_.1) | copy-start | bytes 884740
  0.7 25.4 %copy-start = (bf16[192,3072]{1,0:T(8,128)(2,1)S(1)}, bf16[192,3072]{1,0:T(8,128)(2,1)}, u32[]{:S(2)}) copy-start(bf16[192,3072]{1,0:T(8,128)(2,1)} %refs_7_.3) | copy-start | bytes 3538948
  4.0 1.6 collective-permute-start
  5.6 21.5 %copy-start.39 = (bf16[144,768]{1,0:T(8,128)(2,1)}, bf16[144,768]{1,0:T(8,128)(2,1)S(1)}, u32[]{:S(2)}) copy-start(bf16[144,768]{1,0:T(8,128)(2,1)S(1)} %collective-permute-done.refs_0_) | copy-start | bytes 663556
  5.6 20.4 %collective-permute-start.1 = (bf16[144,768]{1,0:T(8,128)(2,1)S(1)}, bf16[144,768]{1,0:T(8,128)(2,1)S(1)}, u32[]{:S(2)}, u32[]{:S(2)}) collective-permute-start(bf16[144,768]{1,0:T(8,128)(2,1)S(1)} %collective-permute-done.refs_0_), channel_id=1, source_target_pairs={{0,2},{1,3},{2,0},{3,1},{4,6},{5,7},{6,4},{7,5},{8,10},{9,11},{10,... | collective-permute-start | bytes 663560 | tf_op jit(solution)/shard_map/ppermute | solution.py:479
  22.5 13.7 %collective-permute-start.8 = (bf16[592,384]{1,0:T(8,128)(2,1)}, bf16[592,384]{1,0:T(8,128)(2,1)}, u32[]{:S(2)}, u32[]{:S(2)}) collective-permute-start(bf16[592,384]{1,0:T(8,128)(2,1)} %get-tuple-element.87), channel_id=1, source_target_pairs={{0,2},{1,3},{2,0},{3,1},{4,6},{5,7},{6,4},{7,5},{8,10},{9,11},{10,... | collective-permute-start | bytes 1363976 | tf_op jit(solution)/shard_map/ppermute | solution.py:479
  22.6 15.1 %collective-permute-start.9 = (bf16[592,384]{1,0:T(8,128)(2,1)}, bf16[592,384]{1,0:T(8,128)(2,1)}, u32[]{:S(2)}, u32[]{:S(2)}) collective-permute-start(bf16[592,384]{1,0:T(8,128)(2,1)} %get-tuple-element.88.refs_14_), channel_id=1, source_target_pairs={{0,1},{1,0},{2,3},{3,2},{4,5},{5,4},{6,7},{7,6},{8,9},{9,8},{10,11... | collective-permute-start | bytes 1363976 | tf_op jit(solution)/shard_map/ppermute | solution.py:479
  22.6 4.6 %collective-permute-start.11 = (bf16[192,768]{1,0:T(8,128)(2,1)S(1)}, bf16[192,768]{1,0:T(8,128)(2,1)}, u32[]{:S(2)}, u32[]{:S(2)}) collective-permute-start(bf16[192,768]{1,0:T(8,128)(2,1)S(1)} %copy-done.38), channel_id=1, source_target_pairs={{0,1},{1,0},{2,3},{3,2},{4,5},{5,4},{6,7},{7,6},{8,9},{9,8},{10,11... | collective-permute-start | bytes 884744 | tf_op jit(solution)/shard_map/ppermute | solution.py:479
  23.1 7.5 %collective-permute-start.4 = (bf16[144,768]{1,0:T(8,128)(2,1)S(1)}, bf16[144,768]{1,0:T(8,128)(2,1)}, u32[]{:S(2)}, u32[]{:S(2)}) collective-permute-start(bf16[144,768]{1,0:T(8,128)(2,1)S(1)} %collective-permute-done.refs_0_), channel_id=1, source_target_pairs={{0,4},{1,5},{2,6},{3,7},{4,0},{5,1},{6,2},{7,3},{8,12},{9,13},{10,... | collective-permute-start | bytes 663560 | tf_op jit(solution)/shard_map/ppermute | solution.py:479
  26.0 10.2 %collective-permute-start.2 = (bf16[144,768]{1,0:T(8,128)(2,1)S(1)}, bf16[144,768]{1,0:T(8,128)(2,1)}, u32[]{:S(2)}, u32[]{:S(2)}) collective-permute-start(bf16[144,768]{1,0:T(8,128)(2,1)S(1)} %collective-permute-done.refs_0_), channel_id=1, source_target_pairs={{0,1},{1,0},{2,3},{3,2},{4,5},{5,4},{6,7},{7,6},{8,9},{9,8},{10,11... | collective-permute-start | bytes 663560 | tf_op jit(solution)/shard_map/ppermute | solution.py:479
  27.2 19.8 %collective-permute-start.13 = (bf16[192,1536]{1,0:T(8,128)(2,1)}, bf16[192,1536]{1,0:T(8,128)(2,1)S(1)}, u32[]{:S(2)}, u32[]{:S(2)}) collective-permute-start(bf16[192,1536]{1,0:T(8,128)(2,1)} %once.2), channel_id=1, source_target_pairs={{0,2},{1,3},{2,0},{3,1},{4,6},{5,7},{6,4},{7,5},{8,10},{9,11},{10,... | collective-permute-start | bytes 1769480 | tf_op jit(solution)/shard_map/ppermute | solution.py:479
  30.6 29.9 %collective-permute-start.16 = (bf16[768,768]{1,0:T(8,128)(2,1)S(1)}, bf16[768,768]{1,0:T(8,128)(2,1)S(1)}, u32[]{:S(2)}, u32[]{:S(2)}) collective-permute-start(bf16[768,768]{1,0:T(8,128)(2,1)S(1)} %copy-done.1), channel_id=1, source_target_pairs={{0,1},{1,0},{2,3},{3,2},{4,5},{5,4},{6,7},{7,6},{8,9},{9,8},{10,11... | collective-permute-start | bytes 3538952 | tf_op jit(solution)/shard_map/ppermute | solution.py:479
  36.2 11.5 %collective-permute-start.10 = (bf16[592,384]{1,0:T(8,128)(2,1)}, bf16[592,384]{1,0:T(8,128)(2,1)}, u32[]{:S(2)}, u32[]{:S(2)}) collective-permute-start(bf16[592,384]{1,0:T(8,128)(2,1)} %collective-permute-done.8.refs_11_), channel_id=1, source_target_pairs={{0,1},{1,0},{2,3},{3,2},{4,5},{5,4},{6,7},{7,6},{8,9},{9,8},{10,11... | collective-permute-start | bytes 1363976 | tf_op jit(solution)/shard_map/ppermute | solution.py:479
  36.2 8.1 %collective-permute-start.5 = (bf16[144,768]{1,0:T(8,128)(2,1)}, bf16[144,768]{1,0:T(8,128)(2,1)S(1)}, u32[]{:S(2)}, u32[]{:S(2)}) collective-permute-start(bf16[144,768]{1,0:T(8,128)(2,1)} %copy-done.30), channel_id=1, source_target_pairs={{0,4},{1,5},{2,6},{3,7},{4,0},{5,1},{6,2},{7,3},{8,12},{9,13},{10,... | collective-permute-start | bytes 663560 | tf_op jit(solution)/shard_map/ppermute | solution.py:479
  37.7 6.5 %collective-permute-start.3 = (bf16[144,768]{1,0:T(8,128)(2,1)}, bf16[144,768]{1,0:T(8,128)(2,1)S(1)}, u32[]{:S(2)}, u32[]{:S(2)}) collective-permute-start(bf16[144,768]{1,0:T(8,128)(2,1)} %copy-done.30), channel_id=1, source_target_pairs={{0,1},{1,0},{2,3},{3,2},{4,5},{5,4},{6,7},{7,6},{8,9},{9,8},{10,11... | collective-permute-start | bytes 663560 | tf_op jit(solution)/shard_map/ppermute | solution.py:479
  44.3 1.7 collective-permute-start.6
  44.3 2.7 collective-permute-start.7
  46.0 14.5 %collective-permute-start.14 = (bf16[192,1536]{1,0:T(8,128)(2,1)}, bf16[192,1536]{1,0:T(8,128)(2,1)S(1)}, u32[]{:S(2)}, u32[]{:S(2)}) collective-permute-start(bf16[192,1536]{1,0:T(8,128)(2,1)} %get-tuple-element.157), channel_id=1, source_target_pairs={{0,1},{1,0},{2,3},{3,2},{4,5},{5,4},{6,7},{7,6},{8,9},{9,8},{10,11... | collective-permute-start | bytes 1769480 | tf_op jit(solution)/shard_map/ppermute | solution.py:479
  47.0 23.4 %collective-permute-start.15 = (bf16[192,1536]{1,0:T(8,128)(2,1)S(1)}, bf16[192,1536]{1,0:T(8,128)(2,1)}, u32[]{:S(2)}, u32[]{:S(2)}) collective-permute-start(bf16[192,1536]{1,0:T(8,128)(2,1)S(1)} %collective-permute-done.13.refs_6_.refs_8_), channel_id=1, source_target_pairs={{0,1},{1,0},{2,3},{3,2},{4,5},{5,4},{6,7},{7,6},{8,9},{9,8},{10,11... | collective-permute-start | bytes 1769480 | tf_op jit(solution)/shard_map/ppermute | solution.py:479
  58.6 11.7 %collective-permute-start.12 = (bf16[256,768]{1,0:T(8,128)(2,1)}, bf16[256,768]{1,0:T(8,128)(2,1)S(1)}, u32[]{:S(2)}, u32[]{:S(2)}) collective-permute-start(bf16[256,768]{1,0:T(8,128)(2,1)} %get-tuple-element.90), channel_id=1, source_target_pairs={{0,2},{1,3},{2,0},{3,1},{4,6},{5,7},{6,4},{7,5},{8,10},{9,11},{10,... | collective-permute-start | bytes 1179656 | tf_op jit(solution)/shard_map/ppermute | solution.py:479
  78.8 33.2 %collective-permute-start.22 = (bf16[256,1536]{1,0:T(8,128)(2,1)}, bf16[256,1536]{1,0:T(8,128)(2,1)S(1)}, u32[]{:S(2)}, u32[]{:S(2)}) collective-permute-start(bf16[256,1536]{1,0:T(8,128)(2,1)} %get-tuple-element.109), channel_id=1, source_target_pairs={{0,4},{1,5},{2,6},{3,7},{4,0},{5,1},{6,2},{7,3},{8,12},{9,13},{10,... | collective-permute-start | bytes 2359304 | tf_op jit(solution)/shard_map/ppermute | solution.py:479
  80.4 4.3 %collective-permute-start.18 = (bf16[128,768]{1,0:T(8,128)(2,1)}, bf16[128,768]{1,0:T(8,128)(2,1)S(1)}, u32[]{:S(2)}, u32[]{:S(2)}) collective-permute-start(bf16[128,768]{1,0:T(8,128)(2,1)} %once.3), channel_id=1, source_target_pairs={{0,0},{1,16},{2,8},{3,24},{4,4},{5,20},{6,12},{7,28},{8,2},{9,18},... | collective-permute-start | bytes 589832 | tf_op jit(solution)/shard_map/ppermute | solution.py:479
  82.0 19.6 %collective-permute-start.17 = (bf16[256,768]{1,0:T(8,128)(2,1)}, bf16[256,768]{1,0:T(8,128)(2,1)S(1)}, u32[]{:S(2)}, u32[]{:S(2)}) collective-permute-start(bf16[256,768]{1,0:T(8,128)(2,1)} %get-tuple-element.95), channel_id=1, source_target_pairs={{0,2},{1,3},{2,0},{3,1},{4,6},{5,7},{6,4},{7,5},{8,10},{9,11},{10,... | collective-permute-start | bytes 1179656 | tf_op jit(solution)/shard_map/ppermute | solution.py:479
  84.7 16.9 %copy-start.31 = (bf16[128,768]{1,0:T(8,128)(2,1)}, bf16[128,768]{1,0:T(8,128)(2,1)S(1)}, u32[]{:S(2)}) copy-start(bf16[128,768]{1,0:T(8,128)(2,1)S(1)} %collective-permute-done.18.refs_3_) | copy-start | bytes 589828
  84.7 16.9 %collective-permute-start.19 = (bf16[128,768]{1,0:T(8,128)(2,1)S(1)}, bf16[128,768]{1,0:T(8,128)(2,1)S(1)}, u32[]{:S(2)}, u32[]{:S(2)}) collective-permute-start(bf16[128,768]{1,0:T(8,128)(2,1)S(1)} %collective-permute-done.18.refs_3_), channel_id=1, source_target_pairs={{0,2},{1,3},{2,0},{3,1},{4,6},{5,7},{6,4},{7,5},{8,10},{9,11},{10,... | collective-permute-start | bytes 589832 | tf_op jit(solution)/shard_map/ppermute | solution.py:479
  111.5 20.4 %collective-permute-start.25 = (bf16[256,1536]{1,0:T(8,128)(2,1)}, bf16[256,1536]{1,0:T(8,128)(2,1)S(1)}, u32[]{:S(2)}, u32[]{:S(2)}) collective-permute-start(bf16[256,1536]{1,0:T(8,128)(2,1)} %get-tuple-element.115), channel_id=1, source_target_pairs={{0,4},{1,5},{2,6},{3,7},{4,0},{5,1},{6,2},{7,3},{8,12},{9,13},{10,... | collective-permute-start | bytes 2359304 | tf_op jit(solution)/shard_map/ppermute | solution.py:479
  112.0 31.4 %copy-start.3 = (bf16[256,1536]{1,0:T(8,128)(2,1)}, bf16[256,1536]{1,0:T(8,128)(2,1)S(1)}, u32[]{:S(2)}) copy-start(bf16[256,1536]{1,0:T(8,128)(2,1)S(1)} %collective-permute-done.22.refs_1_) | copy-start | bytes 2359300
  112.0 20.0 %collective-permute-start.23 = (bf16[256,1536]{1,0:T(8,128)(2,1)S(1)}, bf16[256,1536]{1,0:T(8,128)(2,1)S(1)}, u32[]{:S(2)}, u32[]{:S(2)}) collective-permute-start(bf16[256,1536]{1,0:T(8,128)(2,1)S(1)} %collective-permute-done.22.refs_1_), channel_id=1, source_target_pairs={{0,1},{1,0},{2,3},{3,2},{4,5},{5,4},{6,7},{7,6},{8,9},{9,8},{10,11... | collective-permute-start | bytes 2359304 | tf_op jit(solution)/shard_map/ppermute | solution.py:479
  113.1 18.9 %collective-permute-start.24 = (bf16[256,1152]{1,0:T(8,128)(2,1)}, bf16[256,1152]{1,0:T(8,128)(2,1)}, u32[]{:S(2)}, u32[]{:S(2)}) collective-permute-start(bf16[256,1152]{1,0:T(8,128)(2,1)} %get-tuple-element.110.refs_0_), channel_id=1, source_target_pairs={{0,1},{1,0},{2,3},{3,2},{4,5},{5,4},{6,7},{7,6},{8,9},{9,8},{10,11... | collective-permute-start | bytes 1769480 | tf_op jit(solution)/shard_map/ppermute | solution.py:479
  113.2 18.9 %collective-permute-start.21 = (bf16[256,768]{1,0:T(8,128)(2,1)}, bf16[256,768]{1,0:T(8,128)(2,1)}, u32[]{:S(2)}, u32[]{:S(2)}) collective-permute-start(bf16[256,768]{1,0:T(8,128)(2,1)} %get-tuple-element.100), channel_id=1, source_target_pairs={{0,2},{1,3},{2,0},{3,1},{4,6},{5,7},{6,4},{7,5},{8,10},{9,11},{10,... | collective-permute-start | bytes 1179656 | tf_op jit(solution)/shard_map/ppermute | solution.py:479
  116.5 33.6 %collective-permute-start.26 = (bf16[256,1152]{1,0:T(8,128)(2,1)}, bf16[256,1152]{1,0:T(8,128)(2,1)}, u32[]{:S(2)}, u32[]{:S(2)}) collective-permute-start(bf16[256,1152]{1,0:T(8,128)(2,1)} %get-tuple-element.116.refs_7_), channel_id=1, source_target_pairs={{0,1},{1,0},{2,3},{3,2},{4,5},{5,4},{6,7},{7,6},{8,9},{9,8},{10,11... | collective-permute-start | bytes 1769480 | tf_op jit(solution)/shard_map/ppermute | solution.py:479
  131.9 18.3 %collective-permute-start.27 = (bf16[256,1536]{1,0:T(8,128)(2,1)S(1)}, bf16[256,1536]{1,0:T(8,128)(2,1)S(1)}, u32[]{:S(2)}, u32[]{:S(2)}) collective-permute-start(bf16[256,1536]{1,0:T(8,128)(2,1)S(1)} %collective-permute-done.25.refs_5_), channel_id=1, source_target_pairs={{0,1},{1,0},{2,3},{3,2},{4,5},{5,4},{6,7},{7,6},{8,9},{9,8},{10,11... | collective-permute-start | bytes 2359304 | tf_op jit(solution)/shard_map/ppermute | solution.py:479
  149.8 38.3 %collective-permute-start.32 = (bf16[1552,384]{1,0:T(8,128)(2,1)}, bf16[1552,384]{1,0:T(8,128)(2,1)S(1)}, u32[]{:S(2)}, u32[]{:S(2)}) collective-permute-start(bf16[1552,384]{1,0:T(8,128)(2,1)} %get-tuple-element.123.refs_8_), channel_id=1, source_target_pairs={{0,1},{1,0},{2,3},{3,2},{4,5},{5,4},{6,7},{7,6},{8,9},{9,8},{10,11... | collective-permute-start | bytes 3575816 | tf_op jit(solution)/shard_map/ppermute | solution.py:479
  155.4 9.7 %collective-permute-start.48 = (bf16[2,96,768]{2,1,0:T(8,128)(2,1)}, bf16[2,96,768]{2,1,0:T(8,128)(2,1)S(1)}, u32[]{:S(2)}, u32[]{:S(2)}) collective-permute-start(bf16[2,96,768]{2,1,0:T(8,128)(2,1)} %get-tuple-element.124.refs_8_), channel_id=1, source_target_pairs={{0,8},{1,9},{2,10},{3,11},{4,12},{5,13},{6,14},{7,15},{8,0},{9,1},... | collective-permute-start | bytes 884744 | tf_op jit(solution)/shard_map/ppermute | solution.py:479
  161.7 10.4 %collective-permute-start.40 = (bf16[2,192,384]{2,1,0:T(8,128)(2,1)}, bf16[2,192,384]{2,1,0:T(8,128)(2,1)S(1)}, u32[]{:S(2)}, u32[]{:S(2)}) collective-permute-start(bf16[2,192,384]{2,1,0:T(8,128)(2,1)} %get-tuple-element.125.refs_3_), channel_id=1, source_target_pairs={{0,8},{1,9},{2,10},{3,11},{4,12},{5,13},{6,14},{7,15},{8,0},{9,1},... | collective-permute-start | bytes 884744 | tf_op jit(solution)/shard_map/ppermute | solution.py:479
  167.7 25.1 %collective-permute-start.49 = (bf16[96,768]{1,0:T(8,128)(2,1)}, bf16[96,768]{1,0:T(8,128)(2,1)S(1)}, u32[]{:S(2)}, u32[]{:S(2)}) collective-permute-start(bf16[96,768]{1,0:T(8,128)(2,1)} %get-tuple-element.156), channel_id=1, source_target_pairs={{0,16},{1,17},{2,18},{3,19},{4,20},{5,21},{6,22},{7,23},{8,24},{9,... | collective-permute-start | bytes 442376 | tf_op jit(solution)/shard_map/ppermute | solution.py:479
  174.7 8.4 %collective-permute-start.41 = (bf16[192,384]{1,0:T(8,128)(2,1)}, bf16[192,384]{1,0:T(8,128)(2,1)S(1)}, u32[]{:S(2)}, u32[]{:S(2)}) collective-permute-start(bf16[192,384]{1,0:T(8,128)(2,1)} %get-tuple-element.149), channel_id=1, source_target_pairs={{0,16},{1,17},{2,18},{3,19},{4,20},{5,21},{6,22},{7,23},{8,24},{9,... | collective-permute-start | bytes 442376 | tf_op jit(solution)/shard_map/ppermute | solution.py:479
  181.0 27.9 %collective-permute-start.28 = (bf16[2,256,768]{2,1,0:T(8,128)(2,1)}, bf16[2,256,768]{2,1,0:T(8,128)(2,1)S(1)}, u32[]{:S(2)}, u32[]{:S(2)}) collective-permute-start(bf16[2,256,768]{2,1,0:T(8,128)(2,1)} %get-tuple-element.127), channel_id=1, source_target_pairs={{0,1},{1,0},{2,3},{3,2},{4,5},{5,4},{6,7},{7,6},{8,9},{9,8},{10,11... | collective-permute-start | bytes 2359304 | tf_op jit(solution)/shard_map/ppermute | solution.py:479
  185.4 10.1 %collective-permute-start.42 = (bf16[48,384]{1,0:T(8,128)(2,1)}, bf16[48,384]{1,0:T(8,128)(2,1)S(1)}, u32[]{:S(2)}, u32[]{:S(2)}) collective-permute-start(bf16[48,384]{1,0:T(8,128)(2,1)} %get-tuple-element.151), channel_id=1, source_target_pairs={{0,1},{1,0},{2,3},{3,2},{4,5},{5,4},{6,7},{7,6},{8,9},{9,8},{10,11... | collective-permute-start | bytes 110600 | tf_op jit(solution)/shard_map/ppermute | solution.py:479
  185.4 10.3 %collective-permute-start.43 = (bf16[48,384]{1,0:T(8,128)(2,1)}, bf16[48,384]{1,0:T(8,128)(2,1)S(1)}, u32[]{:S(2)}, u32[]{:S(2)}) collective-permute-start(bf16[48,384]{1,0:T(8,128)(2,1)} %get-tuple-element.152), channel_id=1, source_target_pairs={{0,2},{1,3},{2,0},{3,1},{4,6},{5,7},{6,4},{7,5},{8,10},{9,11},{10,... | collective-permute-start | bytes 110600 | tf_op jit(solution)/shard_map/ppermute | solution.py:479
  188.1 7.6 %collective-permute-start.44 = (bf16[48,384]{1,0:T(8,128)(2,1)}, bf16[48,384]{1,0:T(8,128)(2,1)S(1)}, u32[]{:S(2)}, u32[]{:S(2)}) collective-permute-start(bf16[48,384]{1,0:T(8,128)(2,1)} %get-tuple-element.153), channel_id=1, source_target_pairs={{0,3},{1,2},{2,1},{3,0},{4,7},{5,6},{6,5},{7,4},{8,11},{9,10},{10,... | collective-permute-start | bytes 110600 | tf_op jit(solution)/shard_map/ppermute | solution.py:479
  192.8 21.3 %collective-permute-start.33 = (bf16[784,384]{1,0:T(8,128)(2,1)}, bf16[784,384]{1,0:T(8,128)(2,1)S(1)}, u32[]{:S(2)}, u32[]{:S(2)}) collective-permute-start(bf16[784,384]{1,0:T(8,128)(2,1)} %get-tuple-element.135), channel_id=1, source_target_pairs={{0,4},{1,5},{2,6},{3,7},{4,0},{5,1},{6,2},{7,3},{8,12},{9,13},{10,... | collective-permute-start | bytes 1806344 | tf_op jit(solution)/shard_map/ppermute | solution.py:479
  195.6 11.7 %collective-permute-start.50 = (bf16[96,768]{1,0:T(8,128)(2,1)}, bf16[96,768]{1,0:T(8,128)(2,1)S(1)}, u32[]{:S(2)}, u32[]{:S(2)}) collective-permute-start(bf16[96,768]{1,0:T(8,128)(2,1)} %down_sum.1), channel_id=1, source_target_pairs={{0,16},{1,17},{2,18},{3,19},{4,20},{5,21},{6,22},{7,23},{8,24},{9,... | collective-permute-start | bytes 442376 | tf_op jit(solution)/shard_map/ppermute | solution.py:479
  195.7 23.7 %collective-permute-start.45 = (bf16[192,384]{1,0:T(8,128)(2,1)S(1)}, bf16[192,384]{1,0:T(8,128)(2,1)S(1)}, u32[]{:S(2)}, u32[]{:S(2)}) collective-permute-start(bf16[192,384]{1,0:T(8,128)(2,1)S(1)} %pad_maximum_fusion.4), channel_id=1, source_target_pairs={{0,16},{1,17},{2,18},{3,19},{4,20},{5,21},{6,22},{7,23},{8,24},{9,... | collective-permute-start | bytes 442376 | tf_op jit(solution)/shard_map/ppermute | solution.py:479
  208.2 12.0 %collective-permute-start.51 = (bf16[192,768]{1,0:T(8,128)(2,1)S(1)}, bf16[192,768]{1,0:T(8,128)(2,1)S(1)}, u32[]{:S(2)}, u32[]{:S(2)}) collective-permute-start(bf16[192,768]{1,0:T(8,128)(2,1)S(1)} %pad_maximum_fusion.2), channel_id=1, source_target_pairs={{0,8},{1,9},{2,10},{3,11},{4,12},{5,13},{6,14},{7,15},{8,0},{9,1},... | collective-permute-start | bytes 884744 | tf_op jit(solution)/shard_map/ppermute | solution.py:479
  212.5 12.2 %collective-permute-start.29 = (bf16[256,768]{1,0:T(8,128)(2,1)}, bf16[256,768]{1,0:T(8,128)(2,1)S(1)}, u32[]{:S(2)}, u32[]{:S(2)}) collective-permute-start(bf16[256,768]{1,0:T(8,128)(2,1)} %get-tuple-element.129), channel_id=1, source_target_pairs={{0,4},{1,5},{2,6},{3,7},{4,0},{5,1},{6,2},{7,3},{8,12},{9,13},{10,... | collective-permute-start | bytes 1179656 | tf_op jit(solution)/shard_map/ppermute | solution.py:479
  217.5 11.2 %collective-permute-start.34 = (bf16[400,384]{1,0:T(8,128)(2,1)}, bf16[400,384]{1,0:T(8,128)(2,1)S(1)}, u32[]{:S(2)}, u32[]{:S(2)}) collective-permute-start(bf16[400,384]{1,0:T(8,128)(2,1)} %get-tuple-element.137), channel_id=1, source_target_pairs={{0,8},{1,9},{2,10},{3,11},{4,12},{5,13},{6,14},{7,15},{8,0},{9,1},... | collective-permute-start | bytes 921608 | tf_op jit(solution)/shard_map/ppermute | solution.py:479
  220.2 13.8 %collective-permute-start.46 = (bf16[384,384]{1,0:T(8,128)(2,1)}, bf16[384,384]{1,0:T(8,128)(2,1)}, u32[]{:S(2)}, u32[]{:S(2)}) collective-permute-start(bf16[384,384]{1,0:T(8,128)(2,1)} %get-tuple-element.159), channel_id=1, source_target_pairs={{0,8},{1,9},{2,10},{3,11},{4,12},{5,13},{6,14},{7,15},{8,0},{9,1},... | collective-permute-start | bytes 884744 | tf_op jit(solution)/shard_map/ppermute | solution.py:479
  220.2 14.8 %copy-start.7 = (bf16[384,768]{1,0:T(8,128)(2,1)}, bf16[384,768]{1,0:T(8,128)(2,1)S(1)}, u32[]{:S(2)}) copy-start(bf16[384,768]{1,0:T(8,128)(2,1)S(1)} %pad_maximum_fusion.refs_0_) | copy-start | bytes 1769476
  220.3 30.0 %collective-permute-start.52 = (bf16[384,768]{1,0:T(8,128)(2,1)S(1)}, bf16[384,768]{1,0:T(8,128)(2,1)S(1)}, u32[]{:S(2)}, u32[]{:S(2)}) collective-permute-start(bf16[384,768]{1,0:T(8,128)(2,1)S(1)} %pad_maximum_fusion.refs_0_), channel_id=1, source_target_pairs={{0,4},{1,5},{2,6},{3,7},{4,0},{5,1},{6,2},{7,3},{8,12},{9,13},{10,... | collective-permute-start | bytes 1769480 | tf_op jit(solution)/shard_map/ppermute | solution.py:479
  227.6 15.6 %copy-start.22 = (f32[128,768]{1,0:T(8,128)S(1)}, f32[128,768]{1,0:T(8,128)}, u32[]{:S(2)}) copy-start(f32[128,768]{1,0:T(8,128)} %get-tuple-element.132) | copy-start | bytes 1179652
  227.6 15.6 %copy-start.23 = (f32[128,768]{1,0:T(8,128)S(1)}, f32[128,768]{1,0:T(8,128)}, u32[]{:S(2)}) copy-start(f32[128,768]{1,0:T(8,128)} %get-tuple-element.130) | copy-start | bytes 1179652
  227.6 15.6 %collective-permute-start.30 = (bf16[128,768]{1,0:T(8,128)(2,1)}, bf16[128,768]{1,0:T(8,128)(2,1)}, u32[]{:S(2)}, u32[]{:S(2)}) collective-permute-start(bf16[128,768]{1,0:T(8,128)(2,1)} %get-tuple-element.131), channel_id=1, source_target_pairs={{0,2},{1,3},{2,0},{3,1},{4,6},{5,7},{6,4},{7,5},{8,10},{9,11},{10,... | collective-permute-start | bytes 589832 | tf_op jit(solution)/shard_map/ppermute | solution.py:479
  231.4 8.8 %collective-permute-start.35 = (bf16[208,384]{1,0:T(8,128)(2,1)}, bf16[208,384]{1,0:T(8,128)(2,1)S(1)}, u32[]{:S(2)}, u32[]{:S(2)}) collective-permute-start(bf16[208,384]{1,0:T(8,128)(2,1)} %get-tuple-element.139), channel_id=1, source_target_pairs={{0,16},{1,17},{2,18},{3,19},{4,20},{5,21},{6,22},{7,23},{8,24},{9,... | collective-permute-start | bytes 479240 | tf_op jit(solution)/shard_map/ppermute | solution.py:479
  235.0 18.8 %copy-start.16 = (bf16[768,384]{1,0:T(8,128)(2,1)}, bf16[768,384]{1,0:T(8,128)(2,1)S(1)}, u32[]{:S(2)}) copy-start(bf16[768,384]{1,0:T(8,128)(2,1)S(1)} %constant_dynamic-update-slice_fusion.9.refs_0_) | copy-start | bytes 1769476
  235.0 18.8 %collective-permute-start.47 = (bf16[768,384]{1,0:T(8,128)(2,1)S(1)}, bf16[768,384]{1,0:T(8,128)(2,1)S(1)}, u32[]{:S(2)}, u32[]{:S(2)}) collective-permute-start(bf16[768,384]{1,0:T(8,128)(2,1)S(1)} %constant_dynamic-update-slice_fusion.9.refs_0_), channel_id=1, source_target_pairs={{0,4},{1,5},{2,6},{3,7},{4,0},{5,1},{6,2},{7,3},{8,12},{9,13},{10,... | collective-permute-start | bytes 1769480 | tf_op jit(solution)/shard_map/ppermute | solution.py:479
  237.2 13.0 %collective-permute-start.20 = (bf16[128,768]{1,0:T(8,128)(2,1)}, bf16[128,768]{1,0:T(8,128)(2,1)}, u32[]{:S(2)}, u32[]{:S(2)}) collective-permute-start(bf16[128,768]{1,0:T(8,128)(2,1)} %get-tuple-element.98), channel_id=1, source_target_pairs={{0,0},{1,16},{2,8},{3,24},{4,4},{5,20},{6,12},{7,28},{8,2},{9,18},... | collective-permute-start | bytes 589832 | tf_op jit(solution)/shard_map/ppermute | solution.py:479
  242.6 4.9 %collective-permute-start.36 = (bf16[72,384]{1,0:T(8,128)(2,1)}, bf16[72,384]{1,0:T(8,128)(2,1)S(1)}, u32[]{:S(2)}, u32[]{:S(2)}) collective-permute-start(bf16[72,384]{1,0:T(8,128)(2,1)} %get-tuple-element.141), channel_id=1, source_target_pairs={{0,2},{1,3},{2,0},{3,1},{4,6},{5,7},{6,4},{7,5},{8,10},{9,11},{10,... | collective-permute-start | bytes 165896 | tf_op jit(solution)/shard_map/ppermute | solution.py:479
  244.9 12.6 %collective-permute-start.31 = (bf16[128,768]{1,0:T(8,128)(2,1)}, bf16[128,768]{1,0:T(8,128)(2,1)S(1)}, u32[]{:S(2)}, u32[]{:S(2)}) collective-permute-start(bf16[128,768]{1,0:T(8,128)(2,1)} %add_convert_fusion), channel_id=1, source_target_pairs={{0,0},{1,16},{2,8},{3,24},{4,4},{5,20},{6,12},{7,28},{8,2},{9,18},... | collective-permute-start | bytes 589832 | tf_op jit(solution)/shard_map/ppermute | solution.py:479
  247.5 14.3 %collective-permute-start.37 = (bf16[192,384]{1,0:T(8,128)(2,1)S(1)}, bf16[192,384]{1,0:T(8,128)(2,1)S(1)}, u32[]{:S(2)}, u32[]{:S(2)}) collective-permute-start(bf16[192,384]{1,0:T(8,128)(2,1)S(1)} %pad_maximum_fusion.3), channel_id=1, source_target_pairs={{0,16},{1,17},{2,18},{3,19},{4,20},{5,21},{6,22},{7,23},{8,24},{9,... | collective-permute-start | bytes 442376 | tf_op jit(solution)/shard_map/ppermute | solution.py:479
  257.5 13.3 %copy-start.37 = (f32[16,384]{1,0:T(8,128)S(1)}, f32[16,384]{1,0:T(8,128)}, u32[]{:S(2)}) copy-start(f32[16,384]{1,0:T(8,128)} %get-tuple-element.143) | copy-start | bytes 73732
  261.8 7.2 %collective-permute-start.38 = (bf16[384,384]{1,0:T(8,128)(2,1)S(1)}, bf16[384,384]{1,0:T(8,128)(2,1)S(1)}, u32[]{:S(2)}, u32[]{:S(2)}) collective-permute-start(bf16[384,384]{1,0:T(8,128)(2,1)S(1)} %pad_maximum_fusion.1), channel_id=1, source_target_pairs={{0,8},{1,9},{2,10},{3,11},{4,12},{5,13},{6,14},{7,15},{8,0},{9,1},... | collective-permute-start | bytes 884744 | tf_op jit(solution)/shard_map/ppermute | solution.py:479
  269.1 13.1 %copy-start.13 = (bf16[768,384]{1,0:T(8,128)(2,1)}, bf16[768,384]{1,0:T(8,128)(2,1)S(1)}, u32[]{:S(2)}) copy-start(bf16[768,384]{1,0:T(8,128)(2,1)S(1)} %constant_dynamic-update-slice_fusion.refs_0_) | copy-start | bytes 1769476
  269.1 13.1 %collective-permute-start.39 = (bf16[768,384]{1,0:T(8,128)(2,1)S(1)}, bf16[768,384]{1,0:T(8,128)(2,1)S(1)}, u32[]{:S(2)}, u32[]{:S(2)}) collective-permute-start(bf16[768,384]{1,0:T(8,128)(2,1)S(1)} %constant_dynamic-update-slice_fusion.refs_0_), channel_id=1, source_target_pairs={{0,4},{1,5},{2,6},{3,7},{4,0},{5,1},{6,2},{7,3},{8,12},{9,13},{10,... | collective-permute-start | bytes 1769480 | tf_op jit(solution)/shard_map/ppermute | solution.py:479
  (32 other events, 100.3 us)

commit v3 on v2

--- a/solution.py
+++ b/solution.py
@@ -458,6 +458,7 @@
 AXES = ("q", "r", "x", "c")
 ANY = pl.BlockSpec(memory_space=pl.ANY)
 WHOLE = pl.BlockSpec(memory_space=pltpu.VMEM)
+HBM = pl.BlockSpec(memory_space=pltpu.HBM)
 
 
 def moved(block, move):
@@ -507,6 +508,10 @@
     return moved(block, lambda q, r, x, c: (2 * c + x, r, q & 1, q >> 1))
 
 
+def regroup_x(block):
+    return moved(block, lambda q, r, x, c: (2 * c + x, r, 1 - (q & 1), q >> 1))
+
+
 def swap_xc(block):
     return moved(block, lambda q, r, x, c: (q, r, 1 - x, 1 - c))
 
@@ -561,31 +566,39 @@
         mask[rows * b : rows * (b + 1), :] = jnp.where(across[:, b : b + 1] == mine, 0.0, masked_fill)
 
 
-def block_kernel(tokens, ids, block):
+def block_kernel(tokens, ids, block, line, sems):
     rows = tokens.shape[0]
-    block[0:rows, :] = tokens[...]
+    copies = Copies(sems)
+    copies.start(tokens, block.at[pl.ds(0, rows)])
+    copies.start(ids, line)
     block[rows:, :] = jnp.zeros((16, block.shape[1]), block.dtype)
-    line = ids[...].astype(jnp.float32)
-    block[rows:, 0:rows] = jnp.broadcast_to(line, (16, rows)).astype(block.dtype)
+    copies.wait()
+    block[rows:, 0:rows] = jnp.broadcast_to(line[...].astype(jnp.float32), (16, rows)).astype(block.dtype)
 
 
 def pack_kernel(w_q, w_k, w_v, *refs):
-    vectors, b_up, theirs, mine, lines = refs[:8], refs[8], refs[9], refs[10], refs[11]
+    vectors, b_up, theirs, mine = refs[:8], refs[8], refs[9], refs[10]
+    lines, thin, thick, sems = refs[11], refs[12:20], refs[20], refs[21]
     q, r, x, c = spot()
     part, width = w_q.shape
     half = width // 2
+    copies = Copies(sems)
     for t, w in enumerate((w_q, w_k, w_v)):
-        rows = slice(part * t, part * (t + 1))
-        mine[rows, :] = w[:, pl.ds(pl.multiple_of(half * x, 128), half)]
-        theirs[rows, :] = w[:, pl.ds(pl.multiple_of(half * (1 - x), 128), half)]
+        rows = pl.ds(part * t, part)
+        copies.start(w.at[:, pl.ds(pl.multiple_of(half * x, 128), half)], mine.at[rows])
+        copies.start(w.at[:, pl.ds(pl.multiple_of(half * (1 - x), 128), half)], theirs.at[rows])
+    for vector, held in zip(vectors, thin):
+        copies.start(vector, held)
+    copies.start(b_up, thick)
     lines[...] = jnp.zeros_like(lines)
-    for i, vector in enumerate(vectors):
+    copies.wait()
+    for i, vector in enumerate(thin):
         line = vector[...].astype(jnp.float32).reshape(1, part)
         none = jnp.zeros_like(line)
         first = jnp.concatenate([line, none], axis=1)
         second = jnp.concatenate([none, line], axis=1)
         lines[i : i + 1, :] = jnp.where(c == 0, first, second)
-    wide = b_up[...].astype(jnp.float32).reshape(1, width)
+    wide = thick[...].astype(jnp.float32).reshape(1, width)
     lines[pl.ds(8 + 2 * c, 1), :] = wide[:, 0:half]
     lines[pl.ds(9 + 2 * c, 1), :] = wide[:, half:]
     low = lines[...].astype(jnp.bfloat16)
@@ -593,9 +606,29 @@
     theirs[3 * part :, :] = low
 
 
+def cut_kernel(w, theirs, mine, sems):
+    q, r, x, c = spot()
+    count = theirs.shape[1]
+    copies = Copies(sems)
+    copies.start(w.at[:, pl.ds(pl.multiple_of(count * (1 - x), 128), count)], theirs)
+    copies.start(w.at[:, pl.ds(pl.multiple_of(count * x, 128), count)], mine)
+    copies.wait()
+
+
+def load_kernel(block, out, sems):
+    copies = Copies(sems)
+    copies.start(block, out)
+    copies.wait()
+
+
+def turn_kernel(keys, out):
+    for p in range(keys.shape[0]):
+        out[2 * p : 2 * p + 2] = jnp.transpose(keys[p]).reshape(2, 64, keys.shape[1])
+
+
 def attend_kernel(
     b0, b1, b2, b3, b4, b5, b6, b7, w_q, w_k, w_v, w_x, w_m, w_mx, own_lines, w_o, w_om,
-    x_out, w_out, wo_out, k_out, v_out, q_out, o_out, lse_out, ids_out, a_out, a_low, vecs, up_bias,
+    a_low, x_out, w_out, wo_out, k_out, v_out, q_out, o_out, lse_out, ids_out, a_out, vecs, up_bias,
     xs, raw, w, wo, lines, k3, v3, vt, q3, ot, mask, sems, outs,
 ):
     q, r, x, c = spot()
@@ -673,18 +706,14 @@
 def load_feedforward(copies, up, down, u_own, u_x, u_m, u_mx, d_own, d_m):
     q, r, x, c = spot()
     part = up.shape[0] // 4
-    wide = up.shape[1] // 4
+    count = up.shape[1]
     shard = 2 * x + c
-    for j in range(4):
-        at = pl.ds(wide * j, wide)
-        slot = (2 * c + r) ^ j
-        pieces = ((0, u_own, 4 * wide * x), (2, u_x, 0), (1, u_m, 0), (3, u_mx, 0))
-        for flip, piece, base in pieces:
-            rows = pl.ds(pl.multiple_of(part * (shard ^ flip), 64), part)
-            columns = pl.ds(pl.multiple_of(base + wide * slot, 128), wide)
-            copies.start(piece.at[:, columns], up.at[rows, at])
-        source = d_own if j < 2 else d_m
-        copies.start(source.at[pl.ds(pl.multiple_of(wide * (r ^ (j & 1)), 128), wide)], down.at[at])
+    own = u_own.at[:, pl.ds(pl.multiple_of(count * x, 128), count)]
+    for flip, piece in ((0, own), (2, u_x), (1, u_m), (3, u_mx)):
+        rows = pl.ds(pl.multiple_of(part * (shard ^ flip), 64), part)
+        copies.start(piece, up.at[rows])
+    for side, piece in ((c, d_own), (1 - c, d_m)):
+        copies.start(piece, down.at[pl.ds(pl.multiple_of(count // 2 * side, 128), count // 2)])
 
 
 def norm_of(value):
@@ -704,8 +733,8 @@
 
 def forward_kernel(
     a_own, a_got, xs, vecs, b_up, u_own, u_x, u_m, u_mx, d_own, d_m,
-    to_r, to_c, z_own, n_out, r_out, slope_out, y_out, y_low,
-    up, down, x_own, z, sems, more,
+    y_low, h_out, z, n_out, r_out, slope, y_out,
+    up, down, x_own, sems, more,
 ):
     q, r, x, c = spot()
     rows = x_own.shape[0]
@@ -719,68 +748,68 @@
     n_out[...] = normed
     r_out[...] = jnp.broadcast_to(rstd, r_out.shape)
     low = (normed * vecs[3:4, :] + vecs[4:5, :]).astype(jnp.bfloat16)
+    h_out[...] = low
+    copies.wait()
     wide = up.shape[1] // 4
-    to_r[:, 2 * wide :] = low
-    to_c[:, wide:] = low
-    copies.wait()
     for j in range(4):
-        pre = dot(low, up[:, wide * j : wide * (j + 1)]) + b_up[(2 * c + r) ^ j, 0:1, :]
+        at = slice(wide * j, wide * (j + 1))
+        pre = dot(low, up[:, at]) + b_up[j, 0:1, :]
         cdf = 0.5 * (1.0 + lax.erf(pre * (1.0 / math.sqrt(2.0))))
         density = jnp.exp(-0.5 * pre * pre) * (1.0 / math.sqrt(2.0 * math.pi))
-        z[:, wide * j : wide * (j + 1)] = (pre * cdf).astype(jnp.bfloat16)
-        slope_out[j] = cdf + pre * density
+        z[:, at] = (pre * cdf).astype(jnp.bfloat16)
+        slope[:, at] = cdf + pre * density
     result = dot(z[...], down[...])
     y_out[...] = result
     y_low[...] = result.astype(jnp.bfloat16)
-    z_own[...] = z[:, 0:wide]
-    to_r[:, 0:wide] = z[:, wide : 2 * wide]
-    to_r[:, wide : 2 * wide] = z[:, 3 * wide :]
-    to_c[:, 0:wide] = z[:, 2 * wide : 3 * wide]
-
-
-def backward_kernel(
-    y_own, y_got, normed1, g_own, g_x, slope, vecs, u_own, u_x, u_m, u_mx, d_own, d_m,
-    hid_out, to_r, to_c, du_own, s_out, p_low, sums, up_sums,
-    up, down, grad, hid, sems, more,
+
+
+def norm_back_kernel(
+    y_own, y_got, normed1, g_own, g_x, vecs, low_out, hid_out, dy_out, sums, grad, hid, sems,
 ):
     q, r, x, c = spot()
     rows = grad.shape[0] // 2
-    first = Copies(more)
-    first.start(g_own, grad.at[pl.ds(pl.multiple_of(rows * x, rows), rows)])
-    first.start(g_x, grad.at[pl.ds(pl.multiple_of(rows * (1 - x), rows), rows)])
     copies = Copies(sems)
-    load_feedforward(copies, up, down, u_own, u_x, u_m, u_mx, d_own, d_m)
-    first.wait()
+    copies.start(g_own, grad.at[pl.ds(pl.multiple_of(rows * x, rows), rows)])
+    copies.start(g_x, grad.at[pl.ds(pl.multiple_of(rows * (1 - x), rows), rows)])
     h1 = normed1[...] * vecs[3:4, :] + vecs[4:5, :]
     normed, rstd = norm_of(h1 + (y_own[...] + y_got[...].astype(jnp.float32) + vecs[5:6, :]))
     hid[...] = (normed * vecs[6:7, :] + vecs[7:8, :]).astype(jnp.bfloat16)
     hid_out[...] = hid[pl.ds(pl.multiple_of(rows * x, rows), rows), :]
+    copies.wait()
     cot = grad[...].astype(jnp.float32)
     dy = norm_pull(cot * vecs[6:7, :], normed, rstd)
     low = dy.astype(jnp.bfloat16)
-    wide = up.shape[1] // 4
-    to_r[:, 2 * wide :] = low
-    to_c[:, wide:] = low
+    dy_out[...] = dy
+    low_out[...] = low
     sums[...] = jnp.zeros_like(sums)
     sums[0:1, :] = jnp.sum(low.astype(jnp.float32), axis=0, keepdims=True)
     sums[1:2, :] = jnp.sum(cot * normed, axis=0, keepdims=True)
     sums[2:3, :] = jnp.sum(cot, axis=0, keepdims=True)
+
+
+def backward_kernel(
+    dy, dy_low, slope, u_own, u_x, u_m, u_mx, d_own, d_m,
+    p_low, s_out, du_out, up_sums, up, down, sems,
+):
+    copies = Copies(sems)
+    load_feedforward(copies, up, down, u_own, u_x, u_m, u_mx, d_own, d_m)
     copies.wait()
-    result = jnp.zeros(dy.shape, jnp.float32)
-    places = (du_own.at[...], to_r.at[:, 0:wide], to_c.at[:, 0:wide], to_r.at[:, wide : 2 * wide])
+    low = dy_low[...]
+    wide = up.shape[1] // 4
     for j in range(4):
-        du = (dot_nt(low, down[wide * j : wide * (j + 1), :]) * slope[j]).astype(jnp.bfloat16)
-        places[j][...] = du
+        at = slice(wide * j, wide * (j + 1))
+        du = (dot_nt(low, down[at, :]) * slope[:, at]).astype(jnp.bfloat16)
+        du_out[:, at] = du
         total = jnp.sum(du.astype(jnp.float32), axis=0, keepdims=True)
         up_sums[j] = jnp.broadcast_to(total, up_sums.shape[1:])
-        result += dot_nt(du, up[:, wide * j : wide * (j + 1)])
-    s_out[...] = dy + result
+    result = dot_nt(du_out[...], up[...])
+    s_out[...] = dy[...] + result
     p_low[...] = result.astype(jnp.bfloat16)
 
 
 def attend_back_kernel(
     s_own, p_got, normed1, rstd1, vecs, wo, mixed, q3, k3, v3, kt, lse, ids,
-    dr_out, da_out, dq_out, dkv_out, sums, qv_sums,
+    dkv_out, dq_out, dr_out, da_out, sums, qv_sums,
     mask, do3, delta, dk, dv, dqt, whole,
 ):
     q, r, x, c = spot()
@@ -843,45 +872,52 @@
     own = pl.ds(pl.multiple_of(rows * (4 * r + 2 * c), rows), 2 * rows)
     whole[own, :] += dot_nt(dq[...], w[:, 0:half])
     for b in range(2):
-        mine = pl.ds(pl.multiple_of(rows * (4 * b + 2 * c), rows), 2 * rows)
-        keep[b] = whole[mine, :]
-        theirs = pl.ds(pl.multiple_of(rows * (4 * b + 2 * (1 - c)), rows), 2 * rows)
-        send[b] = whole[theirs, :].astype(jnp.bfloat16)
-
-
-def down_grad_kernel(z0, r0, c0, f0, dc, dr_, df, c_own, send, keep, whole):
+        for i in range(2):
+            mine = pl.ds(pl.multiple_of(rows * (4 * i + 2 * c + b), rows), rows)
+            keep[2 * rows * b + rows * i : 2 * rows * b + rows * (i + 1), :] = whole[mine, :]
+            theirs = pl.ds(pl.multiple_of(rows * (4 * i + 2 * (1 - c) + b), rows), rows)
+            send[2 * rows * b + rows * i : 2 * rows * b + rows * (i + 1), :] = whole[theirs, :].astype(jnp.bfloat16)
+
+
+def octants():
+    for at in range(8):
+        r, q0, q1 = at >> 2, at >> 1 & 1, at & 1
+        yield at, 4 * r + 2 * q1 + q0
+
+
+def down_grad_kernel(z, dy, send, keep):
     q, r, x, c = spot()
-    wide = z0.shape[1]
-    total = dot_tn(z0[...], c_own[:, wide:])
-    total += dot_tn(r0[:, 0:wide], dr_[:, 2 * wide :])
-    total += dot_tn(c0[:, 0:wide], dc[:, wide:])
-    total += dot_tn(f0[:, wide : 2 * wide], df[:, 2 * wide :])
-    whole[...] = total
-    count = wide // 4
-    for b in range(2):
-        theirs = pl.ds(pl.multiple_of(2 * count * b + count * (1 - q % 2), 32), count)
-        mine = pl.ds(pl.multiple_of(2 * count * b + count * (q % 2), 32), count)
-        send[b] = whole[theirs, :].astype(jnp.bfloat16)
-        keep[b] = whole[mine, :]
-
-
-def up_grad_kernel(h0, hr, hc, hf, d0, dr_, dc, df, send, keep, whole):
+    half = z.shape[1] // 2
+    rows = half // 8
+    for side, out in ((1 - c, send), (c, keep)):
+        part = dot_tn(z[:, pl.ds(pl.multiple_of(half * side, 128), half)], dy[...])
+        for at, within in octants():
+            block = part[rows * within : rows * (within + 1), :]
+            out[rows * at : rows * (at + 1), :] = block.astype(out.dtype)
+
+
+def up_grad_kernel(h, du, send, keep, whole):
     q, r, x, c = spot()
-    wide = d0.shape[1]
-    total = dot_tn(h0[:, wide:], d0[...])
-    total += dot_tn(hr[:, 2 * wide :], dr_[:, 0:wide])
-    total += dot_tn(hc[:, wide:], dc[:, 0:wide])
-    total += dot_tn(hf[:, 2 * wide :], df[:, wide : 2 * wide])
-    whole[...] = total
-    count = whole.shape[0] // 16
-    for b in range(2):
-        for s in range(4):
-            at = 4 * count * s + 2 * count * b
-            rows = slice(count * s, count * (s + 1))
-            theirs = pl.ds(pl.multiple_of(at + count * (1 - q % 2), 16), count)
-            mine = pl.ds(pl.multiple_of(at + count * (q % 2), 16), count)
-            send[b, rows, :] = whole[theirs, :].astype(jnp.bfloat16)
-            keep[b, rows, :] = whole[mine, :]
+    width = h.shape[1]
+    thin = width // 32
+    whole[...] = dot_tn(h[...], du[...])
+    for side, out in ((1 - c, send), (c, keep)):
+        for at, within in octants():
+            pieces = []
+            for xx in range(2):
+                first = 8 * thin * (2 * xx + side) + thin * within
+                rows = pl.ds(pl.multiple_of(first, 8), thin)
+                pieces += [whole[rows, 0:width], whole[rows, width:]]
+            block = jnp.concatenate(pieces)
+            out[4 * thin * at : 4 * thin * (at + 1), :] = block.astype(out.dtype)
+
+
+def join_kernel(*refs):
+    out, at = refs[-1], 0
+    for ref in refs[:-1]:
+        count = ref.shape[0]
+        out[at : at + count, :] = ref[...]
+        at += count
 
 
 def fold_kernel(bit, keep, got, send, kept):
@@ -890,16 +926,22 @@
     kept[...] = keep[at] + got[at].astype(jnp.float32)
 
 
+def copy_kernel(block, out):
+    out[...] = block[...]
+
+
 def sum_kernel(keep, got, out):
     out[...] = (keep[...] + got[...].astype(jnp.float32)).astype(out.dtype)
 
 
-def share_kernel(keep, got, *out):
+def total_kernel(keep, got, more, out):
+    out[...] = (keep[...] + got[...].astype(jnp.float32) + more[...]).astype(out.dtype)
+
+
+def share_kernel(keep, got, side, base):
     q, r, x, c = spot()
-    count = keep.shape[0] // 4
-    for k in range(4):
-        rows = pl.ds(pl.multiple_of(count * ((2 * x + c) ^ k), 16), count)
-        out[k][...] = (keep[rows, :] + got[rows, :].astype(jnp.float32)).astype(jnp.bfloat16)
+    side[...] = (keep[1 - x] + got[1 - x].astype(jnp.float32)).astype(side.dtype)
+    base[...] = (keep[x] + got[x].astype(jnp.float32)).astype(base.dtype)
 
 
 def weight_grad_kernel(
@@ -934,7 +976,7 @@
         packed[cc, for_c : for_c + 16, :] = jnp.zeros((16, half), jnp.float32)
         packed[cc, for_c : for_c + 2, :] = qv_sums[0:2, :]
         for j in range(4):
-            packed[cc, pl.ds(for_c + 2 + ((2 * c + r) ^ j), 1), :] = up_sums[j, 0:1, :]
+            packed[cc, for_c + 2 + j : for_c + 3 + j, :] = up_sums[j, 0:1, :]
         packed[cc, for_c + 6 : for_c + 9, :] = sums1[0:3, columns]
         packed[cc, for_c + 9 : for_c + 12, :] = sums2[0:3, columns]
     send[...] = packed[1 - c].astype(jnp.bfloat16)
@@ -955,16 +997,23 @@
     kept[count:, :] = whole[2 * count :, :]
 
 
-def last_step_kernel(keep, got, side, base, lines, whole):
+def last_step_kernel(keep, got, side, base, *refs):
+    out, b_up, whole = refs[:8], refs[8], refs[9]
     q, r, x, c = spot()
     count = side.shape[0]
+    part = out[0].shape[0]
     whole[...] = keep[...] + got[...].astype(jnp.float32)
     theirs = pl.ds(pl.multiple_of(count * (1 - x), 8), count)
     mine = pl.ds(pl.multiple_of(count * x, 8), count)
     side[...] = whole[theirs, :].astype(jnp.bfloat16)
-    rest = slice(2 * count, whole.shape[0] - 16)
-    base[...] = jnp.concatenate([whole[mine, :], whole[rest, :]]).astype(jnp.bfloat16)
-    lines[...] = whole[whole.shape[0] - 16 :, :]
+    first = whole.shape[0] - 16
+    base[...] = jnp.concatenate([whole[mine, :], whole[2 * count : first, :]]).astype(jnp.bfloat16)
+    for i, one in enumerate(out):
+        at = first + (i if i < 2 else i + 4)
+        line = whole[at : at + 1, :]
+        one[...] = jnp.where(c == 0, line[:, :part], line[:, part:]).reshape(part)
+    line = jnp.concatenate([whole[pl.ds(first + 2 + 2 * c + i, 1), :] for i in range(2)], axis=1)
+    b_up[...] = line.reshape(b_up.shape[0])
 
 
 def down_out_kernel(near, far, out):
@@ -977,21 +1026,23 @@
             out[rows, :] = piece[count * k : count * (k + 1), :].astype(jnp.float32)
 
 
-def up_out_kernel(near, far, out):
+def up_out_kernel(near, far, out, whole):
     q, r, x, c = spot()
-    count, wide = near.shape[0] // 16, near.shape[1]
+    thin, width = near.shape[0] // 16, near.shape[1]
     for d, piece in enumerate((near, far)):
+        whole[...] = piece[...].astype(jnp.float32)
         for k in range(4):
-            at = 2 * ((q // 2) ^ (k & 1)) + ((q % 2) ^ (k >> 1))
-            rows = pl.ds(pl.multiple_of(count * at, 16), count)
+            at = 4 * (r ^ d) + 2 * ((q // 2) ^ (k & 1)) + ((q % 2) ^ (k >> 1))
+            rows = pl.ds(pl.multiple_of(thin * at, 8), thin)
             for s in range(4):
-                place = 2 * ((2 * x + c) ^ s) + (r ^ d)
-                columns = pl.ds(pl.multiple_of(wide * place, 128), wide)
-                first = count * (4 * k + s)
-                out[rows, columns] = piece[first : first + count, :].astype(jnp.float32)
-
-
-def rest_out_kernel(near, far, out_q, out_k, out_v, out_o, whole):
+                columns = pl.ds(pl.multiple_of(width * (2 * (x ^ (s >> 1)) + (s & 1)), 128), width)
+                first = thin * (4 * k + s)
+                out[rows, columns] = whole[first : first + thin, :]
+
+
+def rest_out_kernel(near, far, hidden, total, out_q, out_k, out_v, out_o, out_h, out_t, whole):
+    out_h[...] = hidden[...]
+    out_t[...] = total[...]
     q, r, x, c = spot()
     half = near.shape[1]
     thin = near.shape[0] // 32
@@ -1011,8 +1062,18 @@
                 out_o[rows, columns] = whole[first + thin * (3 + t) : first + thin * (4 + t), :]
 
 
-def kernel_call(body, name, ins, outs, scratch, args, after=(), flops=10**8):
+def kernel_call(body, name, ins, outs, scratch, args, after=(), room=2 << 20):
     count = len(args)
+
+    def size(shape, dtype):
+        return math.prod(shape) * jnp.dtype(dtype).itemsize
+
+    used = sum(size(m.shape, m.dtype) for m in scratch if m.memory_space == pltpu.VMEM)
+
+    args = [
+        pltpu.with_memory_space_constraint(a, pltpu.HBM) if spec is HBM else a
+        for a, spec in zip(args, ins)
+    ]
 
     def run(*refs):
         body(*refs[:count], *refs[count + len(after) :])
@@ -1024,7 +1085,8 @@
         in_specs=list(ins) + [ANY] * len(after),
         out_specs=[spec for _, _, spec in outs],
         scratch_shapes=scratch,
-        cost_estimate=pl.CostEstimate(flops=flops, bytes_accessed=4 << 20, transcendentals=0),
+        cost_estimate=pl.CostEstimate(flops=1, bytes_accessed=1, transcendentals=0),
+        compiler_params=pltpu.CompilerParams(vmem_limit_bytes=used + room),
     )(*args, *after)
 
 
@@ -1036,6 +1098,8 @@
         in_specs=[ANY] * (1 + len(after)),
         out_specs=ANY,
         input_output_aliases={0: 0},
+        cost_estimate=pl.CostEstimate(flops=1, bytes_accessed=1, transcendentals=0),
+        compiler_params=pltpu.CompilerParams(vmem_limit_bytes=1 << 18),
     )(value, *after)
 
 
@@ -1043,7 +1107,6 @@
     tokens, cotangent, seq_ids, w_query, b_query, w_key, w_value, b_value, w_out, b_out,
     attn_gain, attn_shift, w_up, b_up, w_down, b_down, ffn_gain, ffn_shift,
 ):
-    x = lax.axis_index("x")
     low, exact = jnp.bfloat16, jnp.float32
     rows, width = tokens.shape[1:]
     part = w_query.shape[0]
@@ -1054,51 +1117,65 @@
     own = 2 * rows
     pairs = half // 128
 
-    def call(body, name, ins, outs, scratch, args, after=(), flops=10**8):
-        return kernel_call(body, name, ins, outs, scratch, args, after, flops)
+    latest = []
+
+    def call(body, name, ins, outs, scratch, args, after=(), **more):
+        results = kernel_call(body, name, ins, outs, scratch, args, tuple(after) + tuple(latest), **more)
+        if len(results) > 1 or not name.endswith("_out"):
+            latest[:] = results[:1]
+        return results
 
     (block,) = call(
-        block_kernel, "block", [WHOLE] * 2, [((rows + 16, width), low, WHOLE)], [],
+        block_kernel, "block", [HBM] * 2, [((rows + 16, width), low, WHOLE)],
+        [pltpu.VMEM((1, rows), jnp.int32), pltpu.SemaphoreType.DMA((2,))],
         (tokens[0], seq_ids),
     )
-    blocks = [regroup(block)]
+    block = regroup(block)
     theirs, mine = call(
         pack_kernel,
         "pack",
-        [WHOLE] * 12,
+        [HBM] * 12,
         [((3 * part + 16, half), low, WHOLE)] * 2,
-        [pltpu.VMEM((16, half), exact)],
+        [pltpu.VMEM((16, half), exact)]
+        + [pltpu.VMEM((part,), low)] * 8
+        + [pltpu.VMEM((width,), low), pltpu.SemaphoreType.DMA((15,))],
         (w_query, w_key, w_value, b_query, b_value, b_out, attn_gain, attn_shift, b_down, ffn_gain, ffn_shift, b_up),
     )
     qkv_x = swap_x(theirs)
     qkv_m = swap_c(mine)
-    blocks.append(swap_x(blocks[0]))
+    out_m = swap_c(w_out)
+    blocks = [once(block, qkv_m, qkv_x, out_m)]
+    beside_r = swap_r(blocks[0])
+    blocks.append(once(swap_x(blocks[0]), beside_r))
     blocks.append(swap_c(blocks[0]))
     blocks.append(swap_c(blocks[1]))
-    blocks.append(swap_r(blocks[0]))
+    blocks.append(beside_r)
     blocks.append(swap_r(blocks[1]))
     blocks.append(swap_c(blocks[4]))
     blocks.append(swap_c(blocks[5]))
     qkv_mx = swap_c(qkv_x)
-    out_m = swap_c(w_out)
-
-    def cut(w, side, size):
-        return lax.dynamic_slice_in_dim(w, side * size, size, 1)
-
-    up_x = swap_x(once(cut(w_up, 1 - x, 4 * wide), blocks[1]))
-    up_m = swap_c(cut(w_up, x, 4 * wide))
+    up_theirs, up_mine = call(
+        cut_kernel, "cut", [HBM], [((part, 4 * wide), low, WHOLE)] * 2, [pltpu.SemaphoreType.DMA((2,))],
+        (w_up,), after=(blocks[3],),
+    )
+    up_x = swap_x(up_theirs)
+    up_m = swap_c(up_mine)
     up_mx = swap_c(up_x)
     down_m = swap_c(w_down)
-    cot = regroup(once(cotangent[0], blocks[5]))
-    cot_x = swap_x(cot)
+    (cot,) = call(
+        load_kernel, "cotangent", [HBM], [((rows, width), low, WHOLE)], [pltpu.SemaphoreType.DMA((1,))],
+        (cotangent[0],),
+    )
+    cot, cot_x = regroup(cot), regroup_x(cot)
 
     (
-        x_all, w_all, wo_all, k3, v3, q3, mixed, lse, ids, a_own, a_low, vecs, up_bias
+        a_low, x_all, w_all, wo_all, k3, v3, q3, mixed, lse, ids, a_own, vecs, up_bias
     ) = call(
         attend_kernel,
         "attend",
-        [ANY] * 17,
+        [ANY] * 8 + [HBM] * 3 + [ANY] * 4 + [HBM, ANY],
         [
+            ((own, width), low, WHOLE),
             ((keys, width), low, ANY),
             ((width, 3 * half), low, ANY),
             ((half, width), low, ANY),
@@ -1109,7 +1186,6 @@
             ((8, own), exact, WHOLE),
             ((8, rows), exact, WHOLE),
             ((own, width), exact, WHOLE),
-            ((own, width), low, WHOLE),
             ((8, width), exact, WHOLE),
             ((4, 8, wide), exact, WHOLE),
         ],
@@ -1129,83 +1205,122 @@
             pltpu.SemaphoreType.DMA((5,)),
         ],
         (*blocks, w_query, w_key, w_value, qkv_x, qkv_m, qkv_mx, mine, w_out, out_m),
-        flops=3 * 10**9,
+        room=8 << 20,
     )
     a_got = swap_x(a_low)
-    kt = jnp.swapaxes(k3, 1, 2).reshape(2 * pairs, 64, keys)
+    (kt,) = call(turn_kernel, "turn", [WHOLE], [((2 * pairs, 64, keys), low, WHOLE)], [], (k3,))
 
     inner_weights = (w_up, up_x, up_m, up_mx, w_down, down_m)
-    inner_scratch = [
-        pltpu.VMEM((width, 4 * wide), low),
-        pltpu.VMEM((4 * wide, width), low),
-    ]
-    f_r, f_c, z_own, normed1, rstd1, slope, y_own, y_low = call(
+    inner_specs = [HBM, ANY, ANY, ANY, HBM, ANY]
+    inner_scratch = [pltpu.VMEM((width, 4 * wide), low), pltpu.VMEM((4 * wide, width), low)]
+    y_low, h_low, z, normed1, rstd1, slope, y_own = call(
         forward_kernel,
         "feedforward",
-        [WHOLE, WHOLE, ANY, WHOLE, WHOLE] + [ANY] * 6,
+        [WHOLE, WHOLE, ANY, WHOLE, WHOLE] + inner_specs,
         [
-            ((own, 2 * wide + width), low, WHOLE),
-            ((own, wide + width), low, WHOLE),
-            ((own, wide), low, WHOLE),
+            ((own, width), low, WHOLE),
+            ((own, width), low, WHOLE),
+            ((own, 4 * wide), low, WHOLE),
             ((own, width), exact, WHOLE),
             ((own, 128), exact, WHOLE),
-            ((4, own, wide), exact, WHOLE),
+            ((own, 4 * wide), exact, WHOLE),
             ((own, width), exact, WHOLE),
-            ((own, width), low, WHOLE),
         ],
         inner_scratch
-        + [
+        + [pltpu.VMEM((own, width), low), pltpu.SemaphoreType.DMA((6,)), pltpu.SemaphoreType.DMA((1,))],
+        (a_own, a_got, x_all, vecs, up_bias, *inner_weights),
+        after=(cot, cot_x),
+        room=8 << 20,
+    )
+    y_got = swap_x(y_low)
+    dy_low, hidden, dy, sums2 = call(
+        norm_back_kernel,
+        "norm_back",
+        [WHOLE, WHOLE, WHOLE, ANY, ANY, WHOLE],
+        [
+            ((own, width), low, WHOLE),
+            ((rows, width), low, WHOLE),
+            ((own, width), exact, WHOLE),
+            ((8, width), exact, WHOLE),
+        ],
+        [
             pltpu.VMEM((own, width), low),
-            pltpu.VMEM((own, 4 * wide), low),
-            pltpu.SemaphoreType.DMA((20,)),
-            pltpu.SemaphoreType.DMA((1,)),
+            pltpu.VMEM((own, width), low),
+            pltpu.SemaphoreType.DMA((2,)),
         ],
-        (a_own, a_got, x_all, vecs, up_bias, *inner_weights),
-        flops=2 * 10**9,
-    )
-    y_got = swap_x(y_low)
-    f_from_r = swap_r(f_r)
-    f_from_c = swap_c(f_c)
-    f_from_rc = swap_c(f_from_r)
-
-    hidden, b_r, b_c, du_own, s_own, p_low, sums2, up_sums = call(
+        (y_own, y_got, normed1, cot, cot_x, vecs),
+        room=6 << 20,
+    )
+    eighth = wide // 4
+    down_send, down_keep = call(
+        down_grad_kernel,
+        "down_grad",
+        [WHOLE] * 2,
+        [((8 * eighth, width), low, WHOLE), ((8 * eighth, width), exact, WHOLE)],
+        [],
+        (z, dy_low),
+        room=8 << 20,
+    )
+    down_got = swap_c(down_send)
+    p_low, s_own, du, up_sums = call(
         backward_kernel,
         "feedforward_back",
-        [WHOLE, WHOLE, WHOLE, ANY, ANY, WHOLE, WHOLE] + [ANY] * 6,
+        [WHOLE] * 3 + inner_specs,
         [
-            ((rows, width), low, WHOLE),
-            ((own, 2 * wide + width), low, WHOLE),
-            ((own, wide + width), low, WHOLE),
-            ((own, wide), low, WHOLE),
+            ((own, width), low, WHOLE),
             ((own, width), exact, WHOLE),
-            ((own, width), low, WHOLE),
-            ((8, width), exact, WHOLE),
+            ((own, 4 * wide), low, WHOLE),
             ((4, 8, wide), exact, WHOLE),
         ],
-        inner_scratch
-        + [
-            pltpu.VMEM((own, width), low),
-            pltpu.VMEM((own, width), low),
-            pltpu.SemaphoreType.DMA((20,)),
-            pltpu.SemaphoreType.DMA((2,)),
-        ],
-        (y_own, y_got, normed1, cot, cot_x, slope, vecs, *inner_weights),
-        flops=2 * 10**9,
+        inner_scratch + [pltpu.SemaphoreType.DMA((6,))],
+        (dy, dy_low, slope, *inner_weights),
+        room=8 << 20,
     )
     p_got = swap_x(p_low)
-    b_from_r = swap_r(b_r)
-    b_from_c = swap_c(b_c)
-    b_from_rc = swap_c(b_from_r)
-
-    dr, da, dq, dkv, sums1, qv_sums = call(
+
+    def fold(name, bit, keep, got):
+        shape = (keep.shape[0] // 2, keep.shape[1])
+        return call(
+            lambda *refs: fold_kernel(bit, *refs),
+            name,
+            [WHOLE] * 2,
+            [(shape, low, WHOLE), (shape, exact, WHOLE)],
+            [],
+            (keep.reshape(2, *shape), got.reshape(2, *shape)),
+            room=4 << 20,
+        )
+
+    def bit_r(q, r, x, c):
+        return r
+
+    def bit_near(q, r, x, c):
+        return q % 2
+
+    def bit_far(q, r, x, c):
+        return q // 2
+
+    down_send, down_keep = fold("down_r", bit_r, down_keep, down_got)
+    down_got = swap_r(down_send)
+    up_send, up_keep = call(
+        up_grad_kernel,
+        "up_grad",
+        [WHOLE] * 2,
+        [((8 * eighth, width), low, WHOLE), ((8 * eighth, width), exact, WHOLE)],
+        [pltpu.VMEM((width, 4 * wide), exact)],
+        (h_low, du),
+        room=8 << 20,
+    )
+    up_got = swap_c(up_send)
+
+    dkv, dq, dr, da, sums1, qv_sums = call(
         attend_back_kernel,
         "attend_back",
         [WHOLE] * 13,
         [
+            ((keys, 2 * half), low, WHOLE),
+            ((own, half), low, WHOLE),
             ((rows, width), exact, WHOLE),
             ((own, width), low, WHOLE),
-            ((own, half), low, WHOLE),
-            ((keys, 2 * half), low, WHOLE),
             ((8, width), exact, WHOLE),
             ((8, half), exact, WHOLE),
         ],
@@ -1219,70 +1334,11 @@
             pltpu.VMEM((own, width), exact),
         ],
         (s_own, p_got, normed1, rstd1, vecs, wo_all, mixed, q3, k3, v3, kt, lse, ids),
-        after=(f_from_rc, f_from_c),
-        flops=3 * 10**9,
+        room=8 << 20,
     )
 
     thin = part // 8
     count = 64 * thin
-    send, keep = call(
-        weight_grad_kernel,
-        "weight_grad",
-        [WHOLE] * 9,
-        [((count + 16, half), low, WHOLE), ((count + 16, half), exact, ANY)],
-        [pltpu.VMEM((2, count + 16, half), exact), pltpu.SemaphoreType.DMA((1,))],
-        (x_all, dkv, dq, mixed, da, sums1, sums2, qv_sums, up_sums),
-        flops=2 * 10**9,
-    )
-    rest_got = swap_c(send)
-    rest_keep = keep
-
-    quarter = wide // 4
-    down_send, down_keep = call(
-        down_grad_kernel,
-        "down_grad",
-        [WHOLE] * 8,
-        [((2, quarter, width), low, WHOLE), ((2, quarter, width), exact, WHOLE)],
-        [pltpu.VMEM((wide, width), exact)],
-        (z_own, f_from_r, f_from_c, f_from_rc, b_from_c, b_from_r, b_from_rc, b_c),
-        after=(send,),
-        flops=10**9,
-    )
-    down_got = swap_near(down_send)
-    up_send, up_keep = call(
-        up_grad_kernel,
-        "up_grad",
-        [WHOLE] * 8,
-        [((2, part, wide), low, WHOLE), ((2, part, wide), exact, WHOLE)],
-        [pltpu.VMEM((width, wide), exact)],
-        (f_c, f_from_r, f_from_c, f_from_rc, du_own, b_from_r, b_from_c, b_from_rc),
-        after=(down_send,),
-        flops=10**9,
-    )
-    up_got = swap_near(up_send)
-
-    x_send, x_keep = call(
-        input_grad_kernel,
-        "input_grad",
-        [WHOLE] * 3,
-        [((2, own, width), low, WHOLE), ((2, own, width), exact, WHOLE)],
-        [pltpu.VMEM((keys, width), exact)],
-        (dq, dkv, w_all),
-        after=(up_send,),
-        flops=10**9,
-    )
-    x_got = swap_c(x_send)
-
-    def fold(name, bit, keep, got):
-        shape = keep.shape[1:]
-        return call(
-            lambda *refs: fold_kernel(bit, *refs),
-            name,
-            [WHOLE] * 2,
-            [(shape, low, WHOLE), (shape, exact, WHOLE)],
-            [],
-            (keep, got),
-        )
 
     def step(name, bit, keep, got, size):
         return call(
@@ -1294,86 +1350,132 @@
             (keep, got),
         )
 
-    def spread(block):
-        block = beside(block, swap_far(block))
-        block = beside(block, swap_near(block))
-        return block, swap_r(block)
-
-    rest_send, rest_keep = step("rest_r", lambda q, r, x, c: r, rest_keep, rest_got, count // 2)
+    def join(name, *pieces):
+        shape = (sum(p.shape[0] for p in pieces), pieces[0].shape[1])
+        (out,) = call(join_kernel, name, [WHOLE] * len(pieces), [(shape, low, WHOLE)], [], pieces)
+        return out
+
+    up_send, up_keep = fold("up_r", bit_r, up_keep, up_got)
+    up_got = swap_r(up_send)
+    rest_send, rest_keep = call(
+        weight_grad_kernel,
+        "weight_grad",
+        [WHOLE] * 9,
+        [((count + 16, half), low, WHOLE), ((count + 16, half), exact, ANY)],
+        [pltpu.VMEM((2, count + 16, half), exact), pltpu.SemaphoreType.DMA((1,))],
+        (x_all, dkv, dq, mixed, da, sums1, sums2, qv_sums, up_sums),
+        room=8 << 20,
+    )
+    rest_got = swap_c(rest_send)
+    down_send, down_keep = fold("down_near", bit_near, down_keep, down_got)
+    down_got = swap_near(down_send)
+    x_send, x_keep = call(
+        input_grad_kernel,
+        "input_grad",
+        [WHOLE] * 3,
+        [((2 * own, width), low, WHOLE), ((2 * own, width), exact, WHOLE)],
+        [pltpu.VMEM((keys, width), exact)],
+        (dq, dkv, w_all),
+        room=8 << 20,
+    )
+    x_got = swap_c(x_send)
+    rest_send, rest_keep = step("rest_r", bit_r, rest_keep, rest_got, count // 2)
     rest_got = swap_r(rest_send)
-    down_send, down_keep = fold("down_far", lambda q, r, x, c: q // 2, down_keep, down_got)
+    x_send, x_keep = fold("input_x", lambda q, r, x, c: x, x_keep, x_got)
+    x_got = swap_x(x_send)
+    down_send, down_keep = fold("down_far", bit_far, down_keep, down_got)
     down_got = swap_far(down_send)
-    up_send, up_keep = fold("up_far", lambda q, r, x, c: q // 2, up_keep, up_got)
+    up_send, up_keep = fold("up_near", bit_near, up_keep, up_got)
+    up_got = swap_near(up_send)
+    x_send, x_keep = fold("input_r", bit_r, x_keep, x_got)
+    x_got = swap_r(x_send)
+    (down_sum,) = call(
+        sum_kernel, "down_sum", [WHOLE] * 2, [((eighth, width), low, WHOLE)], [], (down_keep, down_got)
+    )
+    down_other = swap_far(down_sum)
+    up_send, up_keep = fold("up_far", bit_far, up_keep, up_got)
     up_got = swap_far(up_send)
-    rest_send, rest_keep = step("rest_near", lambda q, r, x, c: q % 2, rest_keep, rest_got, count // 4)
+    rest_send, rest_keep = step("rest_near", bit_near, rest_keep, rest_got, count // 4)
     rest_got = swap_near(rest_send)
-    (down_sum,) = call(
-        sum_kernel, "down_sum", [WHOLE] * 2, [((quarter, width), low, WHOLE)], [], (down_keep, down_got)
-    )
-    down_near, down_far = spread(down_sum)
-    shares = call(
-        share_kernel, "up_share", [WHOLE] * 2, [((part // 4, wide), low, WHOLE)] * 4, [], (up_keep, up_got)
-    )
-    up_sum = jnp.concatenate([shares[0], swap_c(shares[1]), swap_x(shares[2]), swap_xc(shares[3])])
-    up_near, up_far = spread(up_sum)
-    rest_send, rest_keep = step("rest_far", lambda q, r, x, c: q // 2, rest_keep, rest_got, count // 8)
+    (total,) = call(
+        total_kernel, "input_sum", [WHOLE] * 3, [((rows, width), low, WHOLE)], [], (x_keep, x_got, dr)
+    )
+    total = regroup(total)
+    down_sum = join("down_join", down_sum, down_other)
+    down_other = swap_near(down_sum)
+    side, base = call(
+        share_kernel,
+        "up_share",
+        [WHOLE] * 2,
+        [((eighth // 2, width), low, WHOLE)] * 2,
+        [],
+        (up_keep.reshape(2, eighth // 2, width), up_got.reshape(2, eighth // 2, width)),
+    )
+    side = swap_x(side)
+    rest_send, rest_keep = step("rest_far", bit_far, rest_keep, rest_got, count // 8)
     rest_got = swap_far(rest_send)
-    side, base, lines = call(
+    up_sum = join("up_join", base, side)
+    up_other = swap_far(up_sum)
+    down_near = join("down_join_near", down_sum, down_other)
+    down_far = swap_r(down_near)
+    side, base, *lines, b_up_grad = call(
         last_step_kernel,
         "rest_last",
         [WHOLE] * 2,
-        [((3 * thin, half), low, WHOLE), ((5 * thin, half), low, WHOLE), ((16, half), exact, WHOLE)],
+        [((3 * thin, half), low, WHOLE), ((5 * thin, half), low, WHOLE)]
+        + [((part,), exact, WHOLE)] * 8
+        + [((2 * wide,), exact, WHOLE)],
         [pltpu.VMEM((8 * thin + 16, half), exact)],
         (rest_keep, rest_got),
     )
-    rest_near, rest_far = spread(beside(base, swap_x(side)))
-
-    x_send, x_keep = fold("input_r", lambda q, r, x, c: r, x_keep, x_got)
-    x_got = swap_r(x_send)
-    x_send, x_keep = fold(
-        "input_x", lambda q, r, x, c: x, x_keep.reshape(2, rows, width), x_got.reshape(2, rows, width)
-    )
-    total = x_keep + swap_x(x_send).astype(exact)
-    tokens_grad = regroup((total + dr).astype(low))[None]
-    hidden_out = regroup(hidden)[None]
-
+    side = swap_x(side)
+    hidden = regroup(hidden)
+    up_sum = join("up_join_far", up_sum, up_other)
+    up_other = swap_near(up_sum)
+    rest_sum = join("rest_join", base, side)
+    rest_other = swap_far(rest_sum)
+    up_near = join("up_join_near", up_sum, up_other)
+    up_far = swap_r(up_near)
+    rest_sum = join("rest_join_far", rest_sum, rest_other)
+    rest_other = swap_near(rest_sum)
+    rest_near = join("rest_join_near", rest_sum, rest_other)
+    rest_far = swap_r(rest_near)
     (w_down_grad,) = call(
-        down_out_kernel, "down_out", [WHOLE] * 2, [((2 * wide, width), exact, WHOLE)], [], (down_near, down_far)
+        down_out_kernel, "down_out", [WHOLE] * 2, [((2 * wide, width), exact, WHOLE)], [], (down_near, down_far),
+        room=6 << 20,
     )
     (w_up_grad,) = call(
-        up_out_kernel, "up_out", [WHOLE] * 2, [((part, inner), exact, WHOLE)], [], (up_near, up_far)
-    )
-    w_query_grad, w_key_grad, w_value_grad, w_out_grad = call(
+        up_out_kernel, "up_out", [WHOLE] * 2, [((part, inner), exact, WHOLE)],
+        [pltpu.VMEM((4 * eighth, width), exact)], (up_near, up_far),
+        room=6 << 20,
+    )
+    w_query_grad, w_key_grad, w_value_grad, w_out_grad, hidden_out, tokens_grad = call(
         rest_out_kernel,
         "rest_out",
-        [WHOLE] * 2,
-        [((part, width), exact, WHOLE)] * 4,
+        [WHOLE] * 4,
+        [((part, width), exact, WHOLE)] * 4 + [((rows, width), low, WHOLE)] * 2,
         [pltpu.VMEM((32 * thin, half), exact)],
-        (rest_near, rest_far),
-    )
-
-    c = lax.axis_index("c")
-    pieces = jnp.where(c == 0, lines[:, :part], lines[:, part:])
-    ups = jnp.where(c == 0, lines[2:4], lines[4:6])
-    b_up_grad = ups.reshape(2 * wide)
+        (rest_near, rest_far, hidden, total),
+        room=6 << 20,
+    )
     return (
-        hidden_out,
-        tokens_grad,
+        hidden_out[None],
+        tokens_grad[None],
         w_query_grad,
-        pieces[0],
+        lines[0],
         w_key_grad,
         w_value_grad,
-        pieces[1],
+        lines[1],
         w_out_grad,
-        pieces[6],
-        pieces[7],
-        pieces[8],
+        lines[2],
+        lines[3],
+        lines[4],
         w_up_grad,
         b_up_grad,
         w_down_grad,
-        pieces[9],
-        pieces[10],
-        pieces[11],
+        lines[5],
+        lines[6],
+        lines[7],
     )
 
 

time: 289 us -> 234 us (0.81)
  Pallas kernels: 92.9 us -> 46.3 us
  waiting for transfers between devices: 91.5 us -> 131 us
  local copies, waits for them, and re-layouts: 25.2 us -> 0.01 us
  starting transfers between devices: 74.7 us -> 54.7 us
    pallas_call x23 -> x40, Pallas kernels: 92.9 us -> 46.3 us  [kernel_call(): pl.pallas_call(run, name=name, out_shape=[jax.ShapeDtypeStruct(shape, dty...]
    ppermute x53 -> x49, waiting for transfers between devices: 91.5 us -> 131 us  [moved(): lax.ppermute(block, AXES, [(number(s), number(move(*s))) for s in spots])]
    ppermute x53 -> x49, starting transfers between devices: 74.7 us -> 54.7 us  [moved(): lax.ppermute(block, AXES, [(number(s), number(move(*s))) for s in spots])]
    unnamed x96 -> x4, local copies, waits for them, and re-layouts: 20 us -> 0.01 us
  transfers between devices with their start and end apart: 53 -> 49, of which waited for: 18 -> 28; matrix products, arithmetic and copies ran while one was open for 4% -> 0% of each run, Pallas kernels for 28% -> 15%
where the time goes in v3:
time: 234 us; the launch traced here: 233 us
  waiting for transfers between devices  131 us (56%)
  starting transfers between devices  54.7 us (23%)
  Pallas kernels  46.3 us (20%)
    ppermute x49, waiting for transfers between devices, moved(): lax.ppermute(block, AXES, [(number(s), number(move(*s))) for s in spots])  131 us
    ppermute x49, starting transfers between devices, moved(): lax.ppermute(block, AXES, [(number(s), number(move(*s))) for s in spots])  54.7 us
    pallas_call x40, Pallas kernels, kernel_call(): pl.pallas_call(run, name=name, out_shape=[jax.ShapeDtypeStruct(shape, dty...  46.3 us
  transfers between devices with their start and end apart: 49, of which 28 were waited for; matrix products, arithmetic and copies ran while one was open for 0% of the time, Pallas kernels for 15%

profile of v3, /device:TPU:0, one launch (start us, length us, event | category | flops | bytes accessed | tf_op | source)
XLA Modules:
  0.0 233.4 jit_solution(18325873336402470762)
XLA Ops:
  0.7 1.0 block.1.refs_12_
  1.7 1.5 pack.1
  3.7 2.6 %collective-permute-start.2 = (bf16[592,384]{1,0:T(8,128)(2,1)S(1)}, bf16[592,384]{1,0:T(8,128)(2,1)S(1)}, u32[]{:S(2)}, u32[]{:S(2)}) collective-permute-start(bf16[592,384]{1,0:T(8,128)(2,1)S(1)} %get-tuple-element.105.refs_2_), channel_id=1, source_target_pairs={{0,2},{1,3},{2,0},{3,1},{4,6},{5,7},{6,4},{7,5},{8,10},{9,11},{10,... | collective-permute-start | bytes 1363976 | tf_op jit(solution)/shard_map/ppermute | solution.py:480
  7.1 0.7 collective-permute-done.3.refs_3_.refs_16_
  7.9 13.5 %collective-permute-done.2.refs_2_.refs_11_ = bf16[592,384]{1,0:T(8,128)(2,1)S(1)} collective-permute-done((bf16[592,384]{1,0:T(8,128)(2,1)S(1)}, bf16[592,384]{1,0:T(8,128)(2,1)S(1)}, u32[]{:S(2)}, u32[]{:S(2)}) %collective-permute-start.2) | collective-permute-done | bytes 454688 | tf_op jit(solution)/shard_map/ppermute | solution.py:480
  21.3 1.5 collective-permute-start.5
  22.8 2.5 %collective-permute-start.4 = (bf16[144,768]{1,0:T(8,128)(2,1)S(1)}, bf16[144,768]{1,0:T(8,128)(2,1)S(1)}, u32[]{:S(2)}, u32[]{:S(2)}) collective-permute-start(bf16[144,768]{1,0:T(8,128)(2,1)S(1)} %once.2.refs_0_), channel_id=1, source_target_pairs={{0,2},{1,3},{2,0},{3,1},{4,6},{5,7},{6,4},{7,5},{8,10},{9,11},{10,... | collective-permute-start | bytes 663560 | tf_op jit(solution)/shard_map/ppermute | solution.py:480
  25.3 3.0 %collective-permute-done.5.refs_1_.refs_4_ = bf16[144,768]{1,0:T(8,128)(2,1)S(1)} collective-permute-done((bf16[144,768]{1,0:T(8,128)(2,1)S(1)}, bf16[144,768]{1,0:T(8,128)(2,1)S(1)}, u32[]{:S(2)}, u32[]{:S(2)}) %collective-permute-start.5) | collective-permute-done | bytes 221216 | tf_op jit(solution)/shard_map/ppermute | solution.py:480
  28.3 2.0 collective-permute-done.4.refs_0_
  30.8 1.0 collective-permute-done.7.refs_1_.refs_3_
  31.8 1.3 cut.1
  33.0 1.8 collective-permute-start.13
  36.5 6.2 %collective-permute-done.8.refs_5_ = bf16[144,768]{1,0:T(8,128)(2,1)S(1)} collective-permute-done((bf16[144,768]{1,0:T(8,128)(2,1)S(1)}, bf16[144,768]{1,0:T(8,128)(2,1)S(1)}, u32[]{:S(2)}, u32[]{:S(2)}) %collective-permute-start.8) | collective-permute-done | bytes 221216 | tf_op jit(solution)/shard_map/ppermute | solution.py:480
  43.2 5.3 %collective-permute-done.13.refs_6_.refs_4_ = bf16[192,1536]{1,0:T(8,128)(2,1)S(1)} collective-permute-done((bf16[192,1536]{1,0:T(8,128)(2,1)S(1)}, bf16[192,1536]{1,0:T(8,128)(2,1)S(1)}, u32[]{:S(2)}, u32[]{:S(2)}) %collective-permute-start.13) | collective-permute-done | bytes 589856 | tf_op jit(solution)/shard_map/ppermute | solution.py:480
  48.5 0.9 cotangent.1.refs_17_
  49.4 1.8 collective-permute-start.18
  51.2 11.6 %attend.1 = (bf16[256,768]{1,0:T(8,128)(2,1)S(1)}, bf16[1024,768]{1,0:T(8,128)(2,1)S(1)}, bf16[768,1152]{1,0:T(8,128)(2,1)S(1)}, bf16[384,768]{1,0:T(8,128)(2,1)...) custom-call(bf16[144,768]{1,0:T(8,128)(2,1)S(1)} %once.2.refs_0_, ...), custom_call_target="tpu_custom_call" | custom-call | flops 1 | bytes 1 | tf_op jit(solution)/shard_map/attend/pallas_call | solution.py:1081
  63.3 0.8 collective-permute-start.17
  64.4 11.2 %collective-permute-done.12.refs_1_ = bf16[256,768]{1,0:T(8,128)(2,1)S(1)} collective-permute-done((bf16[256,768]{1,0:T(8,128)(2,1)S(1)}, bf16[256,768]{1,0:T(8,128)(2,1)S(1)}, u32[]{:S(2)}, u32[]{:S(2)}) %collective-permute-start.12) | collective-permute-done | bytes 393248 | tf_op jit(solution)/shard_map/ppermute | solution.py:480
  75.6 3.7 %feedforward.1 = (bf16[256,768]{1,0:T(8,128)(2,1)S(1)}, bf16[256,768]{1,0:T(8,128)(2,1)S(1)}, bf16[256,1536]{1,0:T(8,128)(2,1)S(1)}, f32[256,768]{1,0:T(8,128)S(...) custom-call(f32[256,768]{1,0:T(8,128)S(1)} %get-tuple-element.108.refs_0_, ...), custom_call_target="tpu_custom_call" | custom-call | flops 1 | bytes 1 | tf_op jit(solution)/shard_map/feedforward/pallas_call | solution.py:1081
  79.3 2.7 %collective-permute-start.19 = (bf16[256,768]{1,0:T(8,128)(2,1)S(1)}, bf16[256,768]{1,0:T(8,128)(2,1)S(1)}, u32[]{:S(2)}, u32[]{:S(2)}) collective-permute-start(bf16[256,768]{1,0:T(8,128)(2,1)S(1)} %get-tuple-element.115.refs_6_), channel_id=1, source_target_pairs={{0,2},{1,3},{2,0},{3,1},{4,6},{5,7},{6,4},{7,5},{8,10},{9,11},{10,... | collective-permute-start | bytes 1179656 | tf_op jit(solution)/shard_map/ppermute | solution.py:480
  82.0 9.6 %collective-permute-done.19.refs_1_ = bf16[256,768]{1,0:T(8,128)(2,1)S(1)} collective-permute-done((bf16[256,768]{1,0:T(8,128)(2,1)S(1)}, bf16[256,768]{1,0:T(8,128)(2,1)S(1)}, u32[]{:S(2)}, u32[]{:S(2)}) %collective-permute-start.19) | collective-permute-done | bytes 393248 | tf_op jit(solution)/shard_map/ppermute | solution.py:480
  91.6 1.4 norm_back.1
  93.0 0.8 down_grad.1
  94.1 3.4 %feedforward_back.1 = (bf16[256,768]{1,0:T(8,128)(2,1)S(1)}, f32[256,768]{1,0:T(8,128)S(1)}, bf16[256,1536]{1,0:T(8,128)(2,1)S(1)}, f32[4,8,384]{2,1,0:T(8,128)S(1)}) custom-call(f32[256,768]{1,0:T(8,128)S(1)} %get-tuple-element.117.refs_0_, bf16[256,768]{1,0:T(8,128)(2,1)S(1)} %get-tuple-element.118.refs_1_.refs_2_, ...), custom_call_target="tpu_custom_call" | custom-call | flops 1 | bytes 1 | tf_op jit(solution)/shard_map/feedforward_back/pallas_call | solution.py:1081
  97.7 1.3 up_grad.1
  99.5 2.3 collective-permute-start.20
  102.4 8.7 %collective-permute-done.20.refs_1_ = bf16[256,768]{1,0:T(8,128)(2,1)S(1)} collective-permute-done((bf16[256,768]{1,0:T(8,128)(2,1)S(1)}, bf16[256,768]{1,0:T(8,128)(2,1)S(1)}, u32[]{:S(2)}, u32[]{:S(2)}) %collective-permute-start.20) | collective-permute-done | bytes 393248 | tf_op jit(solution)/shard_map/ppermute | solution.py:480
  111.1 6.6 %attend_back.1 = (bf16[1024,768]{1,0:T(8,128)(2,1)S(1)}, bf16[256,384]{1,0:T(8,128)(2,1)S(1)}, f32[128,768]{1,0:T(8,128)S(1)}, bf16[256,768]{1,0:T(8,128)(2,1)S(...) custom-call(f32[256,768]{1,0:T(8,128)S(1)} %get-tuple-element.122.refs_0_, ...), custom_call_target="tpu_custom_call" | custom-call | flops 1 | bytes 1 | tf_op jit(solution)/shard_map/attend_back/pallas_call | solution.py:1081
  118.0 2.8 %weight_grad.1 = (bf16[1552,384]{1,0:T(8,128)(2,1)S(1)}, f32[1552,384]{1,0:T(8,128)S(1)}) custom-call(bf16[1024,768]{1,0:T(8,128)(2,1)S(1)} %get-tuple-element.107.refs_2_.refs_0_, bf16[1024,768]{1,0:T(8,128)(2,1)S(1)} %get-tuple-element.136.refs_2_.refs_1_, bf16[256,384]{1,0:T(8,128)(2,1)S(1)} %get-tuple-element.137.refs_2_.refs_0_, ...), custom_call_target="tpu_custom_call" | custom-call | flops 1 | bytes 1 | tf_op jit(solution)/shard_map/weight_grad/pallas_call | solution.py:1081
  121.0 2.0 input_grad.1
  124.7 1.5 collective-permute-start.25
  126.1 1.5 collective-permute-start.27
  128.2 6.4 %collective-permute-done.27 = bf16[192,768]{1,0:T(8,128)(2,1)S(1)} collective-permute-done((bf16[192,768]{1,0:T(8,128)(2,1)S(1)}, bf16[192,768]{1,0:T(8,128)(2,1)S(1)}, u32[]{:S(2)}, u32[]{:S(2)}) %collective-permute-start.27) | collective-permute-done | bytes 294944 | tf_op jit(solution)/shard_map/ppermute | solution.py:480
  134.6 5.2 %collective-permute-done.26 = bf16[384,768]{1,0:T(8,128)(2,1)S(1)} collective-permute-done((bf16[384,768]{1,0:T(8,128)(2,1)S(1)}, bf16[384,768]{1,0:T(8,128)(2,1)S(1)}, u32[]{:S(2)}, u32[]{:S(2)}) %collective-permute-start.26) | collective-permute-done | bytes 589856 | tf_op jit(solution)/shard_map/ppermute | solution.py:480
  139.9 1.6 collective-permute-start.29
  141.5 2.2 collective-permute-start.30
  144.4 5.0 %collective-permute-done.30.refs_1_ = bf16[96,768]{1,0:T(8,128)(2,1)S(1)} collective-permute-done((bf16[96,768]{1,0:T(8,128)(2,1)S(1)}, bf16[96,768]{1,0:T(8,128)(2,1)S(1)}, u32[]{:S(2)}, u32[]{:S(2)}) %collective-permute-start.30) | collective-permute-done | bytes 147488 | tf_op jit(solution)/shard_map/ppermute | solution.py:480
  149.5 0.9 collective-permute-done.29
  150.5 2.2 collective-permute-done.25.refs_1_
  152.9 1.6 collective-permute-start.32
  154.5 2.2 collective-permute-start.34
  156.7 0.7 collective-permute-start.33
  157.5 7.9 %collective-permute-done.34.refs_1_ = bf16[96,768]{1,0:T(8,128)(2,1)S(1)} collective-permute-done((bf16[96,768]{1,0:T(8,128)(2,1)S(1)}, bf16[96,768]{1,0:T(8,128)(2,1)S(1)}, u32[]{:S(2)}, u32[]{:S(2)}) %collective-permute-start.34) | collective-permute-done | bytes 147488 | tf_op jit(solution)/shard_map/ppermute | solution.py:480
  165.5 2.9 %collective-permute-start.37 = (bf16[192,768]{1,0:T(8,128)(2,1)S(1)}, bf16[192,768]{1,0:T(8,128)(2,1)S(1)}, u32[]{:S(2)}, u32[]{:S(2)}) collective-permute-start(bf16[192,768]{1,0:T(8,128)(2,1)S(1)} %down_join.1.refs_2_.refs_0_), channel_id=1, source_target_pairs={{0,8},{1,9},{2,10},{3,11},{4,12},{5,13},{6,14},{7,15},{8,0},{9,1},... | collective-permute-start | bytes 884744 | tf_op jit(solution)/shard_map/ppermute | solution.py:480
  168.6 1.5 collective-permute-start.38
  170.3 2.0 collective-permute-start.36
  172.3 0.8 collective-permute-done.38.refs_1_
  173.1 3.4 %collective-permute-start.40 = (bf16[96,768]{1,0:T(8,128)(2,1)S(1)}, bf16[96,768]{1,0:T(8,128)(2,1)S(1)}, u32[]{:S(2)}, u32[]{:S(2)}) collective-permute-start(bf16[96,768]{1,0:T(8,128)(2,1)S(1)} %up_join.1.refs_2_.refs_0_), channel_id=1, source_target_pairs={{0,16},{1,17},{2,18},{3,19},{4,20},{5,21},{6,22},{7,23},{8,24},{9,... | collective-permute-start | bytes 442376 | tf_op jit(solution)/shard_map/ppermute | solution.py:480
  176.5 1.7 collective-permute-done.37.refs_1_
  178.9 4.0 %collective-permute-done.40.refs_1_ = bf16[96,768]{1,0:T(8,128)(2,1)S(1)} collective-permute-done((bf16[96,768]{1,0:T(8,128)(2,1)S(1)}, bf16[96,768]{1,0:T(8,128)(2,1)S(1)}, u32[]{:S(2)}, u32[]{:S(2)}) %collective-permute-start.40) | collective-permute-done | bytes 147488 | tf_op jit(solution)/shard_map/ppermute | solution.py:480
  183.2 2.2 collective-permute-start.39
  185.4 2.1 collective-permute-done.39.refs_1_
  187.6 3.2 %collective-permute-start.41 = (bf16[192,384]{1,0:T(8,128)(2,1)S(1)}, bf16[192,384]{1,0:T(8,128)(2,1)S(1)}, u32[]{:S(2)}, u32[]{:S(2)}) collective-permute-start(bf16[192,384]{1,0:T(8,128)(2,1)S(1)} %rest_join.1.refs_2_.refs_0_), channel_id=1, source_target_pairs={{0,16},{1,17},{2,18},{3,19},{4,20},{5,21},{6,22},{7,23},{8,24},{9,... | collective-permute-start | bytes 442376 | tf_op jit(solution)/shard_map/ppermute | solution.py:480
  191.3 4.1 %collective-permute-done.41.refs_1_ = bf16[192,384]{1,0:T(8,128)(2,1)S(1)} collective-permute-done((bf16[192,384]{1,0:T(8,128)(2,1)S(1)}, bf16[192,384]{1,0:T(8,128)(2,1)S(1)}, u32[]{:S(2)}, u32[]{:S(2)}) %collective-permute-start.41) | collective-permute-done | bytes 147488 | tf_op jit(solution)/shard_map/ppermute | solution.py:480
  195.4 0.9 collective-permute-start.43
  197.0 1.3 collective-permute-start.47
  198.3 3.9 %collective-permute-done.43.refs_1_ = bf16[384,384]{1,0:T(8,128)(2,1)S(1)} collective-permute-done((bf16[384,384]{1,0:T(8,128)(2,1)S(1)}, bf16[384,384]{1,0:T(8,128)(2,1)S(1)}, u32[]{:S(2)}, u32[]{:S(2)}) %collective-permute-start.43) | collective-permute-done | bytes 294944 | tf_op jit(solution)/shard_map/ppermute | solution.py:480
  203.7 8.9 %collective-permute-done.48.refs_1_ = bf16[384,768]{1,0:T(8,128)(2,1)S(1)} collective-permute-done((bf16[384,768]{1,0:T(8,128)(2,1)S(1)}, bf16[384,768]{1,0:T(8,128)(2,1)S(1)}, u32[]{:S(2)}, u32[]{:S(2)}) %collective-permute-start.48) | collective-permute-done | bytes 589856 | tf_op jit(solution)/shard_map/ppermute | solution.py:480
  212.6 1.6 down_out.1
  214.2 11.1 %collective-permute-done.47.refs_1_ = bf16[384,768]{1,0:T(8,128)(2,1)S(1)} collective-permute-done((bf16[384,768]{1,0:T(8,128)(2,1)S(1)}, bf16[384,768]{1,0:T(8,128)(2,1)S(1)}, u32[]{:S(2)}, u32[]{:S(2)}) %collective-permute-start.47) | collective-permute-done | bytes 589856 | tf_op jit(solution)/shard_map/ppermute | solution.py:480
  225.2 1.6 up_out.1
  226.8 4.9 %collective-permute-done.44.refs_1_ = bf16[768,384]{1,0:T(8,128)(2,1)S(1)} collective-permute-done((bf16[768,384]{1,0:T(8,128)(2,1)S(1)}, bf16[768,384]{1,0:T(8,128)(2,1)S(1)}, u32[]{:S(2)}, u32[]{:S(2)}) %collective-permute-start.44) | collective-permute-done | bytes 589856 | tf_op jit(solution)/shard_map/ppermute | solution.py:480
  231.7 1.7 rest_out.1
  (80 shorter events, 14.3 us)
Async XLA Ops:
  0.7 5.6 %copy-start.1 = (bf16[192,768]{1,0:T(8,128)(2,1)S(1)}, bf16[192,768]{1,0:T(8,128)(2,1)}, u32[]{:S(2)}) copy-start(bf16[192,768]{1,0:T(8,128)(2,1)} %refs_15_.1) | copy-start | bytes 884740
  3.2 27.1 %copy-start = (bf16[768,768]{1,0:T(8,128)(2,1)S(1)}, bf16[768,768]{1,0:T(8,128)(2,1)}, u32[]{:S(2)}) copy-start(bf16[768,768]{1,0:T(8,128)(2,1)} %refs_7_.3) | copy-start | bytes 3538948
  3.2 4.7 %collective-permute-start.1 = (bf16[592,384]{1,0:T(8,128)(2,1)S(1)}, bf16[592,384]{1,0:T(8,128)(2,1)S(1)}, u32[]{:S(2)}, u32[]{:S(2)}) collective-permute-start(bf16[592,384]{1,0:T(8,128)(2,1)S(1)} %get-tuple-element.104.refs_14_), channel_id=1, source_target_pairs={{0,1},{1,0},{2,3},{3,2},{4,5},{5,4},{6,7},{7,6},{8,9},{9,8},{10,11... | collective-permute-start | bytes 1363976 | tf_op jit(solution)/shard_map/ppermute | solution.py:480
  3.7 17.6 %collective-permute-start.2 = (bf16[592,384]{1,0:T(8,128)(2,1)S(1)}, bf16[592,384]{1,0:T(8,128)(2,1)S(1)}, u32[]{:S(2)}, u32[]{:S(2)}) collective-permute-start(bf16[592,384]{1,0:T(8,128)(2,1)S(1)} %get-tuple-element.105.refs_2_), channel_id=1, source_target_pairs={{0,2},{1,3},{2,0},{3,1},{4,6},{5,7},{6,4},{7,5},{8,10},{9,11},{10,... | collective-permute-start | bytes 1363976 | tf_op jit(solution)/shard_map/ppermute | solution.py:480
  6.3 1.6 collective-permute-start.3
  6.5 0.7 collective-permute-start
  21.3 7.0 %collective-permute-start.5 = (bf16[144,768]{1,0:T(8,128)(2,1)S(1)}, bf16[144,768]{1,0:T(8,128)(2,1)S(1)}, u32[]{:S(2)}, u32[]{:S(2)}) collective-permute-start(bf16[144,768]{1,0:T(8,128)(2,1)S(1)} %once.2.refs_0_), channel_id=1, source_target_pairs={{0,4},{1,5},{2,6},{3,7},{4,0},{5,1},{6,2},{7,3},{8,12},{9,13},{10,... | collective-permute-start | bytes 663560 | tf_op jit(solution)/shard_map/ppermute | solution.py:480
  22.8 7.5 %collective-permute-start.4 = (bf16[144,768]{1,0:T(8,128)(2,1)S(1)}, bf16[144,768]{1,0:T(8,128)(2,1)S(1)}, u32[]{:S(2)}, u32[]{:S(2)}) collective-permute-start(bf16[144,768]{1,0:T(8,128)(2,1)S(1)} %once.2.refs_0_), channel_id=1, source_target_pairs={{0,2},{1,3},{2,0},{3,1},{4,6},{5,7},{6,4},{7,5},{8,10},{9,11},{10,... | collective-permute-start | bytes 663560 | tf_op jit(solution)/shard_map/ppermute | solution.py:480
  30.3 1.5 collective-permute-start.7
  30.3 34.1 %collective-permute-start.16 = (bf16[768,768]{1,0:T(8,128)(2,1)S(1)}, bf16[768,768]{1,0:T(8,128)(2,1)S(1)}, u32[]{:S(2)}, u32[]{:S(2)}) collective-permute-start(bf16[768,768]{1,0:T(8,128)(2,1)S(1)} %copy-done), channel_id=1, source_target_pairs={{0,1},{1,0},{2,3},{3,2},{4,5},{5,4},{6,7},{7,6},{8,9},{9,8},{10,11... | collective-permute-start | bytes 3538952 | tf_op jit(solution)/shard_map/ppermute | solution.py:480
  33.0 15.4 %collective-permute-start.13 = (bf16[192,1536]{1,0:T(8,128)(2,1)S(1)}, bf16[192,1536]{1,0:T(8,128)(2,1)S(1)}, u32[]{:S(2)}, u32[]{:S(2)}) collective-permute-start(bf16[192,1536]{1,0:T(8,128)(2,1)S(1)} %get-tuple-element.106.refs_1_), channel_id=1, source_target_pairs={{0,2},{1,3},{2,0},{3,1},{4,6},{5,7},{6,4},{7,5},{8,10},{9,11},{10,... | collective-permute-start | bytes 1769480 | tf_op jit(solution)/shard_map/ppermute | solution.py:480
  34.9 1.5 collective-permute-start.6
  34.9 14.6 %collective-permute-start.11 = (bf16[592,384]{1,0:T(8,128)(2,1)S(1)}, bf16[592,384]{1,0:T(8,128)(2,1)S(1)}, u32[]{:S(2)}, u32[]{:S(2)}) collective-permute-start(bf16[592,384]{1,0:T(8,128)(2,1)S(1)} %collective-permute-done.2.refs_2_.refs_11_), channel_id=1, source_target_pairs={{0,1},{1,0},{2,3},{3,2},{4,5},{5,4},{6,7},{7,6},{8,9},{9,8},{10,11... | collective-permute-start | bytes 1363976 | tf_op jit(solution)/shard_map/ppermute | solution.py:480
  35.4 7.3 %collective-permute-start.8 = (bf16[144,768]{1,0:T(8,128)(2,1)S(1)}, bf16[144,768]{1,0:T(8,128)(2,1)S(1)}, u32[]{:S(2)}, u32[]{:S(2)}) collective-permute-start(bf16[144,768]{1,0:T(8,128)(2,1)S(1)} %once.3.refs_1_), channel_id=1, source_target_pairs={{0,4},{1,5},{2,6},{3,7},{4,0},{5,1},{6,2},{7,3},{8,12},{9,13},{10,... | collective-permute-start | bytes 663560 | tf_op jit(solution)/shard_map/ppermute | solution.py:480
  36.3 6.4 %collective-permute-start.9 = (bf16[144,768]{1,0:T(8,128)(2,1)S(1)}, bf16[144,768]{1,0:T(8,128)(2,1)S(1)}, u32[]{:S(2)}, u32[]{:S(2)}) collective-permute-start(bf16[144,768]{1,0:T(8,128)(2,1)S(1)} %collective-permute-done.5.refs_1_.refs_4_), channel_id=1, source_target_pairs={{0,1},{1,0},{2,3},{3,2},{4,5},{5,4},{6,7},{7,6},{8,9},{9,8},{10,11... | collective-permute-start | bytes 663560 | tf_op jit(solution)/shard_map/ppermute | solution.py:480
  42.7 8.5 %collective-permute-start.10 = (bf16[144,768]{1,0:T(8,128)(2,1)S(1)}, bf16[144,768]{1,0:T(8,128)(2,1)S(1)}, u32[]{:S(2)}, u32[]{:S(2)}) collective-permute-start(bf16[144,768]{1,0:T(8,128)(2,1)S(1)} %collective-permute-done.8.refs_5_), channel_id=1, source_target_pairs={{0,1},{1,0},{2,3},{3,2},{4,5},{5,4},{6,7},{7,6},{8,9},{9,8},{10,11... | collective-permute-start | bytes 663560 | tf_op jit(solution)/shard_map/ppermute | solution.py:480
  42.7 21.7 %collective-permute-start.14 = (bf16[192,1536]{1,0:T(8,128)(2,1)S(1)}, bf16[192,1536]{1,0:T(8,128)(2,1)S(1)}, u32[]{:S(2)}, u32[]{:S(2)}) collective-permute-start(bf16[192,1536]{1,0:T(8,128)(2,1)S(1)} %get-tuple-element.112), channel_id=1, source_target_pairs={{0,1},{1,0},{2,3},{3,2},{4,5},{5,4},{6,7},{7,6},{8,9},{9,8},{10,11... | collective-permute-start | bytes 1769480 | tf_op jit(solution)/shard_map/ppermute | solution.py:480
  48.5 27.2 %collective-permute-start.15 = (bf16[192,1536]{1,0:T(8,128)(2,1)S(1)}, bf16[192,1536]{1,0:T(8,128)(2,1)S(1)}, u32[]{:S(2)}, u32[]{:S(2)}) collective-permute-start(bf16[192,1536]{1,0:T(8,128)(2,1)S(1)} %collective-permute-done.13.refs_6_.refs_4_), channel_id=1, source_target_pairs={{0,1},{1,0},{2,3},{3,2},{4,5},{5,4},{6,7},{7,6},{8,9},{9,8},{10,11... | collective-permute-start | bytes 1769480 | tf_op jit(solution)/shard_map/ppermute | solution.py:480
  49.4 13.8 %collective-permute-start.18 = (bf16[128,768]{1,0:T(8,128)(2,1)S(1)}, bf16[128,768]{1,0:T(8,128)(2,1)S(1)}, u32[]{:S(2)}, u32[]{:S(2)}) collective-permute-start(bf16[128,768]{1,0:T(8,128)(2,1)S(1)} %cotangent.1.refs_17_), channel_id=1, source_target_pairs={{0,2},{1,18},{2,10},{3,26},{4,6},{5,22},{6,14},{7,30},{8,0},{9,16}... | collective-permute-start | bytes 589832 | tf_op jit(solution)/shard_map/ppermute | solution.py:480
  62.9 12.8 %collective-permute-start.12 = (bf16[256,768]{1,0:T(8,128)(2,1)S(1)}, bf16[256,768]{1,0:T(8,128)(2,1)S(1)}, u32[]{:S(2)}, u32[]{:S(2)}) collective-permute-start(bf16[256,768]{1,0:T(8,128)(2,1)S(1)} %get-tuple-element.109.refs_1_), channel_id=1, source_target_pairs={{0,2},{1,3},{2,0},{3,1},{4,6},{5,7},{6,4},{7,5},{8,10},{9,11},{10,... | collective-permute-start | bytes 1179656 | tf_op jit(solution)/shard_map/ppermute | solution.py:480
  63.3 1.1 collective-permute-start.17
  79.3 12.3 %collective-permute-start.19 = (bf16[256,768]{1,0:T(8,128)(2,1)S(1)}, bf16[256,768]{1,0:T(8,128)(2,1)S(1)}, u32[]{:S(2)}, u32[]{:S(2)}) collective-permute-start(bf16[256,768]{1,0:T(8,128)(2,1)S(1)} %get-tuple-element.115.refs_6_), channel_id=1, source_target_pairs={{0,2},{1,3},{2,0},{3,1},{4,6},{5,7},{6,4},{7,5},{8,10},{9,11},{10,... | collective-permute-start | bytes 1179656 | tf_op jit(solution)/shard_map/ppermute | solution.py:480
  93.8 3.6 %collective-permute-start.21 = (bf16[768,768]{1,0:T(8,128)(2,1)S(1)}, bf16[768,768]{1,0:T(8,128)(2,1)S(1)}, u32[]{:S(2)}, u32[]{:S(2)}) collective-permute-start(bf16[768,768]{1,0:T(8,128)(2,1)S(1)} %get-tuple-element.121.refs_9_), channel_id=1, source_target_pairs={{0,1},{1,0},{2,3},{3,2},{4,5},{5,4},{6,7},{7,6},{8,9},{9,8},{10,11... | collective-permute-start | bytes 3538952 | tf_op jit(solution)/shard_map/ppermute | solution.py:480
  99.0 18.8 %collective-permute-start.22 = (bf16[768,768]{1,0:T(8,128)(2,1)S(1)}, bf16[768,768]{1,0:T(8,128)(2,1)S(1)}, u32[]{:S(2)}, u32[]{:S(2)}) collective-permute-start(bf16[768,768]{1,0:T(8,128)(2,1)S(1)} %get-tuple-element.135.refs_13_), channel_id=1, source_target_pairs={{0,1},{1,0},{2,3},{3,2},{4,5},{5,4},{6,7},{7,6},{8,9},{9,8},{10,11... | collective-permute-start | bytes 3538952 | tf_op jit(solution)/shard_map/ppermute | solution.py:480
  99.5 11.7 %collective-permute-start.20 = (bf16[256,768]{1,0:T(8,128)(2,1)S(1)}, bf16[256,768]{1,0:T(8,128)(2,1)S(1)}, u32[]{:S(2)}, u32[]{:S(2)}) collective-permute-start(bf16[256,768]{1,0:T(8,128)(2,1)S(1)} %get-tuple-element.123.refs_2_), channel_id=1, source_target_pairs={{0,2},{1,3},{2,0},{3,1},{4,6},{5,7},{6,4},{7,5},{8,10},{9,11},{10,... | collective-permute-start | bytes 1179656 | tf_op jit(solution)/shard_map/ppermute | solution.py:480
  101.8 19.1 %collective-permute-start.24 = (bf16[384,768]{1,0:T(8,128)(2,1)S(1)}, bf16[384,768]{1,0:T(8,128)(2,1)S(1)}, u32[]{:S(2)}, u32[]{:S(2)}) collective-permute-start(bf16[384,768]{1,0:T(8,128)(2,1)S(1)} %get-tuple-element.134.refs_2_), channel_id=1, source_target_pairs={{0,4},{1,5},{2,6},{3,7},{4,0},{5,1},{6,2},{7,3},{8,12},{9,13},{10,... | collective-permute-start | bytes 1769480 | tf_op jit(solution)/shard_map/ppermute | solution.py:480
  120.8 3.5 %collective-permute-start.23 = (bf16[1552,384]{1,0:T(8,128)(2,1)S(1)}, bf16[1552,384]{1,0:T(8,128)(2,1)S(1)}, u32[]{:S(2)}, u32[]{:S(2)}) collective-permute-start(bf16[1552,384]{1,0:T(8,128)(2,1)S(1)} %get-tuple-element.146.refs_2_), channel_id=1, source_target_pairs={{0,1},{1,0},{2,3},{3,2},{4,5},{5,4},{6,7},{7,6},{8,9},{9,8},{10,11... | collective-permute-start | bytes 3575816 | tf_op jit(solution)/shard_map/ppermute | solution.py:480
  123.1 4.6 %collective-permute-start.28 = (bf16[512,768]{1,0:T(8,128)(2,1)S(1)}, bf16[512,768]{1,0:T(8,128)(2,1)S(1)}, u32[]{:S(2)}, u32[]{:S(2)}) collective-permute-start(bf16[512,768]{1,0:T(8,128)(2,1)S(1)} %get-tuple-element.150.refs_2_), channel_id=1, source_target_pairs={{0,1},{1,0},{2,3},{3,2},{4,5},{5,4},{6,7},{7,6},{8,9},{9,8},{10,11... | collective-permute-start | bytes 2359304 | tf_op jit(solution)/shard_map/ppermute | solution.py:480
  123.6 16.2 %collective-permute-start.26 = (bf16[384,768]{1,0:T(8,128)(2,1)S(1)}, bf16[384,768]{1,0:T(8,128)(2,1)S(1)}, u32[]{:S(2)}, u32[]{:S(2)}) collective-permute-start(bf16[384,768]{1,0:T(8,128)(2,1)S(1)} %get-tuple-element.144.refs_9_), channel_id=1, source_target_pairs={{0,4},{1,5},{2,6},{3,7},{4,0},{5,1},{6,2},{7,3},{8,12},{9,13},{10,... | collective-permute-start | bytes 1769480 | tf_op jit(solution)/shard_map/ppermute | solution.py:480
  124.7 28.0 %collective-permute-start.25 = (bf16[784,384]{1,0:T(8,128)(2,1)S(1)}, bf16[784,384]{1,0:T(8,128)(2,1)S(1)}, u32[]{:S(2)}, u32[]{:S(2)}) collective-permute-start(bf16[784,384]{1,0:T(8,128)(2,1)S(1)} %get-tuple-element.152.refs_2_), channel_id=1, source_target_pairs={{0,4},{1,5},{2,6},{3,7},{4,0},{5,1},{6,2},{7,3},{8,12},{9,13},{10,... | collective-permute-start | bytes 1806344 | tf_op jit(solution)/shard_map/ppermute | solution.py:480
  126.1 8.4 %collective-permute-start.27 = (bf16[192,768]{1,0:T(8,128)(2,1)S(1)}, bf16[192,768]{1,0:T(8,128)(2,1)S(1)}, u32[]{:S(2)}, u32[]{:S(2)}) collective-permute-start(bf16[192,768]{1,0:T(8,128)(2,1)S(1)} %get-tuple-element.149.refs_3_), channel_id=1, source_target_pairs={{0,8},{1,9},{2,10},{3,11},{4,12},{5,13},{6,14},{7,15},{8,0},{9,1},... | collective-permute-start | bytes 884744 | tf_op jit(solution)/shard_map/ppermute | solution.py:480
  127.8 15.9 %collective-permute-start.31 = (bf16[256,768]{1,0:T(8,128)(2,1)S(1)}, bf16[256,768]{1,0:T(8,128)(2,1)S(1)}, u32[]{:S(2)}, u32[]{:S(2)}) collective-permute-start(bf16[256,768]{1,0:T(8,128)(2,1)S(1)} %get-tuple-element.156.refs_2_), channel_id=1, source_target_pairs={{0,2},{1,3},{2,0},{3,1},{4,6},{5,7},{6,4},{7,5},{8,10},{9,11},{10,... | collective-permute-start | bytes 1179656 | tf_op jit(solution)/shard_map/ppermute | solution.py:480
  139.9 10.5 %collective-permute-start.29 = (bf16[192,768]{1,0:T(8,128)(2,1)S(1)}, bf16[192,768]{1,0:T(8,128)(2,1)S(1)}, u32[]{:S(2)}, u32[]{:S(2)}) collective-permute-start(bf16[192,768]{1,0:T(8,128)(2,1)S(1)} %get-tuple-element.159.refs_2_), channel_id=1, source_target_pairs={{0,8},{1,9},{2,10},{3,11},{4,12},{5,13},{6,14},{7,15},{8,0},{9,1},... | collective-permute-start | bytes 884744 | tf_op jit(solution)/shard_map/ppermute | solution.py:480
  141.5 8.0 %collective-permute-start.30 = (bf16[96,768]{1,0:T(8,128)(2,1)S(1)}, bf16[96,768]{1,0:T(8,128)(2,1)S(1)}, u32[]{:S(2)}, u32[]{:S(2)}) collective-permute-start(bf16[96,768]{1,0:T(8,128)(2,1)S(1)} %get-tuple-element.157.refs_2_), channel_id=1, source_target_pairs={{0,16},{1,17},{2,18},{3,19},{4,20},{5,21},{6,22},{7,23},{8,24},{9,... | collective-permute-start | bytes 442376 | tf_op jit(solution)/shard_map/ppermute | solution.py:480
  143.8 13.7 %collective-permute-start.35 = (bf16[128,768]{1,0:T(8,128)(2,1)S(1)}, bf16[128,768]{1,0:T(8,128)(2,1)S(1)}, u32[]{:S(2)}, u32[]{:S(2)}) collective-permute-start(bf16[128,768]{1,0:T(8,128)(2,1)S(1)} %get-tuple-element.162.refs_2_), channel_id=1, source_target_pairs={{0,4},{1,5},{2,6},{3,7},{4,0},{5,1},{6,2},{7,3},{8,12},{9,13},{10,... | collective-permute-start | bytes 589832 | tf_op jit(solution)/shard_map/ppermute | solution.py:480
  152.9 17.2 %collective-permute-start.32 = (bf16[400,384]{1,0:T(8,128)(2,1)S(1)}, bf16[400,384]{1,0:T(8,128)(2,1)S(1)}, u32[]{:S(2)}, u32[]{:S(2)}) collective-permute-start(bf16[400,384]{1,0:T(8,128)(2,1)S(1)} %get-tuple-element.165.refs_3_), channel_id=1, source_target_pairs={{0,8},{1,9},{2,10},{3,11},{4,12},{5,13},{6,14},{7,15},{8,0},{9,1},... | collective-permute-start | bytes 921608 | tf_op jit(solution)/shard_map/ppermute | solution.py:480
  154.5 10.9 %collective-permute-start.34 = (bf16[96,768]{1,0:T(8,128)(2,1)S(1)}, bf16[96,768]{1,0:T(8,128)(2,1)S(1)}, u32[]{:S(2)}, u32[]{:S(2)}) collective-permute-start(bf16[96,768]{1,0:T(8,128)(2,1)S(1)} %down_sum.1.refs_2_.refs_0_), channel_id=1, source_target_pairs={{0,16},{1,17},{2,18},{3,19},{4,20},{5,21},{6,22},{7,23},{8,24},{9,... | collective-permute-start | bytes 442376 | tf_op jit(solution)/shard_map/ppermute | solution.py:480
  156.7 11.9 %collective-permute-start.33 = (bf16[96,768]{1,0:T(8,128)(2,1)S(1)}, bf16[96,768]{1,0:T(8,128)(2,1)S(1)}, u32[]{:S(2)}, u32[]{:S(2)}) collective-permute-start(bf16[96,768]{1,0:T(8,128)(2,1)S(1)} %get-tuple-element.163.refs_2_), channel_id=1, source_target_pairs={{0,16},{1,17},{2,18},{3,19},{4,20},{5,21},{6,22},{7,23},{8,24},{9,... | collective-permute-start | bytes 442376 | tf_op jit(solution)/shard_map/ppermute | solution.py:480
  165.5 12.7 %collective-permute-start.37 = (bf16[192,768]{1,0:T(8,128)(2,1)S(1)}, bf16[192,768]{1,0:T(8,128)(2,1)S(1)}, u32[]{:S(2)}, u32[]{:S(2)}) collective-permute-start(bf16[192,768]{1,0:T(8,128)(2,1)S(1)} %down_join.1.refs_2_.refs_0_), channel_id=1, source_target_pairs={{0,8},{1,9},{2,10},{3,11},{4,12},{5,13},{6,14},{7,15},{8,0},{9,1},... | collective-permute-start | bytes 884744 | tf_op jit(solution)/shard_map/ppermute | solution.py:480
  168.6 4.4 %collective-permute-start.38 = (bf16[48,768]{1,0:T(8,128)(2,1)S(1)}, bf16[48,768]{1,0:T(8,128)(2,1)S(1)}, u32[]{:S(2)}, u32[]{:S(2)}) collective-permute-start(bf16[48,768]{1,0:T(8,128)(2,1)S(1)} %get-tuple-element.169.refs_2_), channel_id=1, source_target_pairs={{0,2},{1,3},{2,0},{3,1},{4,6},{5,7},{6,4},{7,5},{8,10},{9,11},{10,... | collective-permute-start | bytes 221192 | tf_op jit(solution)/shard_map/ppermute | solution.py:480
  170.3 8.0 %collective-permute-start.36 = (bf16[208,384]{1,0:T(8,128)(2,1)S(1)}, bf16[208,384]{1,0:T(8,128)(2,1)S(1)}, u32[]{:S(2)}, u32[]{:S(2)}) collective-permute-start(bf16[208,384]{1,0:T(8,128)(2,1)S(1)} %get-tuple-element.171.refs_2_), channel_id=1, source_target_pairs={{0,16},{1,17},{2,18},{3,19},{4,20},{5,21},{6,22},{7,23},{8,24},{9,... | collective-permute-start | bytes 479240 | tf_op jit(solution)/shard_map/ppermute | solution.py:480
  173.1 9.8 %collective-permute-start.40 = (bf16[96,768]{1,0:T(8,128)(2,1)S(1)}, bf16[96,768]{1,0:T(8,128)(2,1)S(1)}, u32[]{:S(2)}, u32[]{:S(2)}) collective-permute-start(bf16[96,768]{1,0:T(8,128)(2,1)S(1)} %up_join.1.refs_2_.refs_0_), channel_id=1, source_target_pairs={{0,16},{1,17},{2,18},{3,19},{4,20},{5,21},{6,22},{7,23},{8,24},{9,... | collective-permute-start | bytes 442376 | tf_op jit(solution)/shard_map/ppermute | solution.py:480
  182.9 8.4 %collective-permute-start.42 = (bf16[192,768]{1,0:T(8,128)(2,1)S(1)}, bf16[192,768]{1,0:T(8,128)(2,1)S(1)}, u32[]{:S(2)}, u32[]{:S(2)}) collective-permute-start(bf16[192,768]{1,0:T(8,128)(2,1)S(1)} %up_join_far.1.refs_2_.refs_0_), channel_id=1, source_target_pairs={{0,8},{1,9},{2,10},{3,11},{4,12},{5,13},{6,14},{7,15},{8,0},{9,1},... | collective-permute-start | bytes 884744 | tf_op jit(solution)/shard_map/ppermute | solution.py:480
  183.2 4.4 %collective-permute-start.39 = (bf16[72,384]{1,0:T(8,128)(2,1)S(1)}, bf16[72,384]{1,0:T(8,128)(2,1)S(1)}, u32[]{:S(2)}, u32[]{:S(2)}) collective-permute-start(bf16[72,384]{1,0:T(8,128)(2,1)S(1)} %get-tuple-element.174.refs_2_), channel_id=1, source_target_pairs={{0,2},{1,3},{2,0},{3,1},{4,6},{5,7},{6,4},{7,5},{8,10},{9,11},{10,... | collective-permute-start | bytes 165896 | tf_op jit(solution)/shard_map/ppermute | solution.py:480
  187.6 7.8 %collective-permute-start.41 = (bf16[192,384]{1,0:T(8,128)(2,1)S(1)}, bf16[192,384]{1,0:T(8,128)(2,1)S(1)}, u32[]{:S(2)}, u32[]{:S(2)}) collective-permute-start(bf16[192,384]{1,0:T(8,128)(2,1)S(1)} %rest_join.1.refs_2_.refs_0_), channel_id=1, source_target_pairs={{0,16},{1,17},{2,18},{3,19},{4,20},{5,21},{6,22},{7,23},{8,24},{9,... | collective-permute-start | bytes 442376 | tf_op jit(solution)/shard_map/ppermute | solution.py:480
  195.4 6.8 %collective-permute-start.43 = (bf16[384,384]{1,0:T(8,128)(2,1)S(1)}, bf16[384,384]{1,0:T(8,128)(2,1)S(1)}, u32[]{:S(2)}, u32[]{:S(2)}) collective-permute-start(bf16[384,384]{1,0:T(8,128)(2,1)S(1)} %rest_join_far.1.refs_0_.refs_2_), channel_id=1, source_target_pairs={{0,8},{1,9},{2,10},{3,11},{4,12},{5,13},{6,14},{7,15},{8,0},{9,1},... | collective-permute-start | bytes 884744 | tf_op jit(solution)/shard_map/ppermute | solution.py:480
  196.3 16.3 %collective-permute-start.48 = (bf16[384,768]{1,0:T(8,128)(2,1)S(1)}, bf16[384,768]{1,0:T(8,128)(2,1)S(1)}, u32[]{:S(2)}, u32[]{:S(2)}) collective-permute-start(bf16[384,768]{1,0:T(8,128)(2,1)S(1)} %down_join_near.1.refs_2_.refs_0_), channel_id=1, source_target_pairs={{0,4},{1,5},{2,6},{3,7},{4,0},{5,1},{6,2},{7,3},{8,12},{9,13},{10,... | collective-permute-start | bytes 1769480 | tf_op jit(solution)/shard_map/ppermute | solution.py:480
  197.0 28.2 %collective-permute-start.47 = (bf16[384,768]{1,0:T(8,128)(2,1)S(1)}, bf16[384,768]{1,0:T(8,128)(2,1)S(1)}, u32[]{:S(2)}, u32[]{:S(2)}) collective-permute-start(bf16[384,768]{1,0:T(8,128)(2,1)S(1)} %up_join_near.1.refs_2_.refs_0_), channel_id=1, source_target_pairs={{0,4},{1,5},{2,6},{3,7},{4,0},{5,1},{6,2},{7,3},{8,12},{9,13},{10,... | collective-permute-start | bytes 1769480 | tf_op jit(solution)/shard_map/ppermute | solution.py:480
  202.3 29.4 %collective-permute-start.44 = (bf16[768,384]{1,0:T(8,128)(2,1)S(1)}, bf16[768,384]{1,0:T(8,128)(2,1)S(1)}, u32[]{:S(2)}, u32[]{:S(2)}) collective-permute-start(bf16[768,384]{1,0:T(8,128)(2,1)S(1)} %rest_join_near.1.refs_0_.refs_4_.refs_2_), channel_id=1, source_target_pairs={{0,4},{1,5},{2,6},{3,7},{4,0},{5,1},{6,2},{7,3},{8,12},{9,13},{10,... | collective-permute-start | bytes 1769480 | tf_op jit(solution)/shard_map/ppermute | solution.py:480
  202.4 24.4 %collective-permute-start.45 = (bf16[128,768]{1,0:T(8,128)(2,1)S(1)}, bf16[128,768]{1,0:T(8,128)(2,1)S(1)}, u32[]{:S(2)}, u32[]{:S(2)}) collective-permute-start(bf16[128,768]{1,0:T(8,128)(2,1)S(1)} %get-tuple-element.175), channel_id=1, source_target_pairs={{0,0},{1,16},{2,8},{3,24},{4,4},{5,20},{6,12},{7,28},{8,2},{9,18},... | collective-permute-start | bytes 589832 | tf_op jit(solution)/shard_map/ppermute | solution.py:480
  203.0 23.8 %collective-permute-start.46 = (bf16[128,768]{1,0:T(8,128)(2,1)S(1)}, bf16[128,768]{1,0:T(8,128)(2,1)S(1)}, u32[]{:S(2)}, u32[]{:S(2)}) collective-permute-start(bf16[128,768]{1,0:T(8,128)(2,1)S(1)} %input_sum.1.refs_2_), channel_id=1, source_target_pairs={{0,0},{1,16},{2,8},{3,24},{4,4},{5,20},{6,12},{7,28},{8,2},{9,18},... | collective-permute-start | bytes 589832 | tf_op jit(solution)/shard_map/ppermute | solution.py:480

commit v4 on v3

--- a/solution.py
+++ b/solution.py
@@ -626,62 +626,73 @@
         out[2 * p : 2 * p + 2] = jnp.transpose(keys[p]).reshape(2, 64, keys.shape[1])
 
 
-def attend_kernel(
-    b0, b1, b2, b3, b4, b5, b6, b7, w_q, w_k, w_v, w_x, w_m, w_mx, own_lines, w_o, w_om,
-    a_low, x_out, w_out, wo_out, k_out, v_out, q_out, o_out, lse_out, ids_out, a_out, vecs, up_bias,
-    xs, raw, w, wo, lines, k3, v3, vt, q3, ot, mask, sems, outs,
+def project_kernel(
+    b0, b1, b2, b3, w_q, w_k, w_v, w_x, w_m, w_mx, own_lines,
+    kv_out, q_out, w, vecs, up_bias, xs, sems,
 ):
     q, r, x, c = spot()
-    rows = xs.shape[0] // 8
+    rows = xs.shape[0] // 4
     part = w.shape[0] // 4
-    half = wo.shape[0]
-    me, shard = 4 * r + 2 * c + x, 2 * x + c
+    half = w.shape[1] // 3
+    me, shard = 2 * c + x, 2 * x + c
+    columns = pl.ds(pl.multiple_of(half * x, 128), half)
     ins = Copies(sems)
-    for j, block in enumerate((b0, b1, b2, b3, b4, b5, b6, b7)):
-        at = me ^ j
-        ins.start(block.at[pl.ds(0, rows)], xs.at[pl.ds(pl.multiple_of(rows * at, rows), rows)])
-        ins.start(block.at[pl.ds(rows, 16)], raw.at[at])
-    columns = pl.ds(pl.multiple_of(half * x, 128), half)
     for t, own in enumerate((w_q, w_k, w_v)):
-        place = pl.ds(half * t, half)
-        ins.start(own.at[:, columns], w.at[pl.ds(pl.multiple_of(part * shard, 64), part), place])
-        for flip, piece in ((2, w_x), (1, w_m), (3, w_mx)):
-            at = pl.ds(pl.multiple_of(part * (shard ^ flip), 64), part)
-            ins.start(piece.at[pl.ds(part * t, part)], w.at[at, place])
-    for i, piece in enumerate((own_lines, w_m, w_x, w_mx)):
-        ins.start(piece.at[pl.ds(3 * part, 16)], lines.at[i])
-    ins.start(w_o, wo.at[pl.ds(pl.multiple_of(part * c, 64), part)])
-    ins.start(w_om, wo.at[pl.ds(pl.multiple_of(part * (1 - c), 64), part)])
-    ins.wait()
-    backs = Copies(outs)
-    backs.start(xs, x_out)
-    backs.start(w, w_out)
-    backs.start(wo, wo_out)
-    mine = lines[0].astype(jnp.float32) + lines[1].astype(jnp.float32)
-    other = lines[2].astype(jnp.float32) + lines[3].astype(jnp.float32)
+        at = pl.ds(pl.multiple_of(part * shard, 64), part)
+        ins.start(own.at[:, columns], w.at[at, pl.ds(half * t, half)])
+    for j, block in enumerate((b0, b1, b2, b3)):
+        xs[pl.ds(pl.multiple_of(rows * (me ^ j), rows), rows), :] = block[0:rows, :]
+    for flip, piece in ((2, w_x), (1, w_m), (3, w_mx)):
+        at = pl.ds(pl.multiple_of(part * (shard ^ flip), 64), part)
+        for t in range(3):
+            w[at, half * t : half * (t + 1)] = piece[part * t : part * (t + 1), :]
+    mine, other = (
+        a[3 * part :, :].astype(jnp.float32) + b[3 * part :, :].astype(jnp.float32)
+        for a, b in ((own_lines, w_m), (w_x, w_mx))
+    )
     vecs[:, columns] = mine[0:8, :]
     vecs[:, pl.ds(pl.multiple_of(half * (1 - x), 128), half)] = other[0:8, :]
     for i in range(4):
         up_bias[i] = jnp.broadcast_to(mine[8 + i : 9 + i, :], (8, half))
-    for b in range(8):
-        ids_out[b : b + 1, :] = raw[b, 0:1, 0:rows].astype(jnp.float32)
+    ins.wait()
+    kv_out[:, 0:half] = dot(xs[...], w[:, half : 2 * half]).astype(jnp.bfloat16)
+    kv_out[:, half:] = (dot(xs[...], w[:, 2 * half :]) + mine[1:2, :]).astype(jnp.bfloat16)
+    own = pl.ds(pl.multiple_of(2 * rows * c, rows), 2 * rows)
+    q_out[...] = (dot(xs[own, :], w[:, 0:half]) + mine[0:1, :]).astype(jnp.bfloat16)
+
+
+def attend_kernel(
+    b0, b1, b2, b3, b4, b5, b6, b7, kv_own, q_own, w, vecs, w_o, w_om,
+    a_low, xs, wo, k3, v3, q3, o_out, lse_out, ids_out, a_out,
+    vt, ot, mask, sems,
+):
+    q, r, x, c = spot()
+    rows = xs.shape[0] // 8
+    half = wo.shape[0]
+    part = half // 2
+    me = 4 * r + 2 * c + x
+    ins = Copies(sems)
+    ins.start(w_o, wo.at[pl.ds(pl.multiple_of(part * c, 64), part)])
+    wo[pl.ds(pl.multiple_of(part * (1 - c), 64), part), :] = w_om[...]
+    for j, block in enumerate((b0, b1, b2, b3, b4, b5, b6, b7)):
+        at = me ^ j
+        xs[pl.ds(pl.multiple_of(rows * at, rows), rows), :] = block[0:rows, :]
+        ids_out[pl.ds(at, 1), :] = block[rows : rows + 16, 0:rows].astype(jnp.float32)[0:1, :]
     fill_mask(ids_out, mask, 4 * r + 2 * c)
-    keyed = dot(xs[...], w[:, half : 2 * half]).astype(jnp.bfloat16)
-    valued = dot(xs[...], w[:, 2 * half : 3 * half]) + mine[1:2, :]
-    own = pl.ds(pl.multiple_of(rows * (4 * r + 2 * c), rows), 2 * rows)
-    asked = (dot(xs[own, :], w[:, 0:half]) + mine[0:1, :]).astype(jnp.bfloat16)
-    valued = valued.astype(jnp.bfloat16)
-    turned = jnp.transpose(valued)
+    rest = pl.ds(pl.multiple_of(4 * rows * (1 - r), rows), 4 * rows)
+    here = pl.ds(pl.multiple_of(4 * rows * r, rows), 4 * rows)
+    bias = vecs[1:2, pl.ds(pl.multiple_of(half * x, 128), half)]
+    keyed = dot(xs[rest, :], w[:, half : 2 * half]).astype(jnp.bfloat16)
+    valued = (dot(xs[rest, :], w[:, 2 * half :]) + bias).astype(jnp.bfloat16)
     pairs = half // 128
     for p in range(pairs):
-        k3[p] = keyed[:, 128 * p : 128 * (p + 1)]
-        v3[p] = valued[:, 128 * p : 128 * (p + 1)]
-        q3[p] = asked[:, 128 * p : 128 * (p + 1)]
-    for h in range(2 * pairs):
-        vt[h] = turned[64 * h : 64 * (h + 1), :]
-    backs.start(k3, k_out)
-    backs.start(v3, v_out)
-    q_out[...] = q3[...]
+        at = slice(128 * p, 128 * (p + 1))
+        k3[p, here, :] = kv_own[:, at]
+        k3[p, rest, :] = keyed[:, at]
+        v3[p, here, :] = kv_own[:, half + 128 * p : half + 128 * (p + 1)]
+        v3[p, rest, :] = valued[:, at]
+        q3[p] = q_own[:, at]
+        vt[2 * p : 2 * p + 2] = jnp.transpose(v3[p]).reshape(2, 64, 8 * rows)
     lane = lax.broadcasted_iota(jnp.int32, (2 * rows, 128), 1) // 64
 
     def head(h, carry):
@@ -697,23 +708,25 @@
     lax.fori_loop(0, 2 * pairs, head, 0)
     mixed = jnp.transpose(ot[...].reshape(half, 2 * rows)).astype(jnp.bfloat16)
     o_out[...] = mixed
+    ins.wait()
     partial = dot(mixed, wo[...])
     a_out[...] = partial
     a_low[...] = partial.astype(jnp.bfloat16)
-    backs.wait()
-
-
-def load_feedforward(copies, up, down, u_own, u_x, u_m, u_mx, d_own, d_m):
+
+
+def inner_kernel(u_own, u_x, u_m, u_mx, d_own, d_m, up, down, sems):
     q, r, x, c = spot()
     part = up.shape[0] // 4
     count = up.shape[1]
     shard = 2 * x + c
+    ins = Copies(sems)
     own = u_own.at[:, pl.ds(pl.multiple_of(count * x, 128), count)]
-    for flip, piece in ((0, own), (2, u_x), (1, u_m), (3, u_mx)):
-        rows = pl.ds(pl.multiple_of(part * (shard ^ flip), 64), part)
-        copies.start(piece, up.at[rows])
-    for side, piece in ((c, d_own), (1 - c, d_m)):
-        copies.start(piece, down.at[pl.ds(pl.multiple_of(count // 2 * side, 128), count // 2)])
+    ins.start(own, up.at[pl.ds(pl.multiple_of(part * shard, 64), part)])
+    ins.start(d_own, down.at[pl.ds(pl.multiple_of(count // 2 * c, 128), count // 2)])
+    for flip, piece in ((2, u_x), (1, u_m), (3, u_mx)):
+        up[pl.ds(pl.multiple_of(part * (shard ^ flip), 64), part), :] = piece[...]
+    down[pl.ds(pl.multiple_of(count // 2 * (1 - c), 128), count // 2), :] = d_m[...]
+    ins.wait()
 
 
 def norm_of(value):
@@ -732,24 +745,18 @@
 
 
 def forward_kernel(
-    a_own, a_got, xs, vecs, b_up, u_own, u_x, u_m, u_mx, d_own, d_m,
-    y_low, h_out, z, n_out, r_out, slope, y_out,
-    up, down, x_own, sems, more,
+    a_own, a_got, xs, vecs, b_up, up, down,
+    y_low, y_more, h_out, z, n_out, r_out, slope, y_out,
 ):
     q, r, x, c = spot()
-    rows = x_own.shape[0]
-    first = Copies(more)
-    first.start(xs.at[pl.ds(pl.multiple_of(rows * (2 * r + c), rows), rows)], x_own)
-    copies = Copies(sems)
-    load_feedforward(copies, up, down, u_own, u_x, u_m, u_mx, d_own, d_m)
-    first.wait()
-    total = x_own[...].astype(jnp.float32) + (a_own[...] + a_got[...].astype(jnp.float32) + vecs[2:3, :])
+    rows = a_own.shape[0]
+    x_own = xs[pl.ds(pl.multiple_of(rows * (2 * r + c), rows), rows), :]
+    total = x_own.astype(jnp.float32) + (a_own[...] + a_got[...].astype(jnp.float32) + vecs[2:3, :])
     normed, rstd = norm_of(total)
     n_out[...] = normed
     r_out[...] = jnp.broadcast_to(rstd, r_out.shape)
     low = (normed * vecs[3:4, :] + vecs[4:5, :]).astype(jnp.bfloat16)
     h_out[...] = low
-    copies.wait()
     wide = up.shape[1] // 4
     for j in range(4):
         at = slice(wide * j, wide * (j + 1))
@@ -760,22 +767,23 @@
         slope[:, at] = cdf + pre * density
     result = dot(z[...], down[...])
     y_out[...] = result
-    y_low[...] = result.astype(jnp.bfloat16)
+    rows = y_low.shape[0]
+    y_low[...] = result[0:rows, :].astype(jnp.bfloat16)
+    y_more[...] = result[rows:, :].astype(jnp.bfloat16)
 
 
 def norm_back_kernel(
-    y_own, y_got, normed1, g_own, g_x, vecs, low_out, hid_out, dy_out, sums, grad, hid, sems,
+    y_own, y_got, y_rest, normed1, g_own, g_x, vecs, low_out, hid_out, dy_out, sums, grad, hid,
 ):
     q, r, x, c = spot()
     rows = grad.shape[0] // 2
-    copies = Copies(sems)
-    copies.start(g_own, grad.at[pl.ds(pl.multiple_of(rows * x, rows), rows)])
-    copies.start(g_x, grad.at[pl.ds(pl.multiple_of(rows * (1 - x), rows), rows)])
+    grad[pl.ds(pl.multiple_of(rows * x, rows), rows), :] = g_own[...]
+    grad[pl.ds(pl.multiple_of(rows * (1 - x), rows), rows), :] = g_x[...]
+    got = jnp.concatenate([y_got[...], y_rest[...]]).astype(jnp.float32)
     h1 = normed1[...] * vecs[3:4, :] + vecs[4:5, :]
-    normed, rstd = norm_of(h1 + (y_own[...] + y_got[...].astype(jnp.float32) + vecs[5:6, :]))
+    normed, rstd = norm_of(h1 + (y_own[...] + got + vecs[5:6, :]))
     hid[...] = (normed * vecs[6:7, :] + vecs[7:8, :]).astype(jnp.bfloat16)
     hid_out[...] = hid[pl.ds(pl.multiple_of(rows * x, rows), rows), :]
-    copies.wait()
     cot = grad[...].astype(jnp.float32)
     dy = norm_pull(cot * vecs[6:7, :], normed, rstd)
     low = dy.astype(jnp.bfloat16)
@@ -787,13 +795,7 @@
     sums[2:3, :] = jnp.sum(cot, axis=0, keepdims=True)
 
 
-def backward_kernel(
-    dy, dy_low, slope, u_own, u_x, u_m, u_mx, d_own, d_m,
-    p_low, s_out, du_out, up_sums, up, down, sems,
-):
-    copies = Copies(sems)
-    load_feedforward(copies, up, down, u_own, u_x, u_m, u_mx, d_own, d_m)
-    copies.wait()
+def backward_kernel(dy, dy_low, slope, up, down, p_low, s_out, du_out, up_sums):
     low = dy_low[...]
     wide = up.shape[1] // 4
     for j in range(4):
@@ -864,7 +866,8 @@
         qv_sums[1:2, at] = jnp.sum(value.astype(jnp.float32), axis=0, keepdims=True)
 
 
-def input_grad_kernel(dq, dkv, w, send, keep, whole):
+def input_grad_kernel(dq, dkv, w, *refs):
+    sends, (keep, whole) = refs[:2], refs[2:]
     q, r, x, c = spot()
     half = dq.shape[1]
     rows = dq.shape[0] // 2
@@ -873,16 +876,32 @@
     whole[own, :] += dot_nt(dq[...], w[:, 0:half])
     for b in range(2):
         for i in range(2):
+            to = slice(2 * rows * b + rows * i, 2 * rows * b + rows * (i + 1))
             mine = pl.ds(pl.multiple_of(rows * (4 * i + 2 * c + b), rows), rows)
-            keep[2 * rows * b + rows * i : 2 * rows * b + rows * (i + 1), :] = whole[mine, :]
+            keep[to, :] = whole[mine, :]
             theirs = pl.ds(pl.multiple_of(rows * (4 * i + 2 * (1 - c) + b), rows), rows)
-            send[2 * rows * b + rows * i : 2 * rows * b + rows * (i + 1), :] = whole[theirs, :].astype(jnp.bfloat16)
+            sends[b][rows * i : rows * (i + 1), :] = whole[theirs, :].astype(jnp.bfloat16)
+
+
+def input_x_kernel(keep, got0, got1, send, kept):
+    q, r, x, c = spot()
+    half = send.shape[0]
+    for side, got in enumerate((got0, got1)):
+        total = keep[half * side : half * (side + 1), :] + got[...].astype(jnp.float32)
+
+        @pl.when(x == side)
+        def _():
+            kept[...] = total
+
+        @pl.when(x != side)
+        def _():
+            send[...] = total.astype(jnp.bfloat16)
 
 
 def octants():
     for at in range(8):
         r, q0, q1 = at >> 2, at >> 1 & 1, at & 1
-        yield at, 4 * r + 2 * q1 + q0
+        yield 4 * r + 2 * q0 + 1 * q1, 1 * r + 4 * q0 + 2 * q1, 4 * r + 2 * q1 + q0
 
 
 def down_grad_kernel(z, dy, send, keep):
@@ -891,7 +910,7 @@
     rows = half // 8
     for side, out in ((1 - c, send), (c, keep)):
         part = dot_tn(z[:, pl.ds(pl.multiple_of(half * side, 128), half)], dy[...])
-        for at, within in octants():
+        for at, _, within in octants():
             block = part[rows * within : rows * (within + 1), :]
             out[rows * at : rows * (at + 1), :] = block.astype(out.dtype)
 
@@ -902,7 +921,7 @@
     thin = width // 32
     whole[...] = dot_tn(h[...], du[...])
     for side, out in ((1 - c, send), (c, keep)):
-        for at, within in octants():
+        for _, at, within in octants():
             pieces = []
             for xx in range(2):
                 first = 8 * thin * (2 * xx + side) + thin * within
@@ -945,8 +964,9 @@
 
 
 def weight_grad_kernel(
-    xs, dkv, dq, mixed, da, sums1, sums2, qv_sums, up_sums, send, keep, packed, sems
+    xs, dkv, dq, mixed, da, sums1, sums2, qv_sums, up_sums, *refs
 ):
+    sends, (keep, packed) = refs[:-2], refs[-2:]
     q, r, x, c = spot()
     width = xs.shape[1]
     own, half = dq.shape
@@ -960,7 +980,7 @@
         for rr in range(2):
             for q1 in range(2):
                 for q0 in range(2):
-                    at = ((4 * rr + 2 * q0 + q1) * 8) * thin
+                    at = ((4 * rr + 2 * q0 + 1 * q1) * 8) * thin
                     within = (4 * rr + 2 * q1 + q0) * thin
                     for xx in range(2):
                         rows = slice((16 * xx + 8 * cc) * thin + within, (16 * xx + 8 * cc + 1) * thin + within)
@@ -979,16 +999,23 @@
             packed[cc, for_c + 2 + j : for_c + 3 + j, :] = up_sums[j, 0:1, :]
         packed[cc, for_c + 6 : for_c + 9, :] = sums1[0:3, columns]
         packed[cc, for_c + 9 : for_c + 12, :] = sums2[0:3, columns]
-    send[...] = packed[1 - c].astype(jnp.bfloat16)
-    copy = pltpu.make_async_copy(packed.at[c], keep, sems.at[0])
-    copy.start()
-    copy.wait()
-
-
-def step_kernel(bit, keep, got, send, kept, whole):
+    first = 0
+    for send in sends:
+        count = send.shape[0]
+        send[...] = packed[1 - c, first : first + count, :].astype(jnp.bfloat16)
+        first += count
+    keep[...] = packed[c]
+
+
+def step_kernel(bit, keep, *refs):
+    gots, (send, kept, whole) = refs[:-3], refs[-3:]
     at = bit(*spot())
     count = send.shape[0] - 16
-    whole[...] = keep[...] + got[...].astype(jnp.float32)
+    first = 0
+    for got in gots:
+        rows = slice(first, first + got.shape[0])
+        whole[rows, :] = keep[rows, :] + got[...].astype(jnp.float32)
+        first += got.shape[0]
     theirs = pl.ds(pl.multiple_of(count * (1 - at), 64), count)
     mine = pl.ds(pl.multiple_of(count * at, 64), count)
     send[0:count, :] = whole[theirs, :].astype(jnp.bfloat16)
@@ -1016,7 +1043,8 @@
     b_up[...] = line.reshape(b_up.shape[0])
 
 
-def down_out_kernel(near, far, out):
+def down_out_kernel(near, far, out, mark):
+    mark[...] = jnp.zeros_like(mark)
     q, r, x, c = spot()
     count = near.shape[0] // 4
     for d, piece in enumerate((near, far)):
@@ -1026,7 +1054,8 @@
             out[rows, :] = piece[count * k : count * (k + 1), :].astype(jnp.float32)
 
 
-def up_out_kernel(near, far, out, whole):
+def up_out_kernel(near, far, out, mark, whole):
+    mark[...] = jnp.zeros_like(mark)
     q, r, x, c = spot()
     thin, width = near.shape[0] // 16, near.shape[1]
     for d, piece in enumerate((near, far)):
@@ -1062,7 +1091,7 @@
                 out_o[rows, columns] = whole[first + thin * (3 + t) : first + thin * (4 + t), :]
 
 
-def kernel_call(body, name, ins, outs, scratch, args, after=(), room=2 << 20):
+def kernel_call(body, name, ins, outs, scratch, args, after=(), room=2 << 20, cost=1):
     count = len(args)
 
     def size(shape, dtype):
@@ -1085,7 +1114,7 @@
         in_specs=list(ins) + [ANY] * len(after),
         out_specs=[spec for _, _, spec in outs],
         scratch_shapes=scratch,
-        cost_estimate=pl.CostEstimate(flops=1, bytes_accessed=1, transcendentals=0),
+        cost_estimate=pl.CostEstimate(flops=cost, bytes_accessed=1, transcendentals=0),
         compiler_params=pltpu.CompilerParams(vmem_limit_bytes=used + room),
     )(*args, *after)
 
@@ -1101,6 +1130,9 @@
         cost_estimate=pl.CostEstimate(flops=1, bytes_accessed=1, transcendentals=0),
         compiler_params=pltpu.CompilerParams(vmem_limit_bytes=1 << 18),
     )(value, *after)
+
+
+HEAVY = ('attend_back', 'down_sum', 'project')
 
 
 def plane_local(
@@ -1120,9 +1152,11 @@
     latest = []
 
     def call(body, name, ins, outs, scratch, args, after=(), **more):
-        results = kernel_call(body, name, ins, outs, scratch, args, tuple(after) + tuple(latest), **more)
-        if len(results) > 1 or not name.endswith("_out"):
-            latest[:] = results[:1]
+        cost = 10**10 if name in HEAVY else 1
+        results = kernel_call(
+            body, name, ins, outs, scratch, args, tuple(after) + tuple(latest), cost=cost, **more
+        )
+        latest[:] = results[-1:] if name.endswith("_out") else results[:1]
         return results
 
     (block,) = call(
@@ -1151,74 +1185,84 @@
     blocks.append(swap_c(blocks[1]))
     blocks.append(beside_r)
     blocks.append(swap_r(blocks[1]))
-    blocks.append(swap_c(blocks[4]))
-    blocks.append(swap_c(blocks[5]))
     qkv_mx = swap_c(qkv_x)
     up_theirs, up_mine = call(
         cut_kernel, "cut", [HBM], [((part, 4 * wide), low, WHOLE)] * 2, [pltpu.SemaphoreType.DMA((2,))],
-        (w_up,), after=(blocks[3],),
+        (w_up,), after=(blocks[1],),
     )
     up_x = swap_x(up_theirs)
     up_m = swap_c(up_mine)
-    up_mx = swap_c(up_x)
     down_m = swap_c(w_down)
     (cot,) = call(
         load_kernel, "cotangent", [HBM], [((rows, width), low, WHOLE)], [pltpu.SemaphoreType.DMA((1,))],
         (cotangent[0],),
     )
     cot, cot_x = regroup(cot), regroup_x(cot)
-
-    (
-        a_low, x_all, w_all, wo_all, k3, v3, q3, mixed, lse, ids, a_own, vecs, up_bias
-    ) = call(
+    kv_own, q_own, w_all, vecs, up_bias = call(
+        project_kernel,
+        "project",
+        [WHOLE] * 4 + [HBM] * 3 + [WHOLE] * 4,
+        [
+            ((4 * rows, width), low, WHOLE),
+            ((own, half), low, WHOLE),
+            ((width, 3 * half), low, WHOLE),
+            ((8, width), exact, WHOLE),
+            ((4, 8, wide), exact, WHOLE),
+        ],
+        [pltpu.VMEM((4 * rows, width), low), pltpu.SemaphoreType.DMA((3,))],
+        (*blocks[:4], w_query, w_key, w_value, qkv_x, qkv_m, qkv_mx, mine),
+        room=8 << 20,
+    )
+    blocks[5] = once(blocks[5], kv_own)
+    blocks.append(swap_c(blocks[4]))
+    blocks.append(swap_c(blocks[5]))
+    a_low, x_all, wo_all, k3, v3, q3, mixed, lse, ids, a_own = call(
         attend_kernel,
         "attend",
-        [ANY] * 8 + [HBM] * 3 + [ANY] * 4 + [HBM, ANY],
+        [WHOLE] * 12 + [HBM, WHOLE],
         [
             ((own, width), low, WHOLE),
-            ((keys, width), low, ANY),
-            ((width, 3 * half), low, ANY),
-            ((half, width), low, ANY),
-            ((pairs, keys, 128), low, ANY),
-            ((pairs, keys, 128), low, ANY),
+            ((keys, width), low, WHOLE),
+            ((half, width), low, WHOLE),
+            ((pairs, keys, 128), low, WHOLE),
+            ((pairs, keys, 128), low, WHOLE),
             ((pairs, own, 128), low, WHOLE),
             ((own, half), low, WHOLE),
             ((8, own), exact, WHOLE),
             ((8, rows), exact, WHOLE),
             ((own, width), exact, WHOLE),
-            ((8, width), exact, WHOLE),
-            ((4, 8, wide), exact, WHOLE),
         ],
         [
-            pltpu.VMEM((keys, width), low),
-            pltpu.VMEM((8, 16, width), low),
-            pltpu.VMEM((width, 3 * half), low),
-            pltpu.VMEM((half, width), low),
-            pltpu.VMEM((4, 16, half), low),
-            pltpu.VMEM((pairs, keys, 128), low),
-            pltpu.VMEM((pairs, keys, 128), low),
             pltpu.VMEM((2 * pairs, 64, keys), low),
-            pltpu.VMEM((pairs, own, 128), low),
             pltpu.VMEM((2 * pairs, 64, own), exact),
             pltpu.VMEM((keys, own), exact),
-            pltpu.SemaphoreType.DMA((34,)),
-            pltpu.SemaphoreType.DMA((5,)),
+            pltpu.SemaphoreType.DMA((1,)),
         ],
-        (*blocks, w_query, w_key, w_value, qkv_x, qkv_m, qkv_mx, mine, w_out, out_m),
+        (*blocks, kv_own, q_own, w_all, vecs, w_out, out_m),
+        after=(down_m,),
         room=8 << 20,
     )
     a_got = swap_x(a_low)
-    (kt,) = call(turn_kernel, "turn", [WHOLE], [((2 * pairs, 64, keys), low, WHOLE)], [], (k3,))
-
-    inner_weights = (w_up, up_x, up_m, up_mx, w_down, down_m)
-    inner_specs = [HBM, ANY, ANY, ANY, HBM, ANY]
-    inner_scratch = [pltpu.VMEM((width, 4 * wide), low), pltpu.VMEM((4 * wide, width), low)]
-    y_low, h_low, z, normed1, rstd1, slope, y_own = call(
+    up_x = once(up_x, a_low)
+    up_mx = swap_c(up_x)
+    (kt,) = call(turn_kernel, "turn", [WHOLE], [((2 * pairs, 64, keys), low, WHOLE)], [], (k3,),
+        after=(up_m,))
+
+    inner_weights = call(
+        inner_kernel,
+        "inner",
+        [HBM, WHOLE, WHOLE, WHOLE, HBM, WHOLE],
+        [((width, 4 * wide), low, WHOLE), ((4 * wide, width), low, WHOLE)],
+        [pltpu.SemaphoreType.DMA((2,))],
+        (w_up, up_x, up_m, up_mx, w_down, down_m),
+    )
+    y_low, y_more, h_low, z, normed1, rstd1, slope, y_own = call(
         forward_kernel,
         "feedforward",
-        [WHOLE, WHOLE, ANY, WHOLE, WHOLE] + inner_specs,
+        [WHOLE] * 7,
         [
-            ((own, width), low, WHOLE),
+            ((rows, width), low, WHOLE),
+            ((rows, width), low, WHOLE),
             ((own, width), low, WHOLE),
             ((own, 4 * wide), low, WHOLE),
             ((own, width), exact, WHOLE),
@@ -1226,17 +1270,15 @@
             ((own, 4 * wide), exact, WHOLE),
             ((own, width), exact, WHOLE),
         ],
-        inner_scratch
-        + [pltpu.VMEM((own, width), low), pltpu.SemaphoreType.DMA((6,)), pltpu.SemaphoreType.DMA((1,))],
+        [],
         (a_own, a_got, x_all, vecs, up_bias, *inner_weights),
-        after=(cot, cot_x),
         room=8 << 20,
     )
-    y_got = swap_x(y_low)
+    y_got, y_rest = swap_x(y_low), swap_x(y_more)
     dy_low, hidden, dy, sums2 = call(
         norm_back_kernel,
         "norm_back",
-        [WHOLE, WHOLE, WHOLE, ANY, ANY, WHOLE],
+        [WHOLE] * 7,
         [
             ((own, width), low, WHOLE),
             ((rows, width), low, WHOLE),
@@ -1246,9 +1288,8 @@
         [
             pltpu.VMEM((own, width), low),
             pltpu.VMEM((own, width), low),
-            pltpu.SemaphoreType.DMA((2,)),
         ],
-        (y_own, y_got, normed1, cot, cot_x, vecs),
+        (y_own, y_got, y_rest, normed1, cot, cot_x, vecs),
         room=6 << 20,
     )
     eighth = wide // 4
@@ -1265,18 +1306,19 @@
     p_low, s_own, du, up_sums = call(
         backward_kernel,
         "feedforward_back",
-        [WHOLE] * 3 + inner_specs,
+        [WHOLE] * 5,
         [
             ((own, width), low, WHOLE),
             ((own, width), exact, WHOLE),
             ((own, 4 * wide), low, WHOLE),
             ((4, 8, wide), exact, WHOLE),
         ],
-        inner_scratch + [pltpu.SemaphoreType.DMA((6,))],
+        [],
         (dy, dy_low, slope, *inner_weights),
         room=8 << 20,
     )
     p_got = swap_x(p_low)
+    hidden = regroup(hidden)
 
     def fold(name, bit, keep, got):
         shape = (keep.shape[0] // 2, keep.shape[1])
@@ -1299,7 +1341,26 @@
     def bit_far(q, r, x, c):
         return q // 2
 
-    down_send, down_keep = fold("down_r", bit_r, down_keep, down_got)
+    thin = part // 8
+    count = 64 * thin
+
+    def step(name, bit, keep, size, *gots):
+        return call(
+            lambda *refs: step_kernel(bit, *refs),
+            name,
+            [WHOLE] * (1 + len(gots)),
+            [((size + 16, half), low, WHOLE), ((size + 16, half), exact, WHOLE)],
+            [pltpu.VMEM((2 * size + 16, half), exact)],
+            (keep, *gots),
+        )
+
+    def join(name, *pieces):
+        shape = (sum(p.shape[0] for p in pieces), pieces[0].shape[1])
+        (out,) = call(join_kernel, name, [WHOLE] * len(pieces), [(shape, low, WHOLE)], [], pieces)
+        return out
+
+    cuts = (count // 3, count // 3, count - 2 * (count // 3) + 16)
+    down_send, down_keep = fold("down_1", bit_r, down_keep, down_got)
     down_got = swap_r(down_send)
     up_send, up_keep = call(
         up_grad_kernel,
@@ -1311,7 +1372,10 @@
         room=8 << 20,
     )
     up_got = swap_c(up_send)
-
+    up_send, up_keep = fold("up_1", bit_near, up_keep, up_got)
+    up_got = swap_near(up_send)
+    down_send, down_keep = fold("down_2", bit_near, down_keep, down_got)
+    down_got = swap_near(down_send)
     dkv, dq, dr, da, sums1, qv_sums = call(
         attend_back_kernel,
         "attend_back",
@@ -1337,72 +1401,53 @@
         room=8 << 20,
     )
 
-    thin = part // 8
-    count = 64 * thin
-
-    def step(name, bit, keep, got, size):
-        return call(
-            lambda *refs: step_kernel(bit, *refs),
-            name,
-            [WHOLE] * 2,
-            [((size + 16, half), low, WHOLE), ((size + 16, half), exact, WHOLE)],
-            [pltpu.VMEM((2 * size + 16, half), exact)],
-            (keep, got),
-        )
-
-    def join(name, *pieces):
-        shape = (sum(p.shape[0] for p in pieces), pieces[0].shape[1])
-        (out,) = call(join_kernel, name, [WHOLE] * len(pieces), [(shape, low, WHOLE)], [], pieces)
-        return out
-
-    up_send, up_keep = fold("up_r", bit_r, up_keep, up_got)
-    up_got = swap_r(up_send)
-    rest_send, rest_keep = call(
+    *rest_sends, rest_keep = call(
         weight_grad_kernel,
         "weight_grad",
         [WHOLE] * 9,
-        [((count + 16, half), low, WHOLE), ((count + 16, half), exact, ANY)],
-        [pltpu.VMEM((2, count + 16, half), exact), pltpu.SemaphoreType.DMA((1,))],
+        [((n, half), low, WHOLE) for n in cuts] + [((count + 16, half), exact, WHOLE)],
+        [pltpu.VMEM((2, count + 16, half), exact)],
         (x_all, dkv, dq, mixed, da, sums1, sums2, qv_sums, up_sums),
+        after=(hidden,),
         room=8 << 20,
     )
-    rest_got = swap_c(rest_send)
-    down_send, down_keep = fold("down_near", bit_near, down_keep, down_got)
-    down_got = swap_near(down_send)
-    x_send, x_keep = call(
+    rest_gots = [swap_c(send) for send in rest_sends]
+    up_send, up_keep = fold("up_2", bit_far, up_keep, up_got)
+    up_got = swap_far(up_send)
+    rest_send, rest_keep = step("rest_1", bit_r, rest_keep, count // 2, *rest_gots)
+    rest_got = swap_r(rest_send)
+    *x_sends, x_keep = call(
         input_grad_kernel,
         "input_grad",
         [WHOLE] * 3,
-        [((2 * own, width), low, WHOLE), ((2 * own, width), exact, WHOLE)],
+        [((own, width), low, WHOLE)] * 2 + [((2 * own, width), exact, WHOLE)],
         [pltpu.VMEM((keys, width), exact)],
         (dq, dkv, w_all),
         room=8 << 20,
     )
-    x_got = swap_c(x_send)
-    rest_send, rest_keep = step("rest_r", bit_r, rest_keep, rest_got, count // 2)
-    rest_got = swap_r(rest_send)
-    x_send, x_keep = fold("input_x", lambda q, r, x, c: x, x_keep, x_got)
+    x_gots = [swap_c(send) for send in x_sends]
+    down_send, down_keep = fold("down_3", bit_far, down_keep, down_got)
+    down_got = swap_far(down_send)
+    x_send, x_keep = call(
+        input_x_kernel,
+        "input_x",
+        [WHOLE] * 3,
+        [((own, width), low, WHOLE), ((own, width), exact, WHOLE)],
+        [],
+        (x_keep, *x_gots),
+        room=4 << 20,
+    )
     x_got = swap_x(x_send)
-    down_send, down_keep = fold("down_far", bit_far, down_keep, down_got)
-    down_got = swap_far(down_send)
-    up_send, up_keep = fold("up_near", bit_near, up_keep, up_got)
-    up_got = swap_near(up_send)
+    up_send, up_keep = fold("up_3", bit_r, up_keep, up_got)
+    up_got = swap_r(up_send)
+    (down_sum,) = call(
+        sum_kernel, "down_sum", [WHOLE] * 2, [((eighth, width), low, WHOLE)], [], (down_keep, down_got)
+    )
+    down_other = swap_far(down_sum)
+    rest_send, rest_keep = step("rest_2", bit_near, rest_keep, count // 4, rest_got)
+    rest_got = swap_near(rest_send)
     x_send, x_keep = fold("input_r", bit_r, x_keep, x_got)
     x_got = swap_r(x_send)
-    (down_sum,) = call(
-        sum_kernel, "down_sum", [WHOLE] * 2, [((eighth, width), low, WHOLE)], [], (down_keep, down_got)
-    )
-    down_other = swap_far(down_sum)
-    up_send, up_keep = fold("up_far", bit_far, up_keep, up_got)
-    up_got = swap_far(up_send)
-    rest_send, rest_keep = step("rest_near", bit_near, rest_keep, rest_got, count // 4)
-    rest_got = swap_near(rest_send)
-    (total,) = call(
-        total_kernel, "input_sum", [WHOLE] * 3, [((rows, width), low, WHOLE)], [], (x_keep, x_got, dr)
-    )
-    total = regroup(total)
-    down_sum = join("down_join", down_sum, down_other)
-    down_other = swap_near(down_sum)
     side, base = call(
         share_kernel,
         "up_share",
@@ -1412,12 +1457,16 @@
         (up_keep.reshape(2, eighth // 2, width), up_got.reshape(2, eighth // 2, width)),
     )
     side = swap_x(side)
-    rest_send, rest_keep = step("rest_far", bit_far, rest_keep, rest_got, count // 8)
+    down_sum = join("down_join", down_sum, down_other)
+    down_other = swap_near(down_sum)
+    rest_send, rest_keep = step("rest_3", bit_far, rest_keep, count // 8, rest_got)
     rest_got = swap_far(rest_send)
     up_sum = join("up_join", base, side)
     up_other = swap_far(up_sum)
-    down_near = join("down_join_near", down_sum, down_other)
-    down_far = swap_r(down_near)
+    (total,) = call(
+        total_kernel, "input_sum", [WHOLE] * 3, [((rows, width), low, WHOLE)], [], (x_keep, x_got, dr)
+    )
+    total = regroup(total)
     side, base, *lines, b_up_grad = call(
         last_step_kernel,
         "rest_last",
@@ -1429,26 +1478,30 @@
         (rest_keep, rest_got),
     )
     side = swap_x(side)
-    hidden = regroup(hidden)
+    down_near = join("down_join_near", down_sum, down_other)
+    down_far = swap_r(down_near)
     up_sum = join("up_join_far", up_sum, up_other)
     up_other = swap_near(up_sum)
     rest_sum = join("rest_join", base, side)
     rest_other = swap_far(rest_sum)
     up_near = join("up_join_near", up_sum, up_other)
     up_far = swap_r(up_near)
+    w_down_grad, _ = call(
+        down_out_kernel, "down_out", [WHOLE] * 2,
+        [((2 * wide, width), exact, WHOLE), ((8, 128), exact, WHOLE)], [], (down_near, down_far),
+        room=6 << 20,
+    )
     rest_sum = join("rest_join_far", rest_sum, rest_other)
     rest_other = swap_near(rest_sum)
     rest_near = join("rest_join_near", rest_sum, rest_other)
     rest_far = swap_r(rest_near)
-    (w_down_grad,) = call(
-        down_out_kernel, "down_out", [WHOLE] * 2, [((2 * wide, width), exact, WHOLE)], [], (down_near, down_far),
-        room=6 << 20,
-    )
-    (w_up_grad,) = call(
-        up_out_kernel, "up_out", [WHOLE] * 2, [((part, inner), exact, WHOLE)],
+    w_up_grad, _ = call(
+        up_out_kernel, "up_out", [WHOLE] * 2, [((part, inner), exact, WHOLE), ((8, 128), exact, WHOLE)],
         [pltpu.VMEM((4 * eighth, width), exact)], (up_near, up_far),
         room=6 << 20,
     )
+
+
     w_query_grad, w_key_grad, w_value_grad, w_out_grad, hidden_out, tokens_grad = call(
         rest_out_kernel,
         "rest_out",
@@ -1458,6 +1511,7 @@
         (rest_near, rest_far, hidden, total),
         room=6 << 20,
     )
+
     return (
         hidden_out[None],
         tokens_grad[None],

time: 234 us -> 212 us (0.906)
  waiting for transfers between devices: 131 us -> 109 us
  starting transfers between devices: 54.7 us -> 60.4 us
  Pallas kernels: 46.3 us -> 41 us
    ppermute x49 -> x53, waiting for transfers between devices: 131 us -> 109 us  [moved(): lax.ppermute(block, AXES, [(number(s), number(move(*s))) for s in spots])]
    ppermute x49 -> x53, starting transfers between devices: 54.7 us -> 60.4 us  [moved(): lax.ppermute(block, AXES, [(number(s), number(move(*s))) for s in spots])]
    pallas_call x40 -> x42, Pallas kernels: 46.3 us -> 41 us  [kernel_call(): pl.pallas_call(run, name=name, out_shape=[jax.ShapeDtypeStruct(shape, dty...]
  transfers between devices with their start and end apart: 49 -> 53, of which waited for: 28 -> 28; matrix products, arithmetic and copies ran while one was open for 0% -> 0% of each run, Pallas kernels for 15% -> 16%
where the time goes in v4:
time: 212 us; the launch traced here: 211 us
  waiting for transfers between devices  109 us (51%)
  starting transfers between devices  60.4 us (28%)
  Pallas kernels  41 us (19%)
    ppermute x53, waiting for transfers between devices, moved(): lax.ppermute(block, AXES, [(number(s), number(move(*s))) for s in spots])  109 us
    ppermute x53, starting transfers between devices, moved(): lax.ppermute(block, AXES, [(number(s), number(move(*s))) for s in spots])  60.4 us
    pallas_call x42, Pallas kernels, kernel_call(): pl.pallas_call(run, name=name, out_shape=[jax.ShapeDtypeStruct(shape, dty...  41 us
  transfers between devices with their start and end apart: 53, of which 28 were waited for; matrix products, arithmetic and copies ran while one was open for 0% of the time, Pallas kernels for 16%

profile of v4, /device:TPU:0, one launch (start us, length us, event | category | flops | bytes accessed | tf_op | source)
XLA Modules:
  0.0 211.3 jit_solution(16094039278185025710)
XLA Ops:
  0.7 1.0 block.1.refs_12_
  1.6 1.6 pack.1
  3.2 3.0 %collective-permute-start.2 = (bf16[592,384]{1,0:T(8,128)(2,1)S(1)}, bf16[592,384]{1,0:T(8,128)(2,1)S(1)}, u32[]{:S(2)}, u32[]{:S(2)}) collective-permute-start(bf16[592,384]{1,0:T(8,128)(2,1)S(1)} %get-tuple-element.117.refs_2_), channel_id=1, source_target_pairs={{0,2},{1,3},{2,0},{3,1},{4,6},{5,7},{6,4},{7,5},{8,10},{9,11},{10,... | collective-permute-start | bytes 1363976 | tf_op jit(solution)/shard_map/ppermute | solution.py:480
  7.4 13.2 %collective-permute-done.2.refs_2_.refs_7_ = bf16[592,384]{1,0:T(8,128)(2,1)S(1)} collective-permute-done((bf16[592,384]{1,0:T(8,128)(2,1)S(1)}, bf16[592,384]{1,0:T(8,128)(2,1)S(1)}, u32[]{:S(2)}, u32[]{:S(2)}) %collective-permute-start.2) | collective-permute-done | bytes 454688 | tf_op jit(solution)/shard_map/ppermute | solution.py:480
  20.7 1.6 collective-permute-start.5
  22.3 2.5 %collective-permute-start.4 = (bf16[144,768]{1,0:T(8,128)(2,1)S(1)}, bf16[144,768]{1,0:T(8,128)(2,1)S(1)}, u32[]{:S(2)}, u32[]{:S(2)}) collective-permute-start(bf16[144,768]{1,0:T(8,128)(2,1)S(1)} %once.4.refs_0_), channel_id=1, source_target_pairs={{0,2},{1,3},{2,0},{3,1},{4,6},{5,7},{6,4},{7,5},{8,10},{9,11},{10,... | collective-permute-start | bytes 663560 | tf_op jit(solution)/shard_map/ppermute | solution.py:480
  24.8 3.8 %collective-permute-done.5.refs_1_.refs_4_ = bf16[144,768]{1,0:T(8,128)(2,1)S(1)} collective-permute-done((bf16[144,768]{1,0:T(8,128)(2,1)S(1)}, bf16[144,768]{1,0:T(8,128)(2,1)S(1)}, u32[]{:S(2)}, u32[]{:S(2)}) %collective-permute-start.5) | collective-permute-done | bytes 221216 | tf_op jit(solution)/shard_map/ppermute | solution.py:480
  28.6 2.0 collective-permute-done.4.refs_0_
  31.6 1.3 cut.1
  32.9 0.9 cotangent.1.refs_11_
  33.8 1.8 collective-permute-start.14
  35.6 2.3 %project.1 = (bf16[512,768]{1,0:T(8,128)(2,1)S(1)}, bf16[256,384]{1,0:T(8,128)(2,1)S(1)}, bf16[768,1152]{1,0:T(8,128)(2,1)S(1)}, f32[8,768]{1,0:T(8,128)S(1)}, f32[4,8,384]{2,1,0:T(8,128)S(1)}) custom-call(bf16[144,768]{1,0:T(8,128)(2,1)S(1)} %once.4.refs_0_, bf16[144,768]{1,0:T(8,128)(2,1)S(1)} %once.5.refs_1_, ...), custom_call_target="tpu_custom_call" | custom-call | flops 10000000000 | bytes 1 | tf_op jit(solution)/shard_map/project/pallas_call | solution.py:1110
  38.9 1.0 collective-permute-done.11.refs_7_
  39.9 6.4 %attend.1 = (bf16[256,768]{1,0:T(8,128)(2,1)S(1)}, bf16[1024,768]{1,0:T(8,128)(2,1)S(1)}, bf16[384,768]{1,0:T(8,128)(2,1)S(1)}, bf16[3,1024,128]{2,1,0:T(8,128)(...) custom-call(bf16[144,768]{1,0:T(8,128)(2,1)S(1)} %once.4.refs_0_, ...), custom_call_target="tpu_custom_call" | custom-call | flops 1 | bytes 1 | tf_op jit(solution)/shard_map/attend/pallas_call | solution.py:1110
  46.4 2.5 %collective-permute-done.14.refs_0_ = bf16[192,1536]{1,0:T(8,128)(2,1)S(1)} collective-permute-done((bf16[192,1536]{1,0:T(8,128)(2,1)S(1)}, bf16[192,1536]{1,0:T(8,128)(2,1)S(1)}, u32[]{:S(2)}, u32[]{:S(2)}) %collective-permute-start.14) | collective-permute-done | bytes 589856 | tf_op jit(solution)/shard_map/ppermute | solution.py:480
  48.8 1.7 collective-permute-start.13
  50.9 0.8 collective-permute-start.19
  52.0 1.5 inner.1
  53.5 10.4 %collective-permute-done.13.refs_1_ = bf16[256,768]{1,0:T(8,128)(2,1)S(1)} collective-permute-done((bf16[256,768]{1,0:T(8,128)(2,1)S(1)}, bf16[256,768]{1,0:T(8,128)(2,1)S(1)}, u32[]{:S(2)}, u32[]{:S(2)}) %collective-permute-start.13) | collective-permute-done | bytes 393248 | tf_op jit(solution)/shard_map/ppermute | solution.py:480
  63.9 2.0 feedforward.1
  65.9 4.6 %collective-permute-start.18 = (bf16[128,768]{1,0:T(8,128)(2,1)S(1)}, bf16[128,768]{1,0:T(8,128)(2,1)S(1)}, u32[]{:S(2)}, u32[]{:S(2)}) collective-permute-start(bf16[128,768]{1,0:T(8,128)(2,1)S(1)} %get-tuple-element.133), channel_id=1, source_target_pairs={{0,2},{1,3},{2,0},{3,1},{4,6},{5,7},{6,4},{7,5},{8,10},{9,11},{10,... | collective-permute-start | bytes 589832 | tf_op jit(solution)/shard_map/ppermute | solution.py:480
  70.6 4.7 %collective-permute-done.18.refs_2_ = bf16[128,768]{1,0:T(8,128)(2,1)S(1)} collective-permute-done((bf16[128,768]{1,0:T(8,128)(2,1)S(1)}, bf16[128,768]{1,0:T(8,128)(2,1)S(1)}, u32[]{:S(2)}, u32[]{:S(2)}) %collective-permute-start.18) | collective-permute-done | bytes 196640 | tf_op jit(solution)/shard_map/ppermute | solution.py:480
  75.3 2.1 collective-permute-done.17.refs_1_
  77.4 0.9 norm_back.1
  79.2 1.7 feedforward_back.1
  80.9 1.2 collective-permute-done.22
  82.3 1.3 up_grad.1
  83.8 1.5 collective-permute-start.23
  85.3 1.7 collective-permute-start.21
  87.1 0.9 collective-permute-start.25
  88.2 3.8 %collective-permute-start.29 = (bf16[384,768]{1,0:T(8,128)(2,1)S(1)}, bf16[384,768]{1,0:T(8,128)(2,1)S(1)}, u32[]{:S(2)}, u32[]{:S(2)}) collective-permute-start(bf16[384,768]{1,0:T(8,128)(2,1)S(1)} %get-tuple-element.156.refs_2_), channel_id=1, source_target_pairs={{0,8},{1,9},{2,10},{3,11},{4,12},{5,13},{6,14},{7,15},{8,0},{9,1},... | collective-permute-start | bytes 1769480 | tf_op jit(solution)/shard_map/ppermute | solution.py:480
  92.0 7.4 %collective-permute-done.23 = bf16[384,768]{1,0:T(8,128)(2,1)S(1)} collective-permute-done((bf16[384,768]{1,0:T(8,128)(2,1)S(1)}, bf16[384,768]{1,0:T(8,128)(2,1)S(1)}, u32[]{:S(2)}, u32[]{:S(2)}) %collective-permute-start.23) | collective-permute-done | bytes 589856 | tf_op jit(solution)/shard_map/ppermute | solution.py:480
  99.9 6.6 %attend_back.1 = (bf16[1024,768]{1,0:T(8,128)(2,1)S(1)}, bf16[256,384]{1,0:T(8,128)(2,1)S(1)}, f32[128,768]{1,0:T(8,128)S(1)}, bf16[256,768]{1,0:T(8,128)(2,1)S(...) custom-call(f32[256,768]{1,0:T(8,128)S(1)} %get-tuple-element.140.refs_0_, ...), custom_call_target="tpu_custom_call" | custom-call | flops 10000000000 | bytes 1 | tf_op jit(solution)/shard_map/attend_back/pallas_call | solution.py:1110
  106.5 2.6 %weight_grad.1 = (bf16[512,384]{1,0:T(8,128)(2,1)S(1)}, bf16[512,384]{1,0:T(8,128)(2,1)S(1)}, bf16[528,384]{1,0:T(8,128)(2,1)S(1)}, f32[1552,384]{1,0:T(8,128)S(1)}) custom-call(bf16[1024,768]{1,0:T(8,128)(2,1)S(1)} %get-tuple-element.123.refs_2_.refs_0_, bf16[1024,768]{1,0:T(8,128)(2,1)S(1)} %get-tuple-element.158.refs_1_.refs_10_, ...), custom_call_target="tpu_custom_call" | custom-call | flops 1 | bytes 1 | tf_op jit(solution)/shard_map/weight_grad/pallas_call | solution.py:1110
  109.8 4.7 %collective-permute-start.31 = (bf16[192,768]{1,0:T(8,128)(2,1)S(1)}, bf16[192,768]{1,0:T(8,128)(2,1)S(1)}, u32[]{:S(2)}, u32[]{:S(2)}) collective-permute-start(bf16[192,768]{1,0:T(8,128)(2,1)S(1)} %get-tuple-element.157.refs_13_), channel_id=1, source_target_pairs={{0,8},{1,9},{2,10},{3,11},{4,12},{5,13},{6,14},{7,15},{8,0},{9,1},... | collective-permute-start | bytes 884744 | tf_op jit(solution)/shard_map/ppermute | solution.py:480
  115.1 2.1 input_grad.1
  117.7 2.6 %collective-permute-start.33 = (bf16[192,768]{1,0:T(8,128)(2,1)S(1)}, bf16[192,768]{1,0:T(8,128)(2,1)S(1)}, u32[]{:S(2)}, u32[]{:S(2)}) collective-permute-start(bf16[192,768]{1,0:T(8,128)(2,1)S(1)} %get-tuple-element.171.refs_4_), channel_id=1, source_target_pairs={{0,16},{1,17},{2,18},{3,19},{4,20},{5,21},{6,22},{7,23},{8,24},{9,... | collective-permute-start | bytes 884744 | tf_op jit(solution)/shard_map/ppermute | solution.py:480
  120.3 4.5 %collective-permute-done.31 = bf16[192,768]{1,0:T(8,128)(2,1)S(1)} collective-permute-done((bf16[192,768]{1,0:T(8,128)(2,1)S(1)}, bf16[192,768]{1,0:T(8,128)(2,1)S(1)}, u32[]{:S(2)}, u32[]{:S(2)}) %collective-permute-start.31) | collective-permute-done | bytes 294944 | tf_op jit(solution)/shard_map/ppermute | solution.py:480
  125.9 1.9 collective-permute-start.39
  127.7 10.2 %collective-permute-done.33 = bf16[192,768]{1,0:T(8,128)(2,1)S(1)} collective-permute-done((bf16[192,768]{1,0:T(8,128)(2,1)S(1)}, bf16[192,768]{1,0:T(8,128)(2,1)S(1)}, u32[]{:S(2)}, u32[]{:S(2)}) %collective-permute-start.33) | collective-permute-done | bytes 294944 | tf_op jit(solution)/shard_map/ppermute | solution.py:480
  138.0 2.3 %collective-permute-done.32.refs_1_ = bf16[96,768]{1,0:T(8,128)(2,1)S(1)} collective-permute-done((bf16[96,768]{1,0:T(8,128)(2,1)S(1)}, bf16[96,768]{1,0:T(8,128)(2,1)S(1)}, u32[]{:S(2)}, u32[]{:S(2)}) %collective-permute-start.32) | collective-permute-done | bytes 147488 | tf_op jit(solution)/shard_map/ppermute | solution.py:480
  140.6 1.2 collective-permute-start.36
  142.3 3.4 %collective-permute-start.37 = (bf16[96,768]{1,0:T(8,128)(2,1)S(1)}, bf16[96,768]{1,0:T(8,128)(2,1)S(1)}, u32[]{:S(2)}, u32[]{:S(2)}) collective-permute-start(bf16[96,768]{1,0:T(8,128)(2,1)S(1)} %down_sum.1.refs_2_.refs_0_), channel_id=1, source_target_pairs={{0,16},{1,17},{2,18},{3,19},{4,20},{5,21},{6,22},{7,23},{8,24},{9,... | collective-permute-start | bytes 442376 | tf_op jit(solution)/shard_map/ppermute | solution.py:480
  145.8 1.2 collective-permute-done.38
  147.0 4.3 %collective-permute-done.37.refs_1_ = bf16[96,768]{1,0:T(8,128)(2,1)S(1)} collective-permute-done((bf16[96,768]{1,0:T(8,128)(2,1)S(1)}, bf16[96,768]{1,0:T(8,128)(2,1)S(1)}, u32[]{:S(2)}, u32[]{:S(2)}) %collective-permute-start.37) | collective-permute-done | bytes 147488 | tf_op jit(solution)/shard_map/ppermute | solution.py:480
  151.4 4.2 %collective-permute-start.45 = (bf16[192,768]{1,0:T(8,128)(2,1)S(1)}, bf16[192,768]{1,0:T(8,128)(2,1)S(1)}, u32[]{:S(2)}, u32[]{:S(2)}) collective-permute-start(bf16[192,768]{1,0:T(8,128)(2,1)S(1)} %down_join.1.refs_2_.refs_0_), channel_id=1, source_target_pairs={{0,8},{1,9},{2,10},{3,11},{4,12},{5,13},{6,14},{7,15},{8,0},{9,1},... | collective-permute-start | bytes 884744 | tf_op jit(solution)/shard_map/ppermute | solution.py:480
  156.6 4.1 %collective-permute-done.42.refs_1_ = bf16[48,768]{1,0:T(8,128)(2,1)S(1)} collective-permute-done((bf16[48,768]{1,0:T(8,128)(2,1)S(1)}, bf16[48,768]{1,0:T(8,128)(2,1)S(1)}, u32[]{:S(2)}, u32[]{:S(2)}) %collective-permute-start.42) | collective-permute-done | bytes 73760 | tf_op jit(solution)/shard_map/ppermute | solution.py:480
  161.3 3.2 %collective-permute-done.40.refs_1_ = bf16[208,384]{1,0:T(8,128)(2,1)S(1)} collective-permute-done((bf16[208,384]{1,0:T(8,128)(2,1)S(1)}, bf16[208,384]{1,0:T(8,128)(2,1)S(1)}, u32[]{:S(2)}, u32[]{:S(2)}) %collective-permute-start.40) | collective-permute-done | bytes 159776 | tf_op jit(solution)/shard_map/ppermute | solution.py:480
  165.3 2.1 %collective-permute-start.47 = (bf16[384,768]{1,0:T(8,128)(2,1)S(1)}, bf16[384,768]{1,0:T(8,128)(2,1)S(1)}, u32[]{:S(2)}, u32[]{:S(2)}) collective-permute-start(bf16[384,768]{1,0:T(8,128)(2,1)S(1)} %down_join_near.1.refs_2_.refs_0_), channel_id=1, source_target_pairs={{0,4},{1,5},{2,6},{3,7},{4,0},{5,1},{6,2},{7,3},{8,12},{9,13},{10,... | collective-permute-start | bytes 1769480 | tf_op jit(solution)/shard_map/ppermute | solution.py:480
  167.5 1.8 collective-permute-start.44
  169.3 5.3 %collective-permute-done.44.refs_1_ = bf16[96,768]{1,0:T(8,128)(2,1)S(1)} collective-permute-done((bf16[96,768]{1,0:T(8,128)(2,1)S(1)}, bf16[96,768]{1,0:T(8,128)(2,1)S(1)}, u32[]{:S(2)}, u32[]{:S(2)}) %collective-permute-start.44) | collective-permute-done | bytes 147488 | tf_op jit(solution)/shard_map/ppermute | solution.py:480
  174.8 4.1 %collective-permute-done.43.refs_1_ = bf16[72,384]{1,0:T(8,128)(2,1)S(1)} collective-permute-done((bf16[72,384]{1,0:T(8,128)(2,1)S(1)}, bf16[72,384]{1,0:T(8,128)(2,1)S(1)}, u32[]{:S(2)}, u32[]{:S(2)}) %collective-permute-start.43) | collective-permute-done | bytes 55328 | tf_op jit(solution)/shard_map/ppermute | solution.py:480
  179.0 1.7 collective-permute-start.46
  180.7 1.8 collective-permute-done.48.refs_1_
  182.5 1.6 down_out.1
  184.1 1.3 collective-permute-done.46.refs_1_
  185.4 3.3 %collective-permute-start.49 = (bf16[384,384]{1,0:T(8,128)(2,1)S(1)}, bf16[384,384]{1,0:T(8,128)(2,1)S(1)}, u32[]{:S(2)}, u32[]{:S(2)}) collective-permute-start(bf16[384,384]{1,0:T(8,128)(2,1)S(1)} %rest_join_far.1.refs_0_.refs_2_), channel_id=1, source_target_pairs={{0,8},{1,9},{2,10},{3,11},{4,12},{5,13},{6,14},{7,15},{8,0},{9,1},... | collective-permute-start | bytes 884744 | tf_op jit(solution)/shard_map/ppermute | solution.py:480
  188.7 1.0 collective-permute-start.52
  189.6 3.7 %collective-permute-done.49.refs_1_ = bf16[384,384]{1,0:T(8,128)(2,1)S(1)} collective-permute-done((bf16[384,384]{1,0:T(8,128)(2,1)S(1)}, bf16[384,384]{1,0:T(8,128)(2,1)S(1)}, u32[]{:S(2)}, u32[]{:S(2)}) %collective-permute-start.49) | collective-permute-done | bytes 294944 | tf_op jit(solution)/shard_map/ppermute | solution.py:480
  193.4 1.0 collective-permute-start.50
  195.1 8.1 %collective-permute-done.52.refs_1_ = bf16[384,768]{1,0:T(8,128)(2,1)S(1)} collective-permute-done((bf16[384,768]{1,0:T(8,128)(2,1)S(1)}, bf16[384,768]{1,0:T(8,128)(2,1)S(1)}, u32[]{:S(2)}, u32[]{:S(2)}) %collective-permute-start.52) | collective-permute-done | bytes 589856 | tf_op jit(solution)/shard_map/ppermute | solution.py:480
  203.2 1.6 up_out.1
  204.8 4.7 %collective-permute-done.50.refs_1_ = bf16[768,384]{1,0:T(8,128)(2,1)S(1)} collective-permute-done((bf16[768,384]{1,0:T(8,128)(2,1)S(1)}, bf16[768,384]{1,0:T(8,128)(2,1)S(1)}, u32[]{:S(2)}, u32[]{:S(2)}) %collective-permute-start.50) | collective-permute-done | bytes 589856 | tf_op jit(solution)/shard_map/ppermute | solution.py:480
  209.5 1.7 rest_out.1
  (90 shorter events, 13.1 us)
Async XLA Ops:
  1.6 29.0 %copy-start = (bf16[768,768]{1,0:T(8,128)(2,1)S(1)}, bf16[768,768]{1,0:T(8,128)(2,1)}, u32[]{:S(2)}) copy-start(bf16[768,768]{1,0:T(8,128)(2,1)} %refs_4_.5) | copy-start | bytes 3538948
  3.2 17.4 %collective-permute-start.2 = (bf16[592,384]{1,0:T(8,128)(2,1)S(1)}, bf16[592,384]{1,0:T(8,128)(2,1)S(1)}, u32[]{:S(2)}, u32[]{:S(2)}) collective-permute-start(bf16[592,384]{1,0:T(8,128)(2,1)S(1)} %get-tuple-element.117.refs_2_), channel_id=1, source_target_pairs={{0,2},{1,3},{2,0},{3,1},{4,6},{5,7},{6,4},{7,5},{8,10},{9,11},{10,... | collective-permute-start | bytes 1363976 | tf_op jit(solution)/shard_map/ppermute | solution.py:480
  6.2 14.4 %collective-permute-start.1 = (bf16[592,384]{1,0:T(8,128)(2,1)S(1)}, bf16[592,384]{1,0:T(8,128)(2,1)S(1)}, u32[]{:S(2)}, u32[]{:S(2)}) collective-permute-start(bf16[592,384]{1,0:T(8,128)(2,1)S(1)} %get-tuple-element.116.refs_10_), channel_id=1, source_target_pairs={{0,1},{1,0},{2,3},{3,2},{4,5},{5,4},{6,7},{7,6},{8,9},{9,8},{10,11... | collective-permute-start | bytes 1363976 | tf_op jit(solution)/shard_map/ppermute | solution.py:480
  6.2 14.4 %collective-permute-start.3 = (bf16[192,768]{1,0:T(8,128)(2,1)}, bf16[192,768]{1,0:T(8,128)(2,1)S(1)}, u32[]{:S(2)}, u32[]{:S(2)}) collective-permute-start(bf16[192,768]{1,0:T(8,128)(2,1)} %refs_12_.1), channel_id=1, source_target_pairs={{0,1},{1,0},{2,3},{3,2},{4,5},{5,4},{6,7},{7,6},{8,9},{9,8},{10,11... | collective-permute-start | bytes 884744 | tf_op jit(solution)/shard_map/ppermute | solution.py:480
  6.7 13.9 %collective-permute-start = (bf16[144,768]{1,0:T(8,128)(2,1)S(1)}, bf16[144,768]{1,0:T(8,128)(2,1)S(1)}, u32[]{:S(2)}, u32[]{:S(2)}) collective-permute-start(bf16[144,768]{1,0:T(8,128)(2,1)S(1)} %block.1.refs_12_), channel_id=1, source_target_pairs={{0,0},{1,16},{2,8},{3,24},{4,4},{5,20},{6,12},{7,28},{8,2},{9,18},... | collective-permute-start | bytes 663560 | tf_op jit(solution)/shard_map/ppermute | solution.py:480
  20.7 15.0 %collective-permute-start.9 = (bf16[592,384]{1,0:T(8,128)(2,1)S(1)}, bf16[592,384]{1,0:T(8,128)(2,1)S(1)}, u32[]{:S(2)}, u32[]{:S(2)}) collective-permute-start(bf16[592,384]{1,0:T(8,128)(2,1)S(1)} %collective-permute-done.2.refs_2_.refs_7_), channel_id=1, source_target_pairs={{0,1},{1,0},{2,3},{3,2},{4,5},{5,4},{6,7},{7,6},{8,9},{9,8},{10,11... | collective-permute-start | bytes 1363976 | tf_op jit(solution)/shard_map/ppermute | solution.py:480
  20.7 7.9 %collective-permute-start.5 = (bf16[144,768]{1,0:T(8,128)(2,1)S(1)}, bf16[144,768]{1,0:T(8,128)(2,1)S(1)}, u32[]{:S(2)}, u32[]{:S(2)}) collective-permute-start(bf16[144,768]{1,0:T(8,128)(2,1)S(1)} %once.4.refs_0_), channel_id=1, source_target_pairs={{0,4},{1,5},{2,6},{3,7},{4,0},{5,1},{6,2},{7,3},{8,12},{9,13},{10,... | collective-permute-start | bytes 663560 | tf_op jit(solution)/shard_map/ppermute | solution.py:480
  22.3 8.3 %collective-permute-start.4 = (bf16[144,768]{1,0:T(8,128)(2,1)S(1)}, bf16[144,768]{1,0:T(8,128)(2,1)S(1)}, u32[]{:S(2)}, u32[]{:S(2)}) collective-permute-start(bf16[144,768]{1,0:T(8,128)(2,1)S(1)} %once.4.refs_0_), channel_id=1, source_target_pairs={{0,2},{1,3},{2,0},{3,1},{4,6},{5,7},{6,4},{7,5},{8,10},{9,11},{10,... | collective-permute-start | bytes 663560 | tf_op jit(solution)/shard_map/ppermute | solution.py:480
  24.8 9.0 %collective-permute-start.6 = (bf16[144,768]{1,0:T(8,128)(2,1)S(1)}, bf16[144,768]{1,0:T(8,128)(2,1)S(1)}, u32[]{:S(2)}, u32[]{:S(2)}) collective-permute-start(bf16[144,768]{1,0:T(8,128)(2,1)S(1)} %once.4.refs_0_), channel_id=1, source_target_pairs={{0,1},{1,0},{2,3},{3,2},{4,5},{5,4},{6,7},{7,6},{8,9},{9,8},{10,11... | collective-permute-start | bytes 663560 | tf_op jit(solution)/shard_map/ppermute | solution.py:480
  30.6 5.1 %collective-permute-start.7 = (bf16[144,768]{1,0:T(8,128)(2,1)S(1)}, bf16[144,768]{1,0:T(8,128)(2,1)S(1)}, u32[]{:S(2)}, u32[]{:S(2)}) collective-permute-start(bf16[144,768]{1,0:T(8,128)(2,1)S(1)} %once.5.refs_1_), channel_id=1, source_target_pairs={{0,1},{1,0},{2,3},{3,2},{4,5},{5,4},{6,7},{7,6},{8,9},{9,8},{10,11... | collective-permute-start | bytes 663560 | tf_op jit(solution)/shard_map/ppermute | solution.py:480
  30.6 9.3 %collective-permute-start.12 = (bf16[768,768]{1,0:T(8,128)(2,1)S(1)}, bf16[768,768]{1,0:T(8,128)(2,1)S(1)}, u32[]{:S(2)}, u32[]{:S(2)}) collective-permute-start(bf16[768,768]{1,0:T(8,128)(2,1)S(1)} %copy-done), channel_id=1, source_target_pairs={{0,1},{1,0},{2,3},{3,2},{4,5},{5,4},{6,7},{7,6},{8,9},{9,8},{10,11... | collective-permute-start | bytes 3538952 | tf_op jit(solution)/shard_map/ppermute | solution.py:480
  31.1 7.3 %collective-permute-start.8 = (bf16[144,768]{1,0:T(8,128)(2,1)S(1)}, bf16[144,768]{1,0:T(8,128)(2,1)S(1)}, u32[]{:S(2)}, u32[]{:S(2)}) collective-permute-start(bf16[144,768]{1,0:T(8,128)(2,1)S(1)} %once.5.refs_1_), channel_id=1, source_target_pairs={{0,4},{1,5},{2,6},{3,7},{4,0},{5,1},{6,2},{7,3},{8,12},{9,13},{10,... | collective-permute-start | bytes 663560 | tf_op jit(solution)/shard_map/ppermute | solution.py:480
  33.8 15.0 %collective-permute-start.14 = (bf16[192,1536]{1,0:T(8,128)(2,1)S(1)}, bf16[192,1536]{1,0:T(8,128)(2,1)S(1)}, u32[]{:S(2)}, u32[]{:S(2)}) collective-permute-start(bf16[192,1536]{1,0:T(8,128)(2,1)S(1)} %get-tuple-element.118.refs_1_), channel_id=1, source_target_pairs={{0,2},{1,3},{2,0},{3,1},{4,6},{5,7},{6,4},{7,5},{8,10},{9,11},{10,... | collective-permute-start | bytes 1769480 | tf_op jit(solution)/shard_map/ppermute | solution.py:480
  35.6 3.3 %collective-permute-start.10 = (bf16[144,768]{1,0:T(8,128)(2,1)S(1)}, bf16[144,768]{1,0:T(8,128)(2,1)S(1)}, u32[]{:S(2)}, u32[]{:S(2)}) collective-permute-start(bf16[144,768]{1,0:T(8,128)(2,1)S(1)} %collective-permute-done.5.refs_1_.refs_4_), channel_id=1, source_target_pairs={{0,1},{1,0},{2,3},{3,2},{4,5},{5,4},{6,7},{7,6},{8,9},{9,8},{10,11... | collective-permute-start | bytes 663560 | tf_op jit(solution)/shard_map/ppermute | solution.py:480
  38.4 1.5 collective-permute-start.11
  38.5 13.2 %collective-permute-start.15 = (bf16[192,1536]{1,0:T(8,128)(2,1)S(1)}, bf16[192,1536]{1,0:T(8,128)(2,1)S(1)}, u32[]{:S(2)}, u32[]{:S(2)}) collective-permute-start(bf16[192,1536]{1,0:T(8,128)(2,1)S(1)} %get-tuple-element.127), channel_id=1, source_target_pairs={{0,1},{1,0},{2,3},{3,2},{4,5},{5,4},{6,7},{7,6},{8,9},{9,8},{10,11... | collective-permute-start | bytes 1769480 | tf_op jit(solution)/shard_map/ppermute | solution.py:480
  48.8 3.2 %collective-permute-start.16 = (bf16[192,1536]{1,0:T(8,128)(2,1)S(1)}, bf16[192,1536]{1,0:T(8,128)(2,1)S(1)}, u32[]{:S(2)}, u32[]{:S(2)}) collective-permute-start(bf16[192,1536]{1,0:T(8,128)(2,1)S(1)} %once.7.refs_1_), channel_id=1, source_target_pairs={{0,1},{1,0},{2,3},{3,2},{4,5},{5,4},{6,7},{7,6},{8,9},{9,8},{10,11... | collective-permute-start | bytes 1769480 | tf_op jit(solution)/shard_map/ppermute | solution.py:480
  48.8 15.0 %collective-permute-start.13 = (bf16[256,768]{1,0:T(8,128)(2,1)S(1)}, bf16[256,768]{1,0:T(8,128)(2,1)S(1)}, u32[]{:S(2)}, u32[]{:S(2)}) collective-permute-start(bf16[256,768]{1,0:T(8,128)(2,1)S(1)} %get-tuple-element.125.refs_1_.refs_2_), channel_id=1, source_target_pairs={{0,2},{1,3},{2,0},{3,1},{4,6},{5,7},{6,4},{7,5},{8,10},{9,11},{10,... | collective-permute-start | bytes 1179656 | tf_op jit(solution)/shard_map/ppermute | solution.py:480
  50.6 20.0 %collective-permute-start.20 = (bf16[128,768]{1,0:T(8,128)(2,1)S(1)}, bf16[128,768]{1,0:T(8,128)(2,1)S(1)}, u32[]{:S(2)}, u32[]{:S(2)}) collective-permute-start(bf16[128,768]{1,0:T(8,128)(2,1)S(1)} %cotangent.1.refs_11_), channel_id=1, source_target_pairs={{0,2},{1,18},{2,10},{3,26},{4,6},{5,22},{6,14},{7,30},{8,0},{9,16}... | collective-permute-start | bytes 589832 | tf_op jit(solution)/shard_map/ppermute | solution.py:480
  50.9 19.8 %collective-permute-start.19 = (bf16[128,768]{1,0:T(8,128)(2,1)S(1)}, bf16[128,768]{1,0:T(8,128)(2,1)S(1)}, u32[]{:S(2)}, u32[]{:S(2)}) collective-permute-start(bf16[128,768]{1,0:T(8,128)(2,1)S(1)} %cotangent.1.refs_11_), channel_id=1, source_target_pairs={{0,0},{1,16},{2,8},{3,24},{4,4},{5,20},{6,12},{7,28},{8,2},{9,18},... | collective-permute-start | bytes 589832 | tf_op jit(solution)/shard_map/ppermute | solution.py:480
  65.9 9.4 %collective-permute-start.18 = (bf16[128,768]{1,0:T(8,128)(2,1)S(1)}, bf16[128,768]{1,0:T(8,128)(2,1)S(1)}, u32[]{:S(2)}, u32[]{:S(2)}) collective-permute-start(bf16[128,768]{1,0:T(8,128)(2,1)S(1)} %get-tuple-element.133), channel_id=1, source_target_pairs={{0,2},{1,3},{2,0},{3,1},{4,6},{5,7},{6,4},{7,5},{8,10},{9,11},{10,... | collective-permute-start | bytes 589832 | tf_op jit(solution)/shard_map/ppermute | solution.py:480
  70.5 6.9 %collective-permute-start.17 = (bf16[128,768]{1,0:T(8,128)(2,1)S(1)}, bf16[128,768]{1,0:T(8,128)(2,1)S(1)}, u32[]{:S(2)}, u32[]{:S(2)}) collective-permute-start(bf16[128,768]{1,0:T(8,128)(2,1)S(1)} %get-tuple-element.132.refs_7_), channel_id=1, source_target_pairs={{0,2},{1,3},{2,0},{3,1},{4,6},{5,7},{6,4},{7,5},{8,10},{9,11},{10,... | collective-permute-start | bytes 589832 | tf_op jit(solution)/shard_map/ppermute | solution.py:480
  79.2 2.9 %collective-permute-start.22 = (bf16[768,768]{1,0:T(8,128)(2,1)S(1)}, bf16[768,768]{1,0:T(8,128)(2,1)S(1)}, u32[]{:S(2)}, u32[]{:S(2)}) collective-permute-start(bf16[768,768]{1,0:T(8,128)(2,1)S(1)} %get-tuple-element.139.refs_5_), channel_id=1, source_target_pairs={{0,1},{1,0},{2,3},{3,2},{4,5},{5,4},{6,7},{7,6},{8,9},{9,8},{10,11... | collective-permute-start | bytes 3538952 | tf_op jit(solution)/shard_map/ppermute | solution.py:480
  83.6 4.4 %collective-permute-start.24 = (bf16[768,768]{1,0:T(8,128)(2,1)S(1)}, bf16[768,768]{1,0:T(8,128)(2,1)S(1)}, u32[]{:S(2)}, u32[]{:S(2)}) collective-permute-start(bf16[768,768]{1,0:T(8,128)(2,1)S(1)} %get-tuple-element.155.refs_2_), channel_id=1, source_target_pairs={{0,1},{1,0},{2,3},{3,2},{4,5},{5,4},{6,7},{7,6},{8,9},{9,8},{10,11... | collective-permute-start | bytes 3538952 | tf_op jit(solution)/shard_map/ppermute | solution.py:480
  83.8 15.6 %collective-permute-start.23 = (bf16[384,768]{1,0:T(8,128)(2,1)S(1)}, bf16[384,768]{1,0:T(8,128)(2,1)S(1)}, u32[]{:S(2)}, u32[]{:S(2)}) collective-permute-start(bf16[384,768]{1,0:T(8,128)(2,1)S(1)} %get-tuple-element.151.refs_2_), channel_id=1, source_target_pairs={{0,4},{1,5},{2,6},{3,7},{4,0},{5,1},{6,2},{7,3},{8,12},{9,13},{10,... | collective-permute-start | bytes 1769480 | tf_op jit(solution)/shard_map/ppermute | solution.py:480
  85.3 14.5 %collective-permute-start.21 = (bf16[256,768]{1,0:T(8,128)(2,1)S(1)}, bf16[256,768]{1,0:T(8,128)(2,1)S(1)}, u32[]{:S(2)}, u32[]{:S(2)}) collective-permute-start(bf16[256,768]{1,0:T(8,128)(2,1)S(1)} %get-tuple-element.141.refs_2_), channel_id=1, source_target_pairs={{0,2},{1,3},{2,0},{3,1},{4,6},{5,7},{6,4},{7,5},{8,10},{9,11},{10,... | collective-permute-start | bytes 1179656 | tf_op jit(solution)/shard_map/ppermute | solution.py:480
  87.1 19.4 %collective-permute-start.25 = (bf16[128,768]{1,0:T(8,128)(2,1)S(1)}, bf16[128,768]{1,0:T(8,128)(2,1)S(1)}, u32[]{:S(2)}, u32[]{:S(2)}) collective-permute-start(bf16[128,768]{1,0:T(8,128)(2,1)S(1)} %get-tuple-element.165), channel_id=1, source_target_pairs={{0,0},{1,16},{2,8},{3,24},{4,4},{5,20},{6,12},{7,28},{8,2},{9,18},... | collective-permute-start | bytes 589832 | tf_op jit(solution)/shard_map/ppermute | solution.py:480
  88.2 26.2 %collective-permute-start.29 = (bf16[384,768]{1,0:T(8,128)(2,1)S(1)}, bf16[384,768]{1,0:T(8,128)(2,1)S(1)}, u32[]{:S(2)}, u32[]{:S(2)}) collective-permute-start(bf16[384,768]{1,0:T(8,128)(2,1)S(1)} %get-tuple-element.156.refs_2_), channel_id=1, source_target_pairs={{0,8},{1,9},{2,10},{3,11},{4,12},{5,13},{6,14},{7,15},{8,0},{9,1},... | collective-permute-start | bytes 1769480 | tf_op jit(solution)/shard_map/ppermute | solution.py:480
  109.1 5.5 %collective-permute-start.28 = (bf16[528,384]{1,0:T(8,128)(2,1)S(1)}, bf16[528,384]{1,0:T(8,128)(2,1)S(1)}, u32[]{:S(2)}, u32[]{:S(2)}) collective-permute-start(bf16[528,384]{1,0:T(8,128)(2,1)S(1)} %get-tuple-element.169), channel_id=1, source_target_pairs={{0,1},{1,0},{2,3},{3,2},{4,5},{5,4},{6,7},{7,6},{8,9},{9,8},{10,11... | collective-permute-start | bytes 1216520 | tf_op jit(solution)/shard_map/ppermute | solution.py:480
  109.2 5.4 %collective-permute-start.27 = (bf16[512,384]{1,0:T(8,128)(2,1)S(1)}, bf16[512,384]{1,0:T(8,128)(2,1)S(1)}, u32[]{:S(2)}, u32[]{:S(2)}) collective-permute-start(bf16[512,384]{1,0:T(8,128)(2,1)S(1)} %get-tuple-element.168), channel_id=1, source_target_pairs={{0,1},{1,0},{2,3},{3,2},{4,5},{5,4},{6,7},{7,6},{8,9},{9,8},{10,11... | collective-permute-start | bytes 1179656 | tf_op jit(solution)/shard_map/ppermute | solution.py:480
  109.7 4.9 %collective-permute-start.26 = (bf16[512,384]{1,0:T(8,128)(2,1)S(1)}, bf16[512,384]{1,0:T(8,128)(2,1)S(1)}, u32[]{:S(2)}, u32[]{:S(2)}) collective-permute-start(bf16[512,384]{1,0:T(8,128)(2,1)S(1)} %get-tuple-element.167.refs_2_), channel_id=1, source_target_pairs={{0,1},{1,0},{2,3},{3,2},{4,5},{5,4},{6,7},{7,6},{8,9},{9,8},{10,11... | collective-permute-start | bytes 1179656 | tf_op jit(solution)/shard_map/ppermute | solution.py:480
  109.8 15.0 %collective-permute-start.31 = (bf16[192,768]{1,0:T(8,128)(2,1)S(1)}, bf16[192,768]{1,0:T(8,128)(2,1)S(1)}, u32[]{:S(2)}, u32[]{:S(2)}) collective-permute-start(bf16[192,768]{1,0:T(8,128)(2,1)S(1)} %get-tuple-element.157.refs_13_), channel_id=1, source_target_pairs={{0,8},{1,9},{2,10},{3,11},{4,12},{5,13},{6,14},{7,15},{8,0},{9,1},... | collective-permute-start | bytes 884744 | tf_op jit(solution)/shard_map/ppermute | solution.py:480
  117.1 8.5 %collective-permute-start.35 = (bf16[256,768]{1,0:T(8,128)(2,1)S(1)}, bf16[256,768]{1,0:T(8,128)(2,1)S(1)}, u32[]{:S(2)}, u32[]{:S(2)}) collective-permute-start(bf16[256,768]{1,0:T(8,128)(2,1)S(1)} %get-tuple-element.180), channel_id=1, source_target_pairs={{0,1},{1,0},{2,3},{3,2},{4,5},{5,4},{6,7},{7,6},{8,9},{9,8},{10,11... | collective-permute-start | bytes 1179656 | tf_op jit(solution)/shard_map/ppermute | solution.py:480
  117.3 8.2 %collective-permute-start.34 = (bf16[256,768]{1,0:T(8,128)(2,1)S(1)}, bf16[256,768]{1,0:T(8,128)(2,1)S(1)}, u32[]{:S(2)}, u32[]{:S(2)}) collective-permute-start(bf16[256,768]{1,0:T(8,128)(2,1)S(1)} %get-tuple-element.175.refs_2_), channel_id=1, source_target_pairs={{0,1},{1,0},{2,3},{3,2},{4,5},{5,4},{6,7},{7,6},{8,9},{9,8},{10,11... | collective-permute-start | bytes 1179656 | tf_op jit(solution)/shard_map/ppermute | solution.py:480
  117.7 20.3 %collective-permute-start.33 = (bf16[192,768]{1,0:T(8,128)(2,1)S(1)}, bf16[192,768]{1,0:T(8,128)(2,1)S(1)}, u32[]{:S(2)}, u32[]{:S(2)}) collective-permute-start(bf16[192,768]{1,0:T(8,128)(2,1)S(1)} %get-tuple-element.171.refs_4_), channel_id=1, source_target_pairs={{0,16},{1,17},{2,18},{3,19},{4,20},{5,21},{6,22},{7,23},{8,24},{9,... | collective-permute-start | bytes 884744 | tf_op jit(solution)/shard_map/ppermute | solution.py:480
  124.9 15.5 %collective-permute-start.32 = (bf16[96,768]{1,0:T(8,128)(2,1)S(1)}, bf16[96,768]{1,0:T(8,128)(2,1)S(1)}, u32[]{:S(2)}, u32[]{:S(2)}) collective-permute-start(bf16[96,768]{1,0:T(8,128)(2,1)S(1)} %get-tuple-element.177.refs_3_), channel_id=1, source_target_pairs={{0,16},{1,17},{2,18},{3,19},{4,20},{5,21},{6,22},{7,23},{8,24},{9,... | collective-permute-start | bytes 442376 | tf_op jit(solution)/shard_map/ppermute | solution.py:480
  125.0 15.4 %collective-permute-start.30 = (bf16[784,384]{1,0:T(8,128)(2,1)S(1)}, bf16[784,384]{1,0:T(8,128)(2,1)S(1)}, u32[]{:S(2)}, u32[]{:S(2)}) collective-permute-start(bf16[784,384]{1,0:T(8,128)(2,1)S(1)} %get-tuple-element.173.refs_3_), channel_id=1, source_target_pairs={{0,4},{1,5},{2,6},{3,7},{4,0},{5,1},{6,2},{7,3},{8,12},{9,13},{10,... | collective-permute-start | bytes 1806344 | tf_op jit(solution)/shard_map/ppermute | solution.py:480
  125.9 19.8 %collective-permute-start.39 = (bf16[256,768]{1,0:T(8,128)(2,1)S(1)}, bf16[256,768]{1,0:T(8,128)(2,1)S(1)}, u32[]{:S(2)}, u32[]{:S(2)}) collective-permute-start(bf16[256,768]{1,0:T(8,128)(2,1)S(1)} %get-tuple-element.181.refs_2_), channel_id=1, source_target_pairs={{0,2},{1,3},{2,0},{3,1},{4,6},{5,7},{6,4},{7,5},{8,10},{9,11},{10,... | collective-permute-start | bytes 1179656 | tf_op jit(solution)/shard_map/ppermute | solution.py:480
  140.6 15.5 %collective-permute-start.36 = (bf16[400,384]{1,0:T(8,128)(2,1)S(1)}, bf16[400,384]{1,0:T(8,128)(2,1)S(1)}, u32[]{:S(2)}, u32[]{:S(2)}) collective-permute-start(bf16[400,384]{1,0:T(8,128)(2,1)S(1)} %get-tuple-element.184.refs_2_), channel_id=1, source_target_pairs={{0,8},{1,9},{2,10},{3,11},{4,12},{5,13},{6,14},{7,15},{8,0},{9,1},... | collective-permute-start | bytes 921608 | tf_op jit(solution)/shard_map/ppermute | solution.py:480
  141.8 5.2 %collective-permute-start.38 = (bf16[96,768]{1,0:T(8,128)(2,1)S(1)}, bf16[96,768]{1,0:T(8,128)(2,1)S(1)}, u32[]{:S(2)}, u32[]{:S(2)}) collective-permute-start(bf16[96,768]{1,0:T(8,128)(2,1)S(1)} %get-tuple-element.182.refs_2_), channel_id=1, source_target_pairs={{0,4},{1,5},{2,6},{3,7},{4,0},{5,1},{6,2},{7,3},{8,12},{9,13},{10,... | collective-permute-start | bytes 442376 | tf_op jit(solution)/shard_map/ppermute | solution.py:480
  142.3 9.1 %collective-permute-start.37 = (bf16[96,768]{1,0:T(8,128)(2,1)S(1)}, bf16[96,768]{1,0:T(8,128)(2,1)S(1)}, u32[]{:S(2)}, u32[]{:S(2)}) collective-permute-start(bf16[96,768]{1,0:T(8,128)(2,1)S(1)} %down_sum.1.refs_2_.refs_0_), channel_id=1, source_target_pairs={{0,16},{1,17},{2,18},{3,19},{4,20},{5,21},{6,22},{7,23},{8,24},{9,... | collective-permute-start | bytes 442376 | tf_op jit(solution)/shard_map/ppermute | solution.py:480
  151.4 13.9 %collective-permute-start.45 = (bf16[192,768]{1,0:T(8,128)(2,1)S(1)}, bf16[192,768]{1,0:T(8,128)(2,1)S(1)}, u32[]{:S(2)}, u32[]{:S(2)}) collective-permute-start(bf16[192,768]{1,0:T(8,128)(2,1)S(1)} %down_join.1.refs_2_.refs_0_), channel_id=1, source_target_pairs={{0,8},{1,9},{2,10},{3,11},{4,12},{5,13},{6,14},{7,15},{8,0},{9,1},... | collective-permute-start | bytes 884744 | tf_op jit(solution)/shard_map/ppermute | solution.py:480
  155.6 5.7 %collective-permute-start.41 = (bf16[128,768]{1,0:T(8,128)(2,1)S(1)}, bf16[128,768]{1,0:T(8,128)(2,1)S(1)}, u32[]{:S(2)}, u32[]{:S(2)}) collective-permute-start(bf16[128,768]{1,0:T(8,128)(2,1)S(1)} %get-tuple-element.187.refs_2_), channel_id=1, source_target_pairs={{0,4},{1,5},{2,6},{3,7},{4,0},{5,1},{6,2},{7,3},{8,12},{9,13},{10,... | collective-permute-start | bytes 589832 | tf_op jit(solution)/shard_map/ppermute | solution.py:480
  156.2 8.3 %collective-permute-start.40 = (bf16[208,384]{1,0:T(8,128)(2,1)S(1)}, bf16[208,384]{1,0:T(8,128)(2,1)S(1)}, u32[]{:S(2)}, u32[]{:S(2)}) collective-permute-start(bf16[208,384]{1,0:T(8,128)(2,1)S(1)} %get-tuple-element.190.refs_2_), channel_id=1, source_target_pairs={{0,16},{1,17},{2,18},{3,19},{4,20},{5,21},{6,22},{7,23},{8,24},{9,... | collective-permute-start | bytes 479240 | tf_op jit(solution)/shard_map/ppermute | solution.py:480
  156.3 4.4 %collective-permute-start.42 = (bf16[48,768]{1,0:T(8,128)(2,1)S(1)}, bf16[48,768]{1,0:T(8,128)(2,1)S(1)}, u32[]{:S(2)}, u32[]{:S(2)}) collective-permute-start(bf16[48,768]{1,0:T(8,128)(2,1)S(1)} %get-tuple-element.188.refs_2_), channel_id=1, source_target_pairs={{0,2},{1,3},{2,0},{3,1},{4,6},{5,7},{6,4},{7,5},{8,10},{9,11},{10,... | collective-permute-start | bytes 221192 | tf_op jit(solution)/shard_map/ppermute | solution.py:480
  165.3 17.1 %collective-permute-start.47 = (bf16[384,768]{1,0:T(8,128)(2,1)S(1)}, bf16[384,768]{1,0:T(8,128)(2,1)S(1)}, u32[]{:S(2)}, u32[]{:S(2)}) collective-permute-start(bf16[384,768]{1,0:T(8,128)(2,1)S(1)} %down_join_near.1.refs_2_.refs_0_), channel_id=1, source_target_pairs={{0,4},{1,5},{2,6},{3,7},{4,0},{5,1},{6,2},{7,3},{8,12},{9,13},{10,... | collective-permute-start | bytes 1769480 | tf_op jit(solution)/shard_map/ppermute | solution.py:480
  167.5 7.2 %collective-permute-start.44 = (bf16[96,768]{1,0:T(8,128)(2,1)S(1)}, bf16[96,768]{1,0:T(8,128)(2,1)S(1)}, u32[]{:S(2)}, u32[]{:S(2)}) collective-permute-start(bf16[96,768]{1,0:T(8,128)(2,1)S(1)} %up_join.1.refs_3_.refs_0_), channel_id=1, source_target_pairs={{0,16},{1,17},{2,18},{3,19},{4,20},{5,21},{6,22},{7,23},{8,24},{9,... | collective-permute-start | bytes 442376 | tf_op jit(solution)/shard_map/ppermute | solution.py:480
  174.7 7.8 %collective-permute-start.48 = (bf16[192,768]{1,0:T(8,128)(2,1)S(1)}, bf16[192,768]{1,0:T(8,128)(2,1)S(1)}, u32[]{:S(2)}, u32[]{:S(2)}) collective-permute-start(bf16[192,768]{1,0:T(8,128)(2,1)S(1)} %up_join_far.1.refs_2_.refs_0_), channel_id=1, source_target_pairs={{0,8},{1,9},{2,10},{3,11},{4,12},{5,13},{6,14},{7,15},{8,0},{9,1},... | collective-permute-start | bytes 884744 | tf_op jit(solution)/shard_map/ppermute | solution.py:480
  174.7 4.2 %collective-permute-start.43 = (bf16[72,384]{1,0:T(8,128)(2,1)S(1)}, bf16[72,384]{1,0:T(8,128)(2,1)S(1)}, u32[]{:S(2)}, u32[]{:S(2)}) collective-permute-start(bf16[72,384]{1,0:T(8,128)(2,1)S(1)} %get-tuple-element.195.refs_2_), channel_id=1, source_target_pairs={{0,2},{1,3},{2,0},{3,1},{4,6},{5,7},{6,4},{7,5},{8,10},{9,11},{10,... | collective-permute-start | bytes 165896 | tf_op jit(solution)/shard_map/ppermute | solution.py:480
  179.0 6.4 %collective-permute-start.46 = (bf16[192,384]{1,0:T(8,128)(2,1)S(1)}, bf16[192,384]{1,0:T(8,128)(2,1)S(1)}, u32[]{:S(2)}, u32[]{:S(2)}) collective-permute-start(bf16[192,384]{1,0:T(8,128)(2,1)S(1)} %rest_join.1.refs_2_.refs_0_), channel_id=1, source_target_pairs={{0,16},{1,17},{2,18},{3,19},{4,20},{5,21},{6,22},{7,23},{8,24},{9,... | collective-permute-start | bytes 442376 | tf_op jit(solution)/shard_map/ppermute | solution.py:480
  185.4 8.0 %collective-permute-start.49 = (bf16[384,384]{1,0:T(8,128)(2,1)S(1)}, bf16[384,384]{1,0:T(8,128)(2,1)S(1)}, u32[]{:S(2)}, u32[]{:S(2)}) collective-permute-start(bf16[384,384]{1,0:T(8,128)(2,1)S(1)} %rest_join_far.1.refs_0_.refs_2_), channel_id=1, source_target_pairs={{0,8},{1,9},{2,10},{3,11},{4,12},{5,13},{6,14},{7,15},{8,0},{9,1},... | collective-permute-start | bytes 884744 | tf_op jit(solution)/shard_map/ppermute | solution.py:480
  188.7 14.5 %collective-permute-start.52 = (bf16[384,768]{1,0:T(8,128)(2,1)S(1)}, bf16[384,768]{1,0:T(8,128)(2,1)S(1)}, u32[]{:S(2)}, u32[]{:S(2)}) collective-permute-start(bf16[384,768]{1,0:T(8,128)(2,1)S(1)} %up_join_near.1.refs_2_.refs_0_), channel_id=1, source_target_pairs={{0,4},{1,5},{2,6},{3,7},{4,0},{5,1},{6,2},{7,3},{8,12},{9,13},{10,... | collective-permute-start | bytes 1769480 | tf_op jit(solution)/shard_map/ppermute | solution.py:480
  193.4 16.1 %collective-permute-start.50 = (bf16[768,384]{1,0:T(8,128)(2,1)S(1)}, bf16[768,384]{1,0:T(8,128)(2,1)S(1)}, u32[]{:S(2)}, u32[]{:S(2)}) collective-permute-start(bf16[768,384]{1,0:T(8,128)(2,1)S(1)} %rest_join_near.1.refs_2_.refs_0_), channel_id=1, source_target_pairs={{0,4},{1,5},{2,6},{3,7},{4,0},{5,1},{6,2},{7,3},{8,12},{9,13},{10,... | collective-permute-start | bytes 1769480 | tf_op jit(solution)/shard_map/ppermute | solution.py:480
  194.5 10.3 %collective-permute-start.51 = (bf16[128,768]{1,0:T(8,128)(2,1)S(1)}, bf16[128,768]{1,0:T(8,128)(2,1)S(1)}, u32[]{:S(2)}, u32[]{:S(2)}) collective-permute-start(bf16[128,768]{1,0:T(8,128)(2,1)S(1)} %input_sum.1.refs_2_), channel_id=1, source_target_pairs={{0,0},{1,16},{2,8},{3,24},{4,4},{5,20},{6,12},{7,28},{8,2},{9,18},... | collective-permute-start | bytes 589832 | tf_op jit(solution)/shard_map/ppermute | solution.py:480

commit v5 on v4

--- a/solution.py
+++ b/solution.py
@@ -714,7 +714,7 @@
     a_low[...] = partial.astype(jnp.bfloat16)
 
 
-def inner_kernel(u_own, u_x, u_m, u_mx, d_own, d_m, up, down, sems):
+def inner_kernel(u_own, u_x, u_m, u_mx0, u_mx1, d_own, d_m, up, down, sems):
     q, r, x, c = spot()
     part = up.shape[0] // 4
     count = up.shape[1]
@@ -723,8 +723,11 @@
     own = u_own.at[:, pl.ds(pl.multiple_of(count * x, 128), count)]
     ins.start(own, up.at[pl.ds(pl.multiple_of(part * shard, 64), part)])
     ins.start(d_own, down.at[pl.ds(pl.multiple_of(count // 2 * c, 128), count // 2)])
-    for flip, piece in ((2, u_x), (1, u_m), (3, u_mx)):
+    for flip, piece in ((2, u_x), (1, u_m)):
         up[pl.ds(pl.multiple_of(part * (shard ^ flip), 64), part), :] = piece[...]
+    for i, piece in enumerate((u_mx0, u_mx1)):
+        at = pl.multiple_of(part * (shard ^ 3) + part // 2 * i, 32)
+        up[pl.ds(at, part // 2), :] = piece[...]
     down[pl.ds(pl.multiple_of(count // 2 * (1 - c), 128), count // 2), :] = d_m[...]
     ins.wait()
 
@@ -915,12 +918,13 @@
             out[rows * at : rows * (at + 1), :] = block.astype(out.dtype)
 
 
-def up_grad_kernel(h, du, send, keep, whole):
-    q, r, x, c = spot()
+def up_grad_kernel(h, du, *refs):
+    q, r, x, c = spot()
+    sends, (keep, whole) = refs[:4], refs[4:]
     width = h.shape[1]
     thin = width // 32
     whole[...] = dot_tn(h[...], du[...])
-    for side, out in ((1 - c, send), (c, keep)):
+    for side in (1 - c, c):
         for _, at, within in octants():
             pieces = []
             for xx in range(2):
@@ -928,7 +932,11 @@
                 rows = pl.ds(pl.multiple_of(first, 8), thin)
                 pieces += [whole[rows, 0:width], whole[rows, width:]]
             block = jnp.concatenate(pieces)
-            out[4 * thin * at : 4 * thin * (at + 1), :] = block.astype(out.dtype)
+            if side is c:
+                keep[4 * thin * at : 4 * thin * (at + 1), :] = block
+            else:
+                to = 4 * thin * (at % 2)
+                sends[at // 2][to : to + 4 * thin, :] = block.astype(jnp.bfloat16)
 
 
 def join_kernel(*refs):
@@ -937,6 +945,21 @@
         count = ref.shape[0]
         out[at : at + count, :] = ref[...]
         at += count
+
+
+def fold_pieces_kernel(bit, count, keep, *refs):
+    gots, sends, (kept, whole) = refs[: -2 - count], refs[-2 - count : -2], refs[-2:]
+    at = bit(*spot())
+    first = 0
+    for got in gots:
+        rows = slice(first, first + got.shape[0])
+        whole[rows, :] = keep[rows, :] + got[...].astype(jnp.float32)
+        first += got.shape[0]
+    half = kept.shape[0]
+    kept[...] = whole[pl.ds(pl.multiple_of(half * at, 64), half), :]
+    for i, send in enumerate(sends):
+        rows = pl.ds(pl.multiple_of(half * (1 - at) + half // count * i, 64), half // count)
+        send[...] = whole[rows, :].astype(send.dtype)
 
 
 def fold_kernel(bit, keep, got, send, kept):
@@ -1132,7 +1155,7 @@
     )(value, *after)
 
 
-HEAVY = ('attend_back', 'down_sum', 'project')
+HEAVY = ('attend_back', 'down_sum', 'input_sum', 'project', 'rest_3')
 
 
 def plane_local(
@@ -1197,7 +1220,6 @@
         load_kernel, "cotangent", [HBM], [((rows, width), low, WHOLE)], [pltpu.SemaphoreType.DMA((1,))],
         (cotangent[0],),
     )
-    cot, cot_x = regroup(cot), regroup_x(cot)
     kv_own, q_own, w_all, vecs, up_bias = call(
         project_kernel,
         "project",
@@ -1243,19 +1265,21 @@
         room=8 << 20,
     )
     a_got = swap_x(a_low)
-    up_x = once(up_x, a_low)
-    up_mx = swap_c(up_x)
     (kt,) = call(turn_kernel, "turn", [WHOLE], [((2 * pairs, 64, keys), low, WHOLE)], [], (k3,),
         after=(up_m,))
 
+    up_x = once(up_x, kt)
+    up_mx = [swap_c(piece) for piece in (up_x[: part // 2], up_x[part // 2 :])]
     inner_weights = call(
         inner_kernel,
         "inner",
-        [HBM, WHOLE, WHOLE, WHOLE, HBM, WHOLE],
+        [HBM] + [WHOLE] * 4 + [HBM, WHOLE],
         [((width, 4 * wide), low, WHOLE), ((4 * wide, width), low, WHOLE)],
         [pltpu.SemaphoreType.DMA((2,))],
-        (w_up, up_x, up_m, up_mx, w_down, down_m),
-    )
+        (w_up, up_x, up_m, *up_mx, w_down, down_m),
+    )
+    cot = once(cot, inner_weights[0])
+    cot, cot_x = regroup(cot), regroup_x(cot)
     y_low, y_more, h_low, z, normed1, rstd1, slope, y_own = call(
         forward_kernel,
         "feedforward",
@@ -1332,6 +1356,19 @@
             room=4 << 20,
         )
 
+    def fold_into(count, name, bit, keep, gots):
+        half_rows = keep.shape[0] // 2
+        *sends, kept = call(
+            lambda *refs: fold_pieces_kernel(bit, count, *refs),
+            name,
+            [WHOLE] * (1 + len(gots)),
+            [((half_rows // count, width), low, WHOLE)] * count + [((half_rows, width), exact, WHOLE)],
+            [pltpu.VMEM(keep.shape, exact)],
+            (keep, *gots),
+            room=4 << 20,
+        )
+        return sends, kept
+
     def bit_r(q, r, x, c):
         return r
 
@@ -1360,22 +1397,20 @@
         return out
 
     cuts = (count // 3, count // 3, count - 2 * (count // 3) + 16)
-    down_send, down_keep = fold("down_1", bit_r, down_keep, down_got)
-    down_got = swap_r(down_send)
-    up_send, up_keep = call(
+    down_sends, down_keep = fold_into(2, "down_1", bit_r, down_keep, (down_got,))
+    down_gots = [swap_r(send) for send in down_sends]
+    *up_sends, up_keep = call(
         up_grad_kernel,
         "up_grad",
         [WHOLE] * 2,
-        [((8 * eighth, width), low, WHOLE), ((8 * eighth, width), exact, WHOLE)],
+        [((2 * eighth, width), low, WHOLE)] * 4 + [((8 * eighth, width), exact, WHOLE)],
         [pltpu.VMEM((width, 4 * wide), exact)],
         (h_low, du),
         room=8 << 20,
     )
-    up_got = swap_c(up_send)
-    up_send, up_keep = fold("up_1", bit_near, up_keep, up_got)
+    up_gots = [swap_c(send) for send in up_sends]
+    (up_send,), up_keep = fold_into(1, "up_1", bit_near, up_keep, up_gots)
     up_got = swap_near(up_send)
-    down_send, down_keep = fold("down_2", bit_near, down_keep, down_got)
-    down_got = swap_near(down_send)
     dkv, dq, dr, da, sums1, qv_sums = call(
         attend_back_kernel,
         "attend_back",
@@ -1401,6 +1436,8 @@
         room=8 << 20,
     )
 
+    (down_send,), down_keep = fold_into(1, "down_2", bit_near, down_keep, down_gots)
+    down_got = swap_near(down_send)
     *rest_sends, rest_keep = call(
         weight_grad_kernel,
         "weight_grad",
@@ -1412,10 +1449,10 @@
         room=8 << 20,
     )
     rest_gots = [swap_c(send) for send in rest_sends]
+    rest_send, rest_keep = step("rest_1", bit_r, rest_keep, count // 2, *rest_gots)
+    rest_got = swap_r(rest_send)
     up_send, up_keep = fold("up_2", bit_far, up_keep, up_got)
     up_got = swap_far(up_send)
-    rest_send, rest_keep = step("rest_1", bit_r, rest_keep, count // 2, *rest_gots)
-    rest_got = swap_r(rest_send)
     *x_sends, x_keep = call(
         input_grad_kernel,
         "input_grad",
@@ -1444,10 +1481,6 @@
         sum_kernel, "down_sum", [WHOLE] * 2, [((eighth, width), low, WHOLE)], [], (down_keep, down_got)
     )
     down_other = swap_far(down_sum)
-    rest_send, rest_keep = step("rest_2", bit_near, rest_keep, count // 4, rest_got)
-    rest_got = swap_near(rest_send)
-    x_send, x_keep = fold("input_r", bit_r, x_keep, x_got)
-    x_got = swap_r(x_send)
     side, base = call(
         share_kernel,
         "up_share",
@@ -1457,6 +1490,10 @@
         (up_keep.reshape(2, eighth // 2, width), up_got.reshape(2, eighth // 2, width)),
     )
     side = swap_x(side)
+    rest_send, rest_keep = step("rest_2", bit_near, rest_keep, count // 4, rest_got)
+    rest_got = swap_near(rest_send)
+    x_send, x_keep = fold("input_r", bit_r, x_keep, x_got)
+    x_got = swap_r(x_send)
     down_sum = join("down_join", down_sum, down_other)
     down_other = swap_near(down_sum)
     rest_send, rest_keep = step("rest_3", bit_far, rest_keep, count // 8, rest_got)
@@ -1467,7 +1504,7 @@
         total_kernel, "input_sum", [WHOLE] * 3, [((rows, width), low, WHOLE)], [], (x_keep, x_got, dr)
     )
     total = regroup(total)
-    side, base, *lines, b_up_grad = call(
+    rest_side, rest_base, *lines, b_up_grad = call(
         last_step_kernel,
         "rest_last",
         [WHOLE] * 2,
@@ -1477,22 +1514,22 @@
         [pltpu.VMEM((8 * thin + 16, half), exact)],
         (rest_keep, rest_got),
     )
-    side = swap_x(side)
+    rest_side = swap_x(rest_side)
     down_near = join("down_join_near", down_sum, down_other)
     down_far = swap_r(down_near)
     up_sum = join("up_join_far", up_sum, up_other)
     up_other = swap_near(up_sum)
-    rest_sum = join("rest_join", base, side)
+    rest_sum = join("rest_join", rest_base, rest_side)
     rest_other = swap_far(rest_sum)
-    up_near = join("up_join_near", up_sum, up_other)
-    up_far = swap_r(up_near)
+    rest_sum = join("rest_join_far", rest_sum, rest_other)
+    rest_other = swap_near(rest_sum)
     w_down_grad, _ = call(
         down_out_kernel, "down_out", [WHOLE] * 2,
         [((2 * wide, width), exact, WHOLE), ((8, 128), exact, WHOLE)], [], (down_near, down_far),
         room=6 << 20,
     )
-    rest_sum = join("rest_join_far", rest_sum, rest_other)
-    rest_other = swap_near(rest_sum)
+    up_near = join("up_join_near", up_sum, up_other)
+    up_far = swap_r(up_near)
     rest_near = join("rest_join_near", rest_sum, rest_other)
     rest_far = swap_r(rest_near)
     w_up_grad, _ = call(

time: 212 us -> 200 us (0.943)
  waiting for transfers between devices: 109 us -> 95 us
    ppermute x53 -> x58, waiting for transfers between devices: 109 us -> 95 us  [moved(): lax.ppermute(block, AXES, [(number(s), number(move(*s))) for s in spots])]
    ppermute x53 -> x58, starting transfers between devices: 60.4 us -> 61.4 us  [moved(): lax.ppermute(block, AXES, [(number(s), number(move(*s))) for s in spots])]
  transfers between devices with their start and end apart: 53 -> 58, of which waited for: 28 -> 27; matrix products, arithmetic and copies ran while one was open for 0% -> 0% of each run, Pallas kernels for 16% -> 18%
where the time goes in v5:
time: 200 us; the launch traced here: 199 us
  waiting for transfers between devices  95 us (48%)
  starting transfers between devices  61.4 us (31%)
  Pallas kernels  41.8 us (21%)
    ppermute x58, waiting for transfers between devices, moved(): lax.ppermute(block, AXES, [(number(s), number(move(*s))) for s in spots])  95 us
    ppermute x58, starting transfers between devices, moved(): lax.ppermute(block, AXES, [(number(s), number(move(*s))) for s in spots])  61.4 us
    pallas_call x42, Pallas kernels, kernel_call(): pl.pallas_call(run, name=name, out_shape=[jax.ShapeDtypeStruct(shape, dty...  41.8 us
  transfers between devices with their start and end apart: 58, of which 27 were waited for; matrix products, arithmetic and copies ran while one was open for 0% of the time, Pallas kernels for 18%

profile of v5, /device:TPU:0, one launch (start us, length us, event | category | flops | bytes accessed | tf_op | source)
XLA Modules:
  0.0 199.3 jit_solution(11512224759315159577)
XLA Ops:
  0.7 1.0 block.1.refs_12_
  1.6 1.6 pack.1
  3.2 3.0 %collective-permute-start.2 = (bf16[592,384]{1,0:T(8,128)(2,1)S(1)}, bf16[592,384]{1,0:T(8,128)(2,1)S(1)}, u32[]{:S(2)}, u32[]{:S(2)}) collective-permute-start(bf16[592,384]{1,0:T(8,128)(2,1)S(1)} %get-tuple-element.121.refs_2_), channel_id=1, source_target_pairs={{0,2},{1,3},{2,0},{3,1},{4,6},{5,7},{6,4},{7,5},{8,10},{9,11},{10,... | collective-permute-start | bytes 1363976 | tf_op jit(solution)/shard_map/ppermute | solution.py:480
  7.4 13.2 %collective-permute-done.2.refs_2_.refs_7_ = bf16[592,384]{1,0:T(8,128)(2,1)S(1)} collective-permute-done((bf16[592,384]{1,0:T(8,128)(2,1)S(1)}, bf16[592,384]{1,0:T(8,128)(2,1)S(1)}, u32[]{:S(2)}, u32[]{:S(2)}) %collective-permute-start.2) | collective-permute-done | bytes 454688 | tf_op jit(solution)/shard_map/ppermute | solution.py:480
  20.7 1.6 collective-permute-start.5
  22.3 2.5 %collective-permute-start.4 = (bf16[144,768]{1,0:T(8,128)(2,1)S(1)}, bf16[144,768]{1,0:T(8,128)(2,1)S(1)}, u32[]{:S(2)}, u32[]{:S(2)}) collective-permute-start(bf16[144,768]{1,0:T(8,128)(2,1)S(1)} %once.5.refs_0_), channel_id=1, source_target_pairs={{0,2},{1,3},{2,0},{3,1},{4,6},{5,7},{6,4},{7,5},{8,10},{9,11},{10,... | collective-permute-start | bytes 663560 | tf_op jit(solution)/shard_map/ppermute | solution.py:480
  24.8 3.8 %collective-permute-done.5.refs_1_.refs_4_ = bf16[144,768]{1,0:T(8,128)(2,1)S(1)} collective-permute-done((bf16[144,768]{1,0:T(8,128)(2,1)S(1)}, bf16[144,768]{1,0:T(8,128)(2,1)S(1)}, u32[]{:S(2)}, u32[]{:S(2)}) %collective-permute-start.5) | collective-permute-done | bytes 221216 | tf_op jit(solution)/shard_map/ppermute | solution.py:480
  28.6 2.0 collective-permute-done.4.refs_0_
  31.6 1.3 cut.1
  32.9 0.9 cotangent.1.refs_11_.refs_0_
  33.8 1.8 collective-permute-start.14
  36.1 2.3 %project.1 = (bf16[512,768]{1,0:T(8,128)(2,1)S(1)}, bf16[256,384]{1,0:T(8,128)(2,1)S(1)}, bf16[768,1152]{1,0:T(8,128)(2,1)S(1)}, f32[8,768]{1,0:T(8,128)S(1)}, f32[4,8,384]{2,1,0:T(8,128)S(1)}) custom-call(bf16[144,768]{1,0:T(8,128)(2,1)S(1)} %once.5.refs_0_, bf16[144,768]{1,0:T(8,128)(2,1)S(1)} %once.6.refs_1_, ...), custom_call_target="tpu_custom_call" | custom-call | flops 10000000000 | bytes 1 | tf_op jit(solution)/shard_map/project/pallas_call | solution.py:1133
  38.6 1.4 collective-permute-done.11.refs_7_
  40.0 6.4 %attend.1 = (bf16[256,768]{1,0:T(8,128)(2,1)S(1)}, bf16[1024,768]{1,0:T(8,128)(2,1)S(1)}, bf16[384,768]{1,0:T(8,128)(2,1)S(1)}, bf16[3,1024,128]{2,1,0:T(8,128)(...) custom-call(bf16[144,768]{1,0:T(8,128)(2,1)S(1)} %once.5.refs_0_, ...), custom_call_target="tpu_custom_call" | custom-call | flops 1 | bytes 1 | tf_op jit(solution)/shard_map/attend/pallas_call | solution.py:1133
  46.5 1.7 collective-permute-start.13
  49.5 1.1 collective-permute-done.17.refs_4_
  51.0 1.5 inner.1
  52.5 1.8 collective-permute-start.21
  55.1 2.6 %collective-permute-done.13.refs_1_ = bf16[256,768]{1,0:T(8,128)(2,1)S(1)} collective-permute-done((bf16[256,768]{1,0:T(8,128)(2,1)S(1)}, bf16[256,768]{1,0:T(8,128)(2,1)S(1)}, u32[]{:S(2)}, u32[]{:S(2)}) %collective-permute-start.13) | collective-permute-done | bytes 393248 | tf_op jit(solution)/shard_map/ppermute | solution.py:480
  57.7 2.0 %feedforward.1 = (bf16[128,768]{1,0:T(8,128)(2,1)S(1)}, bf16[128,768]{1,0:T(8,128)(2,1)S(1)}, bf16[256,768]{1,0:T(8,128)(2,1)S(1)}, bf16[256,1536]{1,0:T(8,128)(...) custom-call(f32[256,768]{1,0:T(8,128)S(1)} %get-tuple-element.128.re, ...), custom_call_target="tpu_custom_call" | custom-call | flops 1 | bytes 1 | tf_op jit(solution)/shard_map/feedforward/pallas_call | solution.py:1133
  59.7 1.7 collective-permute-start.19
  61.8 1.0 collective-permute-done.21.refs_5_
  62.8 7.9 %collective-permute-done.19.refs_2_ = bf16[128,768]{1,0:T(8,128)(2,1)S(1)} collective-permute-done((bf16[128,768]{1,0:T(8,128)(2,1)S(1)}, bf16[128,768]{1,0:T(8,128)(2,1)S(1)}, u32[]{:S(2)}, u32[]{:S(2)}) %collective-permute-start.19) | collective-permute-done | bytes 196640 | tf_op jit(solution)/shard_map/ppermute | solution.py:480
  70.8 4.1 %collective-permute-done.18.refs_1_ = bf16[128,768]{1,0:T(8,128)(2,1)S(1)} collective-permute-done((bf16[128,768]{1,0:T(8,128)(2,1)S(1)}, bf16[128,768]{1,0:T(8,128)(2,1)S(1)}, u32[]{:S(2)}, u32[]{:S(2)}) %collective-permute-start.18) | collective-permute-done | bytes 196640 | tf_op jit(solution)/shard_map/ppermute | solution.py:480
  74.9 0.9 norm_back.1
  76.7 1.7 feedforward_back.1
  78.4 2.6 %collective-permute-start.22 = (bf16[256,768]{1,0:T(8,128)(2,1)S(1)}, bf16[256,768]{1,0:T(8,128)(2,1)S(1)}, u32[]{:S(2)}, u32[]{:S(2)}) collective-permute-start(bf16[256,768]{1,0:T(8,128)(2,1)S(1)} %get-tuple-element.145.refs_2_), channel_id=1, source_target_pairs={{0,2},{1,3},{2,0},{3,1},{4,6},{5,7},{6,4},{7,5},{8,10},{9,11},{10,... | collective-permute-start | bytes 1179656 | tf_op jit(solution)/shard_map/ppermute | solution.py:480
  81.5 1.3 up_grad.1
  84.5 0.9 collective-permute-start.28
  85.4 1.2 collective-permute-start.29
  86.5 0.9 collective-permute-start.30
  87.9 3.9 %collective-permute-start.35 = (bf16[384,768]{1,0:T(8,128)(2,1)S(1)}, bf16[384,768]{1,0:T(8,128)(2,1)S(1)}, u32[]{:S(2)}, u32[]{:S(2)}) collective-permute-start(bf16[384,768]{1,0:T(8,128)(2,1)S(1)} %get-tuple-element.162.refs_13_), channel_id=1, source_target_pairs={{0,8},{1,9},{2,10},{3,11},{4,12},{5,13},{6,14},{7,15},{8,0},{9,1},... | collective-permute-start | bytes 1769480 | tf_op jit(solution)/shard_map/ppermute | solution.py:480
  91.8 6.6 %attend_back.1 = (bf16[1024,768]{1,0:T(8,128)(2,1)S(1)}, bf16[256,384]{1,0:T(8,128)(2,1)S(1)}, f32[128,768]{1,0:T(8,128)S(1)}, bf16[256,768]{1,0:T(8,128)(2,1)S(...) custom-call(f32[256,768]{1,0:T(8,128)S(1)} %get-tuple-element.144.refs_0_, ...), custom_call_target="tpu_custom_call" | custom-call | flops 10000000000 | bytes 1 | tf_op jit(solution)/shard_map/attend_back/pallas_call | solution.py:1133
  98.4 1.2 collective-permute-done.30.refs_2_
  99.9 2.6 %weight_grad.1 = (bf16[512,384]{1,0:T(8,128)(2,1)S(1)}, bf16[512,384]{1,0:T(8,128)(2,1)S(1)}, bf16[528,384]{1,0:T(8,128)(2,1)S(1)}, f32[1552,384]{1,0:T(8,128)S(1)}) custom-call(bf16[1024,768]{1,0:T(8,128)(2,1)S(1)} %get-tuple-element.127.refs_2_.refs_0_, bf16[1024,768]{1,0:T(8,128)(2,1)S(1)} %get-tuple-element.163.refs_3_.refs_1_, ...), custom_call_target="tpu_custom_call" | custom-call | flops 1 | bytes 1 | tf_op jit(solution)/shard_map/weight_grad/pallas_call | solution.py:1133
  102.5 2.1 %collective-permute-start.33 = (bf16[528,384]{1,0:T(8,128)(2,1)S(1)}, bf16[528,384]{1,0:T(8,128)(2,1)S(1)}, u32[]{:S(2)}, u32[]{:S(2)}) collective-permute-start(bf16[528,384]{1,0:T(8,128)(2,1)S(1)} %get-tuple-element.177), channel_id=1, source_target_pairs={{0,1},{1,0},{2,3},{3,2},{4,5},{5,4},{6,7},{7,6},{8,9},{9,8},{10,11... | collective-permute-start | bytes 1216520 | tf_op jit(solution)/shard_map/ppermute | solution.py:480
  105.2 3.0 %collective-permute-start.39 = (bf16[192,768]{1,0:T(8,128)(2,1)S(1)}, bf16[192,768]{1,0:T(8,128)(2,1)S(1)}, u32[]{:S(2)}, u32[]{:S(2)}) collective-permute-start(bf16[192,768]{1,0:T(8,128)(2,1)S(1)} %get-tuple-element.173.refs_10_), channel_id=1, source_target_pairs={{0,8},{1,9},{2,10},{3,11},{4,12},{5,13},{6,14},{7,15},{8,0},{9,1},... | collective-permute-start | bytes 884744 | tf_op jit(solution)/shard_map/ppermute | solution.py:480
  109.5 2.1 %input_grad.1 = (bf16[256,768]{1,0:T(8,128)(2,1)S(1)}, bf16[256,768]{1,0:T(8,128)(2,1)S(1)}, f32[512,768]{1,0:T(8,128)S(1)}) custom-call(bf16[256,384]{1,0:T(8,128)(2,1)S(1)} %get-tuple-element.164.refs_2_.refs_0_, bf16[1024,768]{1,0:T(8,128)(2,1)S(1)} %get-tuple-element.163.refs_3_.refs_1_, bf16[768,1152]{1,0:T(8,128)(2,1)S(1)} %get-tuple-element.125.refs_10_.refs_2_, ...), custom_call_target="tpu_custom_call" | custom-call | flops 1 | bytes 1 | tf_op jit(solution)/shard_map/input_grad/pallas_call | solution.py:1133
  112.7 3.1 %collective-permute-done.39 = bf16[192,768]{1,0:T(8,128)(2,1)S(1)} collective-permute-done((bf16[192,768]{1,0:T(8,128)(2,1)S(1)}, bf16[192,768]{1,0:T(8,128)(2,1)S(1)}, u32[]{:S(2)}, u32[]{:S(2)}) %collective-permute-start.39) | collective-permute-done | bytes 294944 | tf_op jit(solution)/shard_map/ppermute | solution.py:480
  115.8 1.3 collective-permute-start.41
  118.2 2.5 %collective-permute-start.44 = (bf16[256,768]{1,0:T(8,128)(2,1)S(1)}, bf16[256,768]{1,0:T(8,128)(2,1)S(1)}, u32[]{:S(2)}, u32[]{:S(2)}) collective-permute-start(bf16[256,768]{1,0:T(8,128)(2,1)S(1)} %get-tuple-element.188.refs_2_), channel_id=1, source_target_pairs={{0,2},{1,3},{2,0},{3,1},{4,6},{5,7},{6,4},{7,5},{8,10},{9,11},{10,... | collective-permute-start | bytes 1179656 | tf_op jit(solution)/shard_map/ppermute | solution.py:480
  120.7 11.7 %collective-permute-done.36 = bf16[192,768]{1,0:T(8,128)(2,1)S(1)} collective-permute-done((bf16[192,768]{1,0:T(8,128)(2,1)S(1)}, bf16[192,768]{1,0:T(8,128)(2,1)S(1)}, u32[]{:S(2)}, u32[]{:S(2)}) %collective-permute-start.36) | collective-permute-done | bytes 294944 | tf_op jit(solution)/shard_map/ppermute | solution.py:480
  133.3 1.3 collective-permute-done.41.refs_1_
  134.7 3.0 %collective-permute-done.40 = bf16[96,768]{1,0:T(8,128)(2,1)S(1)} collective-permute-done((bf16[96,768]{1,0:T(8,128)(2,1)S(1)}, bf16[96,768]{1,0:T(8,128)(2,1)S(1)}, u32[]{:S(2)}, u32[]{:S(2)}) %collective-permute-start.40) | collective-permute-done | bytes 147488 | tf_op jit(solution)/shard_map/ppermute | solution.py:480
  138.0 2.8 %collective-permute-start.43 = (bf16[96,768]{1,0:T(8,128)(2,1)S(1)}, bf16[96,768]{1,0:T(8,128)(2,1)S(1)}, u32[]{:S(2)}, u32[]{:S(2)}) collective-permute-start(bf16[96,768]{1,0:T(8,128)(2,1)S(1)} %down_sum.1.refs_2_.refs_0_), channel_id=1, source_target_pairs={{0,16},{1,17},{2,18},{3,19},{4,20},{5,21},{6,22},{7,23},{8,24},{9,... | collective-permute-start | bytes 442376 | tf_op jit(solution)/shard_map/ppermute | solution.py:480
  140.9 0.9 collective-permute-start.46
  141.8 3.6 %collective-permute-done.43.refs_1_ = bf16[96,768]{1,0:T(8,128)(2,1)S(1)} collective-permute-done((bf16[96,768]{1,0:T(8,128)(2,1)S(1)}, bf16[96,768]{1,0:T(8,128)(2,1)S(1)}, u32[]{:S(2)}, u32[]{:S(2)}) %collective-permute-start.43) | collective-permute-done | bytes 147488 | tf_op jit(solution)/shard_map/ppermute | solution.py:480
  145.4 4.3 %collective-permute-start.50 = (bf16[192,768]{1,0:T(8,128)(2,1)S(1)}, bf16[192,768]{1,0:T(8,128)(2,1)S(1)}, u32[]{:S(2)}, u32[]{:S(2)}) collective-permute-start(bf16[192,768]{1,0:T(8,128)(2,1)S(1)} %down_join.1.refs_2_.refs_0_), channel_id=1, source_target_pairs={{0,8},{1,9},{2,10},{3,11},{4,12},{5,13},{6,14},{7,15},{8,0},{9,1},... | collective-permute-start | bytes 884744 | tf_op jit(solution)/shard_map/ppermute | solution.py:480
  149.7 1.7 collective-permute-done.42.refs_1_
  151.6 3.0 %collective-permute-start.49 = (bf16[96,768]{1,0:T(8,128)(2,1)S(1)}, bf16[96,768]{1,0:T(8,128)(2,1)S(1)}, u32[]{:S(2)}, u32[]{:S(2)}) collective-permute-start(bf16[96,768]{1,0:T(8,128)(2,1)S(1)} %up_join.1.refs_3_.refs_0_), channel_id=1, source_target_pairs={{0,16},{1,17},{2,18},{3,19},{4,20},{5,21},{6,22},{7,23},{8,24},{9,... | collective-permute-start | bytes 442376 | tf_op jit(solution)/shard_map/ppermute | solution.py:480
  154.6 7.0 %collective-permute-done.45.refs_1_ = bf16[208,384]{1,0:T(8,128)(2,1)S(1)} collective-permute-done((bf16[208,384]{1,0:T(8,128)(2,1)S(1)}, bf16[208,384]{1,0:T(8,128)(2,1)S(1)}, u32[]{:S(2)}, u32[]{:S(2)}) %collective-permute-start.45) | collective-permute-done | bytes 159776 | tf_op jit(solution)/shard_map/ppermute | solution.py:480
  162.4 1.6 collective-permute-start.54
  164.0 1.8 collective-permute-start.48
  165.9 2.3 %collective-permute-done.48.refs_1_ = bf16[72,384]{1,0:T(8,128)(2,1)S(1)} collective-permute-done((bf16[72,384]{1,0:T(8,128)(2,1)S(1)}, bf16[72,384]{1,0:T(8,128)(2,1)S(1)}, u32[]{:S(2)}, u32[]{:S(2)}) %collective-permute-start.48) | collective-permute-done | bytes 55328 | tf_op jit(solution)/shard_map/ppermute | solution.py:480
  168.3 1.5 collective-permute-start.53
  169.8 5.2 %collective-permute-done.51.refs_1_ = bf16[192,384]{1,0:T(8,128)(2,1)S(1)} collective-permute-done((bf16[192,384]{1,0:T(8,128)(2,1)S(1)}, bf16[192,384]{1,0:T(8,128)(2,1)S(1)}, u32[]{:S(2)}, u32[]{:S(2)}) %collective-permute-start.51) | collective-permute-done | bytes 147488 | tf_op jit(solution)/shard_map/ppermute | solution.py:480
  175.1 1.6 down_out.1
  177.0 2.2 %collective-permute-start.57 = (bf16[384,768]{1,0:T(8,128)(2,1)S(1)}, bf16[384,768]{1,0:T(8,128)(2,1)S(1)}, u32[]{:S(2)}, u32[]{:S(2)}) collective-permute-start(bf16[384,768]{1,0:T(8,128)(2,1)S(1)} %up_join_near.1.refs_2_.refs_0_), channel_id=1, source_target_pairs={{0,4},{1,5},{2,6},{3,7},{4,0},{5,1},{6,2},{7,3},{8,12},{9,13},{10,... | collective-permute-start | bytes 1769480 | tf_op jit(solution)/shard_map/ppermute | solution.py:480
  179.1 2.7 %collective-permute-done.52.refs_1_ = bf16[384,384]{1,0:T(8,128)(2,1)S(1)} collective-permute-done((bf16[384,384]{1,0:T(8,128)(2,1)S(1)}, bf16[384,384]{1,0:T(8,128)(2,1)S(1)}, u32[]{:S(2)}, u32[]{:S(2)}) %collective-permute-start.52) | collective-permute-done | bytes 294944 | tf_op jit(solution)/shard_map/ppermute | solution.py:480
  181.8 1.0 collective-permute-start.55
  183.6 7.7 %collective-permute-done.57.refs_1_ = bf16[384,768]{1,0:T(8,128)(2,1)S(1)} collective-permute-done((bf16[384,768]{1,0:T(8,128)(2,1)S(1)}, bf16[384,768]{1,0:T(8,128)(2,1)S(1)}, u32[]{:S(2)}, u32[]{:S(2)}) %collective-permute-start.57) | collective-permute-done | bytes 589856 | tf_op jit(solution)/shard_map/ppermute | solution.py:480
  191.3 1.6 up_out.1
  192.9 4.7 %collective-permute-done.55.refs_1_ = bf16[768,384]{1,0:T(8,128)(2,1)S(1)} collective-permute-done((bf16[768,384]{1,0:T(8,128)(2,1)S(1)}, bf16[768,384]{1,0:T(8,128)(2,1)S(1)}, u32[]{:S(2)}, u32[]{:S(2)}) %collective-permute-start.55) | collective-permute-done | bytes 589856 | tf_op jit(solution)/shard_map/ppermute | solution.py:480
  197.6 1.7 rest_out.1
  (102 shorter events, 17.3 us)
Async XLA Ops:
  1.6 29.0 %copy-start = (bf16[768,768]{1,0:T(8,128)(2,1)S(1)}, bf16[768,768]{1,0:T(8,128)(2,1)}, u32[]{:S(2)}) copy-start(bf16[768,768]{1,0:T(8,128)(2,1)} %refs_5_.5) | copy-start | bytes 3538948
  3.2 17.4 %collective-permute-start.2 = (bf16[592,384]{1,0:T(8,128)(2,1)S(1)}, bf16[592,384]{1,0:T(8,128)(2,1)S(1)}, u32[]{:S(2)}, u32[]{:S(2)}) collective-permute-start(bf16[592,384]{1,0:T(8,128)(2,1)S(1)} %get-tuple-element.121.refs_2_), channel_id=1, source_target_pairs={{0,2},{1,3},{2,0},{3,1},{4,6},{5,7},{6,4},{7,5},{8,10},{9,11},{10,... | collective-permute-start | bytes 1363976 | tf_op jit(solution)/shard_map/ppermute | solution.py:480
  6.2 14.4 %collective-permute-start.1 = (bf16[592,384]{1,0:T(8,128)(2,1)S(1)}, bf16[592,384]{1,0:T(8,128)(2,1)S(1)}, u32[]{:S(2)}, u32[]{:S(2)}) collective-permute-start(bf16[592,384]{1,0:T(8,128)(2,1)S(1)} %get-tuple-element.120.refs_10_), channel_id=1, source_target_pairs={{0,1},{1,0},{2,3},{3,2},{4,5},{5,4},{6,7},{7,6},{8,9},{9,8},{10,11... | collective-permute-start | bytes 1363976 | tf_op jit(solution)/shard_map/ppermute | solution.py:480
  6.2 14.4 %collective-permute-start.3 = (bf16[192,768]{1,0:T(8,128)(2,1)}, bf16[192,768]{1,0:T(8,128)(2,1)S(1)}, u32[]{:S(2)}, u32[]{:S(2)}) collective-permute-start(bf16[192,768]{1,0:T(8,128)(2,1)} %refs_12_.1), channel_id=1, source_target_pairs={{0,1},{1,0},{2,3},{3,2},{4,5},{5,4},{6,7},{7,6},{8,9},{9,8},{10,11... | collective-permute-start | bytes 884744 | tf_op jit(solution)/shard_map/ppermute | solution.py:480
  6.7 13.9 %collective-permute-start = (bf16[144,768]{1,0:T(8,128)(2,1)S(1)}, bf16[144,768]{1,0:T(8,128)(2,1)S(1)}, u32[]{:S(2)}, u32[]{:S(2)}) collective-permute-start(bf16[144,768]{1,0:T(8,128)(2,1)S(1)} %block.1.refs_12_), channel_id=1, source_target_pairs={{0,0},{1,16},{2,8},{3,24},{4,4},{5,20},{6,12},{7,28},{8,2},{9,18},... | collective-permute-start | bytes 663560 | tf_op jit(solution)/shard_map/ppermute | solution.py:480
  20.7 15.0 %collective-permute-start.9 = (bf16[592,384]{1,0:T(8,128)(2,1)S(1)}, bf16[592,384]{1,0:T(8,128)(2,1)S(1)}, u32[]{:S(2)}, u32[]{:S(2)}) collective-permute-start(bf16[592,384]{1,0:T(8,128)(2,1)S(1)} %collective-permute-done.2.refs_2_.refs_7_), channel_id=1, source_target_pairs={{0,1},{1,0},{2,3},{3,2},{4,5},{5,4},{6,7},{7,6},{8,9},{9,8},{10,11... | collective-permute-start | bytes 1363976 | tf_op jit(solution)/shard_map/ppermute | solution.py:480
  20.7 7.9 %collective-permute-start.5 = (bf16[144,768]{1,0:T(8,128)(2,1)S(1)}, bf16[144,768]{1,0:T(8,128)(2,1)S(1)}, u32[]{:S(2)}, u32[]{:S(2)}) collective-permute-start(bf16[144,768]{1,0:T(8,128)(2,1)S(1)} %once.5.refs_0_), channel_id=1, source_target_pairs={{0,4},{1,5},{2,6},{3,7},{4,0},{5,1},{6,2},{7,3},{8,12},{9,13},{10,... | collective-permute-start | bytes 663560 | tf_op jit(solution)/shard_map/ppermute | solution.py:480
  22.3 8.3 %collective-permute-start.4 = (bf16[144,768]{1,0:T(8,128)(2,1)S(1)}, bf16[144,768]{1,0:T(8,128)(2,1)S(1)}, u32[]{:S(2)}, u32[]{:S(2)}) collective-permute-start(bf16[144,768]{1,0:T(8,128)(2,1)S(1)} %once.5.refs_0_), channel_id=1, source_target_pairs={{0,2},{1,3},{2,0},{3,1},{4,6},{5,7},{6,4},{7,5},{8,10},{9,11},{10,... | collective-permute-start | bytes 663560 | tf_op jit(solution)/shard_map/ppermute | solution.py:480
  24.8 9.0 %collective-permute-start.6 = (bf16[144,768]{1,0:T(8,128)(2,1)S(1)}, bf16[144,768]{1,0:T(8,128)(2,1)S(1)}, u32[]{:S(2)}, u32[]{:S(2)}) collective-permute-start(bf16[144,768]{1,0:T(8,128)(2,1)S(1)} %once.5.refs_0_), channel_id=1, source_target_pairs={{0,1},{1,0},{2,3},{3,2},{4,5},{5,4},{6,7},{7,6},{8,9},{9,8},{10,11... | collective-permute-start | bytes 663560 | tf_op jit(solution)/shard_map/ppermute | solution.py:480
  30.6 5.1 %collective-permute-start.7 = (bf16[144,768]{1,0:T(8,128)(2,1)S(1)}, bf16[144,768]{1,0:T(8,128)(2,1)S(1)}, u32[]{:S(2)}, u32[]{:S(2)}) collective-permute-start(bf16[144,768]{1,0:T(8,128)(2,1)S(1)} %once.6.refs_1_), channel_id=1, source_target_pairs={{0,1},{1,0},{2,3},{3,2},{4,5},{5,4},{6,7},{7,6},{8,9},{9,8},{10,11... | collective-permute-start | bytes 663560 | tf_op jit(solution)/shard_map/ppermute | solution.py:480
  30.6 9.4 %collective-permute-start.12 = (bf16[768,768]{1,0:T(8,128)(2,1)S(1)}, bf16[768,768]{1,0:T(8,128)(2,1)S(1)}, u32[]{:S(2)}, u32[]{:S(2)}) collective-permute-start(bf16[768,768]{1,0:T(8,128)(2,1)S(1)} %copy-done), channel_id=1, source_target_pairs={{0,1},{1,0},{2,3},{3,2},{4,5},{5,4},{6,7},{7,6},{8,9},{9,8},{10,11... | collective-permute-start | bytes 3538952 | tf_op jit(solution)/shard_map/ppermute | solution.py:480
  31.1 7.4 %collective-permute-start.8 = (bf16[144,768]{1,0:T(8,128)(2,1)S(1)}, bf16[144,768]{1,0:T(8,128)(2,1)S(1)}, u32[]{:S(2)}, u32[]{:S(2)}) collective-permute-start(bf16[144,768]{1,0:T(8,128)(2,1)S(1)} %once.6.refs_1_), channel_id=1, source_target_pairs={{0,4},{1,5},{2,6},{3,7},{4,0},{5,1},{6,2},{7,3},{8,12},{9,13},{10,... | collective-permute-start | bytes 663560 | tf_op jit(solution)/shard_map/ppermute | solution.py:480
  33.8 15.0 %collective-permute-start.14 = (bf16[192,1536]{1,0:T(8,128)(2,1)S(1)}, bf16[192,1536]{1,0:T(8,128)(2,1)S(1)}, u32[]{:S(2)}, u32[]{:S(2)}) collective-permute-start(bf16[192,1536]{1,0:T(8,128)(2,1)S(1)} %get-tuple-element.122.refs_1_), channel_id=1, source_target_pairs={{0,2},{1,3},{2,0},{3,1},{4,6},{5,7},{6,4},{7,5},{8,10},{9,11},{10,... | collective-permute-start | bytes 1769480 | tf_op jit(solution)/shard_map/ppermute | solution.py:480
  35.6 12.5 %collective-permute-start.15 = (bf16[192,1536]{1,0:T(8,128)(2,1)S(1)}, bf16[192,1536]{1,0:T(8,128)(2,1)S(1)}, u32[]{:S(2)}, u32[]{:S(2)}) collective-permute-start(bf16[192,1536]{1,0:T(8,128)(2,1)S(1)} %get-tuple-element.132), channel_id=1, source_target_pairs={{0,1},{1,0},{2,3},{3,2},{4,5},{5,4},{6,7},{7,6},{8,9},{9,8},{10,11... | collective-permute-start | bytes 1769480 | tf_op jit(solution)/shard_map/ppermute | solution.py:480
  35.6 3.0 %collective-permute-start.10 = (bf16[144,768]{1,0:T(8,128)(2,1)S(1)}, bf16[144,768]{1,0:T(8,128)(2,1)S(1)}, u32[]{:S(2)}, u32[]{:S(2)}) collective-permute-start(bf16[144,768]{1,0:T(8,128)(2,1)S(1)} %collective-permute-done.5.refs_1_.refs_4_), channel_id=1, source_target_pairs={{0,1},{1,0},{2,3},{3,2},{4,5},{5,4},{6,7},{7,6},{8,9},{9,8},{10,11... | collective-permute-start | bytes 663560 | tf_op jit(solution)/shard_map/ppermute | solution.py:480
  38.5 1.5 collective-permute-start.11
  46.5 11.2 %collective-permute-start.13 = (bf16[256,768]{1,0:T(8,128)(2,1)S(1)}, bf16[256,768]{1,0:T(8,128)(2,1)S(1)}, u32[]{:S(2)}, u32[]{:S(2)}) collective-permute-start(bf16[256,768]{1,0:T(8,128)(2,1)S(1)} %get-tuple-element.129.refs_2_), channel_id=1, source_target_pairs={{0,2},{1,3},{2,0},{3,1},{4,6},{5,7},{6,4},{7,5},{8,10},{9,11},{10,... | collective-permute-start | bytes 1179656 | tf_op jit(solution)/shard_map/ppermute | solution.py:480
  48.9 1.6 collective-permute-start.17
  49.0 2.0 collective-permute-start.16
  52.5 10.4 %collective-permute-start.21 = (bf16[128,768]{1,0:T(8,128)(2,1)S(1)}, bf16[128,768]{1,0:T(8,128)(2,1)S(1)}, u32[]{:S(2)}, u32[]{:S(2)}) collective-permute-start(bf16[128,768]{1,0:T(8,128)(2,1)S(1)} %once.9), channel_id=1, source_target_pairs={{0,2},{1,18},{2,10},{3,26},{4,6},{5,22},{6,14},{7,30},{8,0},{9,16}... | collective-permute-start | bytes 589832 | tf_op jit(solution)/shard_map/ppermute | solution.py:480
  54.3 8.6 %collective-permute-start.20 = (bf16[128,768]{1,0:T(8,128)(2,1)S(1)}, bf16[128,768]{1,0:T(8,128)(2,1)S(1)}, u32[]{:S(2)}, u32[]{:S(2)}) collective-permute-start(bf16[128,768]{1,0:T(8,128)(2,1)S(1)} %once.9), channel_id=1, source_target_pairs={{0,0},{1,16},{2,8},{3,24},{4,4},{5,20},{6,12},{7,28},{8,2},{9,18},... | collective-permute-start | bytes 589832 | tf_op jit(solution)/shard_map/ppermute | solution.py:480
  59.7 11.1 %collective-permute-start.19 = (bf16[128,768]{1,0:T(8,128)(2,1)S(1)}, bf16[128,768]{1,0:T(8,128)(2,1)S(1)}, u32[]{:S(2)}, u32[]{:S(2)}) collective-permute-start(bf16[128,768]{1,0:T(8,128)(2,1)S(1)} %get-tuple-element.137), channel_id=1, source_target_pairs={{0,2},{1,3},{2,0},{3,1},{4,6},{5,7},{6,4},{7,5},{8,10},{9,11},{10,... | collective-permute-start | bytes 589832 | tf_op jit(solution)/shard_map/ppermute | solution.py:480
  61.4 13.5 %collective-permute-start.18 = (bf16[128,768]{1,0:T(8,128)(2,1)S(1)}, bf16[128,768]{1,0:T(8,128)(2,1)S(1)}, u32[]{:S(2)}, u32[]{:S(2)}) collective-permute-start(bf16[128,768]{1,0:T(8,128)(2,1)S(1)} %get-tuple-element.136.refs_7_), channel_id=1, source_target_pairs={{0,2},{1,3},{2,0},{3,1},{4,6},{5,7},{6,4},{7,5},{8,10},{9,11},{10,... | collective-permute-start | bytes 589832 | tf_op jit(solution)/shard_map/ppermute | solution.py:480
  76.6 4.3 %collective-permute-start.23 = (bf16[768,768]{1,0:T(8,128)(2,1)S(1)}, bf16[768,768]{1,0:T(8,128)(2,1)S(1)}, u32[]{:S(2)}, u32[]{:S(2)}) collective-permute-start(bf16[768,768]{1,0:T(8,128)(2,1)S(1)} %get-tuple-element.143.refs_5_), channel_id=1, source_target_pairs={{0,1},{1,0},{2,3},{3,2},{4,5},{5,4},{6,7},{7,6},{8,9},{9,8},{10,11... | collective-permute-start | bytes 3538952 | tf_op jit(solution)/shard_map/ppermute | solution.py:480
  78.4 13.4 %collective-permute-start.22 = (bf16[256,768]{1,0:T(8,128)(2,1)S(1)}, bf16[256,768]{1,0:T(8,128)(2,1)S(1)}, u32[]{:S(2)}, u32[]{:S(2)}) collective-permute-start(bf16[256,768]{1,0:T(8,128)(2,1)S(1)} %get-tuple-element.145.refs_2_), channel_id=1, source_target_pairs={{0,2},{1,3},{2,0},{3,1},{4,6},{5,7},{6,4},{7,5},{8,10},{9,11},{10,... | collective-permute-start | bytes 1179656 | tf_op jit(solution)/shard_map/ppermute | solution.py:480
  82.8 1.6 collective-permute-start.25
  83.1 2.2 %collective-permute-start.26 = (bf16[192,768]{1,0:T(8,128)(2,1)S(1)}, bf16[192,768]{1,0:T(8,128)(2,1)S(1)}, u32[]{:S(2)}, u32[]{:S(2)}) collective-permute-start(bf16[192,768]{1,0:T(8,128)(2,1)S(1)} %get-tuple-element.160), channel_id=1, source_target_pairs={{0,1},{1,0},{2,3},{3,2},{4,5},{5,4},{6,7},{7,6},{8,9},{9,8},{10,11... | collective-permute-start | bytes 884744 | tf_op jit(solution)/shard_map/ppermute | solution.py:480
  83.4 3.1 %collective-permute-start.27 = (bf16[192,768]{1,0:T(8,128)(2,1)S(1)}, bf16[192,768]{1,0:T(8,128)(2,1)S(1)}, u32[]{:S(2)}, u32[]{:S(2)}) collective-permute-start(bf16[192,768]{1,0:T(8,128)(2,1)S(1)} %get-tuple-element.161), channel_id=1, source_target_pairs={{0,1},{1,0},{2,3},{3,2},{4,5},{5,4},{6,7},{7,6},{8,9},{9,8},{10,11... | collective-permute-start | bytes 884744 | tf_op jit(solution)/shard_map/ppermute | solution.py:480
  83.7 3.8 %collective-permute-start.24 = (bf16[192,768]{1,0:T(8,128)(2,1)S(1)}, bf16[192,768]{1,0:T(8,128)(2,1)S(1)}, u32[]{:S(2)}, u32[]{:S(2)}) collective-permute-start(bf16[192,768]{1,0:T(8,128)(2,1)S(1)} %get-tuple-element.158.refs_5_), channel_id=1, source_target_pairs={{0,1},{1,0},{2,3},{3,2},{4,5},{5,4},{6,7},{7,6},{8,9},{9,8},{10,11... | collective-permute-start | bytes 884744 | tf_op jit(solution)/shard_map/ppermute | solution.py:480
  84.5 15.4 %collective-permute-start.28 = (bf16[128,768]{1,0:T(8,128)(2,1)S(1)}, bf16[128,768]{1,0:T(8,128)(2,1)S(1)}, u32[]{:S(2)}, u32[]{:S(2)}) collective-permute-start(bf16[128,768]{1,0:T(8,128)(2,1)S(1)} %get-tuple-element.170), channel_id=1, source_target_pairs={{0,0},{1,16},{2,8},{3,24},{4,4},{5,20},{6,12},{7,28},{8,2},{9,18},... | collective-permute-start | bytes 589832 | tf_op jit(solution)/shard_map/ppermute | solution.py:480
  85.4 14.3 %collective-permute-start.29 = (bf16[192,768]{1,0:T(8,128)(2,1)S(1)}, bf16[192,768]{1,0:T(8,128)(2,1)S(1)}, u32[]{:S(2)}, u32[]{:S(2)}) collective-permute-start(bf16[192,768]{1,0:T(8,128)(2,1)S(1)} %get-tuple-element.156.refs_2_), channel_id=1, source_target_pairs={{0,4},{1,5},{2,6},{3,7},{4,0},{5,1},{6,2},{7,3},{8,12},{9,13},{10,... | collective-permute-start | bytes 884744 | tf_op jit(solution)/shard_map/ppermute | solution.py:480
  86.5 13.1 %collective-permute-start.30 = (bf16[192,768]{1,0:T(8,128)(2,1)S(1)}, bf16[192,768]{1,0:T(8,128)(2,1)S(1)}, u32[]{:S(2)}, u32[]{:S(2)}) collective-permute-start(bf16[192,768]{1,0:T(8,128)(2,1)S(1)} %get-tuple-element.172), channel_id=1, source_target_pairs={{0,4},{1,5},{2,6},{3,7},{4,0},{5,1},{6,2},{7,3},{8,12},{9,13},{10,... | collective-permute-start | bytes 884744 | tf_op jit(solution)/shard_map/ppermute | solution.py:480
  87.9 21.5 %collective-permute-start.35 = (bf16[384,768]{1,0:T(8,128)(2,1)S(1)}, bf16[384,768]{1,0:T(8,128)(2,1)S(1)}, u32[]{:S(2)}, u32[]{:S(2)}) collective-permute-start(bf16[384,768]{1,0:T(8,128)(2,1)S(1)} %get-tuple-element.162.refs_13_), channel_id=1, source_target_pairs={{0,8},{1,9},{2,10},{3,11},{4,12},{5,13},{6,14},{7,15},{8,0},{9,1},... | collective-permute-start | bytes 1769480 | tf_op jit(solution)/shard_map/ppermute | solution.py:480
  102.5 5.6 %collective-permute-start.33 = (bf16[528,384]{1,0:T(8,128)(2,1)S(1)}, bf16[528,384]{1,0:T(8,128)(2,1)S(1)}, u32[]{:S(2)}, u32[]{:S(2)}) collective-permute-start(bf16[528,384]{1,0:T(8,128)(2,1)S(1)} %get-tuple-element.177), channel_id=1, source_target_pairs={{0,1},{1,0},{2,3},{3,2},{4,5},{5,4},{6,7},{7,6},{8,9},{9,8},{10,11... | collective-permute-start | bytes 1216520 | tf_op jit(solution)/shard_map/ppermute | solution.py:480
  104.7 3.5 %collective-permute-start.32 = (bf16[512,384]{1,0:T(8,128)(2,1)S(1)}, bf16[512,384]{1,0:T(8,128)(2,1)S(1)}, u32[]{:S(2)}, u32[]{:S(2)}) collective-permute-start(bf16[512,384]{1,0:T(8,128)(2,1)S(1)} %get-tuple-element.176), channel_id=1, source_target_pairs={{0,1},{1,0},{2,3},{3,2},{4,5},{5,4},{6,7},{7,6},{8,9},{9,8},{10,11... | collective-permute-start | bytes 1179656 | tf_op jit(solution)/shard_map/ppermute | solution.py:480
  104.8 3.4 %collective-permute-start.31 = (bf16[512,384]{1,0:T(8,128)(2,1)S(1)}, bf16[512,384]{1,0:T(8,128)(2,1)S(1)}, u32[]{:S(2)}, u32[]{:S(2)}) collective-permute-start(bf16[512,384]{1,0:T(8,128)(2,1)S(1)} %get-tuple-element.175.refs_4_), channel_id=1, source_target_pairs={{0,1},{1,0},{2,3},{3,2},{4,5},{5,4},{6,7},{7,6},{8,9},{9,8},{10,11... | collective-permute-start | bytes 1179656 | tf_op jit(solution)/shard_map/ppermute | solution.py:480
  105.2 10.6 %collective-permute-start.39 = (bf16[192,768]{1,0:T(8,128)(2,1)S(1)}, bf16[192,768]{1,0:T(8,128)(2,1)S(1)}, u32[]{:S(2)}, u32[]{:S(2)}) collective-permute-start(bf16[192,768]{1,0:T(8,128)(2,1)S(1)} %get-tuple-element.173.refs_10_), channel_id=1, source_target_pairs={{0,8},{1,9},{2,10},{3,11},{4,12},{5,13},{6,14},{7,15},{8,0},{9,1},... | collective-permute-start | bytes 884744 | tf_op jit(solution)/shard_map/ppermute | solution.py:480
  111.6 6.4 %collective-permute-start.38 = (bf16[256,768]{1,0:T(8,128)(2,1)S(1)}, bf16[256,768]{1,0:T(8,128)(2,1)S(1)}, u32[]{:S(2)}, u32[]{:S(2)}) collective-permute-start(bf16[256,768]{1,0:T(8,128)(2,1)S(1)} %get-tuple-element.185), channel_id=1, source_target_pairs={{0,1},{1,0},{2,3},{3,2},{4,5},{5,4},{6,7},{7,6},{8,9},{9,8},{10,11... | collective-permute-start | bytes 1179656 | tf_op jit(solution)/shard_map/ppermute | solution.py:480
  111.6 6.3 %collective-permute-start.37 = (bf16[256,768]{1,0:T(8,128)(2,1)S(1)}, bf16[256,768]{1,0:T(8,128)(2,1)S(1)}, u32[]{:S(2)}, u32[]{:S(2)}) collective-permute-start(bf16[256,768]{1,0:T(8,128)(2,1)S(1)} %get-tuple-element.184.refs_2_), channel_id=1, source_target_pairs={{0,1},{1,0},{2,3},{3,2},{4,5},{5,4},{6,7},{7,6},{8,9},{9,8},{10,11... | collective-permute-start | bytes 1179656 | tf_op jit(solution)/shard_map/ppermute | solution.py:480
  112.1 20.2 %collective-permute-start.36 = (bf16[192,768]{1,0:T(8,128)(2,1)S(1)}, bf16[192,768]{1,0:T(8,128)(2,1)S(1)}, u32[]{:S(2)}, u32[]{:S(2)}) collective-permute-start(bf16[192,768]{1,0:T(8,128)(2,1)S(1)} %get-tuple-element.182.refs_3_), channel_id=1, source_target_pairs={{0,16},{1,17},{2,18},{3,19},{4,20},{5,21},{6,22},{7,23},{8,24},{9,... | collective-permute-start | bytes 884744 | tf_op jit(solution)/shard_map/ppermute | solution.py:480
  115.8 18.8 %collective-permute-start.41 = (bf16[96,768]{1,0:T(8,128)(2,1)S(1)}, bf16[96,768]{1,0:T(8,128)(2,1)S(1)}, u32[]{:S(2)}, u32[]{:S(2)}) collective-permute-start(bf16[96,768]{1,0:T(8,128)(2,1)S(1)} %get-tuple-element.187.refs_3_), channel_id=1, source_target_pairs={{0,16},{1,17},{2,18},{3,19},{4,20},{5,21},{6,22},{7,23},{8,24},{9,... | collective-permute-start | bytes 442376 | tf_op jit(solution)/shard_map/ppermute | solution.py:480
  117.2 20.5 %collective-permute-start.34 = (bf16[784,384]{1,0:T(8,128)(2,1)S(1)}, bf16[784,384]{1,0:T(8,128)(2,1)S(1)}, u32[]{:S(2)}, u32[]{:S(2)}) collective-permute-start(bf16[784,384]{1,0:T(8,128)(2,1)S(1)} %get-tuple-element.179.refs_2_), channel_id=1, source_target_pairs={{0,4},{1,5},{2,6},{3,7},{4,0},{5,1},{6,2},{7,3},{8,12},{9,13},{10,... | collective-permute-start | bytes 1806344 | tf_op jit(solution)/shard_map/ppermute | solution.py:480
  118.2 22.6 %collective-permute-start.44 = (bf16[256,768]{1,0:T(8,128)(2,1)S(1)}, bf16[256,768]{1,0:T(8,128)(2,1)S(1)}, u32[]{:S(2)}, u32[]{:S(2)}) collective-permute-start(bf16[256,768]{1,0:T(8,128)(2,1)S(1)} %get-tuple-element.188.refs_2_), channel_id=1, source_target_pairs={{0,2},{1,3},{2,0},{3,1},{4,6},{5,7},{6,4},{7,5},{8,10},{9,11},{10,... | collective-permute-start | bytes 1179656 | tf_op jit(solution)/shard_map/ppermute | solution.py:480
  132.4 5.2 %collective-permute-start.40 = (bf16[96,768]{1,0:T(8,128)(2,1)S(1)}, bf16[96,768]{1,0:T(8,128)(2,1)S(1)}, u32[]{:S(2)}, u32[]{:S(2)}) collective-permute-start(bf16[96,768]{1,0:T(8,128)(2,1)S(1)} %get-tuple-element.190.refs_2_), channel_id=1, source_target_pairs={{0,4},{1,5},{2,6},{3,7},{4,0},{5,1},{6,2},{7,3},{8,12},{9,13},{10,... | collective-permute-start | bytes 442376 | tf_op jit(solution)/shard_map/ppermute | solution.py:480
  137.9 13.4 %collective-permute-start.42 = (bf16[400,384]{1,0:T(8,128)(2,1)S(1)}, bf16[400,384]{1,0:T(8,128)(2,1)S(1)}, u32[]{:S(2)}, u32[]{:S(2)}) collective-permute-start(bf16[400,384]{1,0:T(8,128)(2,1)S(1)} %get-tuple-element.194.refs_2_), channel_id=1, source_target_pairs={{0,8},{1,9},{2,10},{3,11},{4,12},{5,13},{6,14},{7,15},{8,0},{9,1},... | collective-permute-start | bytes 921608 | tf_op jit(solution)/shard_map/ppermute | solution.py:480
  138.0 7.4 %collective-permute-start.43 = (bf16[96,768]{1,0:T(8,128)(2,1)S(1)}, bf16[96,768]{1,0:T(8,128)(2,1)S(1)}, u32[]{:S(2)}, u32[]{:S(2)}) collective-permute-start(bf16[96,768]{1,0:T(8,128)(2,1)S(1)} %down_sum.1.refs_2_.refs_0_), channel_id=1, source_target_pairs={{0,16},{1,17},{2,18},{3,19},{4,20},{5,21},{6,22},{7,23},{8,24},{9,... | collective-permute-start | bytes 442376 | tf_op jit(solution)/shard_map/ppermute | solution.py:480
  140.8 10.8 %collective-permute-start.47 = (bf16[48,768]{1,0:T(8,128)(2,1)S(1)}, bf16[48,768]{1,0:T(8,128)(2,1)S(1)}, u32[]{:S(2)}, u32[]{:S(2)}) collective-permute-start(bf16[48,768]{1,0:T(8,128)(2,1)S(1)} %get-tuple-element.192.refs_2_), channel_id=1, source_target_pairs={{0,2},{1,3},{2,0},{3,1},{4,6},{5,7},{6,4},{7,5},{8,10},{9,11},{10,... | collective-permute-start | bytes 221192 | tf_op jit(solution)/shard_map/ppermute | solution.py:480
  140.9 13.7 %collective-permute-start.46 = (bf16[128,768]{1,0:T(8,128)(2,1)S(1)}, bf16[128,768]{1,0:T(8,128)(2,1)S(1)}, u32[]{:S(2)}, u32[]{:S(2)}) collective-permute-start(bf16[128,768]{1,0:T(8,128)(2,1)S(1)} %get-tuple-element.196.refs_2_), channel_id=1, source_target_pairs={{0,4},{1,5},{2,6},{3,7},{4,0},{5,1},{6,2},{7,3},{8,12},{9,13},{10,... | collective-permute-start | bytes 589832 | tf_op jit(solution)/shard_map/ppermute | solution.py:480
  145.4 16.9 %collective-permute-start.50 = (bf16[192,768]{1,0:T(8,128)(2,1)S(1)}, bf16[192,768]{1,0:T(8,128)(2,1)S(1)}, u32[]{:S(2)}, u32[]{:S(2)}) collective-permute-start(bf16[192,768]{1,0:T(8,128)(2,1)S(1)} %down_join.1.refs_2_.refs_0_), channel_id=1, source_target_pairs={{0,8},{1,9},{2,10},{3,11},{4,12},{5,13},{6,14},{7,15},{8,0},{9,1},... | collective-permute-start | bytes 884744 | tf_op jit(solution)/shard_map/ppermute | solution.py:480
  151.5 10.2 %collective-permute-start.45 = (bf16[208,384]{1,0:T(8,128)(2,1)S(1)}, bf16[208,384]{1,0:T(8,128)(2,1)S(1)}, u32[]{:S(2)}, u32[]{:S(2)}) collective-permute-start(bf16[208,384]{1,0:T(8,128)(2,1)S(1)} %get-tuple-element.198.refs_2_), channel_id=1, source_target_pairs={{0,16},{1,17},{2,18},{3,19},{4,20},{5,21},{6,22},{7,23},{8,24},{9,... | collective-permute-start | bytes 479240 | tf_op jit(solution)/shard_map/ppermute | solution.py:480
  151.6 14.2 %collective-permute-start.49 = (bf16[96,768]{1,0:T(8,128)(2,1)S(1)}, bf16[96,768]{1,0:T(8,128)(2,1)S(1)}, u32[]{:S(2)}, u32[]{:S(2)}) collective-permute-start(bf16[96,768]{1,0:T(8,128)(2,1)S(1)} %up_join.1.refs_3_.refs_0_), channel_id=1, source_target_pairs={{0,16},{1,17},{2,18},{3,19},{4,20},{5,21},{6,22},{7,23},{8,24},{9,... | collective-permute-start | bytes 442376 | tf_op jit(solution)/shard_map/ppermute | solution.py:480
  162.4 12.7 %collective-permute-start.54 = (bf16[384,768]{1,0:T(8,128)(2,1)S(1)}, bf16[384,768]{1,0:T(8,128)(2,1)S(1)}, u32[]{:S(2)}, u32[]{:S(2)}) collective-permute-start(bf16[384,768]{1,0:T(8,128)(2,1)S(1)} %down_join_near.1.refs_2_.refs_0_), channel_id=1, source_target_pairs={{0,4},{1,5},{2,6},{3,7},{4,0},{5,1},{6,2},{7,3},{8,12},{9,13},{10,... | collective-permute-start | bytes 1769480 | tf_op jit(solution)/shard_map/ppermute | solution.py:480
  164.0 4.2 %collective-permute-start.48 = (bf16[72,384]{1,0:T(8,128)(2,1)S(1)}, bf16[72,384]{1,0:T(8,128)(2,1)S(1)}, u32[]{:S(2)}, u32[]{:S(2)}) collective-permute-start(bf16[72,384]{1,0:T(8,128)(2,1)S(1)} %get-tuple-element.203.refs_2_), channel_id=1, source_target_pairs={{0,2},{1,3},{2,0},{3,1},{4,6},{5,7},{6,4},{7,5},{8,10},{9,11},{10,... | collective-permute-start | bytes 165896 | tf_op jit(solution)/shard_map/ppermute | solution.py:480
  168.2 6.8 %collective-permute-start.51 = (bf16[192,384]{1,0:T(8,128)(2,1)S(1)}, bf16[192,384]{1,0:T(8,128)(2,1)S(1)}, u32[]{:S(2)}, u32[]{:S(2)}) collective-permute-start(bf16[192,384]{1,0:T(8,128)(2,1)S(1)} %rest_join.1.refs_0_.refs_2_), channel_id=1, source_target_pairs={{0,16},{1,17},{2,18},{3,19},{4,20},{5,21},{6,22},{7,23},{8,24},{9,... | collective-permute-start | bytes 442376 | tf_op jit(solution)/shard_map/ppermute | solution.py:480
  168.3 8.7 %collective-permute-start.53 = (bf16[192,768]{1,0:T(8,128)(2,1)S(1)}, bf16[192,768]{1,0:T(8,128)(2,1)S(1)}, u32[]{:S(2)}, u32[]{:S(2)}) collective-permute-start(bf16[192,768]{1,0:T(8,128)(2,1)S(1)} %up_join_far.1.refs_2_.refs_0_), channel_id=1, source_target_pairs={{0,8},{1,9},{2,10},{3,11},{4,12},{5,13},{6,14},{7,15},{8,0},{9,1},... | collective-permute-start | bytes 884744 | tf_op jit(solution)/shard_map/ppermute | solution.py:480
  175.0 6.8 %collective-permute-start.52 = (bf16[384,384]{1,0:T(8,128)(2,1)S(1)}, bf16[384,384]{1,0:T(8,128)(2,1)S(1)}, u32[]{:S(2)}, u32[]{:S(2)}) collective-permute-start(bf16[384,384]{1,0:T(8,128)(2,1)S(1)} %rest_join_far.1.refs_2_.refs_0_), channel_id=1, source_target_pairs={{0,8},{1,9},{2,10},{3,11},{4,12},{5,13},{6,14},{7,15},{8,0},{9,1},... | collective-permute-start | bytes 884744 | tf_op jit(solution)/shard_map/ppermute | solution.py:480
  177.0 14.3 %collective-permute-start.57 = (bf16[384,768]{1,0:T(8,128)(2,1)S(1)}, bf16[384,768]{1,0:T(8,128)(2,1)S(1)}, u32[]{:S(2)}, u32[]{:S(2)}) collective-permute-start(bf16[384,768]{1,0:T(8,128)(2,1)S(1)} %up_join_near.1.refs_2_.refs_0_), channel_id=1, source_target_pairs={{0,4},{1,5},{2,6},{3,7},{4,0},{5,1},{6,2},{7,3},{8,12},{9,13},{10,... | collective-permute-start | bytes 1769480 | tf_op jit(solution)/shard_map/ppermute | solution.py:480
  181.8 15.8 %collective-permute-start.55 = (bf16[768,384]{1,0:T(8,128)(2,1)S(1)}, bf16[768,384]{1,0:T(8,128)(2,1)S(1)}, u32[]{:S(2)}, u32[]{:S(2)}) collective-permute-start(bf16[768,384]{1,0:T(8,128)(2,1)S(1)} %rest_join_near.1.refs_2_.refs_0_), channel_id=1, source_target_pairs={{0,4},{1,5},{2,6},{3,7},{4,0},{5,1},{6,2},{7,3},{8,12},{9,13},{10,... | collective-permute-start | bytes 1769480 | tf_op jit(solution)/shard_map/ppermute | solution.py:480
  182.9 10.0 %collective-permute-start.56 = (bf16[128,768]{1,0:T(8,128)(2,1)S(1)}, bf16[128,768]{1,0:T(8,128)(2,1)S(1)}, u32[]{:S(2)}, u32[]{:S(2)}) collective-permute-start(bf16[128,768]{1,0:T(8,128)(2,1)S(1)} %input_sum.1.refs_2_), channel_id=1, source_target_pairs={{0,0},{1,16},{2,8},{3,24},{4,4},{5,20},{6,12},{7,28},{8,2},{9,18},... | collective-permute-start | bytes 589832 | tf_op jit(solution)/shard_map/ppermute | solution.py:480

commit v6 on v5

--- a/solution.py
+++ b/solution.py
@@ -583,10 +583,13 @@
     part, width = w_q.shape
     half = width // 2
     copies = Copies(sems)
+    few = part // 2
     for t, w in enumerate((w_q, w_k, w_v)):
-        rows = pl.ds(part * t, part)
-        copies.start(w.at[:, pl.ds(pl.multiple_of(half * x, 128), half)], mine.at[rows])
-        copies.start(w.at[:, pl.ds(pl.multiple_of(half * (1 - x), 128), half)], theirs.at[rows])
+        copies.start(w.at[:, pl.ds(pl.multiple_of(half * x, 128), half)], mine.at[pl.ds(part * t, part)])
+        copies.start(
+            w.at[pl.ds(pl.multiple_of(few * r, 32), few), pl.ds(pl.multiple_of(half * (1 - x), 128), half)],
+            theirs.at[pl.ds(few * t, few)],
+        )
     for vector, held in zip(vectors, thin):
         copies.start(vector, held)
     copies.start(b_up, thick)
@@ -603,7 +606,7 @@
     lines[pl.ds(9 + 2 * c, 1), :] = wide[:, half:]
     low = lines[...].astype(jnp.bfloat16)
     mine[3 * part :, :] = low
-    theirs[3 * part :, :] = low
+    theirs[3 * few :, :] = low
 
 
 def cut_kernel(w, theirs, mine, sems):
@@ -627,7 +630,7 @@
 
 
 def project_kernel(
-    b0, b1, b2, b3, w_q, w_k, w_v, w_x, w_m, w_mx, own_lines,
+    b0, b1, b2, b3, w_q, w_k, w_v, w_m, xa, xb, ma, mb, own_lines,
     kv_out, q_out, w, vecs, up_bias, xs, sems,
 ):
     q, r, x, c = spot()
@@ -642,13 +645,17 @@
         ins.start(own.at[:, columns], w.at[at, pl.ds(half * t, half)])
     for j, block in enumerate((b0, b1, b2, b3)):
         xs[pl.ds(pl.multiple_of(rows * (me ^ j), rows), rows), :] = block[0:rows, :]
-    for flip, piece in ((2, w_x), (1, w_m), (3, w_mx)):
-        at = pl.ds(pl.multiple_of(part * (shard ^ flip), 64), part)
-        for t in range(3):
-            w[at, half * t : half * (t + 1)] = piece[part * t : part * (t + 1), :]
+    few = part // 2
+    for t in range(3):
+        place = slice(half * t, half * (t + 1))
+        at = pl.ds(pl.multiple_of(part * (shard ^ 1), 64), part)
+        w[at, place] = w_m[part * t : part * (t + 1), :]
+        for flip, side, piece in ((2, r, xa), (2, 1 - r, xb), (3, r, ma), (3, 1 - r, mb)):
+            at = pl.ds(pl.multiple_of(part * (shard ^ flip) + few * side, 32), few)
+            w[at, place] = piece[few * t : few * (t + 1), :]
     mine, other = (
-        a[3 * part :, :].astype(jnp.float32) + b[3 * part :, :].astype(jnp.float32)
-        for a, b in ((own_lines, w_m), (w_x, w_mx))
+        a[at:, :].astype(jnp.float32) + b[at:, :].astype(jnp.float32)
+        for a, b, at in ((own_lines, w_m, 3 * part), (xa, ma, 3 * few))
     )
     vecs[:, columns] = mine[0:8, :]
     vecs[:, pl.ds(pl.multiple_of(half * (1 - x), 128), half)] = other[0:8, :]
@@ -1155,7 +1162,7 @@
     )(value, *after)
 
 
-HEAVY = ('attend_back', 'down_sum', 'input_sum', 'project', 'rest_3')
+HEAVY = ('attend_back', 'down_sum', 'input_sum', 'project', 'rest_3', 'up_share')
 
 
 def plane_local(
@@ -1192,7 +1199,7 @@
         pack_kernel,
         "pack",
         [HBM] * 12,
-        [((3 * part + 16, half), low, WHOLE)] * 2,
+        [((3 * part // 2 + 16, half), low, WHOLE), ((3 * part + 16, half), low, WHOLE)],
         [pltpu.VMEM((16, half), exact)]
         + [pltpu.VMEM((part,), low)] * 8
         + [pltpu.VMEM((width,), low), pltpu.SemaphoreType.DMA((15,))],
@@ -1201,14 +1208,15 @@
     qkv_x = swap_x(theirs)
     qkv_m = swap_c(mine)
     out_m = swap_c(w_out)
-    blocks = [once(block, qkv_m, qkv_x, out_m)]
+    blocks = [once(block, qkv_m, out_m)]
     beside_r = swap_r(blocks[0])
     blocks.append(once(swap_x(blocks[0]), beside_r))
     blocks.append(swap_c(blocks[0]))
     blocks.append(swap_c(blocks[1]))
     blocks.append(beside_r)
     blocks.append(swap_r(blocks[1]))
-    qkv_mx = swap_c(qkv_x)
+    qkv_x = (qkv_x, swap_r(qkv_x))
+    qkv_mx = [swap_c(piece) for piece in qkv_x]
     up_theirs, up_mine = call(
         cut_kernel, "cut", [HBM], [((part, 4 * wide), low, WHOLE)] * 2, [pltpu.SemaphoreType.DMA((2,))],
         (w_up,), after=(blocks[1],),
@@ -1223,7 +1231,7 @@
     kv_own, q_own, w_all, vecs, up_bias = call(
         project_kernel,
         "project",
-        [WHOLE] * 4 + [HBM] * 3 + [WHOLE] * 4,
+        [WHOLE] * 4 + [HBM] * 3 + [WHOLE] * 6,
         [
             ((4 * rows, width), low, WHOLE),
             ((own, half), low, WHOLE),
@@ -1232,7 +1240,7 @@
             ((4, 8, wide), exact, WHOLE),
         ],
         [pltpu.VMEM((4 * rows, width), low), pltpu.SemaphoreType.DMA((3,))],
-        (*blocks[:4], w_query, w_key, w_value, qkv_x, qkv_m, qkv_mx, mine),
+        (*blocks[:4], w_query, w_key, w_value, qkv_m, *qkv_x, *qkv_mx, mine),
         room=8 << 20,
     )
     blocks[5] = once(blocks[5], kv_own)
@@ -1397,8 +1405,6 @@
         return out
 
     cuts = (count // 3, count // 3, count - 2 * (count // 3) + 16)
-    down_sends, down_keep = fold_into(2, "down_1", bit_r, down_keep, (down_got,))
-    down_gots = [swap_r(send) for send in down_sends]
     *up_sends, up_keep = call(
         up_grad_kernel,
         "up_grad",
@@ -1409,6 +1415,8 @@
         room=8 << 20,
     )
     up_gots = [swap_c(send) for send in up_sends]
+    down_sends, down_keep = fold_into(2, "down_1", bit_r, down_keep, (down_got,))
+    down_gots = [swap_r(send) for send in down_sends]
     (up_send,), up_keep = fold_into(1, "up_1", bit_near, up_keep, up_gots)
     up_got = swap_near(up_send)
     dkv, dq, dr, da, sums1, qv_sums = call(
@@ -1481,6 +1489,8 @@
         sum_kernel, "down_sum", [WHOLE] * 2, [((eighth, width), low, WHOLE)], [], (down_keep, down_got)
     )
     down_other = swap_far(down_sum)
+    x_send, x_keep = fold("input_r", bit_r, x_keep, x_got)
+    x_got = swap_r(x_send)
     side, base = call(
         share_kernel,
         "up_share",
@@ -1492,18 +1502,14 @@
     side = swap_x(side)
     rest_send, rest_keep = step("rest_2", bit_near, rest_keep, count // 4, rest_got)
     rest_got = swap_near(rest_send)
-    x_send, x_keep = fold("input_r", bit_r, x_keep, x_got)
-    x_got = swap_r(x_send)
     down_sum = join("down_join", down_sum, down_other)
     down_other = swap_near(down_sum)
     rest_send, rest_keep = step("rest_3", bit_far, rest_keep, count // 8, rest_got)
     rest_got = swap_far(rest_send)
     up_sum = join("up_join", base, side)
     up_other = swap_far(up_sum)
-    (total,) = call(
-        total_kernel, "input_sum", [WHOLE] * 3, [((rows, width), low, WHOLE)], [], (x_keep, x_got, dr)
-    )
-    total = regroup(total)
+    down_near = join("down_join_near", down_sum, down_other)
+    down_far = swap_r(down_near)
     rest_side, rest_base, *lines, b_up_grad = call(
         last_step_kernel,
         "rest_last",
@@ -1515,10 +1521,12 @@
         (rest_keep, rest_got),
     )
     rest_side = swap_x(rest_side)
-    down_near = join("down_join_near", down_sum, down_other)
-    down_far = swap_r(down_near)
     up_sum = join("up_join_far", up_sum, up_other)
     up_other = swap_near(up_sum)
+    (total,) = call(
+        total_kernel, "input_sum", [WHOLE] * 3, [((rows, width), low, WHOLE)], [], (x_keep, x_got, dr)
+    )
+    total = regroup(total)
     rest_sum = join("rest_join", rest_base, rest_side)
     rest_other = swap_far(rest_sum)
     rest_sum = join("rest_join_far", rest_sum, rest_other)

time: 200 us -> 197 us (0.985)
  waiting for transfers between devices: 95 us -> 82.2 us
  starting transfers between devices: 61.4 us -> 71.9 us
    ppermute x58 -> x60, waiting for transfers between devices: 95 us -> 82.2 us  [moved(): lax.ppermute(block, AXES, [(number(s), number(move(*s))) for s in spots])]
    ppermute x58 -> x60, starting transfers between devices: 61.4 us -> 71.9 us  [moved(): lax.ppermute(block, AXES, [(number(s), number(move(*s))) for s in spots])]
  transfers between devices with their start and end apart: 58 -> 60, of which waited for: 27 -> 23; matrix products, arithmetic and copies ran while one was open for 0% -> 0% of each run, Pallas kernels for 18% -> 18%
where the time goes in v6:
time: 197 us
  waiting for transfers between devices  82.2 us (42%)
  starting transfers between devices  71.9 us (36%)
  Pallas kernels  41.7 us (21%)
    ppermute x60, waiting for transfers between devices, moved(): lax.ppermute(block, AXES, [(number(s), number(move(*s))) for s in spots])  82.2 us
    ppermute x60, starting transfers between devices, moved(): lax.ppermute(block, AXES, [(number(s), number(move(*s))) for s in spots])  71.9 us
    pallas_call x42, Pallas kernels, kernel_call(): pl.pallas_call(run, name=name, out_shape=[jax.ShapeDtypeStruct(shape, dty...  41.7 us
  transfers between devices with their start and end apart: 60, of which 23 were waited for; matrix products, arithmetic and copies ran while one was open for 0% of the time, Pallas kernels for 18%

profile of v6, /device:TPU:0, one launch (start us, length us, event | category | flops | bytes accessed | tf_op | source)
XLA Modules:
  0.0 197.0 jit_solution(885161953439308944)
XLA Ops:
  0.7 1.0 block.1.refs_12_
  1.6 1.5 pack.1
  3.8 2.9 %collective-permute-start.8 = (bf16[304,384]{1,0:T(8,128)(2,1)S(1)}, bf16[304,384]{1,0:T(8,128)(2,1)S(1)}, u32[]{:S(2)}, u32[]{:S(2)}) collective-permute-start(bf16[304,384]{1,0:T(8,128)(2,1)S(1)} %get-tuple-element.121.refs_2_), channel_id=1, source_target_pairs={{0,2},{1,3},{2,0},{3,1},{4,6},{5,7},{6,4},{7,5},{8,10},{9,11},{10,... | collective-permute-start | bytes 700424 | tf_op jit(solution)/shard_map/ppermute | solution.py:480
  7.3 5.6 %collective-permute-done.8.refs_8_ = bf16[304,384]{1,0:T(8,128)(2,1)S(1)} collective-permute-done((bf16[304,384]{1,0:T(8,128)(2,1)S(1)}, bf16[304,384]{1,0:T(8,128)(2,1)S(1)}, u32[]{:S(2)}, u32[]{:S(2)}) %collective-permute-start.8) | collective-permute-done | bytes 233504 | tf_op jit(solution)/shard_map/ppermute | solution.py:480
  13.0 1.4 collective-permute-start.9
  15.1 7.2 %collective-permute-start.3 = (bf16[144,768]{1,0:T(8,128)(2,1)S(1)}, bf16[144,768]{1,0:T(8,128)(2,1)S(1)}, u32[]{:S(2)}, u32[]{:S(2)}) collective-permute-start(bf16[144,768]{1,0:T(8,128)(2,1)S(1)} %once.5.refs_0_), channel_id=1, source_target_pairs={{0,2},{1,3},{2,0},{3,1},{4,6},{5,7},{6,4},{7,5},{8,10},{9,11},{10,... | collective-permute-start | bytes 663560 | tf_op jit(solution)/shard_map/ppermute | solution.py:480
  22.8 1.7 collective-permute-done.4.refs_1_.refs_4_
  24.5 1.7 collective-permute-done.3.refs_0_
  26.7 1.3 cut.1
  27.9 0.9 cotangent.1.refs_13_.refs_0_
  29.2 2.0 collective-permute-start.16
  31.7 2.3 %project.1 = (bf16[512,768]{1,0:T(8,128)(2,1)S(1)}, bf16[256,384]{1,0:T(8,128)(2,1)S(1)}, bf16[768,1152]{1,0:T(8,128)(2,1)S(1)}, f32[8,768]{1,0:T(8,128)S(1)}, f32[4,8,384]{2,1,0:T(8,128)S(1)}) custom-call(bf16[144,768]{1,0:T(8,128)(2,1)S(1)} %once.5.refs_0_, bf16[144,768]{1,0:T(8,128)(2,1)S(1)} %once.6.refs_1_, ...), custom_call_target="tpu_custom_call" | custom-call | flops 10000000000 | bytes 1 | tf_op jit(solution)/shard_map/project/pallas_call | solution.py:1140
  34.0 2.3 %collective-permute-done.7.refs_0_ = bf16[144,768]{1,0:T(8,128)(2,1)S(1)} collective-permute-done((bf16[144,768]{1,0:T(8,128)(2,1)S(1)}, bf16[144,768]{1,0:T(8,128)(2,1)S(1)}, u32[]{:S(2)}, u32[]{:S(2)}) %collective-permute-start.7) | collective-permute-done | bytes 221216 | tf_op jit(solution)/shard_map/ppermute | solution.py:480
  36.3 1.5 collective-permute-done.13.refs_7_
  37.8 6.4 %attend.1 = (bf16[256,768]{1,0:T(8,128)(2,1)S(1)}, bf16[1024,768]{1,0:T(8,128)(2,1)S(1)}, bf16[384,768]{1,0:T(8,128)(2,1)S(1)}, bf16[3,1024,128]{2,1,0:T(8,128)(...) custom-call(bf16[144,768]{1,0:T(8,128)(2,1)S(1)} %once.5.refs_0_, ...), custom_call_target="tpu_custom_call" | custom-call | flops 1 | bytes 1 | tf_op jit(solution)/shard_map/attend/pallas_call | solution.py:1140
  44.2 2.1 %collective-permute-start.15 = (bf16[256,768]{1,0:T(8,128)(2,1)S(1)}, bf16[256,768]{1,0:T(8,128)(2,1)S(1)}, u32[]{:S(2)}, u32[]{:S(2)}) collective-permute-start(bf16[256,768]{1,0:T(8,128)(2,1)S(1)} %get-tuple-element.129.refs_2_), channel_id=1, source_target_pairs={{0,2},{1,3},{2,0},{3,1},{4,6},{5,7},{6,4},{7,5},{8,10},{9,11},{10,... | collective-permute-start | bytes 1179656 | tf_op jit(solution)/shard_map/ppermute | solution.py:480
  47.2 1.1 collective-permute-done.19.refs_4_
  48.7 1.5 inner.1
  50.3 0.8 collective-permute-start.22
  51.1 4.6 %collective-permute-done.15.refs_1_ = bf16[256,768]{1,0:T(8,128)(2,1)S(1)} collective-permute-done((bf16[256,768]{1,0:T(8,128)(2,1)S(1)}, bf16[256,768]{1,0:T(8,128)(2,1)S(1)}, u32[]{:S(2)}, u32[]{:S(2)}) %collective-permute-start.15) | collective-permute-done | bytes 393248 | tf_op jit(solution)/shard_map/ppermute | solution.py:480
  55.7 2.0 %feedforward.1 = (bf16[128,768]{1,0:T(8,128)(2,1)S(1)}, bf16[128,768]{1,0:T(8,128)(2,1)S(1)}, bf16[256,768]{1,0:T(8,128)(2,1)S(1)}, bf16[256,1536]{1,0:T(8,128)(...) custom-call(f32[256,768]{1,0:T(8,128)S(1)} %get-tuple-element.128.re, ...), custom_call_target="tpu_custom_call" | custom-call | flops 1 | bytes 1 | tf_op jit(solution)/shard_map/feedforward/pallas_call | solution.py:1140
  57.8 1.8 collective-permute-start.21
  60.2 7.4 %collective-permute-done.21.refs_2_ = bf16[128,768]{1,0:T(8,128)(2,1)S(1)} collective-permute-done((bf16[128,768]{1,0:T(8,128)(2,1)S(1)}, bf16[128,768]{1,0:T(8,128)(2,1)S(1)}, u32[]{:S(2)}, u32[]{:S(2)}) %collective-permute-start.21) | collective-permute-done | bytes 196640 | tf_op jit(solution)/shard_map/ppermute | solution.py:480
  67.6 4.2 %collective-permute-done.20.refs_1_ = bf16[128,768]{1,0:T(8,128)(2,1)S(1)} collective-permute-done((bf16[128,768]{1,0:T(8,128)(2,1)S(1)}, bf16[128,768]{1,0:T(8,128)(2,1)S(1)}, u32[]{:S(2)}, u32[]{:S(2)}) %collective-permute-start.20) | collective-permute-done | bytes 196640 | tf_op jit(solution)/shard_map/ppermute | solution.py:480
  71.8 0.9 norm_back.1
  72.7 0.8 down_grad.1
  73.8 1.7 feedforward_back.1
  75.5 2.5 %collective-permute-start.24 = (bf16[256,768]{1,0:T(8,128)(2,1)S(1)}, bf16[256,768]{1,0:T(8,128)(2,1)S(1)}, u32[]{:S(2)}, u32[]{:S(2)}) collective-permute-start(bf16[256,768]{1,0:T(8,128)(2,1)S(1)} %get-tuple-element.145.refs_2_), channel_id=1, source_target_pairs={{0,2},{1,3},{2,0},{3,1},{4,6},{5,7},{6,4},{7,5},{8,10},{9,11},{10,... | collective-permute-start | bytes 1179656 | tf_op jit(solution)/shard_map/ppermute | solution.py:480
  77.9 1.3 up_grad.1
  80.9 0.9 collective-permute-start.30
  82.2 1.7 collective-permute-start.31
  84.4 2.8 %collective-permute-start.37 = (bf16[384,768]{1,0:T(8,128)(2,1)S(1)}, bf16[384,768]{1,0:T(8,128)(2,1)S(1)}, u32[]{:S(2)}, u32[]{:S(2)}) collective-permute-start(bf16[384,768]{1,0:T(8,128)(2,1)S(1)} %get-tuple-element.162.refs_13_), channel_id=1, source_target_pairs={{0,8},{1,9},{2,10},{3,11},{4,12},{5,13},{6,14},{7,15},{8,0},{9,1},... | collective-permute-start | bytes 1769480 | tf_op jit(solution)/shard_map/ppermute | solution.py:480
  87.2 3.7 %collective-permute-done.24.refs_1_ = bf16[256,768]{1,0:T(8,128)(2,1)S(1)} collective-permute-done((bf16[256,768]{1,0:T(8,128)(2,1)S(1)}, bf16[256,768]{1,0:T(8,128)(2,1)S(1)}, u32[]{:S(2)}, u32[]{:S(2)}) %collective-permute-start.24) | collective-permute-done | bytes 393248 | tf_op jit(solution)/shard_map/ppermute | solution.py:480
  90.9 6.6 %attend_back.1 = (bf16[1024,768]{1,0:T(8,128)(2,1)S(1)}, bf16[256,384]{1,0:T(8,128)(2,1)S(1)}, f32[128,768]{1,0:T(8,128)S(1)}, bf16[256,768]{1,0:T(8,128)(2,1)S(...) custom-call(f32[256,768]{1,0:T(8,128)S(1)} %get-tuple-element.144.refs_0_, ...), custom_call_target="tpu_custom_call" | custom-call | flops 10000000000 | bytes 1 | tf_op jit(solution)/shard_map/attend_back/pallas_call | solution.py:1140
  97.8 2.6 %weight_grad.1 = (bf16[512,384]{1,0:T(8,128)(2,1)S(1)}, bf16[512,384]{1,0:T(8,128)(2,1)S(1)}, bf16[528,384]{1,0:T(8,128)(2,1)S(1)}, f32[1552,384]{1,0:T(8,128)S(1)}) custom-call(bf16[1024,768]{1,0:T(8,128)(2,1)S(1)} %get-tuple-element.127.refs_2_.refs_0_, bf16[1024,768]{1,0:T(8,128)(2,1)S(1)} %get-tuple-element.163.refs_3_.refs_1_, ...), custom_call_target="tpu_custom_call" | custom-call | flops 1 | bytes 1 | tf_op jit(solution)/shard_map/weight_grad/pallas_call | solution.py:1140
  101.7 2.7 %collective-permute-start.41 = (bf16[192,768]{1,0:T(8,128)(2,1)S(1)}, bf16[192,768]{1,0:T(8,128)(2,1)S(1)}, u32[]{:S(2)}, u32[]{:S(2)}) collective-permute-start(bf16[192,768]{1,0:T(8,128)(2,1)S(1)} %get-tuple-element.173.refs_10_), channel_id=1, source_target_pairs={{0,8},{1,9},{2,10},{3,11},{4,12},{5,13},{6,14},{7,15},{8,0},{9,1},... | collective-permute-start | bytes 884744 | tf_op jit(solution)/shard_map/ppermute | solution.py:480
  105.0 2.1 %input_grad.1 = (bf16[256,768]{1,0:T(8,128)(2,1)S(1)}, bf16[256,768]{1,0:T(8,128)(2,1)S(1)}, f32[512,768]{1,0:T(8,128)S(1)}) custom-call(bf16[256,384]{1,0:T(8,128)(2,1)S(1)} %get-tuple-element.164.refs_2_.refs_0_, bf16[1024,768]{1,0:T(8,128)(2,1)S(1)} %get-tuple-element.163.refs_3_.refs_1_, bf16[768,1152]{1,0:T(8,128)(2,1)S(1)} %get-tuple-element.125.refs_10_.refs_2_, ...), custom_call_target="tpu_custom_call" | custom-call | flops 1 | bytes 1 | tf_op jit(solution)/shard_map/input_grad/pallas_call | solution.py:1140
  107.6 4.4 %collective-permute-start.38 = (bf16[192,768]{1,0:T(8,128)(2,1)S(1)}, bf16[192,768]{1,0:T(8,128)(2,1)S(1)}, u32[]{:S(2)}, u32[]{:S(2)}) collective-permute-start(bf16[192,768]{1,0:T(8,128)(2,1)S(1)} %get-tuple-element.182.refs_3_), channel_id=1, source_target_pairs={{0,16},{1,17},{2,18},{3,19},{4,20},{5,21},{6,22},{7,23},{8,24},{9,... | collective-permute-start | bytes 884744 | tf_op jit(solution)/shard_map/ppermute | solution.py:480
  112.1 4.4 %collective-permute-start.44 = (bf16[96,768]{1,0:T(8,128)(2,1)S(1)}, bf16[96,768]{1,0:T(8,128)(2,1)S(1)}, u32[]{:S(2)}, u32[]{:S(2)}) collective-permute-start(bf16[96,768]{1,0:T(8,128)(2,1)S(1)} %get-tuple-element.187.refs_3_), channel_id=1, source_target_pairs={{0,16},{1,17},{2,18},{3,19},{4,20},{5,21},{6,22},{7,23},{8,24},{9,... | collective-permute-start | bytes 442376 | tf_op jit(solution)/shard_map/ppermute | solution.py:480
  116.5 1.5 collective-permute-start.36
  118.3 2.6 %collective-permute-start.43 = (bf16[256,768]{1,0:T(8,128)(2,1)S(1)}, bf16[256,768]{1,0:T(8,128)(2,1)S(1)}, u32[]{:S(2)}, u32[]{:S(2)}) collective-permute-start(bf16[256,768]{1,0:T(8,128)(2,1)S(1)} %get-tuple-element.188.refs_2_), channel_id=1, source_target_pairs={{0,2},{1,3},{2,0},{3,1},{4,6},{5,7},{6,4},{7,5},{8,10},{9,11},{10,... | collective-permute-start | bytes 1179656 | tf_op jit(solution)/shard_map/ppermute | solution.py:480
  120.9 8.5 %collective-permute-done.38 = bf16[192,768]{1,0:T(8,128)(2,1)S(1)} collective-permute-done((bf16[192,768]{1,0:T(8,128)(2,1)S(1)}, bf16[192,768]{1,0:T(8,128)(2,1)S(1)}, u32[]{:S(2)}, u32[]{:S(2)}) %collective-permute-start.38) | collective-permute-done | bytes 294944 | tf_op jit(solution)/shard_map/ppermute | solution.py:480
  129.4 1.6 collective-permute-start.42
  131.0 1.0 collective-permute-done.44.refs_1_
  132.1 2.5 %collective-permute-done.42 = bf16[96,768]{1,0:T(8,128)(2,1)S(1)} collective-permute-done((bf16[96,768]{1,0:T(8,128)(2,1)S(1)}, bf16[96,768]{1,0:T(8,128)(2,1)S(1)}, u32[]{:S(2)}, u32[]{:S(2)}) %collective-permute-start.42) | collective-permute-done | bytes 147488 | tf_op jit(solution)/shard_map/ppermute | solution.py:480
  134.9 1.5 collective-permute-start.45
  136.4 1.5 collective-permute-start.46
  137.9 2.3 %collective-permute-start.49 = (bf16[48,768]{1,0:T(8,128)(2,1)S(1)}, bf16[48,768]{1,0:T(8,128)(2,1)S(1)}, u32[]{:S(2)}, u32[]{:S(2)}) collective-permute-start(bf16[48,768]{1,0:T(8,128)(2,1)S(1)} %get-tuple-element.194.refs_2_), channel_id=1, source_target_pairs={{0,2},{1,3},{2,0},{3,1},{4,6},{5,7},{6,4},{7,5},{8,10},{9,11},{10,... | collective-permute-start | bytes 221192 | tf_op jit(solution)/shard_map/ppermute | solution.py:480
  140.2 1.5 collective-permute-start.51
  141.7 4.9 %collective-permute-done.46.refs_1_ = bf16[96,768]{1,0:T(8,128)(2,1)S(1)} collective-permute-done((bf16[96,768]{1,0:T(8,128)(2,1)S(1)}, bf16[96,768]{1,0:T(8,128)(2,1)S(1)}, u32[]{:S(2)}, u32[]{:S(2)}) %collective-permute-start.46) | collective-permute-done | bytes 147488 | tf_op jit(solution)/shard_map/ppermute | solution.py:480
  146.8 3.4 %collective-permute-start.47 = (bf16[208,384]{1,0:T(8,128)(2,1)S(1)}, bf16[208,384]{1,0:T(8,128)(2,1)S(1)}, u32[]{:S(2)}, u32[]{:S(2)}) collective-permute-start(bf16[208,384]{1,0:T(8,128)(2,1)S(1)} %get-tuple-element.198.refs_2_), channel_id=1, source_target_pairs={{0,16},{1,17},{2,18},{3,19},{4,20},{5,21},{6,22},{7,23},{8,24},{9,... | collective-permute-start | bytes 479240 | tf_op jit(solution)/shard_map/ppermute | solution.py:480
  150.4 8.3 %collective-permute-done.48.refs_1_ = bf16[192,768]{1,0:T(8,128)(2,1)S(1)} collective-permute-done((bf16[192,768]{1,0:T(8,128)(2,1)S(1)}, bf16[192,768]{1,0:T(8,128)(2,1)S(1)}, u32[]{:S(2)}, u32[]{:S(2)}) %collective-permute-start.48) | collective-permute-done | bytes 294944 | tf_op jit(solution)/shard_map/ppermute | solution.py:480
  158.7 1.6 collective-permute-start.56
  161.0 2.5 %collective-permute-start.50 = (bf16[72,384]{1,0:T(8,128)(2,1)S(1)}, bf16[72,384]{1,0:T(8,128)(2,1)S(1)}, u32[]{:S(2)}, u32[]{:S(2)}) collective-permute-start(bf16[72,384]{1,0:T(8,128)(2,1)S(1)} %get-tuple-element.201.refs_2_), channel_id=1, source_target_pairs={{0,2},{1,3},{2,0},{3,1},{4,6},{5,7},{6,4},{7,5},{8,10},{9,11},{10,... | collective-permute-start | bytes 165896 | tf_op jit(solution)/shard_map/ppermute | solution.py:480
  163.6 2.0 %collective-permute-done.50.refs_1_ = bf16[72,384]{1,0:T(8,128)(2,1)S(1)} collective-permute-done((bf16[72,384]{1,0:T(8,128)(2,1)S(1)}, bf16[72,384]{1,0:T(8,128)(2,1)S(1)}, u32[]{:S(2)}, u32[]{:S(2)}) %collective-permute-start.50) | collective-permute-done | bytes 55328 | tf_op jit(solution)/shard_map/ppermute | solution.py:480
  165.8 3.1 %collective-permute-start.55 = (bf16[192,768]{1,0:T(8,128)(2,1)S(1)}, bf16[192,768]{1,0:T(8,128)(2,1)S(1)}, u32[]{:S(2)}, u32[]{:S(2)}) collective-permute-start(bf16[192,768]{1,0:T(8,128)(2,1)S(1)} %up_join_far.1.refs_3_.refs_0_), channel_id=1, source_target_pairs={{0,8},{1,9},{2,10},{3,11},{4,12},{5,13},{6,14},{7,15},{8,0},{9,1},... | collective-permute-start | bytes 884744 | tf_op jit(solution)/shard_map/ppermute | solution.py:480
  168.9 4.4 %collective-permute-done.53.refs_1_ = bf16[192,384]{1,0:T(8,128)(2,1)S(1)} collective-permute-done((bf16[192,384]{1,0:T(8,128)(2,1)S(1)}, bf16[192,384]{1,0:T(8,128)(2,1)S(1)}, u32[]{:S(2)}, u32[]{:S(2)}) %collective-permute-start.53) | collective-permute-done | bytes 147488 | tf_op jit(solution)/shard_map/ppermute | solution.py:480
  173.7 1.6 down_out.1
  175.8 1.4 collective-permute-start.59
  177.3 2.9 %collective-permute-done.54.refs_1_ = bf16[384,384]{1,0:T(8,128)(2,1)S(1)} collective-permute-done((bf16[384,384]{1,0:T(8,128)(2,1)S(1)}, bf16[384,384]{1,0:T(8,128)(2,1)S(1)}, u32[]{:S(2)}, u32[]{:S(2)}) %collective-permute-start.54) | collective-permute-done | bytes 294944 | tf_op jit(solution)/shard_map/ppermute | solution.py:480
  181.1 7.9 %collective-permute-done.59.refs_1_ = bf16[384,768]{1,0:T(8,128)(2,1)S(1)} collective-permute-done((bf16[384,768]{1,0:T(8,128)(2,1)S(1)}, bf16[384,768]{1,0:T(8,128)(2,1)S(1)}, u32[]{:S(2)}, u32[]{:S(2)}) %collective-permute-start.59) | collective-permute-done | bytes 589856 | tf_op jit(solution)/shard_map/ppermute | solution.py:480
  188.9 1.6 up_out.1
  190.5 4.7 %collective-permute-done.57.refs_1_ = bf16[768,384]{1,0:T(8,128)(2,1)S(1)} collective-permute-done((bf16[768,384]{1,0:T(8,128)(2,1)S(1)}, bf16[768,384]{1,0:T(8,128)(2,1)S(1)}, u32[]{:S(2)}, u32[]{:S(2)}) %collective-permute-start.57) | collective-permute-done | bytes 589856 | tf_op jit(solution)/shard_map/ppermute | solution.py:480
  195.3 1.7 rest_out.1
  (106 shorter events, 15.0 us)
Async XLA Ops:
  1.6 24.6 %copy-start = (bf16[768,768]{1,0:T(8,128)(2,1)S(1)}, bf16[768,768]{1,0:T(8,128)(2,1)}, u32[]{:S(2)}) copy-start(bf16[768,768]{1,0:T(8,128)(2,1)} %refs_5_.5) | copy-start | bytes 3538948
  3.2 11.2 %collective-permute-start.1 = (bf16[592,384]{1,0:T(8,128)(2,1)S(1)}, bf16[592,384]{1,0:T(8,128)(2,1)S(1)}, u32[]{:S(2)}, u32[]{:S(2)}) collective-permute-start(bf16[592,384]{1,0:T(8,128)(2,1)S(1)} %get-tuple-element.120.refs_12_), channel_id=1, source_target_pairs={{0,1},{1,0},{2,3},{3,2},{4,5},{5,4},{6,7},{7,6},{8,9},{9,8},{10,11... | collective-permute-start | bytes 1363976 | tf_op jit(solution)/shard_map/ppermute | solution.py:480
  3.7 10.7 %collective-permute-start.2 = (bf16[192,768]{1,0:T(8,128)(2,1)}, bf16[192,768]{1,0:T(8,128)(2,1)S(1)}, u32[]{:S(2)}, u32[]{:S(2)}) collective-permute-start(bf16[192,768]{1,0:T(8,128)(2,1)} %refs_12_.1), channel_id=1, source_target_pairs={{0,1},{1,0},{2,3},{3,2},{4,5},{5,4},{6,7},{7,6},{8,9},{9,8},{10,11... | collective-permute-start | bytes 884744 | tf_op jit(solution)/shard_map/ppermute | solution.py:480
  3.8 9.2 %collective-permute-start.8 = (bf16[304,384]{1,0:T(8,128)(2,1)S(1)}, bf16[304,384]{1,0:T(8,128)(2,1)S(1)}, u32[]{:S(2)}, u32[]{:S(2)}) collective-permute-start(bf16[304,384]{1,0:T(8,128)(2,1)S(1)} %get-tuple-element.121.refs_2_), channel_id=1, source_target_pairs={{0,2},{1,3},{2,0},{3,1},{4,6},{5,7},{6,4},{7,5},{8,10},{9,11},{10,... | collective-permute-start | bytes 700424 | tf_op jit(solution)/shard_map/ppermute | solution.py:480
  6.7 7.7 %collective-permute-start = (bf16[144,768]{1,0:T(8,128)(2,1)S(1)}, bf16[144,768]{1,0:T(8,128)(2,1)S(1)}, u32[]{:S(2)}, u32[]{:S(2)}) collective-permute-start(bf16[144,768]{1,0:T(8,128)(2,1)S(1)} %block.1.refs_12_), channel_id=1, source_target_pairs={{0,0},{1,16},{2,8},{3,24},{4,4},{5,20},{6,12},{7,28},{8,2},{9,18},... | collective-permute-start | bytes 663560 | tf_op jit(solution)/shard_map/ppermute | solution.py:480
  13.0 9.3 %collective-permute-start.9 = (bf16[304,384]{1,0:T(8,128)(2,1)S(1)}, bf16[304,384]{1,0:T(8,128)(2,1)S(1)}, u32[]{:S(2)}, u32[]{:S(2)}) collective-permute-start(bf16[304,384]{1,0:T(8,128)(2,1)S(1)} %collective-permute-done.8.refs_8_), channel_id=1, source_target_pairs={{0,4},{1,5},{2,6},{3,7},{4,0},{5,1},{6,2},{7,3},{8,12},{9,13},{10,... | collective-permute-start | bytes 700424 | tf_op jit(solution)/shard_map/ppermute | solution.py:480
  14.4 10.1 %collective-permute-start.4 = (bf16[144,768]{1,0:T(8,128)(2,1)S(1)}, bf16[144,768]{1,0:T(8,128)(2,1)S(1)}, u32[]{:S(2)}, u32[]{:S(2)}) collective-permute-start(bf16[144,768]{1,0:T(8,128)(2,1)S(1)} %once.5.refs_0_), channel_id=1, source_target_pairs={{0,4},{1,5},{2,6},{3,7},{4,0},{5,1},{6,2},{7,3},{8,12},{9,13},{10,... | collective-permute-start | bytes 663560 | tf_op jit(solution)/shard_map/ppermute | solution.py:480
  15.1 11.1 %collective-permute-start.3 = (bf16[144,768]{1,0:T(8,128)(2,1)S(1)}, bf16[144,768]{1,0:T(8,128)(2,1)S(1)}, u32[]{:S(2)}, u32[]{:S(2)}) collective-permute-start(bf16[144,768]{1,0:T(8,128)(2,1)S(1)} %once.5.refs_0_), channel_id=1, source_target_pairs={{0,2},{1,3},{2,0},{3,1},{4,6},{5,7},{6,4},{7,5},{8,10},{9,11},{10,... | collective-permute-start | bytes 663560 | tf_op jit(solution)/shard_map/ppermute | solution.py:480
  22.3 6.6 %collective-permute-start.10 = (bf16[304,384]{1,0:T(8,128)(2,1)S(1)}, bf16[304,384]{1,0:T(8,128)(2,1)S(1)}, u32[]{:S(2)}, u32[]{:S(2)}) collective-permute-start(bf16[304,384]{1,0:T(8,128)(2,1)S(1)} %collective-permute-done.8.refs_8_), channel_id=1, source_target_pairs={{0,1},{1,0},{2,3},{3,2},{4,5},{5,4},{6,7},{7,6},{8,9},{9,8},{10,11... | collective-permute-start | bytes 700424 | tf_op jit(solution)/shard_map/ppermute | solution.py:480
  22.3 8.9 %collective-permute-start.11 = (bf16[304,384]{1,0:T(8,128)(2,1)S(1)}, bf16[304,384]{1,0:T(8,128)(2,1)S(1)}, u32[]{:S(2)}, u32[]{:S(2)}) collective-permute-start(bf16[304,384]{1,0:T(8,128)(2,1)S(1)} %collective-permute-done.9.refs_9_), channel_id=1, source_target_pairs={{0,1},{1,0},{2,3},{3,2},{4,5},{5,4},{6,7},{7,6},{8,9},{9,8},{10,11... | collective-permute-start | bytes 700424 | tf_op jit(solution)/shard_map/ppermute | solution.py:480
  22.8 6.4 %collective-permute-start.5 = (bf16[144,768]{1,0:T(8,128)(2,1)S(1)}, bf16[144,768]{1,0:T(8,128)(2,1)S(1)}, u32[]{:S(2)}, u32[]{:S(2)}) collective-permute-start(bf16[144,768]{1,0:T(8,128)(2,1)S(1)} %once.5.refs_0_), channel_id=1, source_target_pairs={{0,1},{1,0},{2,3},{3,2},{4,5},{5,4},{6,7},{7,6},{8,9},{9,8},{10,11... | collective-permute-start | bytes 663560 | tf_op jit(solution)/shard_map/ppermute | solution.py:480
  26.2 5.0 %collective-permute-start.6 = (bf16[144,768]{1,0:T(8,128)(2,1)S(1)}, bf16[144,768]{1,0:T(8,128)(2,1)S(1)}, u32[]{:S(2)}, u32[]{:S(2)}) collective-permute-start(bf16[144,768]{1,0:T(8,128)(2,1)S(1)} %once.6.refs_1_), channel_id=1, source_target_pairs={{0,1},{1,0},{2,3},{3,2},{4,5},{5,4},{6,7},{7,6},{8,9},{9,8},{10,11... | collective-permute-start | bytes 663560 | tf_op jit(solution)/shard_map/ppermute | solution.py:480
  26.2 11.6 %collective-permute-start.14 = (bf16[768,768]{1,0:T(8,128)(2,1)S(1)}, bf16[768,768]{1,0:T(8,128)(2,1)S(1)}, u32[]{:S(2)}, u32[]{:S(2)}) collective-permute-start(bf16[768,768]{1,0:T(8,128)(2,1)S(1)} %copy-done), channel_id=1, source_target_pairs={{0,1},{1,0},{2,3},{3,2},{4,5},{5,4},{6,7},{7,6},{8,9},{9,8},{10,11... | collective-permute-start | bytes 3538952 | tf_op jit(solution)/shard_map/ppermute | solution.py:480
  28.9 7.4 %collective-permute-start.7 = (bf16[144,768]{1,0:T(8,128)(2,1)S(1)}, bf16[144,768]{1,0:T(8,128)(2,1)S(1)}, u32[]{:S(2)}, u32[]{:S(2)}) collective-permute-start(bf16[144,768]{1,0:T(8,128)(2,1)S(1)} %once.6.refs_1_), channel_id=1, source_target_pairs={{0,4},{1,5},{2,6},{3,7},{4,0},{5,1},{6,2},{7,3},{8,12},{9,13},{10,... | collective-permute-start | bytes 663560 | tf_op jit(solution)/shard_map/ppermute | solution.py:480
  29.2 17.4 %collective-permute-start.16 = (bf16[192,1536]{1,0:T(8,128)(2,1)S(1)}, bf16[192,1536]{1,0:T(8,128)(2,1)S(1)}, u32[]{:S(2)}, u32[]{:S(2)}) collective-permute-start(bf16[192,1536]{1,0:T(8,128)(2,1)S(1)} %get-tuple-element.122.refs_1_), channel_id=1, source_target_pairs={{0,2},{1,3},{2,0},{3,1},{4,6},{5,7},{6,4},{7,5},{8,10},{9,11},{10,... | collective-permute-start | bytes 1769480 | tf_op jit(solution)/shard_map/ppermute | solution.py:480
  31.1 15.2 %collective-permute-start.17 = (bf16[192,1536]{1,0:T(8,128)(2,1)S(1)}, bf16[192,1536]{1,0:T(8,128)(2,1)S(1)}, u32[]{:S(2)}, u32[]{:S(2)}) collective-permute-start(bf16[192,1536]{1,0:T(8,128)(2,1)S(1)} %get-tuple-element.132), channel_id=1, source_target_pairs={{0,1},{1,0},{2,3},{3,2},{4,5},{5,4},{6,7},{7,6},{8,9},{9,8},{10,11... | collective-permute-start | bytes 1769480 | tf_op jit(solution)/shard_map/ppermute | solution.py:480
  31.1 5.2 %collective-permute-start.12 = (bf16[144,768]{1,0:T(8,128)(2,1)S(1)}, bf16[144,768]{1,0:T(8,128)(2,1)S(1)}, u32[]{:S(2)}, u32[]{:S(2)}) collective-permute-start(bf16[144,768]{1,0:T(8,128)(2,1)S(1)} %collective-permute-done.4.refs_1_.refs_4_), channel_id=1, source_target_pairs={{0,1},{1,0},{2,3},{3,2},{4,5},{5,4},{6,7},{7,6},{8,9},{9,8},{10,11... | collective-permute-start | bytes 663560 | tf_op jit(solution)/shard_map/ppermute | solution.py:480
  36.3 1.5 collective-permute-start.13
  44.2 11.5 %collective-permute-start.15 = (bf16[256,768]{1,0:T(8,128)(2,1)S(1)}, bf16[256,768]{1,0:T(8,128)(2,1)S(1)}, u32[]{:S(2)}, u32[]{:S(2)}) collective-permute-start(bf16[256,768]{1,0:T(8,128)(2,1)S(1)} %get-tuple-element.129.refs_2_), channel_id=1, source_target_pairs={{0,2},{1,3},{2,0},{3,1},{4,6},{5,7},{6,4},{7,5},{8,10},{9,11},{10,... | collective-permute-start | bytes 1179656 | tf_op jit(solution)/shard_map/ppermute | solution.py:480
  46.6 1.6 collective-permute-start.19
  46.7 2.0 %collective-permute-start.18 = (bf16[96,1536]{1,0:T(8,128)(2,1)S(1)}, bf16[96,1536]{1,0:T(8,128)(2,1)S(1)}, u32[]{:S(2)}, u32[]{:S(2)}) collective-permute-start(bf16[96,1536]{1,0:T(8,128)(2,1)S(1)} %get-tuple-element.224), channel_id=1, source_target_pairs={{0,1},{1,0},{2,3},{3,2},{4,5},{5,4},{6,7},{7,6},{8,9},{9,8},{10,11... | collective-permute-start | bytes 884744 | tf_op jit(solution)/shard_map/ppermute | solution.py:480
  50.2 9.9 %collective-permute-start.23 = (bf16[128,768]{1,0:T(8,128)(2,1)S(1)}, bf16[128,768]{1,0:T(8,128)(2,1)S(1)}, u32[]{:S(2)}, u32[]{:S(2)}) collective-permute-start(bf16[128,768]{1,0:T(8,128)(2,1)S(1)} %once.9), channel_id=1, source_target_pairs={{0,2},{1,18},{2,10},{3,26},{4,6},{5,22},{6,14},{7,30},{8,0},{9,16}... | collective-permute-start | bytes 589832 | tf_op jit(solution)/shard_map/ppermute | solution.py:480
  50.3 9.9 %collective-permute-start.22 = (bf16[128,768]{1,0:T(8,128)(2,1)S(1)}, bf16[128,768]{1,0:T(8,128)(2,1)S(1)}, u32[]{:S(2)}, u32[]{:S(2)}) collective-permute-start(bf16[128,768]{1,0:T(8,128)(2,1)S(1)} %once.9), channel_id=1, source_target_pairs={{0,0},{1,16},{2,8},{3,24},{4,4},{5,20},{6,12},{7,28},{8,2},{9,18},... | collective-permute-start | bytes 589832 | tf_op jit(solution)/shard_map/ppermute | solution.py:480
  57.8 9.8 %collective-permute-start.21 = (bf16[128,768]{1,0:T(8,128)(2,1)S(1)}, bf16[128,768]{1,0:T(8,128)(2,1)S(1)}, u32[]{:S(2)}, u32[]{:S(2)}) collective-permute-start(bf16[128,768]{1,0:T(8,128)(2,1)S(1)} %get-tuple-element.137), channel_id=1, source_target_pairs={{0,2},{1,3},{2,0},{3,1},{4,6},{5,7},{6,4},{7,5},{8,10},{9,11},{10,... | collective-permute-start | bytes 589832 | tf_op jit(solution)/shard_map/ppermute | solution.py:480
  59.6 12.2 %collective-permute-start.20 = (bf16[128,768]{1,0:T(8,128)(2,1)S(1)}, bf16[128,768]{1,0:T(8,128)(2,1)S(1)}, u32[]{:S(2)}, u32[]{:S(2)}) collective-permute-start(bf16[128,768]{1,0:T(8,128)(2,1)S(1)} %get-tuple-element.136.refs_7_), channel_id=1, source_target_pairs={{0,2},{1,3},{2,0},{3,1},{4,6},{5,7},{6,4},{7,5},{8,10},{9,11},{10,... | collective-permute-start | bytes 589832 | tf_op jit(solution)/shard_map/ppermute | solution.py:480
  73.5 6.5 %collective-permute-start.29 = (bf16[768,768]{1,0:T(8,128)(2,1)S(1)}, bf16[768,768]{1,0:T(8,128)(2,1)S(1)}, u32[]{:S(2)}, u32[]{:S(2)}) collective-permute-start(bf16[768,768]{1,0:T(8,128)(2,1)S(1)} %get-tuple-element.143.refs_5_), channel_id=1, source_target_pairs={{0,1},{1,0},{2,3},{3,2},{4,5},{5,4},{6,7},{7,6},{8,9},{9,8},{10,11... | collective-permute-start | bytes 3538952 | tf_op jit(solution)/shard_map/ppermute | solution.py:480
  75.5 15.4 %collective-permute-start.24 = (bf16[256,768]{1,0:T(8,128)(2,1)S(1)}, bf16[256,768]{1,0:T(8,128)(2,1)S(1)}, u32[]{:S(2)}, u32[]{:S(2)}) collective-permute-start(bf16[256,768]{1,0:T(8,128)(2,1)S(1)} %get-tuple-element.145.refs_2_), channel_id=1, source_target_pairs={{0,2},{1,3},{2,0},{3,1},{4,6},{5,7},{6,4},{7,5},{8,10},{9,11},{10,... | collective-permute-start | bytes 1179656 | tf_op jit(solution)/shard_map/ppermute | solution.py:480
  79.3 1.7 collective-permute-start.26
  79.5 2.3 %collective-permute-start.27 = (bf16[192,768]{1,0:T(8,128)(2,1)S(1)}, bf16[192,768]{1,0:T(8,128)(2,1)S(1)}, u32[]{:S(2)}, u32[]{:S(2)}) collective-permute-start(bf16[192,768]{1,0:T(8,128)(2,1)S(1)} %get-tuple-element.158), channel_id=1, source_target_pairs={{0,1},{1,0},{2,3},{3,2},{4,5},{5,4},{6,7},{7,6},{8,9},{9,8},{10,11... | collective-permute-start | bytes 884744 | tf_op jit(solution)/shard_map/ppermute | solution.py:480
  79.8 2.4 %collective-permute-start.28 = (bf16[192,768]{1,0:T(8,128)(2,1)S(1)}, bf16[192,768]{1,0:T(8,128)(2,1)S(1)}, u32[]{:S(2)}, u32[]{:S(2)}) collective-permute-start(bf16[192,768]{1,0:T(8,128)(2,1)S(1)} %get-tuple-element.159), channel_id=1, source_target_pairs={{0,1},{1,0},{2,3},{3,2},{4,5},{5,4},{6,7},{7,6},{8,9},{9,8},{10,11... | collective-permute-start | bytes 884744 | tf_op jit(solution)/shard_map/ppermute | solution.py:480
  80.0 3.9 %collective-permute-start.25 = (bf16[192,768]{1,0:T(8,128)(2,1)S(1)}, bf16[192,768]{1,0:T(8,128)(2,1)S(1)}, u32[]{:S(2)}, u32[]{:S(2)}) collective-permute-start(bf16[192,768]{1,0:T(8,128)(2,1)S(1)} %get-tuple-element.156.refs_2_), channel_id=1, source_target_pairs={{0,1},{1,0},{2,3},{3,2},{4,5},{5,4},{6,7},{7,6},{8,9},{9,8},{10,11... | collective-permute-start | bytes 884744 | tf_op jit(solution)/shard_map/ppermute | solution.py:480
  80.9 16.8 %collective-permute-start.30 = (bf16[128,768]{1,0:T(8,128)(2,1)S(1)}, bf16[128,768]{1,0:T(8,128)(2,1)S(1)}, u32[]{:S(2)}, u32[]{:S(2)}) collective-permute-start(bf16[128,768]{1,0:T(8,128)(2,1)S(1)} %get-tuple-element.170), channel_id=1, source_target_pairs={{0,0},{1,16},{2,8},{3,24},{4,4},{5,20},{6,12},{7,28},{8,2},{9,18},... | collective-permute-start | bytes 589832 | tf_op jit(solution)/shard_map/ppermute | solution.py:480
  81.9 15.7 %collective-permute-start.32 = (bf16[192,768]{1,0:T(8,128)(2,1)S(1)}, bf16[192,768]{1,0:T(8,128)(2,1)S(1)}, u32[]{:S(2)}, u32[]{:S(2)}) collective-permute-start(bf16[192,768]{1,0:T(8,128)(2,1)S(1)} %get-tuple-element.172), channel_id=1, source_target_pairs={{0,4},{1,5},{2,6},{3,7},{4,0},{5,1},{6,2},{7,3},{8,12},{9,13},{10,... | collective-permute-start | bytes 884744 | tf_op jit(solution)/shard_map/ppermute | solution.py:480
  82.2 15.3 %collective-permute-start.31 = (bf16[192,768]{1,0:T(8,128)(2,1)S(1)}, bf16[192,768]{1,0:T(8,128)(2,1)S(1)}, u32[]{:S(2)}, u32[]{:S(2)}) collective-permute-start(bf16[192,768]{1,0:T(8,128)(2,1)S(1)} %get-tuple-element.161.refs_5_), channel_id=1, source_target_pairs={{0,4},{1,5},{2,6},{3,7},{4,0},{5,1},{6,2},{7,3},{8,12},{9,13},{10,... | collective-permute-start | bytes 884744 | tf_op jit(solution)/shard_map/ppermute | solution.py:480
  84.4 20.5 %collective-permute-start.37 = (bf16[384,768]{1,0:T(8,128)(2,1)S(1)}, bf16[384,768]{1,0:T(8,128)(2,1)S(1)}, u32[]{:S(2)}, u32[]{:S(2)}) collective-permute-start(bf16[384,768]{1,0:T(8,128)(2,1)S(1)} %get-tuple-element.162.refs_13_), channel_id=1, source_target_pairs={{0,8},{1,9},{2,10},{3,11},{4,12},{5,13},{6,14},{7,15},{8,0},{9,1},... | collective-permute-start | bytes 1769480 | tf_op jit(solution)/shard_map/ppermute | solution.py:480
  100.4 4.0 %collective-permute-start.35 = (bf16[528,384]{1,0:T(8,128)(2,1)S(1)}, bf16[528,384]{1,0:T(8,128)(2,1)S(1)}, u32[]{:S(2)}, u32[]{:S(2)}) collective-permute-start(bf16[528,384]{1,0:T(8,128)(2,1)S(1)} %get-tuple-element.177), channel_id=1, source_target_pairs={{0,1},{1,0},{2,3},{3,2},{4,5},{5,4},{6,7},{7,6},{8,9},{9,8},{10,11... | collective-permute-start | bytes 1216520 | tf_op jit(solution)/shard_map/ppermute | solution.py:480
  101.2 3.2 %collective-permute-start.34 = (bf16[512,384]{1,0:T(8,128)(2,1)S(1)}, bf16[512,384]{1,0:T(8,128)(2,1)S(1)}, u32[]{:S(2)}, u32[]{:S(2)}) collective-permute-start(bf16[512,384]{1,0:T(8,128)(2,1)S(1)} %get-tuple-element.176), channel_id=1, source_target_pairs={{0,1},{1,0},{2,3},{3,2},{4,5},{5,4},{6,7},{7,6},{8,9},{9,8},{10,11... | collective-permute-start | bytes 1179656 | tf_op jit(solution)/shard_map/ppermute | solution.py:480
  101.2 3.2 %collective-permute-start.33 = (bf16[512,384]{1,0:T(8,128)(2,1)S(1)}, bf16[512,384]{1,0:T(8,128)(2,1)S(1)}, u32[]{:S(2)}, u32[]{:S(2)}) collective-permute-start(bf16[512,384]{1,0:T(8,128)(2,1)S(1)} %get-tuple-element.175.refs_4_), channel_id=1, source_target_pairs={{0,1},{1,0},{2,3},{3,2},{4,5},{5,4},{6,7},{7,6},{8,9},{9,8},{10,11... | collective-permute-start | bytes 1179656 | tf_op jit(solution)/shard_map/ppermute | solution.py:480
  101.7 10.4 %collective-permute-start.41 = (bf16[192,768]{1,0:T(8,128)(2,1)S(1)}, bf16[192,768]{1,0:T(8,128)(2,1)S(1)}, u32[]{:S(2)}, u32[]{:S(2)}) collective-permute-start(bf16[192,768]{1,0:T(8,128)(2,1)S(1)} %get-tuple-element.173.refs_10_), channel_id=1, source_target_pairs={{0,8},{1,9},{2,10},{3,11},{4,12},{5,13},{6,14},{7,15},{8,0},{9,1},... | collective-permute-start | bytes 884744 | tf_op jit(solution)/shard_map/ppermute | solution.py:480
  107.1 11.0 %collective-permute-start.40 = (bf16[256,768]{1,0:T(8,128)(2,1)S(1)}, bf16[256,768]{1,0:T(8,128)(2,1)S(1)}, u32[]{:S(2)}, u32[]{:S(2)}) collective-permute-start(bf16[256,768]{1,0:T(8,128)(2,1)S(1)} %get-tuple-element.185), channel_id=1, source_target_pairs={{0,1},{1,0},{2,3},{3,2},{4,5},{5,4},{6,7},{7,6},{8,9},{9,8},{10,11... | collective-permute-start | bytes 1179656 | tf_op jit(solution)/shard_map/ppermute | solution.py:480
  107.1 10.9 %collective-permute-start.39 = (bf16[256,768]{1,0:T(8,128)(2,1)S(1)}, bf16[256,768]{1,0:T(8,128)(2,1)S(1)}, u32[]{:S(2)}, u32[]{:S(2)}) collective-permute-start(bf16[256,768]{1,0:T(8,128)(2,1)S(1)} %get-tuple-element.184.refs_2_), channel_id=1, source_target_pairs={{0,1},{1,0},{2,3},{3,2},{4,5},{5,4},{6,7},{7,6},{8,9},{9,8},{10,11... | collective-permute-start | bytes 1179656 | tf_op jit(solution)/shard_map/ppermute | solution.py:480
  107.6 21.7 %collective-permute-start.38 = (bf16[192,768]{1,0:T(8,128)(2,1)S(1)}, bf16[192,768]{1,0:T(8,128)(2,1)S(1)}, u32[]{:S(2)}, u32[]{:S(2)}) collective-permute-start(bf16[192,768]{1,0:T(8,128)(2,1)S(1)} %get-tuple-element.182.refs_3_), channel_id=1, source_target_pairs={{0,16},{1,17},{2,18},{3,19},{4,20},{5,21},{6,22},{7,23},{8,24},{9,... | collective-permute-start | bytes 884744 | tf_op jit(solution)/shard_map/ppermute | solution.py:480
  112.1 19.9 %collective-permute-start.44 = (bf16[96,768]{1,0:T(8,128)(2,1)S(1)}, bf16[96,768]{1,0:T(8,128)(2,1)S(1)}, u32[]{:S(2)}, u32[]{:S(2)}) collective-permute-start(bf16[96,768]{1,0:T(8,128)(2,1)S(1)} %get-tuple-element.187.refs_3_), channel_id=1, source_target_pairs={{0,16},{1,17},{2,18},{3,19},{4,20},{5,21},{6,22},{7,23},{8,24},{9,... | collective-permute-start | bytes 442376 | tf_op jit(solution)/shard_map/ppermute | solution.py:480
  116.5 18.1 %collective-permute-start.36 = (bf16[784,384]{1,0:T(8,128)(2,1)S(1)}, bf16[784,384]{1,0:T(8,128)(2,1)S(1)}, u32[]{:S(2)}, u32[]{:S(2)}) collective-permute-start(bf16[784,384]{1,0:T(8,128)(2,1)S(1)} %get-tuple-element.179.refs_2_), channel_id=1, source_target_pairs={{0,4},{1,5},{2,6},{3,7},{4,0},{5,1},{6,2},{7,3},{8,12},{9,13},{10,... | collective-permute-start | bytes 1806344 | tf_op jit(solution)/shard_map/ppermute | solution.py:480
  118.3 13.7 %collective-permute-start.43 = (bf16[256,768]{1,0:T(8,128)(2,1)S(1)}, bf16[256,768]{1,0:T(8,128)(2,1)S(1)}, u32[]{:S(2)}, u32[]{:S(2)}) collective-permute-start(bf16[256,768]{1,0:T(8,128)(2,1)S(1)} %get-tuple-element.188.refs_2_), channel_id=1, source_target_pairs={{0,2},{1,3},{2,0},{3,1},{4,6},{5,7},{6,4},{7,5},{8,10},{9,11},{10,... | collective-permute-start | bytes 1179656 | tf_op jit(solution)/shard_map/ppermute | solution.py:480
  129.4 5.2 %collective-permute-start.42 = (bf16[96,768]{1,0:T(8,128)(2,1)S(1)}, bf16[96,768]{1,0:T(8,128)(2,1)S(1)}, u32[]{:S(2)}, u32[]{:S(2)}) collective-permute-start(bf16[96,768]{1,0:T(8,128)(2,1)S(1)} %get-tuple-element.190.refs_2_), channel_id=1, source_target_pairs={{0,4},{1,5},{2,6},{3,7},{4,0},{5,1},{6,2},{7,3},{8,12},{9,13},{10,... | collective-permute-start | bytes 442376 | tf_op jit(solution)/shard_map/ppermute | solution.py:480
  134.9 11.8 %collective-permute-start.45 = (bf16[400,384]{1,0:T(8,128)(2,1)S(1)}, bf16[400,384]{1,0:T(8,128)(2,1)S(1)}, u32[]{:S(2)}, u32[]{:S(2)}) collective-permute-start(bf16[400,384]{1,0:T(8,128)(2,1)S(1)} %get-tuple-element.196.refs_2_), channel_id=1, source_target_pairs={{0,8},{1,9},{2,10},{3,11},{4,12},{5,13},{6,14},{7,15},{8,0},{9,1},... | collective-permute-start | bytes 921608 | tf_op jit(solution)/shard_map/ppermute | solution.py:480
  136.4 10.2 %collective-permute-start.46 = (bf16[96,768]{1,0:T(8,128)(2,1)S(1)}, bf16[96,768]{1,0:T(8,128)(2,1)S(1)}, u32[]{:S(2)}, u32[]{:S(2)}) collective-permute-start(bf16[96,768]{1,0:T(8,128)(2,1)S(1)} %down_sum.1.refs_2_.refs_0_), channel_id=1, source_target_pairs={{0,16},{1,17},{2,18},{3,19},{4,20},{5,21},{6,22},{7,23},{8,24},{9,... | collective-permute-start | bytes 442376 | tf_op jit(solution)/shard_map/ppermute | solution.py:480
  137.9 12.4 %collective-permute-start.49 = (bf16[48,768]{1,0:T(8,128)(2,1)S(1)}, bf16[48,768]{1,0:T(8,128)(2,1)S(1)}, u32[]{:S(2)}, u32[]{:S(2)}) collective-permute-start(bf16[48,768]{1,0:T(8,128)(2,1)S(1)} %get-tuple-element.194.refs_2_), channel_id=1, source_target_pairs={{0,2},{1,3},{2,0},{3,1},{4,6},{5,7},{6,4},{7,5},{8,10},{9,11},{10,... | collective-permute-start | bytes 221192 | tf_op jit(solution)/shard_map/ppermute | solution.py:480
  140.2 23.3 %collective-permute-start.51 = (bf16[128,768]{1,0:T(8,128)(2,1)S(1)}, bf16[128,768]{1,0:T(8,128)(2,1)S(1)}, u32[]{:S(2)}, u32[]{:S(2)}) collective-permute-start(bf16[128,768]{1,0:T(8,128)(2,1)S(1)} %get-tuple-element.193.refs_2_), channel_id=1, source_target_pairs={{0,4},{1,5},{2,6},{3,7},{4,0},{5,1},{6,2},{7,3},{8,12},{9,13},{10,... | collective-permute-start | bytes 589832 | tf_op jit(solution)/shard_map/ppermute | solution.py:480
  146.6 12.0 %collective-permute-start.48 = (bf16[192,768]{1,0:T(8,128)(2,1)S(1)}, bf16[192,768]{1,0:T(8,128)(2,1)S(1)}, u32[]{:S(2)}, u32[]{:S(2)}) collective-permute-start(bf16[192,768]{1,0:T(8,128)(2,1)S(1)} %down_join.1.refs_2_.refs_0_), channel_id=1, source_target_pairs={{0,8},{1,9},{2,10},{3,11},{4,12},{5,13},{6,14},{7,15},{8,0},{9,1},... | collective-permute-start | bytes 884744 | tf_op jit(solution)/shard_map/ppermute | solution.py:480
  146.8 13.5 %collective-permute-start.47 = (bf16[208,384]{1,0:T(8,128)(2,1)S(1)}, bf16[208,384]{1,0:T(8,128)(2,1)S(1)}, u32[]{:S(2)}, u32[]{:S(2)}) collective-permute-start(bf16[208,384]{1,0:T(8,128)(2,1)S(1)} %get-tuple-element.198.refs_2_), channel_id=1, source_target_pairs={{0,16},{1,17},{2,18},{3,19},{4,20},{5,21},{6,22},{7,23},{8,24},{9,... | collective-permute-start | bytes 479240 | tf_op jit(solution)/shard_map/ppermute | solution.py:480
  150.3 13.2 %collective-permute-start.52 = (bf16[96,768]{1,0:T(8,128)(2,1)S(1)}, bf16[96,768]{1,0:T(8,128)(2,1)S(1)}, u32[]{:S(2)}, u32[]{:S(2)}) collective-permute-start(bf16[96,768]{1,0:T(8,128)(2,1)S(1)} %up_join.1.refs_2_.refs_0_), channel_id=1, source_target_pairs={{0,16},{1,17},{2,18},{3,19},{4,20},{5,21},{6,22},{7,23},{8,24},{9,... | collective-permute-start | bytes 442376 | tf_op jit(solution)/shard_map/ppermute | solution.py:480
  158.7 15.0 %collective-permute-start.56 = (bf16[384,768]{1,0:T(8,128)(2,1)S(1)}, bf16[384,768]{1,0:T(8,128)(2,1)S(1)}, u32[]{:S(2)}, u32[]{:S(2)}) collective-permute-start(bf16[384,768]{1,0:T(8,128)(2,1)S(1)} %down_join_near.1.refs_2_.refs_0_), channel_id=1, source_target_pairs={{0,4},{1,5},{2,6},{3,7},{4,0},{5,1},{6,2},{7,3},{8,12},{9,13},{10,... | collective-permute-start | bytes 1769480 | tf_op jit(solution)/shard_map/ppermute | solution.py:480
  161.0 4.6 %collective-permute-start.50 = (bf16[72,384]{1,0:T(8,128)(2,1)S(1)}, bf16[72,384]{1,0:T(8,128)(2,1)S(1)}, u32[]{:S(2)}, u32[]{:S(2)}) collective-permute-start(bf16[72,384]{1,0:T(8,128)(2,1)S(1)} %get-tuple-element.201.refs_2_), channel_id=1, source_target_pairs={{0,2},{1,3},{2,0},{3,1},{4,6},{5,7},{6,4},{7,5},{8,10},{9,11},{10,... | collective-permute-start | bytes 165896 | tf_op jit(solution)/shard_map/ppermute | solution.py:480
  165.7 7.6 %collective-permute-start.53 = (bf16[192,384]{1,0:T(8,128)(2,1)S(1)}, bf16[192,384]{1,0:T(8,128)(2,1)S(1)}, u32[]{:S(2)}, u32[]{:S(2)}) collective-permute-start(bf16[192,384]{1,0:T(8,128)(2,1)S(1)} %rest_join.1.refs_0_.refs_2_), channel_id=1, source_target_pairs={{0,16},{1,17},{2,18},{3,19},{4,20},{5,21},{6,22},{7,23},{8,24},{9,... | collective-permute-start | bytes 442376 | tf_op jit(solution)/shard_map/ppermute | solution.py:480
  165.8 10.0 %collective-permute-start.55 = (bf16[192,768]{1,0:T(8,128)(2,1)S(1)}, bf16[192,768]{1,0:T(8,128)(2,1)S(1)}, u32[]{:S(2)}, u32[]{:S(2)}) collective-permute-start(bf16[192,768]{1,0:T(8,128)(2,1)S(1)} %up_join_far.1.refs_3_.refs_0_), channel_id=1, source_target_pairs={{0,8},{1,9},{2,10},{3,11},{4,12},{5,13},{6,14},{7,15},{8,0},{9,1},... | collective-permute-start | bytes 884744 | tf_op jit(solution)/shard_map/ppermute | solution.py:480
  173.3 6.8 %collective-permute-start.54 = (bf16[384,384]{1,0:T(8,128)(2,1)S(1)}, bf16[384,384]{1,0:T(8,128)(2,1)S(1)}, u32[]{:S(2)}, u32[]{:S(2)}) collective-permute-start(bf16[384,384]{1,0:T(8,128)(2,1)S(1)} %rest_join_far.1.refs_2_.refs_0_), channel_id=1, source_target_pairs={{0,8},{1,9},{2,10},{3,11},{4,12},{5,13},{6,14},{7,15},{8,0},{9,1},... | collective-permute-start | bytes 884744 | tf_op jit(solution)/shard_map/ppermute | solution.py:480
  175.8 13.1 %collective-permute-start.59 = (bf16[384,768]{1,0:T(8,128)(2,1)S(1)}, bf16[384,768]{1,0:T(8,128)(2,1)S(1)}, u32[]{:S(2)}, u32[]{:S(2)}) collective-permute-start(bf16[384,768]{1,0:T(8,128)(2,1)S(1)} %up_join_near.1.refs_2_.refs_0_), channel_id=1, source_target_pairs={{0,4},{1,5},{2,6},{3,7},{4,0},{5,1},{6,2},{7,3},{8,12},{9,13},{10,... | collective-permute-start | bytes 1769480 | tf_op jit(solution)/shard_map/ppermute | solution.py:480
  180.2 15.1 %collective-permute-start.57 = (bf16[768,384]{1,0:T(8,128)(2,1)S(1)}, bf16[768,384]{1,0:T(8,128)(2,1)S(1)}, u32[]{:S(2)}, u32[]{:S(2)}) collective-permute-start(bf16[768,384]{1,0:T(8,128)(2,1)S(1)} %rest_join_near.1.refs_2_.refs_0_), channel_id=1, source_target_pairs={{0,4},{1,5},{2,6},{3,7},{4,0},{5,1},{6,2},{7,3},{8,12},{9,13},{10,... | collective-permute-start | bytes 1769480 | tf_op jit(solution)/shard_map/ppermute | solution.py:480
  180.4 10.2 %collective-permute-start.58 = (bf16[128,768]{1,0:T(8,128)(2,1)S(1)}, bf16[128,768]{1,0:T(8,128)(2,1)S(1)}, u32[]{:S(2)}, u32[]{:S(2)}) collective-permute-start(bf16[128,768]{1,0:T(8,128)(2,1)S(1)} %input_sum.1.refs_2_), channel_id=1, source_target_pairs={{0,0},{1,16},{2,8},{3,24},{4,4},{5,20},{6,12},{7,28},{8,2},{9,18},... | collective-permute-start | bytes 589832 | tf_op jit(solution)/shard_map/ppermute | solution.py:480

commit v7 on v6

--- a/solution.py
+++ b/solution.py
@@ -712,7 +712,7 @@
         lse_out[pl.ds(h, 1), :] = top + jnp.log(total)
         return carry
 
-    lax.fori_loop(0, 2 * pairs, head, 0)
+    lax.fori_loop(0, 2 * pairs, head, 0, unroll=3)
     mixed = jnp.transpose(ot[...].reshape(half, 2 * rows)).astype(jnp.bfloat16)
     o_out[...] = mixed
     ins.wait()
@@ -863,7 +863,7 @@
         dqt[h] = dot(kt[h], d_scores)
         return carry
 
-    lax.fori_loop(0, 2 * pairs, head, 0)
+    lax.fori_loop(0, 2 * pairs, head, 0, unroll=3)
     dq = (jnp.transpose(dqt[...].reshape(half, 2 * rows)) * 0.125).astype(jnp.bfloat16)
     dq_out[...] = dq
     qv_sums[...] = jnp.zeros_like(qv_sums)

time: 197 us -> 196 us (level)
  no operation moved by 1% of the time
where the time goes in v7:
time: 196 us
  waiting for transfers between devices  82.3 us (42%)
  starting transfers between devices  71.5 us (36%)
  Pallas kernels  41.1 us (21%)
    ppermute x60, waiting for transfers between devices, moved(): lax.ppermute(block, AXES, [(number(s), number(move(*s))) for s in spots])  82.3 us
    ppermute x60, starting transfers between devices, moved(): lax.ppermute(block, AXES, [(number(s), number(move(*s))) for s in spots])  71.5 us
    pallas_call x42, Pallas kernels, kernel_call(): pl.pallas_call(run, name=name, out_shape=[jax.ShapeDtypeStruct(shape, dty...  41.1 us
  transfers between devices with their start and end apart: 60, of which 23 were waited for; matrix products, arithmetic and copies ran while one was open for 0% of the time, Pallas kernels for 18%

profile of v7, /device:TPU:0, one launch (start us, length us, event | category | flops | bytes accessed | tf_op | source)
XLA Modules:
  0.0 196.1 jit_solution(6263922181225109950)
XLA Ops:
  0.7 1.0 block.1.refs_12_
  1.6 1.5 pack.1
  3.8 2.9 %collective-permute-start.8 = (bf16[304,384]{1,0:T(8,128)(2,1)S(1)}, bf16[304,384]{1,0:T(8,128)(2,1)S(1)}, u32[]{:S(2)}, u32[]{:S(2)}) collective-permute-start(bf16[304,384]{1,0:T(8,128)(2,1)S(1)} %get-tuple-element.121.refs_2_), channel_id=1, source_target_pairs={{0,2},{1,3},{2,0},{3,1},{4,6},{5,7},{6,4},{7,5},{8,10},{9,11},{10,... | collective-permute-start | bytes 700424 | tf_op jit(solution)/shard_map/ppermute | solution.py:480
  7.3 5.6 %collective-permute-done.8.refs_8_ = bf16[304,384]{1,0:T(8,128)(2,1)S(1)} collective-permute-done((bf16[304,384]{1,0:T(8,128)(2,1)S(1)}, bf16[304,384]{1,0:T(8,128)(2,1)S(1)}, u32[]{:S(2)}, u32[]{:S(2)}) %collective-permute-start.8) | collective-permute-done | bytes 233504 | tf_op jit(solution)/shard_map/ppermute | solution.py:480
  13.0 1.4 collective-permute-start.9
  15.1 7.2 %collective-permute-start.3 = (bf16[144,768]{1,0:T(8,128)(2,1)S(1)}, bf16[144,768]{1,0:T(8,128)(2,1)S(1)}, u32[]{:S(2)}, u32[]{:S(2)}) collective-permute-start(bf16[144,768]{1,0:T(8,128)(2,1)S(1)} %once.5.refs_0_), channel_id=1, source_target_pairs={{0,2},{1,3},{2,0},{3,1},{4,6},{5,7},{6,4},{7,5},{8,10},{9,11},{10,... | collective-permute-start | bytes 663560 | tf_op jit(solution)/shard_map/ppermute | solution.py:480
  22.8 1.7 collective-permute-done.4.refs_1_.refs_4_
  24.5 1.7 collective-permute-done.3.refs_0_
  26.7 1.3 cut.1
  27.9 0.9 cotangent.1.refs_13_.refs_0_
  29.2 2.0 collective-permute-start.16
  31.7 2.3 %project.1 = (bf16[512,768]{1,0:T(8,128)(2,1)S(1)}, bf16[256,384]{1,0:T(8,128)(2,1)S(1)}, bf16[768,1152]{1,0:T(8,128)(2,1)S(1)}, f32[8,768]{1,0:T(8,128)S(1)}, f32[4,8,384]{2,1,0:T(8,128)S(1)}) custom-call(bf16[144,768]{1,0:T(8,128)(2,1)S(1)} %once.5.refs_0_, bf16[144,768]{1,0:T(8,128)(2,1)S(1)} %once.6.refs_1_, ...), custom_call_target="tpu_custom_call" | custom-call | flops 10000000000 | bytes 1 | tf_op jit(solution)/shard_map/project/pallas_call | solution.py:1140
  34.0 2.3 %collective-permute-done.7.refs_0_ = bf16[144,768]{1,0:T(8,128)(2,1)S(1)} collective-permute-done((bf16[144,768]{1,0:T(8,128)(2,1)S(1)}, bf16[144,768]{1,0:T(8,128)(2,1)S(1)}, u32[]{:S(2)}, u32[]{:S(2)}) %collective-permute-start.7) | collective-permute-done | bytes 221216 | tf_op jit(solution)/shard_map/ppermute | solution.py:480
  36.3 1.5 collective-permute-done.13.refs_7_
  37.8 6.1 %attend.1 = (bf16[256,768]{1,0:T(8,128)(2,1)S(1)}, bf16[1024,768]{1,0:T(8,128)(2,1)S(1)}, bf16[384,768]{1,0:T(8,128)(2,1)S(1)}, bf16[3,1024,128]{2,1,0:T(8,128)(...) custom-call(bf16[144,768]{1,0:T(8,128)(2,1)S(1)} %once.5.refs_0_, ...), custom_call_target="tpu_custom_call" | custom-call | flops 1 | bytes 1 | tf_op jit(solution)/shard_map/attend/pallas_call | solution.py:1140
  43.9 2.1 %collective-permute-start.15 = (bf16[256,768]{1,0:T(8,128)(2,1)S(1)}, bf16[256,768]{1,0:T(8,128)(2,1)S(1)}, u32[]{:S(2)}, u32[]{:S(2)}) collective-permute-start(bf16[256,768]{1,0:T(8,128)(2,1)S(1)} %get-tuple-element.129.refs_2_), channel_id=1, source_target_pairs={{0,2},{1,3},{2,0},{3,1},{4,6},{5,7},{6,4},{7,5},{8,10},{9,11},{10,... | collective-permute-start | bytes 1179656 | tf_op jit(solution)/shard_map/ppermute | solution.py:480
  46.9 1.1 collective-permute-done.19.refs_4_
  48.4 1.5 inner.1
  50.0 0.8 collective-permute-start.22
  50.8 4.6 %collective-permute-done.15.refs_1_ = bf16[256,768]{1,0:T(8,128)(2,1)S(1)} collective-permute-done((bf16[256,768]{1,0:T(8,128)(2,1)S(1)}, bf16[256,768]{1,0:T(8,128)(2,1)S(1)}, u32[]{:S(2)}, u32[]{:S(2)}) %collective-permute-start.15) | collective-permute-done | bytes 393248 | tf_op jit(solution)/shard_map/ppermute | solution.py:480
  55.4 2.0 %feedforward.1 = (bf16[128,768]{1,0:T(8,128)(2,1)S(1)}, bf16[128,768]{1,0:T(8,128)(2,1)S(1)}, bf16[256,768]{1,0:T(8,128)(2,1)S(1)}, bf16[256,1536]{1,0:T(8,128)(...) custom-call(f32[256,768]{1,0:T(8,128)S(1)} %get-tuple-element.128.re, ...), custom_call_target="tpu_custom_call" | custom-call | flops 1 | bytes 1 | tf_op jit(solution)/shard_map/feedforward/pallas_call | solution.py:1140
  57.5 1.8 collective-permute-start.21
  59.8 7.5 %collective-permute-done.21.refs_2_ = bf16[128,768]{1,0:T(8,128)(2,1)S(1)} collective-permute-done((bf16[128,768]{1,0:T(8,128)(2,1)S(1)}, bf16[128,768]{1,0:T(8,128)(2,1)S(1)}, u32[]{:S(2)}, u32[]{:S(2)}) %collective-permute-start.21) | collective-permute-done | bytes 196640 | tf_op jit(solution)/shard_map/ppermute | solution.py:480
  67.3 4.2 %collective-permute-done.20.refs_1_ = bf16[128,768]{1,0:T(8,128)(2,1)S(1)} collective-permute-done((bf16[128,768]{1,0:T(8,128)(2,1)S(1)}, bf16[128,768]{1,0:T(8,128)(2,1)S(1)}, u32[]{:S(2)}, u32[]{:S(2)}) %collective-permute-start.20) | collective-permute-done | bytes 196640 | tf_op jit(solution)/shard_map/ppermute | solution.py:480
  71.5 0.9 norm_back.1
  73.5 1.7 feedforward_back.1
  75.1 2.5 %collective-permute-start.24 = (bf16[256,768]{1,0:T(8,128)(2,1)S(1)}, bf16[256,768]{1,0:T(8,128)(2,1)S(1)}, u32[]{:S(2)}, u32[]{:S(2)}) collective-permute-start(bf16[256,768]{1,0:T(8,128)(2,1)S(1)} %get-tuple-element.145.refs_2_), channel_id=1, source_target_pairs={{0,2},{1,3},{2,0},{3,1},{4,6},{5,7},{6,4},{7,5},{8,10},{9,11},{10,... | collective-permute-start | bytes 1179656 | tf_op jit(solution)/shard_map/ppermute | solution.py:480
  77.6 1.3 up_grad.1
  80.7 0.9 collective-permute-start.30
  82.0 1.6 collective-permute-start.31
  84.1 2.8 %collective-permute-start.37 = (bf16[384,768]{1,0:T(8,128)(2,1)S(1)}, bf16[384,768]{1,0:T(8,128)(2,1)S(1)}, u32[]{:S(2)}, u32[]{:S(2)}) collective-permute-start(bf16[384,768]{1,0:T(8,128)(2,1)S(1)} %get-tuple-element.162.refs_13_), channel_id=1, source_target_pairs={{0,8},{1,9},{2,10},{3,11},{4,12},{5,13},{6,14},{7,15},{8,0},{9,1},... | collective-permute-start | bytes 1769480 | tf_op jit(solution)/shard_map/ppermute | solution.py:480
  86.9 3.7 %collective-permute-done.24.refs_1_ = bf16[256,768]{1,0:T(8,128)(2,1)S(1)} collective-permute-done((bf16[256,768]{1,0:T(8,128)(2,1)S(1)}, bf16[256,768]{1,0:T(8,128)(2,1)S(1)}, u32[]{:S(2)}, u32[]{:S(2)}) %collective-permute-start.24) | collective-permute-done | bytes 393248 | tf_op jit(solution)/shard_map/ppermute | solution.py:480
  90.6 6.1 %attend_back.1 = (bf16[1024,768]{1,0:T(8,128)(2,1)S(1)}, bf16[256,384]{1,0:T(8,128)(2,1)S(1)}, f32[128,768]{1,0:T(8,128)S(1)}, bf16[256,768]{1,0:T(8,128)(2,1)S(...) custom-call(f32[256,768]{1,0:T(8,128)S(1)} %get-tuple-element.144.refs_0_, ...), custom_call_target="tpu_custom_call" | custom-call | flops 10000000000 | bytes 1 | tf_op jit(solution)/shard_map/attend_back/pallas_call | solution.py:1140
  97.0 2.6 %weight_grad.1 = (bf16[512,384]{1,0:T(8,128)(2,1)S(1)}, bf16[512,384]{1,0:T(8,128)(2,1)S(1)}, bf16[528,384]{1,0:T(8,128)(2,1)S(1)}, f32[1552,384]{1,0:T(8,128)S(1)}) custom-call(bf16[1024,768]{1,0:T(8,128)(2,1)S(1)} %get-tuple-element.127.refs_2_.refs_0_, bf16[1024,768]{1,0:T(8,128)(2,1)S(1)} %get-tuple-element.163.refs_3_.refs_1_, ...), custom_call_target="tpu_custom_call" | custom-call | flops 1 | bytes 1 | tf_op jit(solution)/shard_map/weight_grad/pallas_call | solution.py:1140
  99.6 1.3 collective-permute-start.35
  101.4 2.7 %collective-permute-start.41 = (bf16[192,768]{1,0:T(8,128)(2,1)S(1)}, bf16[192,768]{1,0:T(8,128)(2,1)S(1)}, u32[]{:S(2)}, u32[]{:S(2)}) collective-permute-start(bf16[192,768]{1,0:T(8,128)(2,1)S(1)} %get-tuple-element.173.refs_10_), channel_id=1, source_target_pairs={{0,8},{1,9},{2,10},{3,11},{4,12},{5,13},{6,14},{7,15},{8,0},{9,1},... | collective-permute-start | bytes 884744 | tf_op jit(solution)/shard_map/ppermute | solution.py:480
  104.7 2.1 %input_grad.1 = (bf16[256,768]{1,0:T(8,128)(2,1)S(1)}, bf16[256,768]{1,0:T(8,128)(2,1)S(1)}, f32[512,768]{1,0:T(8,128)S(1)}) custom-call(bf16[256,384]{1,0:T(8,128)(2,1)S(1)} %get-tuple-element.164.refs_2_.refs_0_, bf16[1024,768]{1,0:T(8,128)(2,1)S(1)} %get-tuple-element.163.refs_3_.refs_1_, bf16[768,1152]{1,0:T(8,128)(2,1)S(1)} %get-tuple-element.125.refs_10_.refs_2_, ...), custom_call_target="tpu_custom_call" | custom-call | flops 1 | bytes 1 | tf_op jit(solution)/shard_map/input_grad/pallas_call | solution.py:1140
  107.3 4.0 %collective-permute-start.38 = (bf16[192,768]{1,0:T(8,128)(2,1)S(1)}, bf16[192,768]{1,0:T(8,128)(2,1)S(1)}, u32[]{:S(2)}, u32[]{:S(2)}) collective-permute-start(bf16[192,768]{1,0:T(8,128)(2,1)S(1)} %get-tuple-element.182.refs_3_), channel_id=1, source_target_pairs={{0,16},{1,17},{2,18},{3,19},{4,20},{5,21},{6,22},{7,23},{8,24},{9,... | collective-permute-start | bytes 884744 | tf_op jit(solution)/shard_map/ppermute | solution.py:480
  111.4 4.4 %collective-permute-start.44 = (bf16[96,768]{1,0:T(8,128)(2,1)S(1)}, bf16[96,768]{1,0:T(8,128)(2,1)S(1)}, u32[]{:S(2)}, u32[]{:S(2)}) collective-permute-start(bf16[96,768]{1,0:T(8,128)(2,1)S(1)} %get-tuple-element.187.refs_3_), channel_id=1, source_target_pairs={{0,16},{1,17},{2,18},{3,19},{4,20},{5,21},{6,22},{7,23},{8,24},{9,... | collective-permute-start | bytes 442376 | tf_op jit(solution)/shard_map/ppermute | solution.py:480
  115.8 1.5 collective-permute-start.36
  117.9 2.4 %collective-permute-start.43 = (bf16[256,768]{1,0:T(8,128)(2,1)S(1)}, bf16[256,768]{1,0:T(8,128)(2,1)S(1)}, u32[]{:S(2)}, u32[]{:S(2)}) collective-permute-start(bf16[256,768]{1,0:T(8,128)(2,1)S(1)} %get-tuple-element.188.refs_2_), channel_id=1, source_target_pairs={{0,2},{1,3},{2,0},{3,1},{4,6},{5,7},{6,4},{7,5},{8,10},{9,11},{10,... | collective-permute-start | bytes 1179656 | tf_op jit(solution)/shard_map/ppermute | solution.py:480
  120.3 8.3 %collective-permute-done.38 = bf16[192,768]{1,0:T(8,128)(2,1)S(1)} collective-permute-done((bf16[192,768]{1,0:T(8,128)(2,1)S(1)}, bf16[192,768]{1,0:T(8,128)(2,1)S(1)}, u32[]{:S(2)}, u32[]{:S(2)}) %collective-permute-start.38) | collective-permute-done | bytes 294944 | tf_op jit(solution)/shard_map/ppermute | solution.py:480
  128.7 1.6 collective-permute-start.42
  130.3 1.0 collective-permute-done.44.refs_1_
  131.4 2.5 %collective-permute-done.42 = bf16[96,768]{1,0:T(8,128)(2,1)S(1)} collective-permute-done((bf16[96,768]{1,0:T(8,128)(2,1)S(1)}, bf16[96,768]{1,0:T(8,128)(2,1)S(1)}, u32[]{:S(2)}, u32[]{:S(2)}) %collective-permute-start.42) | collective-permute-done | bytes 147488 | tf_op jit(solution)/shard_map/ppermute | solution.py:480
  134.2 1.5 collective-permute-start.45
  135.7 1.9 collective-permute-start.46
  137.6 1.8 collective-permute-start.49
  139.4 1.5 collective-permute-start.51
  140.9 5.0 %collective-permute-done.46.refs_1_ = bf16[96,768]{1,0:T(8,128)(2,1)S(1)} collective-permute-done((bf16[96,768]{1,0:T(8,128)(2,1)S(1)}, bf16[96,768]{1,0:T(8,128)(2,1)S(1)}, u32[]{:S(2)}, u32[]{:S(2)}) %collective-permute-start.46) | collective-permute-done | bytes 147488 | tf_op jit(solution)/shard_map/ppermute | solution.py:480
  146.2 3.3 %collective-permute-start.47 = (bf16[208,384]{1,0:T(8,128)(2,1)S(1)}, bf16[208,384]{1,0:T(8,128)(2,1)S(1)}, u32[]{:S(2)}, u32[]{:S(2)}) collective-permute-start(bf16[208,384]{1,0:T(8,128)(2,1)S(1)} %get-tuple-element.198.refs_2_), channel_id=1, source_target_pairs={{0,16},{1,17},{2,18},{3,19},{4,20},{5,21},{6,22},{7,23},{8,24},{9,... | collective-permute-start | bytes 479240 | tf_op jit(solution)/shard_map/ppermute | solution.py:480
  149.7 8.4 %collective-permute-done.48.refs_1_ = bf16[192,768]{1,0:T(8,128)(2,1)S(1)} collective-permute-done((bf16[192,768]{1,0:T(8,128)(2,1)S(1)}, bf16[192,768]{1,0:T(8,128)(2,1)S(1)}, u32[]{:S(2)}, u32[]{:S(2)}) %collective-permute-start.48) | collective-permute-done | bytes 294944 | tf_op jit(solution)/shard_map/ppermute | solution.py:480
  158.1 1.5 collective-permute-start.56
  160.3 2.4 %collective-permute-start.50 = (bf16[72,384]{1,0:T(8,128)(2,1)S(1)}, bf16[72,384]{1,0:T(8,128)(2,1)S(1)}, u32[]{:S(2)}, u32[]{:S(2)}) collective-permute-start(bf16[72,384]{1,0:T(8,128)(2,1)S(1)} %get-tuple-element.201.refs_2_), channel_id=1, source_target_pairs={{0,2},{1,3},{2,0},{3,1},{4,6},{5,7},{6,4},{7,5},{8,10},{9,11},{10,... | collective-permute-start | bytes 165896 | tf_op jit(solution)/shard_map/ppermute | solution.py:480
  162.8 2.0 %collective-permute-done.50.refs_1_ = bf16[72,384]{1,0:T(8,128)(2,1)S(1)} collective-permute-done((bf16[72,384]{1,0:T(8,128)(2,1)S(1)}, bf16[72,384]{1,0:T(8,128)(2,1)S(1)}, u32[]{:S(2)}, u32[]{:S(2)}) %collective-permute-start.50) | collective-permute-done | bytes 55328 | tf_op jit(solution)/shard_map/ppermute | solution.py:480
  164.9 3.1 %collective-permute-start.55 = (bf16[192,768]{1,0:T(8,128)(2,1)S(1)}, bf16[192,768]{1,0:T(8,128)(2,1)S(1)}, u32[]{:S(2)}, u32[]{:S(2)}) collective-permute-start(bf16[192,768]{1,0:T(8,128)(2,1)S(1)} %up_join_far.1.refs_3_.refs_0_), channel_id=1, source_target_pairs={{0,8},{1,9},{2,10},{3,11},{4,12},{5,13},{6,14},{7,15},{8,0},{9,1},... | collective-permute-start | bytes 884744 | tf_op jit(solution)/shard_map/ppermute | solution.py:480
  168.0 4.4 %collective-permute-done.53.refs_1_ = bf16[192,384]{1,0:T(8,128)(2,1)S(1)} collective-permute-done((bf16[192,384]{1,0:T(8,128)(2,1)S(1)}, bf16[192,384]{1,0:T(8,128)(2,1)S(1)}, u32[]{:S(2)}, u32[]{:S(2)}) %collective-permute-start.53) | collective-permute-done | bytes 147488 | tf_op jit(solution)/shard_map/ppermute | solution.py:480
  172.8 1.6 down_out.1
  174.9 1.5 collective-permute-start.59
  176.4 2.8 %collective-permute-done.54.refs_1_ = bf16[384,384]{1,0:T(8,128)(2,1)S(1)} collective-permute-done((bf16[384,384]{1,0:T(8,128)(2,1)S(1)}, bf16[384,384]{1,0:T(8,128)(2,1)S(1)}, u32[]{:S(2)}, u32[]{:S(2)}) %collective-permute-start.54) | collective-permute-done | bytes 294944 | tf_op jit(solution)/shard_map/ppermute | solution.py:480
  180.2 7.9 %collective-permute-done.59.refs_1_ = bf16[384,768]{1,0:T(8,128)(2,1)S(1)} collective-permute-done((bf16[384,768]{1,0:T(8,128)(2,1)S(1)}, bf16[384,768]{1,0:T(8,128)(2,1)S(1)}, u32[]{:S(2)}, u32[]{:S(2)}) %collective-permute-start.59) | collective-permute-done | bytes 589856 | tf_op jit(solution)/shard_map/ppermute | solution.py:480
  188.1 1.6 up_out.1
  189.7 4.7 %collective-permute-done.57.refs_1_ = bf16[768,384]{1,0:T(8,128)(2,1)S(1)} collective-permute-done((bf16[768,384]{1,0:T(8,128)(2,1)S(1)}, bf16[768,384]{1,0:T(8,128)(2,1)S(1)}, u32[]{:S(2)}, u32[]{:S(2)}) %collective-permute-start.57) | collective-permute-done | bytes 589856 | tf_op jit(solution)/shard_map/ppermute | solution.py:480
  194.4 1.7 rest_out.1
  (106 shorter events, 15.6 us)
Async XLA Ops:
  1.6 24.6 %copy-start = (bf16[768,768]{1,0:T(8,128)(2,1)S(1)}, bf16[768,768]{1,0:T(8,128)(2,1)}, u32[]{:S(2)}) copy-start(bf16[768,768]{1,0:T(8,128)(2,1)} %refs_5_.5) | copy-start | bytes 3538948
  3.2 11.2 %collective-permute-start.1 = (bf16[592,384]{1,0:T(8,128)(2,1)S(1)}, bf16[592,384]{1,0:T(8,128)(2,1)S(1)}, u32[]{:S(2)}, u32[]{:S(2)}) collective-permute-start(bf16[592,384]{1,0:T(8,128)(2,1)S(1)} %get-tuple-element.120.refs_12_), channel_id=1, source_target_pairs={{0,1},{1,0},{2,3},{3,2},{4,5},{5,4},{6,7},{7,6},{8,9},{9,8},{10,11... | collective-permute-start | bytes 1363976 | tf_op jit(solution)/shard_map/ppermute | solution.py:480
  3.7 10.7 %collective-permute-start.2 = (bf16[192,768]{1,0:T(8,128)(2,1)}, bf16[192,768]{1,0:T(8,128)(2,1)S(1)}, u32[]{:S(2)}, u32[]{:S(2)}) collective-permute-start(bf16[192,768]{1,0:T(8,128)(2,1)} %refs_12_.1), channel_id=1, source_target_pairs={{0,1},{1,0},{2,3},{3,2},{4,5},{5,4},{6,7},{7,6},{8,9},{9,8},{10,11... | collective-permute-start | bytes 884744 | tf_op jit(solution)/shard_map/ppermute | solution.py:480
  3.8 9.2 %collective-permute-start.8 = (bf16[304,384]{1,0:T(8,128)(2,1)S(1)}, bf16[304,384]{1,0:T(8,128)(2,1)S(1)}, u32[]{:S(2)}, u32[]{:S(2)}) collective-permute-start(bf16[304,384]{1,0:T(8,128)(2,1)S(1)} %get-tuple-element.121.refs_2_), channel_id=1, source_target_pairs={{0,2},{1,3},{2,0},{3,1},{4,6},{5,7},{6,4},{7,5},{8,10},{9,11},{10,... | collective-permute-start | bytes 700424 | tf_op jit(solution)/shard_map/ppermute | solution.py:480
  6.7 7.7 %collective-permute-start = (bf16[144,768]{1,0:T(8,128)(2,1)S(1)}, bf16[144,768]{1,0:T(8,128)(2,1)S(1)}, u32[]{:S(2)}, u32[]{:S(2)}) collective-permute-start(bf16[144,768]{1,0:T(8,128)(2,1)S(1)} %block.1.refs_12_), channel_id=1, source_target_pairs={{0,0},{1,16},{2,8},{3,24},{4,4},{5,20},{6,12},{7,28},{8,2},{9,18},... | collective-permute-start | bytes 663560 | tf_op jit(solution)/shard_map/ppermute | solution.py:480
  13.0 9.3 %collective-permute-start.9 = (bf16[304,384]{1,0:T(8,128)(2,1)S(1)}, bf16[304,384]{1,0:T(8,128)(2,1)S(1)}, u32[]{:S(2)}, u32[]{:S(2)}) collective-permute-start(bf16[304,384]{1,0:T(8,128)(2,1)S(1)} %collective-permute-done.8.refs_8_), channel_id=1, source_target_pairs={{0,4},{1,5},{2,6},{3,7},{4,0},{5,1},{6,2},{7,3},{8,12},{9,13},{10,... | collective-permute-start | bytes 700424 | tf_op jit(solution)/shard_map/ppermute | solution.py:480
  14.4 10.1 %collective-permute-start.4 = (bf16[144,768]{1,0:T(8,128)(2,1)S(1)}, bf16[144,768]{1,0:T(8,128)(2,1)S(1)}, u32[]{:S(2)}, u32[]{:S(2)}) collective-permute-start(bf16[144,768]{1,0:T(8,128)(2,1)S(1)} %once.5.refs_0_), channel_id=1, source_target_pairs={{0,4},{1,5},{2,6},{3,7},{4,0},{5,1},{6,2},{7,3},{8,12},{9,13},{10,... | collective-permute-start | bytes 663560 | tf_op jit(solution)/shard_map/ppermute | solution.py:480
  15.1 11.1 %collective-permute-start.3 = (bf16[144,768]{1,0:T(8,128)(2,1)S(1)}, bf16[144,768]{1,0:T(8,128)(2,1)S(1)}, u32[]{:S(2)}, u32[]{:S(2)}) collective-permute-start(bf16[144,768]{1,0:T(8,128)(2,1)S(1)} %once.5.refs_0_), channel_id=1, source_target_pairs={{0,2},{1,3},{2,0},{3,1},{4,6},{5,7},{6,4},{7,5},{8,10},{9,11},{10,... | collective-permute-start | bytes 663560 | tf_op jit(solution)/shard_map/ppermute | solution.py:480
  22.3 6.6 %collective-permute-start.10 = (bf16[304,384]{1,0:T(8,128)(2,1)S(1)}, bf16[304,384]{1,0:T(8,128)(2,1)S(1)}, u32[]{:S(2)}, u32[]{:S(2)}) collective-permute-start(bf16[304,384]{1,0:T(8,128)(2,1)S(1)} %collective-permute-done.8.refs_8_), channel_id=1, source_target_pairs={{0,1},{1,0},{2,3},{3,2},{4,5},{5,4},{6,7},{7,6},{8,9},{9,8},{10,11... | collective-permute-start | bytes 700424 | tf_op jit(solution)/shard_map/ppermute | solution.py:480
  22.3 8.9 %collective-permute-start.11 = (bf16[304,384]{1,0:T(8,128)(2,1)S(1)}, bf16[304,384]{1,0:T(8,128)(2,1)S(1)}, u32[]{:S(2)}, u32[]{:S(2)}) collective-permute-start(bf16[304,384]{1,0:T(8,128)(2,1)S(1)} %collective-permute-done.9.refs_9_), channel_id=1, source_target_pairs={{0,1},{1,0},{2,3},{3,2},{4,5},{5,4},{6,7},{7,6},{8,9},{9,8},{10,11... | collective-permute-start | bytes 700424 | tf_op jit(solution)/shard_map/ppermute | solution.py:480
  22.8 6.4 %collective-permute-start.5 = (bf16[144,768]{1,0:T(8,128)(2,1)S(1)}, bf16[144,768]{1,0:T(8,128)(2,1)S(1)}, u32[]{:S(2)}, u32[]{:S(2)}) collective-permute-start(bf16[144,768]{1,0:T(8,128)(2,1)S(1)} %once.5.refs_0_), channel_id=1, source_target_pairs={{0,1},{1,0},{2,3},{3,2},{4,5},{5,4},{6,7},{7,6},{8,9},{9,8},{10,11... | collective-permute-start | bytes 663560 | tf_op jit(solution)/shard_map/ppermute | solution.py:480
  26.2 5.0 %collective-permute-start.6 = (bf16[144,768]{1,0:T(8,128)(2,1)S(1)}, bf16[144,768]{1,0:T(8,128)(2,1)S(1)}, u32[]{:S(2)}, u32[]{:S(2)}) collective-permute-start(bf16[144,768]{1,0:T(8,128)(2,1)S(1)} %once.6.refs_1_), channel_id=1, source_target_pairs={{0,1},{1,0},{2,3},{3,2},{4,5},{5,4},{6,7},{7,6},{8,9},{9,8},{10,11... | collective-permute-start | bytes 663560 | tf_op jit(solution)/shard_map/ppermute | solution.py:480
  26.2 11.6 %collective-permute-start.14 = (bf16[768,768]{1,0:T(8,128)(2,1)S(1)}, bf16[768,768]{1,0:T(8,128)(2,1)S(1)}, u32[]{:S(2)}, u32[]{:S(2)}) collective-permute-start(bf16[768,768]{1,0:T(8,128)(2,1)S(1)} %copy-done), channel_id=1, source_target_pairs={{0,1},{1,0},{2,3},{3,2},{4,5},{5,4},{6,7},{7,6},{8,9},{9,8},{10,11... | collective-permute-start | bytes 3538952 | tf_op jit(solution)/shard_map/ppermute | solution.py:480
  28.9 7.4 %collective-permute-start.7 = (bf16[144,768]{1,0:T(8,128)(2,1)S(1)}, bf16[144,768]{1,0:T(8,128)(2,1)S(1)}, u32[]{:S(2)}, u32[]{:S(2)}) collective-permute-start(bf16[144,768]{1,0:T(8,128)(2,1)S(1)} %once.6.refs_1_), channel_id=1, source_target_pairs={{0,4},{1,5},{2,6},{3,7},{4,0},{5,1},{6,2},{7,3},{8,12},{9,13},{10,... | collective-permute-start | bytes 663560 | tf_op jit(solution)/shard_map/ppermute | solution.py:480
  29.2 17.1 %collective-permute-start.16 = (bf16[192,1536]{1,0:T(8,128)(2,1)S(1)}, bf16[192,1536]{1,0:T(8,128)(2,1)S(1)}, u32[]{:S(2)}, u32[]{:S(2)}) collective-permute-start(bf16[192,1536]{1,0:T(8,128)(2,1)S(1)} %get-tuple-element.122.refs_1_), channel_id=1, source_target_pairs={{0,2},{1,3},{2,0},{3,1},{4,6},{5,7},{6,4},{7,5},{8,10},{9,11},{10,... | collective-permute-start | bytes 1769480 | tf_op jit(solution)/shard_map/ppermute | solution.py:480
  31.1 14.9 %collective-permute-start.17 = (bf16[192,1536]{1,0:T(8,128)(2,1)S(1)}, bf16[192,1536]{1,0:T(8,128)(2,1)S(1)}, u32[]{:S(2)}, u32[]{:S(2)}) collective-permute-start(bf16[192,1536]{1,0:T(8,128)(2,1)S(1)} %get-tuple-element.132), channel_id=1, source_target_pairs={{0,1},{1,0},{2,3},{3,2},{4,5},{5,4},{6,7},{7,6},{8,9},{9,8},{10,11... | collective-permute-start | bytes 1769480 | tf_op jit(solution)/shard_map/ppermute | solution.py:480
  31.1 5.2 %collective-permute-start.12 = (bf16[144,768]{1,0:T(8,128)(2,1)S(1)}, bf16[144,768]{1,0:T(8,128)(2,1)S(1)}, u32[]{:S(2)}, u32[]{:S(2)}) collective-permute-start(bf16[144,768]{1,0:T(8,128)(2,1)S(1)} %collective-permute-done.4.refs_1_.refs_4_), channel_id=1, source_target_pairs={{0,1},{1,0},{2,3},{3,2},{4,5},{5,4},{6,7},{7,6},{8,9},{9,8},{10,11... | collective-permute-start | bytes 663560 | tf_op jit(solution)/shard_map/ppermute | solution.py:480
  36.3 1.5 collective-permute-start.13
  43.9 11.5 %collective-permute-start.15 = (bf16[256,768]{1,0:T(8,128)(2,1)S(1)}, bf16[256,768]{1,0:T(8,128)(2,1)S(1)}, u32[]{:S(2)}, u32[]{:S(2)}) collective-permute-start(bf16[256,768]{1,0:T(8,128)(2,1)S(1)} %get-tuple-element.129.refs_2_), channel_id=1, source_target_pairs={{0,2},{1,3},{2,0},{3,1},{4,6},{5,7},{6,4},{7,5},{8,10},{9,11},{10,... | collective-permute-start | bytes 1179656 | tf_op jit(solution)/shard_map/ppermute | solution.py:480
  46.3 1.6 collective-permute-start.19
  46.4 2.0 %collective-permute-start.18 = (bf16[96,1536]{1,0:T(8,128)(2,1)S(1)}, bf16[96,1536]{1,0:T(8,128)(2,1)S(1)}, u32[]{:S(2)}, u32[]{:S(2)}) collective-permute-start(bf16[96,1536]{1,0:T(8,128)(2,1)S(1)} %get-tuple-element.224), channel_id=1, source_target_pairs={{0,1},{1,0},{2,3},{3,2},{4,5},{5,4},{6,7},{7,6},{8,9},{9,8},{10,11... | collective-permute-start | bytes 884744 | tf_op jit(solution)/shard_map/ppermute | solution.py:480
  49.9 9.9 %collective-permute-start.23 = (bf16[128,768]{1,0:T(8,128)(2,1)S(1)}, bf16[128,768]{1,0:T(8,128)(2,1)S(1)}, u32[]{:S(2)}, u32[]{:S(2)}) collective-permute-start(bf16[128,768]{1,0:T(8,128)(2,1)S(1)} %once.9), channel_id=1, source_target_pairs={{0,2},{1,18},{2,10},{3,26},{4,6},{5,22},{6,14},{7,30},{8,0},{9,16}... | collective-permute-start | bytes 589832 | tf_op jit(solution)/shard_map/ppermute | solution.py:480
  50.0 9.9 %collective-permute-start.22 = (bf16[128,768]{1,0:T(8,128)(2,1)S(1)}, bf16[128,768]{1,0:T(8,128)(2,1)S(1)}, u32[]{:S(2)}, u32[]{:S(2)}) collective-permute-start(bf16[128,768]{1,0:T(8,128)(2,1)S(1)} %once.9), channel_id=1, source_target_pairs={{0,0},{1,16},{2,8},{3,24},{4,4},{5,20},{6,12},{7,28},{8,2},{9,18},... | collective-permute-start | bytes 589832 | tf_op jit(solution)/shard_map/ppermute | solution.py:480
  57.5 9.8 %collective-permute-start.21 = (bf16[128,768]{1,0:T(8,128)(2,1)S(1)}, bf16[128,768]{1,0:T(8,128)(2,1)S(1)}, u32[]{:S(2)}, u32[]{:S(2)}) collective-permute-start(bf16[128,768]{1,0:T(8,128)(2,1)S(1)} %get-tuple-element.137), channel_id=1, source_target_pairs={{0,2},{1,3},{2,0},{3,1},{4,6},{5,7},{6,4},{7,5},{8,10},{9,11},{10,... | collective-permute-start | bytes 589832 | tf_op jit(solution)/shard_map/ppermute | solution.py:480
  59.3 12.2 %collective-permute-start.20 = (bf16[128,768]{1,0:T(8,128)(2,1)S(1)}, bf16[128,768]{1,0:T(8,128)(2,1)S(1)}, u32[]{:S(2)}, u32[]{:S(2)}) collective-permute-start(bf16[128,768]{1,0:T(8,128)(2,1)S(1)} %get-tuple-element.136.refs_7_), channel_id=1, source_target_pairs={{0,2},{1,3},{2,0},{3,1},{4,6},{5,7},{6,4},{7,5},{8,10},{9,11},{10,... | collective-permute-start | bytes 589832 | tf_op jit(solution)/shard_map/ppermute | solution.py:480
  73.2 6.5 %collective-permute-start.29 = (bf16[768,768]{1,0:T(8,128)(2,1)S(1)}, bf16[768,768]{1,0:T(8,128)(2,1)S(1)}, u32[]{:S(2)}, u32[]{:S(2)}) collective-permute-start(bf16[768,768]{1,0:T(8,128)(2,1)S(1)} %get-tuple-element.143.refs_5_), channel_id=1, source_target_pairs={{0,1},{1,0},{2,3},{3,2},{4,5},{5,4},{6,7},{7,6},{8,9},{9,8},{10,11... | collective-permute-start | bytes 3538952 | tf_op jit(solution)/shard_map/ppermute | solution.py:480
  75.1 15.5 %collective-permute-start.24 = (bf16[256,768]{1,0:T(8,128)(2,1)S(1)}, bf16[256,768]{1,0:T(8,128)(2,1)S(1)}, u32[]{:S(2)}, u32[]{:S(2)}) collective-permute-start(bf16[256,768]{1,0:T(8,128)(2,1)S(1)} %get-tuple-element.145.refs_2_), channel_id=1, source_target_pairs={{0,2},{1,3},{2,0},{3,1},{4,6},{5,7},{6,4},{7,5},{8,10},{9,11},{10,... | collective-permute-start | bytes 1179656 | tf_op jit(solution)/shard_map/ppermute | solution.py:480
  79.0 1.7 collective-permute-start.26
  79.2 2.3 %collective-permute-start.27 = (bf16[192,768]{1,0:T(8,128)(2,1)S(1)}, bf16[192,768]{1,0:T(8,128)(2,1)S(1)}, u32[]{:S(2)}, u32[]{:S(2)}) collective-permute-start(bf16[192,768]{1,0:T(8,128)(2,1)S(1)} %get-tuple-element.158), channel_id=1, source_target_pairs={{0,1},{1,0},{2,3},{3,2},{4,5},{5,4},{6,7},{7,6},{8,9},{9,8},{10,11... | collective-permute-start | bytes 884744 | tf_op jit(solution)/shard_map/ppermute | solution.py:480
  79.5 2.5 %collective-permute-start.28 = (bf16[192,768]{1,0:T(8,128)(2,1)S(1)}, bf16[192,768]{1,0:T(8,128)(2,1)S(1)}, u32[]{:S(2)}, u32[]{:S(2)}) collective-permute-start(bf16[192,768]{1,0:T(8,128)(2,1)S(1)} %get-tuple-element.159), channel_id=1, source_target_pairs={{0,1},{1,0},{2,3},{3,2},{4,5},{5,4},{6,7},{7,6},{8,9},{9,8},{10,11... | collective-permute-start | bytes 884744 | tf_op jit(solution)/shard_map/ppermute | solution.py:480
  79.7 3.9 %collective-permute-start.25 = (bf16[192,768]{1,0:T(8,128)(2,1)S(1)}, bf16[192,768]{1,0:T(8,128)(2,1)S(1)}, u32[]{:S(2)}, u32[]{:S(2)}) collective-permute-start(bf16[192,768]{1,0:T(8,128)(2,1)S(1)} %get-tuple-element.156.refs_2_), channel_id=1, source_target_pairs={{0,1},{1,0},{2,3},{3,2},{4,5},{5,4},{6,7},{7,6},{8,9},{9,8},{10,11... | collective-permute-start | bytes 884744 | tf_op jit(solution)/shard_map/ppermute | solution.py:480
  80.7 16.3 %collective-permute-start.30 = (bf16[128,768]{1,0:T(8,128)(2,1)S(1)}, bf16[128,768]{1,0:T(8,128)(2,1)S(1)}, u32[]{:S(2)}, u32[]{:S(2)}) collective-permute-start(bf16[128,768]{1,0:T(8,128)(2,1)S(1)} %get-tuple-element.170), channel_id=1, source_target_pairs={{0,0},{1,16},{2,8},{3,24},{4,4},{5,20},{6,12},{7,28},{8,2},{9,18},... | collective-permute-start | bytes 589832 | tf_op jit(solution)/shard_map/ppermute | solution.py:480
  81.6 15.1 %collective-permute-start.32 = (bf16[192,768]{1,0:T(8,128)(2,1)S(1)}, bf16[192,768]{1,0:T(8,128)(2,1)S(1)}, u32[]{:S(2)}, u32[]{:S(2)}) collective-permute-start(bf16[192,768]{1,0:T(8,128)(2,1)S(1)} %get-tuple-element.172), channel_id=1, source_target_pairs={{0,4},{1,5},{2,6},{3,7},{4,0},{5,1},{6,2},{7,3},{8,12},{9,13},{10,... | collective-permute-start | bytes 884744 | tf_op jit(solution)/shard_map/ppermute | solution.py:480
  82.0 14.7 %collective-permute-start.31 = (bf16[192,768]{1,0:T(8,128)(2,1)S(1)}, bf16[192,768]{1,0:T(8,128)(2,1)S(1)}, u32[]{:S(2)}, u32[]{:S(2)}) collective-permute-start(bf16[192,768]{1,0:T(8,128)(2,1)S(1)} %get-tuple-element.161.refs_5_), channel_id=1, source_target_pairs={{0,4},{1,5},{2,6},{3,7},{4,0},{5,1},{6,2},{7,3},{8,12},{9,13},{10,... | collective-permute-start | bytes 884744 | tf_op jit(solution)/shard_map/ppermute | solution.py:480
  84.1 20.5 %collective-permute-start.37 = (bf16[384,768]{1,0:T(8,128)(2,1)S(1)}, bf16[384,768]{1,0:T(8,128)(2,1)S(1)}, u32[]{:S(2)}, u32[]{:S(2)}) collective-permute-start(bf16[384,768]{1,0:T(8,128)(2,1)S(1)} %get-tuple-element.162.refs_13_), channel_id=1, source_target_pairs={{0,8},{1,9},{2,10},{3,11},{4,12},{5,13},{6,14},{7,15},{8,0},{9,1},... | collective-permute-start | bytes 1769480 | tf_op jit(solution)/shard_map/ppermute | solution.py:480
  99.6 4.6 %collective-permute-start.35 = (bf16[528,384]{1,0:T(8,128)(2,1)S(1)}, bf16[528,384]{1,0:T(8,128)(2,1)S(1)}, u32[]{:S(2)}, u32[]{:S(2)}) collective-permute-start(bf16[528,384]{1,0:T(8,128)(2,1)S(1)} %get-tuple-element.177), channel_id=1, source_target_pairs={{0,1},{1,0},{2,3},{3,2},{4,5},{5,4},{6,7},{7,6},{8,9},{9,8},{10,11... | collective-permute-start | bytes 1216520 | tf_op jit(solution)/shard_map/ppermute | solution.py:480
  100.9 3.2 %collective-permute-start.34 = (bf16[512,384]{1,0:T(8,128)(2,1)S(1)}, bf16[512,384]{1,0:T(8,128)(2,1)S(1)}, u32[]{:S(2)}, u32[]{:S(2)}) collective-permute-start(bf16[512,384]{1,0:T(8,128)(2,1)S(1)} %get-tuple-element.176), channel_id=1, source_target_pairs={{0,1},{1,0},{2,3},{3,2},{4,5},{5,4},{6,7},{7,6},{8,9},{9,8},{10,11... | collective-permute-start | bytes 1179656 | tf_op jit(solution)/shard_map/ppermute | solution.py:480
  100.9 3.2 %collective-permute-start.33 = (bf16[512,384]{1,0:T(8,128)(2,1)S(1)}, bf16[512,384]{1,0:T(8,128)(2,1)S(1)}, u32[]{:S(2)}, u32[]{:S(2)}) collective-permute-start(bf16[512,384]{1,0:T(8,128)(2,1)S(1)} %get-tuple-element.175.refs_4_), channel_id=1, source_target_pairs={{0,1},{1,0},{2,3},{3,2},{4,5},{5,4},{6,7},{7,6},{8,9},{9,8},{10,11... | collective-permute-start | bytes 1179656 | tf_op jit(solution)/shard_map/ppermute | solution.py:480
  101.4 10.0 %collective-permute-start.41 = (bf16[192,768]{1,0:T(8,128)(2,1)S(1)}, bf16[192,768]{1,0:T(8,128)(2,1)S(1)}, u32[]{:S(2)}, u32[]{:S(2)}) collective-permute-start(bf16[192,768]{1,0:T(8,128)(2,1)S(1)} %get-tuple-element.173.refs_10_), channel_id=1, source_target_pairs={{0,8},{1,9},{2,10},{3,11},{4,12},{5,13},{6,14},{7,15},{8,0},{9,1},... | collective-permute-start | bytes 884744 | tf_op jit(solution)/shard_map/ppermute | solution.py:480
  106.8 10.6 %collective-permute-start.40 = (bf16[256,768]{1,0:T(8,128)(2,1)S(1)}, bf16[256,768]{1,0:T(8,128)(2,1)S(1)}, u32[]{:S(2)}, u32[]{:S(2)}) collective-permute-start(bf16[256,768]{1,0:T(8,128)(2,1)S(1)} %get-tuple-element.185), channel_id=1, source_target_pairs={{0,1},{1,0},{2,3},{3,2},{4,5},{5,4},{6,7},{7,6},{8,9},{9,8},{10,11... | collective-permute-start | bytes 1179656 | tf_op jit(solution)/shard_map/ppermute | solution.py:480
  106.8 10.5 %collective-permute-start.39 = (bf16[256,768]{1,0:T(8,128)(2,1)S(1)}, bf16[256,768]{1,0:T(8,128)(2,1)S(1)}, u32[]{:S(2)}, u32[]{:S(2)}) collective-permute-start(bf16[256,768]{1,0:T(8,128)(2,1)S(1)} %get-tuple-element.184.refs_2_), channel_id=1, source_target_pairs={{0,1},{1,0},{2,3},{3,2},{4,5},{5,4},{6,7},{7,6},{8,9},{9,8},{10,11... | collective-permute-start | bytes 1179656 | tf_op jit(solution)/shard_map/ppermute | solution.py:480
  107.3 21.3 %collective-permute-start.38 = (bf16[192,768]{1,0:T(8,128)(2,1)S(1)}, bf16[192,768]{1,0:T(8,128)(2,1)S(1)}, u32[]{:S(2)}, u32[]{:S(2)}) collective-permute-start(bf16[192,768]{1,0:T(8,128)(2,1)S(1)} %get-tuple-element.182.refs_3_), channel_id=1, source_target_pairs={{0,16},{1,17},{2,18},{3,19},{4,20},{5,21},{6,22},{7,23},{8,24},{9,... | collective-permute-start | bytes 884744 | tf_op jit(solution)/shard_map/ppermute | solution.py:480
  111.4 19.9 %collective-permute-start.44 = (bf16[96,768]{1,0:T(8,128)(2,1)S(1)}, bf16[96,768]{1,0:T(8,128)(2,1)S(1)}, u32[]{:S(2)}, u32[]{:S(2)}) collective-permute-start(bf16[96,768]{1,0:T(8,128)(2,1)S(1)} %get-tuple-element.187.refs_3_), channel_id=1, source_target_pairs={{0,16},{1,17},{2,18},{3,19},{4,20},{5,21},{6,22},{7,23},{8,24},{9,... | collective-permute-start | bytes 442376 | tf_op jit(solution)/shard_map/ppermute | solution.py:480
  115.8 18.1 %collective-permute-start.36 = (bf16[784,384]{1,0:T(8,128)(2,1)S(1)}, bf16[784,384]{1,0:T(8,128)(2,1)S(1)}, u32[]{:S(2)}, u32[]{:S(2)}) collective-permute-start(bf16[784,384]{1,0:T(8,128)(2,1)S(1)} %get-tuple-element.179.refs_2_), channel_id=1, source_target_pairs={{0,4},{1,5},{2,6},{3,7},{4,0},{5,1},{6,2},{7,3},{8,12},{9,13},{10,... | collective-permute-start | bytes 1806344 | tf_op jit(solution)/shard_map/ppermute | solution.py:480
  117.9 13.5 %collective-permute-start.43 = (bf16[256,768]{1,0:T(8,128)(2,1)S(1)}, bf16[256,768]{1,0:T(8,128)(2,1)S(1)}, u32[]{:S(2)}, u32[]{:S(2)}) collective-permute-start(bf16[256,768]{1,0:T(8,128)(2,1)S(1)} %get-tuple-element.188.refs_2_), channel_id=1, source_target_pairs={{0,2},{1,3},{2,0},{3,1},{4,6},{5,7},{6,4},{7,5},{8,10},{9,11},{10,... | collective-permute-start | bytes 1179656 | tf_op jit(solution)/shard_map/ppermute | solution.py:480
  128.7 5.2 %collective-permute-start.42 = (bf16[96,768]{1,0:T(8,128)(2,1)S(1)}, bf16[96,768]{1,0:T(8,128)(2,1)S(1)}, u32[]{:S(2)}, u32[]{:S(2)}) collective-permute-start(bf16[96,768]{1,0:T(8,128)(2,1)S(1)} %get-tuple-element.190.refs_2_), channel_id=1, source_target_pairs={{0,4},{1,5},{2,6},{3,7},{4,0},{5,1},{6,2},{7,3},{8,12},{9,13},{10,... | collective-permute-start | bytes 442376 | tf_op jit(solution)/shard_map/ppermute | solution.py:480
  134.2 11.9 %collective-permute-start.45 = (bf16[400,384]{1,0:T(8,128)(2,1)S(1)}, bf16[400,384]{1,0:T(8,128)(2,1)S(1)}, u32[]{:S(2)}, u32[]{:S(2)}) collective-permute-start(bf16[400,384]{1,0:T(8,128)(2,1)S(1)} %get-tuple-element.196.refs_2_), channel_id=1, source_target_pairs={{0,8},{1,9},{2,10},{3,11},{4,12},{5,13},{6,14},{7,15},{8,0},{9,1},... | collective-permute-start | bytes 921608 | tf_op jit(solution)/shard_map/ppermute | solution.py:480
  135.7 10.2 %collective-permute-start.46 = (bf16[96,768]{1,0:T(8,128)(2,1)S(1)}, bf16[96,768]{1,0:T(8,128)(2,1)S(1)}, u32[]{:S(2)}, u32[]{:S(2)}) collective-permute-start(bf16[96,768]{1,0:T(8,128)(2,1)S(1)} %down_sum.1.refs_2_.refs_0_), channel_id=1, source_target_pairs={{0,16},{1,17},{2,18},{3,19},{4,20},{5,21},{6,22},{7,23},{8,24},{9,... | collective-permute-start | bytes 442376 | tf_op jit(solution)/shard_map/ppermute | solution.py:480
  137.6 12.0 %collective-permute-start.49 = (bf16[48,768]{1,0:T(8,128)(2,1)S(1)}, bf16[48,768]{1,0:T(8,128)(2,1)S(1)}, u32[]{:S(2)}, u32[]{:S(2)}) collective-permute-start(bf16[48,768]{1,0:T(8,128)(2,1)S(1)} %get-tuple-element.194.refs_2_), channel_id=1, source_target_pairs={{0,2},{1,3},{2,0},{3,1},{4,6},{5,7},{6,4},{7,5},{8,10},{9,11},{10,... | collective-permute-start | bytes 221192 | tf_op jit(solution)/shard_map/ppermute | solution.py:480
  139.4 23.3 %collective-permute-start.51 = (bf16[128,768]{1,0:T(8,128)(2,1)S(1)}, bf16[128,768]{1,0:T(8,128)(2,1)S(1)}, u32[]{:S(2)}, u32[]{:S(2)}) collective-permute-start(bf16[128,768]{1,0:T(8,128)(2,1)S(1)} %get-tuple-element.193.refs_2_), channel_id=1, source_target_pairs={{0,4},{1,5},{2,6},{3,7},{4,0},{5,1},{6,2},{7,3},{8,12},{9,13},{10,... | collective-permute-start | bytes 589832 | tf_op jit(solution)/shard_map/ppermute | solution.py:480
  145.9 12.2 %collective-permute-start.48 = (bf16[192,768]{1,0:T(8,128)(2,1)S(1)}, bf16[192,768]{1,0:T(8,128)(2,1)S(1)}, u32[]{:S(2)}, u32[]{:S(2)}) collective-permute-start(bf16[192,768]{1,0:T(8,128)(2,1)S(1)} %down_join.1.refs_2_.refs_0_), channel_id=1, source_target_pairs={{0,8},{1,9},{2,10},{3,11},{4,12},{5,13},{6,14},{7,15},{8,0},{9,1},... | collective-permute-start | bytes 884744 | tf_op jit(solution)/shard_map/ppermute | solution.py:480
  146.2 13.4 %collective-permute-start.47 = (bf16[208,384]{1,0:T(8,128)(2,1)S(1)}, bf16[208,384]{1,0:T(8,128)(2,1)S(1)}, u32[]{:S(2)}, u32[]{:S(2)}) collective-permute-start(bf16[208,384]{1,0:T(8,128)(2,1)S(1)} %get-tuple-element.198.refs_2_), channel_id=1, source_target_pairs={{0,16},{1,17},{2,18},{3,19},{4,20},{5,21},{6,22},{7,23},{8,24},{9,... | collective-permute-start | bytes 479240 | tf_op jit(solution)/shard_map/ppermute | solution.py:480
  149.6 13.1 %collective-permute-start.52 = (bf16[96,768]{1,0:T(8,128)(2,1)S(1)}, bf16[96,768]{1,0:T(8,128)(2,1)S(1)}, u32[]{:S(2)}, u32[]{:S(2)}) collective-permute-start(bf16[96,768]{1,0:T(8,128)(2,1)S(1)} %up_join.1.refs_2_.refs_0_), channel_id=1, source_target_pairs={{0,16},{1,17},{2,18},{3,19},{4,20},{5,21},{6,22},{7,23},{8,24},{9,... | collective-permute-start | bytes 442376 | tf_op jit(solution)/shard_map/ppermute | solution.py:480
  158.1 14.7 %collective-permute-start.56 = (bf16[384,768]{1,0:T(8,128)(2,1)S(1)}, bf16[384,768]{1,0:T(8,128)(2,1)S(1)}, u32[]{:S(2)}, u32[]{:S(2)}) collective-permute-start(bf16[384,768]{1,0:T(8,128)(2,1)S(1)} %down_join_near.1.refs_2_.refs_0_), channel_id=1, source_target_pairs={{0,4},{1,5},{2,6},{3,7},{4,0},{5,1},{6,2},{7,3},{8,12},{9,13},{10,... | collective-permute-start | bytes 1769480 | tf_op jit(solution)/shard_map/ppermute | solution.py:480
  160.3 4.5 %collective-permute-start.50 = (bf16[72,384]{1,0:T(8,128)(2,1)S(1)}, bf16[72,384]{1,0:T(8,128)(2,1)S(1)}, u32[]{:S(2)}, u32[]{:S(2)}) collective-permute-start(bf16[72,384]{1,0:T(8,128)(2,1)S(1)} %get-tuple-element.201.refs_2_), channel_id=1, source_target_pairs={{0,2},{1,3},{2,0},{3,1},{4,6},{5,7},{6,4},{7,5},{8,10},{9,11},{10,... | collective-permute-start | bytes 165896 | tf_op jit(solution)/shard_map/ppermute | solution.py:480
  164.8 7.6 %collective-permute-start.53 = (bf16[192,384]{1,0:T(8,128)(2,1)S(1)}, bf16[192,384]{1,0:T(8,128)(2,1)S(1)}, u32[]{:S(2)}, u32[]{:S(2)}) collective-permute-start(bf16[192,384]{1,0:T(8,128)(2,1)S(1)} %rest_join.1.refs_0_.refs_2_), channel_id=1, source_target_pairs={{0,16},{1,17},{2,18},{3,19},{4,20},{5,21},{6,22},{7,23},{8,24},{9,... | collective-permute-start | bytes 442376 | tf_op jit(solution)/shard_map/ppermute | solution.py:480
  164.9 10.0 %collective-permute-start.55 = (bf16[192,768]{1,0:T(8,128)(2,1)S(1)}, bf16[192,768]{1,0:T(8,128)(2,1)S(1)}, u32[]{:S(2)}, u32[]{:S(2)}) collective-permute-start(bf16[192,768]{1,0:T(8,128)(2,1)S(1)} %up_join_far.1.refs_3_.refs_0_), channel_id=1, source_target_pairs={{0,8},{1,9},{2,10},{3,11},{4,12},{5,13},{6,14},{7,15},{8,0},{9,1},... | collective-permute-start | bytes 884744 | tf_op jit(solution)/shard_map/ppermute | solution.py:480
  172.5 6.8 %collective-permute-start.54 = (bf16[384,384]{1,0:T(8,128)(2,1)S(1)}, bf16[384,384]{1,0:T(8,128)(2,1)S(1)}, u32[]{:S(2)}, u32[]{:S(2)}) collective-permute-start(bf16[384,384]{1,0:T(8,128)(2,1)S(1)} %rest_join_far.1.refs_2_.refs_0_), channel_id=1, source_target_pairs={{0,8},{1,9},{2,10},{3,11},{4,12},{5,13},{6,14},{7,15},{8,0},{9,1},... | collective-permute-start | bytes 884744 | tf_op jit(solution)/shard_map/ppermute | solution.py:480
  174.9 13.1 %collective-permute-start.59 = (bf16[384,768]{1,0:T(8,128)(2,1)S(1)}, bf16[384,768]{1,0:T(8,128)(2,1)S(1)}, u32[]{:S(2)}, u32[]{:S(2)}) collective-permute-start(bf16[384,768]{1,0:T(8,128)(2,1)S(1)} %up_join_near.1.refs_2_.refs_0_), channel_id=1, source_target_pairs={{0,4},{1,5},{2,6},{3,7},{4,0},{5,1},{6,2},{7,3},{8,12},{9,13},{10,... | collective-permute-start | bytes 1769480 | tf_op jit(solution)/shard_map/ppermute | solution.py:480
  179.3 15.1 %collective-permute-start.57 = (bf16[768,384]{1,0:T(8,128)(2,1)S(1)}, bf16[768,384]{1,0:T(8,128)(2,1)S(1)}, u32[]{:S(2)}, u32[]{:S(2)}) collective-permute-start(bf16[768,384]{1,0:T(8,128)(2,1)S(1)} %rest_join_near.1.refs_2_.refs_0_), channel_id=1, source_target_pairs={{0,4},{1,5},{2,6},{3,7},{4,0},{5,1},{6,2},{7,3},{8,12},{9,13},{10,... | collective-permute-start | bytes 1769480 | tf_op jit(solution)/shard_map/ppermute | solution.py:480
  179.6 10.1 %collective-permute-start.58 = (bf16[128,768]{1,0:T(8,128)(2,1)S(1)}, bf16[128,768]{1,0:T(8,128)(2,1)S(1)}, u32[]{:S(2)}, u32[]{:S(2)}) collective-permute-start(bf16[128,768]{1,0:T(8,128)(2,1)S(1)} %input_sum.1.refs_2_), channel_id=1, source_target_pairs={{0,0},{1,16},{2,8},{3,24},{4,4},{5,20},{6,12},{7,28},{8,2},{9,18},... | collective-permute-start | bytes 589832 | tf_op jit(solution)/shard_map/ppermute | solution.py:480

commit v8 on v7

--- a/solution.py
+++ b/solution.py
@@ -712,7 +712,7 @@
         lse_out[pl.ds(h, 1), :] = top + jnp.log(total)
         return carry
 
-    lax.fori_loop(0, 2 * pairs, head, 0, unroll=3)
+    lax.fori_loop(0, 2 * pairs, head, 0, unroll=6)
     mixed = jnp.transpose(ot[...].reshape(half, 2 * rows)).astype(jnp.bfloat16)
     o_out[...] = mixed
     ins.wait()
@@ -863,7 +863,7 @@
         dqt[h] = dot(kt[h], d_scores)
         return carry
 
-    lax.fori_loop(0, 2 * pairs, head, 0, unroll=3)
+    lax.fori_loop(0, 2 * pairs, head, 0, unroll=6)
     dq = (jnp.transpose(dqt[...].reshape(half, 2 * rows)) * 0.125).astype(jnp.bfloat16)
     dq_out[...] = dq
     qv_sums[...] = jnp.zeros_like(qv_sums)

time: 196 us -> 197 us (level)
  waiting for transfers between devices: 82.3 us -> 84.6 us
    ppermute x60, waiting for transfers between devices: 82.3 us -> 84.6 us  [moved(): lax.ppermute(block, AXES, [(number(s), number(move(*s))) for s in spots])]
  transfers between devices with their start and end apart: 60 -> 60, of which waited for: 23 -> 24; matrix products, arithmetic and copies ran while one was open for 0% -> 0% of each run, Pallas kernels for 18% -> 18%
where the time goes in v8:
time: 197 us; the launch traced here: 196 us
  waiting for transfers between devices  84.6 us (43%)
  starting transfers between devices  69.9 us (35%)
  Pallas kernels  40.6 us (21%)
    ppermute x60, waiting for transfers between devices, moved(): lax.ppermute(block, AXES, [(number(s), number(move(*s))) for s in spots])  84.6 us
    ppermute x60, starting transfers between devices, moved(): lax.ppermute(block, AXES, [(number(s), number(move(*s))) for s in spots])  69.9 us
    pallas_call x42, Pallas kernels, kernel_call(): pl.pallas_call(run, name=name, out_shape=[jax.ShapeDtypeStruct(shape, dty...  40.6 us
  transfers between devices with their start and end apart: 60, of which 24 were waited for; matrix products, arithmetic and copies ran while one was open for 0% of the time, Pallas kernels for 18%

profile of v8, /device:TPU:0, one launch (start us, length us, event | category | flops | bytes accessed | tf_op | source)
XLA Modules:
  0.0 196.3 jit_solution(14626536233609088692)
XLA Ops:
  0.7 1.0 block.1.refs_12_
  1.6 1.5 pack.1
  3.8 2.9 %collective-permute-start.8 = (bf16[304,384]{1,0:T(8,128)(2,1)S(1)}, bf16[304,384]{1,0:T(8,128)(2,1)S(1)}, u32[]{:S(2)}, u32[]{:S(2)}) collective-permute-start(bf16[304,384]{1,0:T(8,128)(2,1)S(1)} %get-tuple-element.121.refs_2_), channel_id=1, source_target_pairs={{0,2},{1,3},{2,0},{3,1},{4,6},{5,7},{6,4},{7,5},{8,10},{9,11},{10,... | collective-permute-start | bytes 700424 | tf_op jit(solution)/shard_map/ppermute | solution.py:480
  7.3 5.6 %collective-permute-done.8.refs_8_ = bf16[304,384]{1,0:T(8,128)(2,1)S(1)} collective-permute-done((bf16[304,384]{1,0:T(8,128)(2,1)S(1)}, bf16[304,384]{1,0:T(8,128)(2,1)S(1)}, u32[]{:S(2)}, u32[]{:S(2)}) %collective-permute-start.8) | collective-permute-done | bytes 233504 | tf_op jit(solution)/shard_map/ppermute | solution.py:480
  13.0 1.4 collective-permute-start.9
  15.1 7.2 %collective-permute-start.3 = (bf16[144,768]{1,0:T(8,128)(2,1)S(1)}, bf16[144,768]{1,0:T(8,128)(2,1)S(1)}, u32[]{:S(2)}, u32[]{:S(2)}) collective-permute-start(bf16[144,768]{1,0:T(8,128)(2,1)S(1)} %once.5.refs_0_), channel_id=1, source_target_pairs={{0,2},{1,3},{2,0},{3,1},{4,6},{5,7},{6,4},{7,5},{8,10},{9,11},{10,... | collective-permute-start | bytes 663560 | tf_op jit(solution)/shard_map/ppermute | solution.py:480
  22.8 1.7 collective-permute-done.4.refs_1_.refs_4_
  24.5 1.7 collective-permute-done.3.refs_0_
  26.7 1.3 cut.1
  27.9 0.9 cotangent.1.refs_13_.refs_0_
  29.2 2.0 collective-permute-start.16
  31.7 2.3 %project.1 = (bf16[512,768]{1,0:T(8,128)(2,1)S(1)}, bf16[256,384]{1,0:T(8,128)(2,1)S(1)}, bf16[768,1152]{1,0:T(8,128)(2,1)S(1)}, f32[8,768]{1,0:T(8,128)S(1)}, f32[4,8,384]{2,1,0:T(8,128)S(1)}) custom-call(bf16[144,768]{1,0:T(8,128)(2,1)S(1)} %once.5.refs_0_, bf16[144,768]{1,0:T(8,128)(2,1)S(1)} %once.6.refs_1_, ...), custom_call_target="tpu_custom_call" | custom-call | flops 10000000000 | bytes 1 | tf_op jit(solution)/shard_map/project/pallas_call | solution.py:1140
  34.0 2.3 %collective-permute-done.7.refs_0_ = bf16[144,768]{1,0:T(8,128)(2,1)S(1)} collective-permute-done((bf16[144,768]{1,0:T(8,128)(2,1)S(1)}, bf16[144,768]{1,0:T(8,128)(2,1)S(1)}, u32[]{:S(2)}, u32[]{:S(2)}) %collective-permute-start.7) | collective-permute-done | bytes 221216 | tf_op jit(solution)/shard_map/ppermute | solution.py:480
  36.3 1.5 collective-permute-done.13.refs_7_
  37.8 6.6 %attend.1 = (bf16[256,768]{1,0:T(8,128)(2,1)S(1)}, bf16[1024,768]{1,0:T(8,128)(2,1)S(1)}, bf16[384,768]{1,0:T(8,128)(2,1)S(1)}, bf16[3,1024,128]{2,1,0:T(8,128)(...) custom-call(bf16[144,768]{1,0:T(8,128)(2,1)S(1)} %once.5.refs_0_, ...), custom_call_target="tpu_custom_call" | custom-call | flops 1 | bytes 1 | tf_op jit(solution)/shard_map/attend/pallas_call | solution.py:1140
  44.4 2.1 %collective-permute-start.15 = (bf16[256,768]{1,0:T(8,128)(2,1)S(1)}, bf16[256,768]{1,0:T(8,128)(2,1)S(1)}, u32[]{:S(2)}, u32[]{:S(2)}) collective-permute-start(bf16[256,768]{1,0:T(8,128)(2,1)S(1)} %get-tuple-element.129.refs_2_), channel_id=1, source_target_pairs={{0,2},{1,3},{2,0},{3,1},{4,6},{5,7},{6,4},{7,5},{8,10},{9,11},{10,... | collective-permute-start | bytes 1179656 | tf_op jit(solution)/shard_map/ppermute | solution.py:480
  47.4 1.1 collective-permute-done.19.refs_4_
  48.9 1.5 inner.1
  50.4 0.8 collective-permute-start.22
  51.3 4.6 %collective-permute-done.15.refs_1_ = bf16[256,768]{1,0:T(8,128)(2,1)S(1)} collective-permute-done((bf16[256,768]{1,0:T(8,128)(2,1)S(1)}, bf16[256,768]{1,0:T(8,128)(2,1)S(1)}, u32[]{:S(2)}, u32[]{:S(2)}) %collective-permute-start.15) | collective-permute-done | bytes 393248 | tf_op jit(solution)/shard_map/ppermute | solution.py:480
  55.9 2.0 %feedforward.1 = (bf16[128,768]{1,0:T(8,128)(2,1)S(1)}, bf16[128,768]{1,0:T(8,128)(2,1)S(1)}, bf16[256,768]{1,0:T(8,128)(2,1)S(1)}, bf16[256,1536]{1,0:T(8,128)(...) custom-call(f32[256,768]{1,0:T(8,128)S(1)} %get-tuple-element.128.re, ...), custom_call_target="tpu_custom_call" | custom-call | flops 1 | bytes 1 | tf_op jit(solution)/shard_map/feedforward/pallas_call | solution.py:1140
  57.9 1.8 collective-permute-start.21
  60.3 7.4 %collective-permute-done.21.refs_2_ = bf16[128,768]{1,0:T(8,128)(2,1)S(1)} collective-permute-done((bf16[128,768]{1,0:T(8,128)(2,1)S(1)}, bf16[128,768]{1,0:T(8,128)(2,1)S(1)}, u32[]{:S(2)}, u32[]{:S(2)}) %collective-permute-start.21) | collective-permute-done | bytes 196640 | tf_op jit(solution)/shard_map/ppermute | solution.py:480
  67.7 4.2 %collective-permute-done.20.refs_1_ = bf16[128,768]{1,0:T(8,128)(2,1)S(1)} collective-permute-done((bf16[128,768]{1,0:T(8,128)(2,1)S(1)}, bf16[128,768]{1,0:T(8,128)(2,1)S(1)}, u32[]{:S(2)}, u32[]{:S(2)}) %collective-permute-start.20) | collective-permute-done | bytes 196640 | tf_op jit(solution)/shard_map/ppermute | solution.py:480
  71.9 0.9 norm_back.1
  73.9 1.7 feedforward_back.1
  75.6 2.5 %collective-permute-start.24 = (bf16[256,768]{1,0:T(8,128)(2,1)S(1)}, bf16[256,768]{1,0:T(8,128)(2,1)S(1)}, u32[]{:S(2)}, u32[]{:S(2)}) collective-permute-start(bf16[256,768]{1,0:T(8,128)(2,1)S(1)} %get-tuple-element.145.refs_2_), channel_id=1, source_target_pairs={{0,2},{1,3},{2,0},{3,1},{4,6},{5,7},{6,4},{7,5},{8,10},{9,11},{10,... | collective-permute-start | bytes 1179656 | tf_op jit(solution)/shard_map/ppermute | solution.py:480
  78.1 1.3 up_grad.1
  81.1 0.9 collective-permute-start.30
  82.4 1.7 collective-permute-start.31
  84.6 2.8 %collective-permute-start.37 = (bf16[384,768]{1,0:T(8,128)(2,1)S(1)}, bf16[384,768]{1,0:T(8,128)(2,1)S(1)}, u32[]{:S(2)}, u32[]{:S(2)}) collective-permute-start(bf16[384,768]{1,0:T(8,128)(2,1)S(1)} %get-tuple-element.162.refs_13_), channel_id=1, source_target_pairs={{0,8},{1,9},{2,10},{3,11},{4,12},{5,13},{6,14},{7,15},{8,0},{9,1},... | collective-permute-start | bytes 1769480 | tf_op jit(solution)/shard_map/ppermute | solution.py:480
  87.4 3.7 %collective-permute-done.24.refs_1_ = bf16[256,768]{1,0:T(8,128)(2,1)S(1)} collective-permute-done((bf16[256,768]{1,0:T(8,128)(2,1)S(1)}, bf16[256,768]{1,0:T(8,128)(2,1)S(1)}, u32[]{:S(2)}, u32[]{:S(2)}) %collective-permute-start.24) | collective-permute-done | bytes 393248 | tf_op jit(solution)/shard_map/ppermute | solution.py:480
  91.0 5.1 %attend_back.1 = (bf16[1024,768]{1,0:T(8,128)(2,1)S(1)}, bf16[256,384]{1,0:T(8,128)(2,1)S(1)}, f32[128,768]{1,0:T(8,128)S(1)}, bf16[256,768]{1,0:T(8,128)(2,1)S(...) custom-call(f32[256,768]{1,0:T(8,128)S(1)} %get-tuple-element.144.refs_0_, ...), custom_call_target="tpu_custom_call" | custom-call | flops 10000000000 | bytes 1 | tf_op jit(solution)/shard_map/attend_back/pallas_call | solution.py:1140
  96.4 2.6 %weight_grad.1 = (bf16[512,384]{1,0:T(8,128)(2,1)S(1)}, bf16[512,384]{1,0:T(8,128)(2,1)S(1)}, bf16[528,384]{1,0:T(8,128)(2,1)S(1)}, f32[1552,384]{1,0:T(8,128)S(1)}) custom-call(bf16[1024,768]{1,0:T(8,128)(2,1)S(1)} %get-tuple-element.127.refs_2_.refs_0_, bf16[1024,768]{1,0:T(8,128)(2,1)S(1)} %get-tuple-element.163.refs_3_.refs_1_, ...), custom_call_target="tpu_custom_call" | custom-call | flops 1 | bytes 1 | tf_op jit(solution)/shard_map/weight_grad/pallas_call | solution.py:1140
  99.0 2.3 %collective-permute-start.35 = (bf16[528,384]{1,0:T(8,128)(2,1)S(1)}, bf16[528,384]{1,0:T(8,128)(2,1)S(1)}, u32[]{:S(2)}, u32[]{:S(2)}) collective-permute-start(bf16[528,384]{1,0:T(8,128)(2,1)S(1)} %get-tuple-element.177), channel_id=1, source_target_pairs={{0,1},{1,0},{2,3},{3,2},{4,5},{5,4},{6,7},{7,6},{8,9},{9,8},{10,11... | collective-permute-start | bytes 1216520 | tf_op jit(solution)/shard_map/ppermute | solution.py:480
  101.8 2.7 %collective-permute-start.41 = (bf16[192,768]{1,0:T(8,128)(2,1)S(1)}, bf16[192,768]{1,0:T(8,128)(2,1)S(1)}, u32[]{:S(2)}, u32[]{:S(2)}) collective-permute-start(bf16[192,768]{1,0:T(8,128)(2,1)S(1)} %get-tuple-element.173.refs_10_), channel_id=1, source_target_pairs={{0,8},{1,9},{2,10},{3,11},{4,12},{5,13},{6,14},{7,15},{8,0},{9,1},... | collective-permute-start | bytes 884744 | tf_op jit(solution)/shard_map/ppermute | solution.py:480
  105.2 2.1 %input_grad.1 = (bf16[256,768]{1,0:T(8,128)(2,1)S(1)}, bf16[256,768]{1,0:T(8,128)(2,1)S(1)}, f32[512,768]{1,0:T(8,128)S(1)}) custom-call(bf16[256,384]{1,0:T(8,128)(2,1)S(1)} %get-tuple-element.164.refs_2_.refs_0_, bf16[1024,768]{1,0:T(8,128)(2,1)S(1)} %get-tuple-element.163.refs_3_.refs_1_, bf16[768,1152]{1,0:T(8,128)(2,1)S(1)} %get-tuple-element.125.refs_10_.refs_2_, ...), custom_call_target="tpu_custom_call" | custom-call | flops 1 | bytes 1 | tf_op jit(solution)/shard_map/input_grad/pallas_call | solution.py:1140
  107.8 4.0 %collective-permute-start.38 = (bf16[192,768]{1,0:T(8,128)(2,1)S(1)}, bf16[192,768]{1,0:T(8,128)(2,1)S(1)}, u32[]{:S(2)}, u32[]{:S(2)}) collective-permute-start(bf16[192,768]{1,0:T(8,128)(2,1)S(1)} %get-tuple-element.182.refs_3_), channel_id=1, source_target_pairs={{0,16},{1,17},{2,18},{3,19},{4,20},{5,21},{6,22},{7,23},{8,24},{9,... | collective-permute-start | bytes 884744 | tf_op jit(solution)/shard_map/ppermute | solution.py:480
  111.9 4.4 %collective-permute-start.44 = (bf16[96,768]{1,0:T(8,128)(2,1)S(1)}, bf16[96,768]{1,0:T(8,128)(2,1)S(1)}, u32[]{:S(2)}, u32[]{:S(2)}) collective-permute-start(bf16[96,768]{1,0:T(8,128)(2,1)S(1)} %get-tuple-element.187.refs_3_), channel_id=1, source_target_pairs={{0,16},{1,17},{2,18},{3,19},{4,20},{5,21},{6,22},{7,23},{8,24},{9,... | collective-permute-start | bytes 442376 | tf_op jit(solution)/shard_map/ppermute | solution.py:480
  116.3 1.5 collective-permute-start.36
  118.3 1.6 collective-permute-start.43
  120.0 9.1 %collective-permute-done.38 = bf16[192,768]{1,0:T(8,128)(2,1)S(1)} collective-permute-done((bf16[192,768]{1,0:T(8,128)(2,1)S(1)}, bf16[192,768]{1,0:T(8,128)(2,1)S(1)}, u32[]{:S(2)}, u32[]{:S(2)}) %collective-permute-start.38) | collective-permute-done | bytes 294944 | tf_op jit(solution)/shard_map/ppermute | solution.py:480
  129.2 1.6 collective-permute-start.42
  130.7 1.0 collective-permute-done.44.refs_1_
  131.9 2.5 %collective-permute-done.42 = bf16[96,768]{1,0:T(8,128)(2,1)S(1)} collective-permute-done((bf16[96,768]{1,0:T(8,128)(2,1)S(1)}, bf16[96,768]{1,0:T(8,128)(2,1)S(1)}, u32[]{:S(2)}, u32[]{:S(2)}) %collective-permute-start.42) | collective-permute-done | bytes 147488 | tf_op jit(solution)/shard_map/ppermute | solution.py:480
  134.6 1.5 collective-permute-start.45
  136.2 1.8 collective-permute-start.46
  138.0 1.0 collective-permute-start.49
  139.0 1.5 collective-permute-start.51
  140.6 5.8 %collective-permute-done.46.refs_1_ = bf16[96,768]{1,0:T(8,128)(2,1)S(1)} collective-permute-done((bf16[96,768]{1,0:T(8,128)(2,1)S(1)}, bf16[96,768]{1,0:T(8,128)(2,1)S(1)}, u32[]{:S(2)}, u32[]{:S(2)}) %collective-permute-start.46) | collective-permute-done | bytes 147488 | tf_op jit(solution)/shard_map/ppermute | solution.py:480
  146.7 3.4 %collective-permute-start.47 = (bf16[208,384]{1,0:T(8,128)(2,1)S(1)}, bf16[208,384]{1,0:T(8,128)(2,1)S(1)}, u32[]{:S(2)}, u32[]{:S(2)}) collective-permute-start(bf16[208,384]{1,0:T(8,128)(2,1)S(1)} %get-tuple-element.198.refs_2_), channel_id=1, source_target_pairs={{0,16},{1,17},{2,18},{3,19},{4,20},{5,21},{6,22},{7,23},{8,24},{9,... | collective-permute-start | bytes 479240 | tf_op jit(solution)/shard_map/ppermute | solution.py:480
  150.1 8.4 %collective-permute-done.48.refs_1_ = bf16[192,768]{1,0:T(8,128)(2,1)S(1)} collective-permute-done((bf16[192,768]{1,0:T(8,128)(2,1)S(1)}, bf16[192,768]{1,0:T(8,128)(2,1)S(1)}, u32[]{:S(2)}, u32[]{:S(2)}) %collective-permute-start.48) | collective-permute-done | bytes 294944 | tf_op jit(solution)/shard_map/ppermute | solution.py:480
  158.6 1.5 collective-permute-start.56
  160.8 1.6 collective-permute-start.50
  163.1 1.8 collective-permute-done.50.refs_1_
  165.0 3.2 %collective-permute-start.55 = (bf16[192,768]{1,0:T(8,128)(2,1)S(1)}, bf16[192,768]{1,0:T(8,128)(2,1)S(1)}, u32[]{:S(2)}, u32[]{:S(2)}) collective-permute-start(bf16[192,768]{1,0:T(8,128)(2,1)S(1)} %up_join_far.1.refs_3_.refs_0_), channel_id=1, source_target_pairs={{0,8},{1,9},{2,10},{3,11},{4,12},{5,13},{6,14},{7,15},{8,0},{9,1},... | collective-permute-start | bytes 884744 | tf_op jit(solution)/shard_map/ppermute | solution.py:480
  168.2 4.4 %collective-permute-done.53.refs_1_ = bf16[192,384]{1,0:T(8,128)(2,1)S(1)} collective-permute-done((bf16[192,384]{1,0:T(8,128)(2,1)S(1)}, bf16[192,384]{1,0:T(8,128)(2,1)S(1)}, u32[]{:S(2)}, u32[]{:S(2)}) %collective-permute-start.53) | collective-permute-done | bytes 147488 | tf_op jit(solution)/shard_map/ppermute | solution.py:480
  173.0 1.6 down_out.1
  175.1 1.2 collective-permute-start.59
  176.2 3.2 %collective-permute-done.54.refs_1_ = bf16[384,384]{1,0:T(8,128)(2,1)S(1)} collective-permute-done((bf16[384,384]{1,0:T(8,128)(2,1)S(1)}, bf16[384,384]{1,0:T(8,128)(2,1)S(1)}, u32[]{:S(2)}, u32[]{:S(2)}) %collective-permute-start.54) | collective-permute-done | bytes 294944 | tf_op jit(solution)/shard_map/ppermute | solution.py:480
  180.3 7.9 %collective-permute-done.59.refs_1_ = bf16[384,768]{1,0:T(8,128)(2,1)S(1)} collective-permute-done((bf16[384,768]{1,0:T(8,128)(2,1)S(1)}, bf16[384,768]{1,0:T(8,128)(2,1)S(1)}, u32[]{:S(2)}, u32[]{:S(2)}) %collective-permute-start.59) | collective-permute-done | bytes 589856 | tf_op jit(solution)/shard_map/ppermute | solution.py:480
  188.2 1.6 up_out.1
  189.8 4.7 %collective-permute-done.57.refs_1_ = bf16[768,384]{1,0:T(8,128)(2,1)S(1)} collective-permute-done((bf16[768,384]{1,0:T(8,128)(2,1)S(1)}, bf16[768,384]{1,0:T(8,128)(2,1)S(1)}, u32[]{:S(2)}, u32[]{:S(2)}) %collective-permute-start.57) | collective-permute-done | bytes 589856 | tf_op jit(solution)/shard_map/ppermute | solution.py:480
  194.5 1.7 rest_out.1
  (106 shorter events, 16.1 us)
Async XLA Ops:
  1.6 24.6 %copy-start = (bf16[768,768]{1,0:T(8,128)(2,1)S(1)}, bf16[768,768]{1,0:T(8,128)(2,1)}, u32[]{:S(2)}) copy-start(bf16[768,768]{1,0:T(8,128)(2,1)} %refs_5_.5) | copy-start | bytes 3538948
  3.2 11.2 %collective-permute-start.1 = (bf16[592,384]{1,0:T(8,128)(2,1)S(1)}, bf16[592,384]{1,0:T(8,128)(2,1)S(1)}, u32[]{:S(2)}, u32[]{:S(2)}) collective-permute-start(bf16[592,384]{1,0:T(8,128)(2,1)S(1)} %get-tuple-element.120.refs_12_), channel_id=1, source_target_pairs={{0,1},{1,0},{2,3},{3,2},{4,5},{5,4},{6,7},{7,6},{8,9},{9,8},{10,11... | collective-permute-start | bytes 1363976 | tf_op jit(solution)/shard_map/ppermute | solution.py:480
  3.7 10.7 %collective-permute-start.2 = (bf16[192,768]{1,0:T(8,128)(2,1)}, bf16[192,768]{1,0:T(8,128)(2,1)S(1)}, u32[]{:S(2)}, u32[]{:S(2)}) collective-permute-start(bf16[192,768]{1,0:T(8,128)(2,1)} %refs_12_.1), channel_id=1, source_target_pairs={{0,1},{1,0},{2,3},{3,2},{4,5},{5,4},{6,7},{7,6},{8,9},{9,8},{10,11... | collective-permute-start | bytes 884744 | tf_op jit(solution)/shard_map/ppermute | solution.py:480
  3.8 9.2 %collective-permute-start.8 = (bf16[304,384]{1,0:T(8,128)(2,1)S(1)}, bf16[304,384]{1,0:T(8,128)(2,1)S(1)}, u32[]{:S(2)}, u32[]{:S(2)}) collective-permute-start(bf16[304,384]{1,0:T(8,128)(2,1)S(1)} %get-tuple-element.121.refs_2_), channel_id=1, source_target_pairs={{0,2},{1,3},{2,0},{3,1},{4,6},{5,7},{6,4},{7,5},{8,10},{9,11},{10,... | collective-permute-start | bytes 700424 | tf_op jit(solution)/shard_map/ppermute | solution.py:480
  6.7 7.7 %collective-permute-start = (bf16[144,768]{1,0:T(8,128)(2,1)S(1)}, bf16[144,768]{1,0:T(8,128)(2,1)S(1)}, u32[]{:S(2)}, u32[]{:S(2)}) collective-permute-start(bf16[144,768]{1,0:T(8,128)(2,1)S(1)} %block.1.refs_12_), channel_id=1, source_target_pairs={{0,0},{1,16},{2,8},{3,24},{4,4},{5,20},{6,12},{7,28},{8,2},{9,18},... | collective-permute-start | bytes 663560 | tf_op jit(solution)/shard_map/ppermute | solution.py:480
  13.0 9.3 %collective-permute-start.9 = (bf16[304,384]{1,0:T(8,128)(2,1)S(1)}, bf16[304,384]{1,0:T(8,128)(2,1)S(1)}, u32[]{:S(2)}, u32[]{:S(2)}) collective-permute-start(bf16[304,384]{1,0:T(8,128)(2,1)S(1)} %collective-permute-done.8.refs_8_), channel_id=1, source_target_pairs={{0,4},{1,5},{2,6},{3,7},{4,0},{5,1},{6,2},{7,3},{8,12},{9,13},{10,... | collective-permute-start | bytes 700424 | tf_op jit(solution)/shard_map/ppermute | solution.py:480
  14.4 10.1 %collective-permute-start.4 = (bf16[144,768]{1,0:T(8,128)(2,1)S(1)}, bf16[144,768]{1,0:T(8,128)(2,1)S(1)}, u32[]{:S(2)}, u32[]{:S(2)}) collective-permute-start(bf16[144,768]{1,0:T(8,128)(2,1)S(1)} %once.5.refs_0_), channel_id=1, source_target_pairs={{0,4},{1,5},{2,6},{3,7},{4,0},{5,1},{6,2},{7,3},{8,12},{9,13},{10,... | collective-permute-start | bytes 663560 | tf_op jit(solution)/shard_map/ppermute | solution.py:480
  15.1 11.1 %collective-permute-start.3 = (bf16[144,768]{1,0:T(8,128)(2,1)S(1)}, bf16[144,768]{1,0:T(8,128)(2,1)S(1)}, u32[]{:S(2)}, u32[]{:S(2)}) collective-permute-start(bf16[144,768]{1,0:T(8,128)(2,1)S(1)} %once.5.refs_0_), channel_id=1, source_target_pairs={{0,2},{1,3},{2,0},{3,1},{4,6},{5,7},{6,4},{7,5},{8,10},{9,11},{10,... | collective-permute-start | bytes 663560 | tf_op jit(solution)/shard_map/ppermute | solution.py:480
  22.3 6.6 %collective-permute-start.10 = (bf16[304,384]{1,0:T(8,128)(2,1)S(1)}, bf16[304,384]{1,0:T(8,128)(2,1)S(1)}, u32[]{:S(2)}, u32[]{:S(2)}) collective-permute-start(bf16[304,384]{1,0:T(8,128)(2,1)S(1)} %collective-permute-done.8.refs_8_), channel_id=1, source_target_pairs={{0,1},{1,0},{2,3},{3,2},{4,5},{5,4},{6,7},{7,6},{8,9},{9,8},{10,11... | collective-permute-start | bytes 700424 | tf_op jit(solution)/shard_map/ppermute | solution.py:480
  22.3 8.9 %collective-permute-start.11 = (bf16[304,384]{1,0:T(8,128)(2,1)S(1)}, bf16[304,384]{1,0:T(8,128)(2,1)S(1)}, u32[]{:S(2)}, u32[]{:S(2)}) collective-permute-start(bf16[304,384]{1,0:T(8,128)(2,1)S(1)} %collective-permute-done.9.refs_9_), channel_id=1, source_target_pairs={{0,1},{1,0},{2,3},{3,2},{4,5},{5,4},{6,7},{7,6},{8,9},{9,8},{10,11... | collective-permute-start | bytes 700424 | tf_op jit(solution)/shard_map/ppermute | solution.py:480
  22.8 6.4 %collective-permute-start.5 = (bf16[144,768]{1,0:T(8,128)(2,1)S(1)}, bf16[144,768]{1,0:T(8,128)(2,1)S(1)}, u32[]{:S(2)}, u32[]{:S(2)}) collective-permute-start(bf16[144,768]{1,0:T(8,128)(2,1)S(1)} %once.5.refs_0_), channel_id=1, source_target_pairs={{0,1},{1,0},{2,3},{3,2},{4,5},{5,4},{6,7},{7,6},{8,9},{9,8},{10,11... | collective-permute-start | bytes 663560 | tf_op jit(solution)/shard_map/ppermute | solution.py:480
  26.2 5.0 %collective-permute-start.6 = (bf16[144,768]{1,0:T(8,128)(2,1)S(1)}, bf16[144,768]{1,0:T(8,128)(2,1)S(1)}, u32[]{:S(2)}, u32[]{:S(2)}) collective-permute-start(bf16[144,768]{1,0:T(8,128)(2,1)S(1)} %once.6.refs_1_), channel_id=1, source_target_pairs={{0,1},{1,0},{2,3},{3,2},{4,5},{5,4},{6,7},{7,6},{8,9},{9,8},{10,11... | collective-permute-start | bytes 663560 | tf_op jit(solution)/shard_map/ppermute | solution.py:480
  26.2 11.6 %collective-permute-start.14 = (bf16[768,768]{1,0:T(8,128)(2,1)S(1)}, bf16[768,768]{1,0:T(8,128)(2,1)S(1)}, u32[]{:S(2)}, u32[]{:S(2)}) collective-permute-start(bf16[768,768]{1,0:T(8,128)(2,1)S(1)} %copy-done), channel_id=1, source_target_pairs={{0,1},{1,0},{2,3},{3,2},{4,5},{5,4},{6,7},{7,6},{8,9},{9,8},{10,11... | collective-permute-start | bytes 3538952 | tf_op jit(solution)/shard_map/ppermute | solution.py:480
  28.9 7.4 %collective-permute-start.7 = (bf16[144,768]{1,0:T(8,128)(2,1)S(1)}, bf16[144,768]{1,0:T(8,128)(2,1)S(1)}, u32[]{:S(2)}, u32[]{:S(2)}) collective-permute-start(bf16[144,768]{1,0:T(8,128)(2,1)S(1)} %once.6.refs_1_), channel_id=1, source_target_pairs={{0,4},{1,5},{2,6},{3,7},{4,0},{5,1},{6,2},{7,3},{8,12},{9,13},{10,... | collective-permute-start | bytes 663560 | tf_op jit(solution)/shard_map/ppermute | solution.py:480
  29.2 17.5 %collective-permute-start.16 = (bf16[192,1536]{1,0:T(8,128)(2,1)S(1)}, bf16[192,1536]{1,0:T(8,128)(2,1)S(1)}, u32[]{:S(2)}, u32[]{:S(2)}) collective-permute-start(bf16[192,1536]{1,0:T(8,128)(2,1)S(1)} %get-tuple-element.122.refs_1_), channel_id=1, source_target_pairs={{0,2},{1,3},{2,0},{3,1},{4,6},{5,7},{6,4},{7,5},{8,10},{9,11},{10,... | collective-permute-start | bytes 1769480 | tf_op jit(solution)/shard_map/ppermute | solution.py:480
  31.1 15.3 %collective-permute-start.17 = (bf16[192,1536]{1,0:T(8,128)(2,1)S(1)}, bf16[192,1536]{1,0:T(8,128)(2,1)S(1)}, u32[]{:S(2)}, u32[]{:S(2)}) collective-permute-start(bf16[192,1536]{1,0:T(8,128)(2,1)S(1)} %get-tuple-element.132), channel_id=1, source_target_pairs={{0,1},{1,0},{2,3},{3,2},{4,5},{5,4},{6,7},{7,6},{8,9},{9,8},{10,11... | collective-permute-start | bytes 1769480 | tf_op jit(solution)/shard_map/ppermute | solution.py:480
  31.1 5.2 %collective-permute-start.12 = (bf16[144,768]{1,0:T(8,128)(2,1)S(1)}, bf16[144,768]{1,0:T(8,128)(2,1)S(1)}, u32[]{:S(2)}, u32[]{:S(2)}) collective-permute-start(bf16[144,768]{1,0:T(8,128)(2,1)S(1)} %collective-permute-done.4.refs_1_.refs_4_), channel_id=1, source_target_pairs={{0,1},{1,0},{2,3},{3,2},{4,5},{5,4},{6,7},{7,6},{8,9},{9,8},{10,11... | collective-permute-start | bytes 663560 | tf_op jit(solution)/shard_map/ppermute | solution.py:480
  36.3 1.5 collective-permute-start.13
  44.4 11.5 %collective-permute-start.15 = (bf16[256,768]{1,0:T(8,128)(2,1)S(1)}, bf16[256,768]{1,0:T(8,128)(2,1)S(1)}, u32[]{:S(2)}, u32[]{:S(2)}) collective-permute-start(bf16[256,768]{1,0:T(8,128)(2,1)S(1)} %get-tuple-element.129.refs_2_), channel_id=1, source_target_pairs={{0,2},{1,3},{2,0},{3,1},{4,6},{5,7},{6,4},{7,5},{8,10},{9,11},{10,... | collective-permute-start | bytes 1179656 | tf_op jit(solution)/shard_map/ppermute | solution.py:480
  46.8 1.6 collective-permute-start.19
  46.9 2.0 %collective-permute-start.18 = (bf16[96,1536]{1,0:T(8,128)(2,1)S(1)}, bf16[96,1536]{1,0:T(8,128)(2,1)S(1)}, u32[]{:S(2)}, u32[]{:S(2)}) collective-permute-start(bf16[96,1536]{1,0:T(8,128)(2,1)S(1)} %get-tuple-element.224), channel_id=1, source_target_pairs={{0,1},{1,0},{2,3},{3,2},{4,5},{5,4},{6,7},{7,6},{8,9},{9,8},{10,11... | collective-permute-start | bytes 884744 | tf_op jit(solution)/shard_map/ppermute | solution.py:480
  50.4 9.9 %collective-permute-start.23 = (bf16[128,768]{1,0:T(8,128)(2,1)S(1)}, bf16[128,768]{1,0:T(8,128)(2,1)S(1)}, u32[]{:S(2)}, u32[]{:S(2)}) collective-permute-start(bf16[128,768]{1,0:T(8,128)(2,1)S(1)} %once.9), channel_id=1, source_target_pairs={{0,2},{1,18},{2,10},{3,26},{4,6},{5,22},{6,14},{7,30},{8,0},{9,16}... | collective-permute-start | bytes 589832 | tf_op jit(solution)/shard_map/ppermute | solution.py:480
  50.4 9.9 %collective-permute-start.22 = (bf16[128,768]{1,0:T(8,128)(2,1)S(1)}, bf16[128,768]{1,0:T(8,128)(2,1)S(1)}, u32[]{:S(2)}, u32[]{:S(2)}) collective-permute-start(bf16[128,768]{1,0:T(8,128)(2,1)S(1)} %once.9), channel_id=1, source_target_pairs={{0,0},{1,16},{2,8},{3,24},{4,4},{5,20},{6,12},{7,28},{8,2},{9,18},... | collective-permute-start | bytes 589832 | tf_op jit(solution)/shard_map/ppermute | solution.py:480
  57.9 9.8 %collective-permute-start.21 = (bf16[128,768]{1,0:T(8,128)(2,1)S(1)}, bf16[128,768]{1,0:T(8,128)(2,1)S(1)}, u32[]{:S(2)}, u32[]{:S(2)}) collective-permute-start(bf16[128,768]{1,0:T(8,128)(2,1)S(1)} %get-tuple-element.137), channel_id=1, source_target_pairs={{0,2},{1,3},{2,0},{3,1},{4,6},{5,7},{6,4},{7,5},{8,10},{9,11},{10,... | collective-permute-start | bytes 589832 | tf_op jit(solution)/shard_map/ppermute | solution.py:480
  59.7 12.2 %collective-permute-start.20 = (bf16[128,768]{1,0:T(8,128)(2,1)S(1)}, bf16[128,768]{1,0:T(8,128)(2,1)S(1)}, u32[]{:S(2)}, u32[]{:S(2)}) collective-permute-start(bf16[128,768]{1,0:T(8,128)(2,1)S(1)} %get-tuple-element.136.refs_7_), channel_id=1, source_target_pairs={{0,2},{1,3},{2,0},{3,1},{4,6},{5,7},{6,4},{7,5},{8,10},{9,11},{10,... | collective-permute-start | bytes 589832 | tf_op jit(solution)/shard_map/ppermute | solution.py:480
  73.7 6.5 %collective-permute-start.29 = (bf16[768,768]{1,0:T(8,128)(2,1)S(1)}, bf16[768,768]{1,0:T(8,128)(2,1)S(1)}, u32[]{:S(2)}, u32[]{:S(2)}) collective-permute-start(bf16[768,768]{1,0:T(8,128)(2,1)S(1)} %get-tuple-element.143.refs_5_), channel_id=1, source_target_pairs={{0,1},{1,0},{2,3},{3,2},{4,5},{5,4},{6,7},{7,6},{8,9},{9,8},{10,11... | collective-permute-start | bytes 3538952 | tf_op jit(solution)/shard_map/ppermute | solution.py:480
  75.6 15.4 %collective-permute-start.24 = (bf16[256,768]{1,0:T(8,128)(2,1)S(1)}, bf16[256,768]{1,0:T(8,128)(2,1)S(1)}, u32[]{:S(2)}, u32[]{:S(2)}) collective-permute-start(bf16[256,768]{1,0:T(8,128)(2,1)S(1)} %get-tuple-element.145.refs_2_), channel_id=1, source_target_pairs={{0,2},{1,3},{2,0},{3,1},{4,6},{5,7},{6,4},{7,5},{8,10},{9,11},{10,... | collective-permute-start | bytes 1179656 | tf_op jit(solution)/shard_map/ppermute | solution.py:480
  79.4 1.7 collective-permute-start.26
  79.7 2.3 %collective-permute-start.27 = (bf16[192,768]{1,0:T(8,128)(2,1)S(1)}, bf16[192,768]{1,0:T(8,128)(2,1)S(1)}, u32[]{:S(2)}, u32[]{:S(2)}) collective-permute-start(bf16[192,768]{1,0:T(8,128)(2,1)S(1)} %get-tuple-element.158), channel_id=1, source_target_pairs={{0,1},{1,0},{2,3},{3,2},{4,5},{5,4},{6,7},{7,6},{8,9},{9,8},{10,11... | collective-permute-start | bytes 884744 | tf_op jit(solution)/shard_map/ppermute | solution.py:480
  80.0 2.4 %collective-permute-start.28 = (bf16[192,768]{1,0:T(8,128)(2,1)S(1)}, bf16[192,768]{1,0:T(8,128)(2,1)S(1)}, u32[]{:S(2)}, u32[]{:S(2)}) collective-permute-start(bf16[192,768]{1,0:T(8,128)(2,1)S(1)} %get-tuple-element.159), channel_id=1, source_target_pairs={{0,1},{1,0},{2,3},{3,2},{4,5},{5,4},{6,7},{7,6},{8,9},{9,8},{10,11... | collective-permute-start | bytes 884744 | tf_op jit(solution)/shard_map/ppermute | solution.py:480
  80.2 3.9 %collective-permute-start.25 = (bf16[192,768]{1,0:T(8,128)(2,1)S(1)}, bf16[192,768]{1,0:T(8,128)(2,1)S(1)}, u32[]{:S(2)}, u32[]{:S(2)}) collective-permute-start(bf16[192,768]{1,0:T(8,128)(2,1)S(1)} %get-tuple-element.156.refs_2_), channel_id=1, source_target_pairs={{0,1},{1,0},{2,3},{3,2},{4,5},{5,4},{6,7},{7,6},{8,9},{9,8},{10,11... | collective-permute-start | bytes 884744 | tf_op jit(solution)/shard_map/ppermute | solution.py:480
  81.1 15.3 %collective-permute-start.30 = (bf16[128,768]{1,0:T(8,128)(2,1)S(1)}, bf16[128,768]{1,0:T(8,128)(2,1)S(1)}, u32[]{:S(2)}, u32[]{:S(2)}) collective-permute-start(bf16[128,768]{1,0:T(8,128)(2,1)S(1)} %get-tuple-element.170), channel_id=1, source_target_pairs={{0,0},{1,16},{2,8},{3,24},{4,4},{5,20},{6,12},{7,28},{8,2},{9,18},... | collective-permute-start | bytes 589832 | tf_op jit(solution)/shard_map/ppermute | solution.py:480
  82.0 14.1 %collective-permute-start.32 = (bf16[192,768]{1,0:T(8,128)(2,1)S(1)}, bf16[192,768]{1,0:T(8,128)(2,1)S(1)}, u32[]{:S(2)}, u32[]{:S(2)}) collective-permute-start(bf16[192,768]{1,0:T(8,128)(2,1)S(1)} %get-tuple-element.172), channel_id=1, source_target_pairs={{0,4},{1,5},{2,6},{3,7},{4,0},{5,1},{6,2},{7,3},{8,12},{9,13},{10,... | collective-permute-start | bytes 884744 | tf_op jit(solution)/shard_map/ppermute | solution.py:480
  82.4 13.7 %collective-permute-start.31 = (bf16[192,768]{1,0:T(8,128)(2,1)S(1)}, bf16[192,768]{1,0:T(8,128)(2,1)S(1)}, u32[]{:S(2)}, u32[]{:S(2)}) collective-permute-start(bf16[192,768]{1,0:T(8,128)(2,1)S(1)} %get-tuple-element.161.refs_5_), channel_id=1, source_target_pairs={{0,4},{1,5},{2,6},{3,7},{4,0},{5,1},{6,2},{7,3},{8,12},{9,13},{10,... | collective-permute-start | bytes 884744 | tf_op jit(solution)/shard_map/ppermute | solution.py:480
  84.6 20.5 %collective-permute-start.37 = (bf16[384,768]{1,0:T(8,128)(2,1)S(1)}, bf16[384,768]{1,0:T(8,128)(2,1)S(1)}, u32[]{:S(2)}, u32[]{:S(2)}) collective-permute-start(bf16[384,768]{1,0:T(8,128)(2,1)S(1)} %get-tuple-element.162.refs_13_), channel_id=1, source_target_pairs={{0,8},{1,9},{2,10},{3,11},{4,12},{5,13},{6,14},{7,15},{8,0},{9,1},... | collective-permute-start | bytes 1769480 | tf_op jit(solution)/shard_map/ppermute | solution.py:480
  99.0 5.6 %collective-permute-start.35 = (bf16[528,384]{1,0:T(8,128)(2,1)S(1)}, bf16[528,384]{1,0:T(8,128)(2,1)S(1)}, u32[]{:S(2)}, u32[]{:S(2)}) collective-permute-start(bf16[528,384]{1,0:T(8,128)(2,1)S(1)} %get-tuple-element.177), channel_id=1, source_target_pairs={{0,1},{1,0},{2,3},{3,2},{4,5},{5,4},{6,7},{7,6},{8,9},{9,8},{10,11... | collective-permute-start | bytes 1216520 | tf_op jit(solution)/shard_map/ppermute | solution.py:480
  101.3 3.2 %collective-permute-start.34 = (bf16[512,384]{1,0:T(8,128)(2,1)S(1)}, bf16[512,384]{1,0:T(8,128)(2,1)S(1)}, u32[]{:S(2)}, u32[]{:S(2)}) collective-permute-start(bf16[512,384]{1,0:T(8,128)(2,1)S(1)} %get-tuple-element.176), channel_id=1, source_target_pairs={{0,1},{1,0},{2,3},{3,2},{4,5},{5,4},{6,7},{7,6},{8,9},{9,8},{10,11... | collective-permute-start | bytes 1179656 | tf_op jit(solution)/shard_map/ppermute | solution.py:480
  101.4 3.2 %collective-permute-start.33 = (bf16[512,384]{1,0:T(8,128)(2,1)S(1)}, bf16[512,384]{1,0:T(8,128)(2,1)S(1)}, u32[]{:S(2)}, u32[]{:S(2)}) collective-permute-start(bf16[512,384]{1,0:T(8,128)(2,1)S(1)} %get-tuple-element.175.refs_4_), channel_id=1, source_target_pairs={{0,1},{1,0},{2,3},{3,2},{4,5},{5,4},{6,7},{7,6},{8,9},{9,8},{10,11... | collective-permute-start | bytes 1179656 | tf_op jit(solution)/shard_map/ppermute | solution.py:480
  101.8 10.0 %collective-permute-start.41 = (bf16[192,768]{1,0:T(8,128)(2,1)S(1)}, bf16[192,768]{1,0:T(8,128)(2,1)S(1)}, u32[]{:S(2)}, u32[]{:S(2)}) collective-permute-start(bf16[192,768]{1,0:T(8,128)(2,1)S(1)} %get-tuple-element.173.refs_10_), channel_id=1, source_target_pairs={{0,8},{1,9},{2,10},{3,11},{4,12},{5,13},{6,14},{7,15},{8,0},{9,1},... | collective-permute-start | bytes 884744 | tf_op jit(solution)/shard_map/ppermute | solution.py:480
  107.2 10.6 %collective-permute-start.40 = (bf16[256,768]{1,0:T(8,128)(2,1)S(1)}, bf16[256,768]{1,0:T(8,128)(2,1)S(1)}, u32[]{:S(2)}, u32[]{:S(2)}) collective-permute-start(bf16[256,768]{1,0:T(8,128)(2,1)S(1)} %get-tuple-element.185), channel_id=1, source_target_pairs={{0,1},{1,0},{2,3},{3,2},{4,5},{5,4},{6,7},{7,6},{8,9},{9,8},{10,11... | collective-permute-start | bytes 1179656 | tf_op jit(solution)/shard_map/ppermute | solution.py:480
  107.3 10.5 %collective-permute-start.39 = (bf16[256,768]{1,0:T(8,128)(2,1)S(1)}, bf16[256,768]{1,0:T(8,128)(2,1)S(1)}, u32[]{:S(2)}, u32[]{:S(2)}) collective-permute-start(bf16[256,768]{1,0:T(8,128)(2,1)S(1)} %get-tuple-element.184.refs_2_), channel_id=1, source_target_pairs={{0,1},{1,0},{2,3},{3,2},{4,5},{5,4},{6,7},{7,6},{8,9},{9,8},{10,11... | collective-permute-start | bytes 1179656 | tf_op jit(solution)/shard_map/ppermute | solution.py:480
  107.8 21.3 %collective-permute-start.38 = (bf16[192,768]{1,0:T(8,128)(2,1)S(1)}, bf16[192,768]{1,0:T(8,128)(2,1)S(1)}, u32[]{:S(2)}, u32[]{:S(2)}) collective-permute-start(bf16[192,768]{1,0:T(8,128)(2,1)S(1)} %get-tuple-element.182.refs_3_), channel_id=1, source_target_pairs={{0,16},{1,17},{2,18},{3,19},{4,20},{5,21},{6,22},{7,23},{8,24},{9,... | collective-permute-start | bytes 884744 | tf_op jit(solution)/shard_map/ppermute | solution.py:480
  111.9 19.9 %collective-permute-start.44 = (bf16[96,768]{1,0:T(8,128)(2,1)S(1)}, bf16[96,768]{1,0:T(8,128)(2,1)S(1)}, u32[]{:S(2)}, u32[]{:S(2)}) collective-permute-start(bf16[96,768]{1,0:T(8,128)(2,1)S(1)} %get-tuple-element.187.refs_3_), channel_id=1, source_target_pairs={{0,16},{1,17},{2,18},{3,19},{4,20},{5,21},{6,22},{7,23},{8,24},{9,... | collective-permute-start | bytes 442376 | tf_op jit(solution)/shard_map/ppermute | solution.py:480
  116.3 18.1 %collective-permute-start.36 = (bf16[784,384]{1,0:T(8,128)(2,1)S(1)}, bf16[784,384]{1,0:T(8,128)(2,1)S(1)}, u32[]{:S(2)}, u32[]{:S(2)}) collective-permute-start(bf16[784,384]{1,0:T(8,128)(2,1)S(1)} %get-tuple-element.179.refs_2_), channel_id=1, source_target_pairs={{0,4},{1,5},{2,6},{3,7},{4,0},{5,1},{6,2},{7,3},{8,12},{9,13},{10,... | collective-permute-start | bytes 1806344 | tf_op jit(solution)/shard_map/ppermute | solution.py:480
  118.3 13.5 %collective-permute-start.43 = (bf16[256,768]{1,0:T(8,128)(2,1)S(1)}, bf16[256,768]{1,0:T(8,128)(2,1)S(1)}, u32[]{:S(2)}, u32[]{:S(2)}) collective-permute-start(bf16[256,768]{1,0:T(8,128)(2,1)S(1)} %get-tuple-element.188.refs_2_), channel_id=1, source_target_pairs={{0,2},{1,3},{2,0},{3,1},{4,6},{5,7},{6,4},{7,5},{8,10},{9,11},{10,... | collective-permute-start | bytes 1179656 | tf_op jit(solution)/shard_map/ppermute | solution.py:480
  129.2 5.2 %collective-permute-start.42 = (bf16[96,768]{1,0:T(8,128)(2,1)S(1)}, bf16[96,768]{1,0:T(8,128)(2,1)S(1)}, u32[]{:S(2)}, u32[]{:S(2)}) collective-permute-start(bf16[96,768]{1,0:T(8,128)(2,1)S(1)} %get-tuple-element.190.refs_2_), channel_id=1, source_target_pairs={{0,4},{1,5},{2,6},{3,7},{4,0},{5,1},{6,2},{7,3},{8,12},{9,13},{10,... | collective-permute-start | bytes 442376 | tf_op jit(solution)/shard_map/ppermute | solution.py:480
  134.6 11.9 %collective-permute-start.45 = (bf16[400,384]{1,0:T(8,128)(2,1)S(1)}, bf16[400,384]{1,0:T(8,128)(2,1)S(1)}, u32[]{:S(2)}, u32[]{:S(2)}) collective-permute-start(bf16[400,384]{1,0:T(8,128)(2,1)S(1)} %get-tuple-element.196.refs_2_), channel_id=1, source_target_pairs={{0,8},{1,9},{2,10},{3,11},{4,12},{5,13},{6,14},{7,15},{8,0},{9,1},... | collective-permute-start | bytes 921608 | tf_op jit(solution)/shard_map/ppermute | solution.py:480
  136.2 10.2 %collective-permute-start.46 = (bf16[96,768]{1,0:T(8,128)(2,1)S(1)}, bf16[96,768]{1,0:T(8,128)(2,1)S(1)}, u32[]{:S(2)}, u32[]{:S(2)}) collective-permute-start(bf16[96,768]{1,0:T(8,128)(2,1)S(1)} %down_sum.1.refs_2_.refs_0_), channel_id=1, source_target_pairs={{0,16},{1,17},{2,18},{3,19},{4,20},{5,21},{6,22},{7,23},{8,24},{9,... | collective-permute-start | bytes 442376 | tf_op jit(solution)/shard_map/ppermute | solution.py:480
  138.0 12.0 %collective-permute-start.49 = (bf16[48,768]{1,0:T(8,128)(2,1)S(1)}, bf16[48,768]{1,0:T(8,128)(2,1)S(1)}, u32[]{:S(2)}, u32[]{:S(2)}) collective-permute-start(bf16[48,768]{1,0:T(8,128)(2,1)S(1)} %get-tuple-element.194.refs_2_), channel_id=1, source_target_pairs={{0,2},{1,3},{2,0},{3,1},{4,6},{5,7},{6,4},{7,5},{8,10},{9,11},{10,... | collective-permute-start | bytes 221192 | tf_op jit(solution)/shard_map/ppermute | solution.py:480
  139.0 24.0 %collective-permute-start.51 = (bf16[128,768]{1,0:T(8,128)(2,1)S(1)}, bf16[128,768]{1,0:T(8,128)(2,1)S(1)}, u32[]{:S(2)}, u32[]{:S(2)}) collective-permute-start(bf16[128,768]{1,0:T(8,128)(2,1)S(1)} %get-tuple-element.193.refs_2_), channel_id=1, source_target_pairs={{0,4},{1,5},{2,6},{3,7},{4,0},{5,1},{6,2},{7,3},{8,12},{9,13},{10,... | collective-permute-start | bytes 589832 | tf_op jit(solution)/shard_map/ppermute | solution.py:480
  146.4 12.2 %collective-permute-start.48 = (bf16[192,768]{1,0:T(8,128)(2,1)S(1)}, bf16[192,768]{1,0:T(8,128)(2,1)S(1)}, u32[]{:S(2)}, u32[]{:S(2)}) collective-permute-start(bf16[192,768]{1,0:T(8,128)(2,1)S(1)} %down_join.1.refs_2_.refs_0_), channel_id=1, source_target_pairs={{0,8},{1,9},{2,10},{3,11},{4,12},{5,13},{6,14},{7,15},{8,0},{9,1},... | collective-permute-start | bytes 884744 | tf_op jit(solution)/shard_map/ppermute | solution.py:480
  146.7 13.4 %collective-permute-start.47 = (bf16[208,384]{1,0:T(8,128)(2,1)S(1)}, bf16[208,384]{1,0:T(8,128)(2,1)S(1)}, u32[]{:S(2)}, u32[]{:S(2)}) collective-permute-start(bf16[208,384]{1,0:T(8,128)(2,1)S(1)} %get-tuple-element.198.refs_2_), channel_id=1, source_target_pairs={{0,16},{1,17},{2,18},{3,19},{4,20},{5,21},{6,22},{7,23},{8,24},{9,... | collective-permute-start | bytes 479240 | tf_op jit(solution)/shard_map/ppermute | solution.py:480
  150.0 13.0 %collective-permute-start.52 = (bf16[96,768]{1,0:T(8,128)(2,1)S(1)}, bf16[96,768]{1,0:T(8,128)(2,1)S(1)}, u32[]{:S(2)}, u32[]{:S(2)}) collective-permute-start(bf16[96,768]{1,0:T(8,128)(2,1)S(1)} %up_join.1.refs_2_.refs_0_), channel_id=1, source_target_pairs={{0,16},{1,17},{2,18},{3,19},{4,20},{5,21},{6,22},{7,23},{8,24},{9,... | collective-permute-start | bytes 442376 | tf_op jit(solution)/shard_map/ppermute | solution.py:480
  158.6 14.4 %collective-permute-start.56 = (bf16[384,768]{1,0:T(8,128)(2,1)S(1)}, bf16[384,768]{1,0:T(8,128)(2,1)S(1)}, u32[]{:S(2)}, u32[]{:S(2)}) collective-permute-start(bf16[384,768]{1,0:T(8,128)(2,1)S(1)} %down_join_near.1.refs_2_.refs_0_), channel_id=1, source_target_pairs={{0,4},{1,5},{2,6},{3,7},{4,0},{5,1},{6,2},{7,3},{8,12},{9,13},{10,... | collective-permute-start | bytes 1769480 | tf_op jit(solution)/shard_map/ppermute | solution.py:480
  160.8 4.2 %collective-permute-start.50 = (bf16[72,384]{1,0:T(8,128)(2,1)S(1)}, bf16[72,384]{1,0:T(8,128)(2,1)S(1)}, u32[]{:S(2)}, u32[]{:S(2)}) collective-permute-start(bf16[72,384]{1,0:T(8,128)(2,1)S(1)} %get-tuple-element.201.refs_2_), channel_id=1, source_target_pairs={{0,2},{1,3},{2,0},{3,1},{4,6},{5,7},{6,4},{7,5},{8,10},{9,11},{10,... | collective-permute-start | bytes 165896 | tf_op jit(solution)/shard_map/ppermute | solution.py:480
  164.9 7.6 %collective-permute-start.53 = (bf16[192,384]{1,0:T(8,128)(2,1)S(1)}, bf16[192,384]{1,0:T(8,128)(2,1)S(1)}, u32[]{:S(2)}, u32[]{:S(2)}) collective-permute-start(bf16[192,384]{1,0:T(8,128)(2,1)S(1)} %rest_join.1.refs_0_.refs_2_), channel_id=1, source_target_pairs={{0,16},{1,17},{2,18},{3,19},{4,20},{5,21},{6,22},{7,23},{8,24},{9,... | collective-permute-start | bytes 442376 | tf_op jit(solution)/shard_map/ppermute | solution.py:480
  165.0 10.0 %collective-permute-start.55 = (bf16[192,768]{1,0:T(8,128)(2,1)S(1)}, bf16[192,768]{1,0:T(8,128)(2,1)S(1)}, u32[]{:S(2)}, u32[]{:S(2)}) collective-permute-start(bf16[192,768]{1,0:T(8,128)(2,1)S(1)} %up_join_far.1.refs_3_.refs_0_), channel_id=1, source_target_pairs={{0,8},{1,9},{2,10},{3,11},{4,12},{5,13},{6,14},{7,15},{8,0},{9,1},... | collective-permute-start | bytes 884744 | tf_op jit(solution)/shard_map/ppermute | solution.py:480
  172.6 6.8 %collective-permute-start.54 = (bf16[384,384]{1,0:T(8,128)(2,1)S(1)}, bf16[384,384]{1,0:T(8,128)(2,1)S(1)}, u32[]{:S(2)}, u32[]{:S(2)}) collective-permute-start(bf16[384,384]{1,0:T(8,128)(2,1)S(1)} %rest_join_far.1.refs_2_.refs_0_), channel_id=1, source_target_pairs={{0,8},{1,9},{2,10},{3,11},{4,12},{5,13},{6,14},{7,15},{8,0},{9,1},... | collective-permute-start | bytes 884744 | tf_op jit(solution)/shard_map/ppermute | solution.py:480
  175.1 13.2 %collective-permute-start.59 = (bf16[384,768]{1,0:T(8,128)(2,1)S(1)}, bf16[384,768]{1,0:T(8,128)(2,1)S(1)}, u32[]{:S(2)}, u32[]{:S(2)}) collective-permute-start(bf16[384,768]{1,0:T(8,128)(2,1)S(1)} %up_join_near.1.refs_2_.refs_0_), channel_id=1, source_target_pairs={{0,4},{1,5},{2,6},{3,7},{4,0},{5,1},{6,2},{7,3},{8,12},{9,13},{10,... | collective-permute-start | bytes 1769480 | tf_op jit(solution)/shard_map/ppermute | solution.py:480
  179.5 15.1 %collective-permute-start.57 = (bf16[768,384]{1,0:T(8,128)(2,1)S(1)}, bf16[768,384]{1,0:T(8,128)(2,1)S(1)}, u32[]{:S(2)}, u32[]{:S(2)}) collective-permute-start(bf16[768,384]{1,0:T(8,128)(2,1)S(1)} %rest_join_near.1.refs_2_.refs_0_), channel_id=1, source_target_pairs={{0,4},{1,5},{2,6},{3,7},{4,0},{5,1},{6,2},{7,3},{8,12},{9,13},{10,... | collective-permute-start | bytes 1769480 | tf_op jit(solution)/shard_map/ppermute | solution.py:480
  179.6 10.2 %collective-permute-start.58 = (bf16[128,768]{1,0:T(8,128)(2,1)S(1)}, bf16[128,768]{1,0:T(8,128)(2,1)S(1)}, u32[]{:S(2)}, u32[]{:S(2)}) collective-permute-start(bf16[128,768]{1,0:T(8,128)(2,1)S(1)} %input_sum.1.refs_2_), channel_id=1, source_target_pairs={{0,0},{1,16},{2,8},{3,24},{4,4},{5,20},{6,12},{7,28},{8,2},{9,18},... | collective-permute-start | bytes 589832 | tf_op jit(solution)/shard_map/ppermute | solution.py:480
